TPU v7x, 256 devices: a whole 4x4x8 slice. The times are simulated.
256 devices in a mesh: prow: 32 (over z_hi, y, x), pcol: 8 (over z_lo, core).
Axes of the slice: x: 4, y: 4, z: 8 (z_hi: 2, z_lo: 4; z = z_hi * 4 + z_lo), core: 2. Of those that a mesh axis runs over, the one named last changes fastest.
Arguments:
- eigen_rows: float32 [1024, 229376], P(('pcol', 'prow')), may hold values from -6 to 6
- reflectors: float32 [229376, 512], P('prow', 'pcol'), may hold values from -0.375 to 0.375
- tfactors: float32 [2, 256, 256], replicated, may hold values from -0.01171875 to 0.01171875
Outputs:
- back_rows: float32 [1024, 229376], P('pcol', 'prow')
All inputs are finite; a program needn't handle non-finite values.
Results may differ from a plain program's by a relative error of at most 0.000084.
Values sent between devices are 32-bit elements; how exact they have to be, the bound alone decides.
No kernel may reach another device: no remote copies, remote signals or barrier semaphores. Data moves between devices by JAX's collectives and lax.ppermute only.
A program may use at most 128 MiB of HBM per device.

v0:
```python
import functools

import jax
import jax.numpy as jnp
from jax import lax
from jax.experimental import pallas as pl
from jax.experimental.pallas import tpu as pltpu
from jax.sharding import PartitionSpec as P

UP_ONE = [(c, c + 2) for c in range(6)]
DOWN_ONE = [(c, c - 2) for c in range(2, 8)]
UP_TWO = [(c, c + 2) for c in range(2, 6)]
DOWN_TWO = [(c, c - 2) for c in range(2, 6)]
UP_END = [(4, 6), (5, 7)]
DOWN_END = [(2, 0), (3, 1)]
SIBLING = [(c, c ^ 1) for c in range(8)]
FAR = [(r, (r + 16) % 32) for r in range(32)]
PLANES = [list(range(16)), list(range(16, 32))]


def along_x(step):
    return [(r, r // 4 * 4 + (r + step) % 4) for r in range(32)]


def along_y(step):
    return [(r, r // 16 * 16 + (r + 4 * step) % 16) for r in range(32)]


def upper_part(square):
    width = square.shape[0]
    rows = lax.broadcasted_iota(jnp.int32, (width, width), 0)
    cols = lax.broadcasted_iota(jnp.int32, (width, width), 1)
    return jnp.where(cols >= rows, square, jnp.zeros_like(square))


def matmul(left, right, precision=lax.Precision.HIGHEST):
    return jnp.dot(left, right, precision=precision, preferred_element_type=jnp.float32)


def matmul_nt(left, right):
    return lax.dot_general(
        left, right, (((1,), (1,)), ((), ())),
        precision=lax.Precision.HIGH, preferred_element_type=jnp.float32,
    )


def sum_over_prow(values):
    x = lax.axis_index("prow") % 4

    def send(value, pairs):
        return lax.ppermute(value, "prow", pairs)

    def quarter(step):
        return lax.dynamic_index_in_dim(values, (x + step) % 4, 0, keepdims=False)

    total = quarter(0)
    for step in (1, 2, 3):
        total = total + send(quarter(step), along_x(step))
    total = total + send(total, along_y(1)) + send(total, along_y(2)) + send(total, along_y(3))
    far = send(total, FAR)
    total = total + jnp.concatenate([far[64:128], far[:64], far[128:]], axis=0)
    return jnp.stack([total, *(send(total, along_x(4 - step)) for step in (1, 2, 3))])


def turned(parts, start):
    return lax.dynamic_slice_in_dim(jnp.concatenate([parts, parts], axis=0), start % 4, 4, 0)


def split(value):
    high = lax.reduce_precision(value, 8, 7)
    return high.astype(jnp.bfloat16), (value - high).astype(jnp.bfloat16)


def update_kernel(half_ref, rows_ref, scaled_ref, *refs):
    out_ref = refs[-1]
    high = [ref[...] for ref in refs[:4]]
    low = [ref[...] for ref in refs[4:8]]
    count = rows_ref.shape[0]
    dot = functools.partial(jnp.dot, preferred_element_type=jnp.float32)
    change = None
    for pair in (0, 1):
        columns = slice(256 * pair, 256 * pair + 256)
        left = scaled_ref[:, columns]
        both = dot(left, jnp.concatenate(high[2 * pair : 2 * pair + 2], axis=0))
        part = both[:count] + both[count:]
        part = part + dot(left[:count], jnp.concatenate(low[2 * pair : 2 * pair + 2], axis=0))
        change = part if change is None else change + part
    result = rows_ref[...] - change
    mid = count // 2
    here = pl.multiple_of(half_ref[0] * mid, mid)
    there = pl.multiple_of((1 - half_ref[0]) * mid, mid)
    out_ref[pl.ds(here, mid), :] = result[:mid]
    out_ref[pl.ds(there, mid), :] = result[mid:]


def update(half, rows, scaled, high, low):
    count, length = rows.shape
    tile = 1024
    block = pl.BlockSpec((128, tile), lambda i, h: (0, i))
    return pl.pallas_call(
        update_kernel,
        out_shape=jax.ShapeDtypeStruct(rows.shape, jnp.float32),
        grid_spec=pltpu.PrefetchScalarGridSpec(
            num_scalar_prefetch=1,
            grid=(length // tile,),
            in_specs=[
                pl.BlockSpec((count, tile), lambda i, h: (0, i)),
                pl.BlockSpec(scaled.shape, lambda i, h: (0, 0)),
                *[block] * 8,
            ],
            out_specs=pl.BlockSpec((count, tile), lambda i, h: (0, i)),
        ),
        compiler_params=pltpu.CompilerParams(vmem_limit_bytes=32 * 1024 * 1024),
        cost_estimate=pl.CostEstimate(
            flops=6 * count * 512 * length, bytes_accessed=length * (512 * 4 + count * 8), transcendentals=0
        ),
    )(half.reshape(1), rows, scaled, *high, *low)


def body(eigen_rows, reflectors, tfactors):
    count = eigen_rows.shape[0]
    prow = lax.axis_index("prow")
    x, half = prow % 4, prow // 16
    column = lax.axis_index("pcol")
    chip, core = column // 2, column % 2
    length = reflectors.shape[0]
    mine = reflectors.T

    def send(value, pairs):
        return lax.ppermute(value, "pcol", pairs)

    def ordered(piece, other, axis):
        return jnp.concatenate(
            [jnp.where(core == 0, piece, other), jnp.where(core == 0, other, piece)], axis=axis
        )

    def both_cores(piece):
        return ordered(piece, send(piece, SIBLING), 0)

    blocks = eigen_rows.reshape(count, 32, length).transpose(1, 0, 2)
    leaving = lax.dynamic_slice_in_dim(blocks, (1 - half) * 16, 16, 0)
    staying = lax.dynamic_slice_in_dim(blocks, half * 16, 16, 0)
    mine, leaving = lax.optimization_barrier((mine, leaving))
    arriving = lax.ppermute(leaving, "prow", FAR)
    below = send(mine, UP_ONE)
    above = send(mine, DOWN_ONE)

    def over_plane(value):
        value = lax.all_to_all(
            value, "prow", split_axis=0, concat_axis=0, tiled=True, axis_index_groups=PLANES
        )
        return value.reshape(16 * count, length)

    staying = over_plane(staying)
    below_two = send(below, UP_TWO)
    above_two = send(above, DOWN_TWO)
    arriving, below_two, above_two = lax.optimization_barrier((arriving, below_two, above_two))
    below_end = send(below_two, UP_END)
    above_end = send(above_two, DOWN_END)
    arriving = over_plane(arriving)
    rows = jnp.concatenate([staying, arriving], axis=0)
    two = below_two + above_two

    all_mine, all_below, all_above, all_two = (
        both_cores(piece) for piece in (mine, below, above, two)
    )

    left = jnp.where(chip == 0, two, jnp.where(chip == 3, mine, above))
    right = jnp.where(chip == 0, all_above, jnp.where(chip == 1, all_below, all_two))
    cross = matmul_nt(left, right)
    on_mine, on_two = matmul_nt(rows, all_mine), matmul_nt(rows, all_two)
    on_above, on_below = matmul_nt(rows, all_above), matmul_nt(rows, all_below)
    below_end, above_end, cross, on_mine, on_two, on_above, on_below = lax.optimization_barrier(
        (below_end, above_end, cross, on_mine, on_two, on_above, on_below)
    )

    last = below_end + above_end
    last_other = send(last, SIBLING)
    zero = jnp.zeros_like
    on_last = ordered(matmul_nt(rows, last), matmul_nt(rows, last_other), 1)
    slots = jnp.stack(
        [
            on_mine,
            on_above + jnp.where(chip == 3, on_last, zero(on_last)),
            on_two,
            on_below + jnp.where(chip == 0, on_last, zero(on_last)),
        ]
    )
    summed = sum_over_prow(jnp.concatenate([slots, cross.reshape(4, 16, 128)], axis=1))
    cross = turned(summed[:, 128:], 4 - x).reshape(64, 128)
    cross = lax.all_to_all(
        jnp.broadcast_to(cross, (8, *cross.shape)), "pcol", split_axis=0, concat_axis=0, tiled=True
    ).reshape(4, 128, 128)
    cross = jnp.concatenate(
        [
            jnp.concatenate([cross[1], cross[0]], axis=1),
            jnp.concatenate([cross[2], cross[3]], axis=1),
        ],
        axis=0,
    )
    projected = turned(summed[:, :128], 8 - chip - x)
    first = jnp.concatenate([projected[0], projected[1]], axis=1)
    second = jnp.concatenate([projected[2], projected[3]], axis=1)
    scaled_second = matmul(second, upper_part(tfactors[1]).T)
    scaled_first = matmul(first - matmul(scaled_second, cross), upper_part(tfactors[0]).T)
    scaled = jnp.stack(
        [scaled_first[:, :128], scaled_first[:, 128:], scaled_second[:, :128], scaled_second[:, 128:]]
    )
    scaled = turned(scaled, chip)
    scaled = jnp.concatenate([scaled[j] for j in range(4)], axis=1)
    scaled = jnp.concatenate(split(scaled), axis=0)

    all_last = ordered(last, last_other, 0)
    at_above = all_above + jnp.where(chip == 3, all_last, zero(all_last))
    at_below = all_below + jnp.where(chip == 0, all_last, zero(all_last))
    high, low = zip(*(split(piece) for piece in (all_mine, at_above, all_two, at_below)))
    return update(half, rows, scaled, high, low)


def solution(mesh):
    return jax.shard_map(
        body,
        mesh=mesh,
        in_specs=(P(("pcol", "prow"), None), P("prow", "pcol"), P()),
        out_specs=P("pcol", "prow"),
        check_vma=False,
    )
```

profile of v0, /device:TPU:2, one launch (start us, length us, event | category | flops | bytes accessed | tf_op | source)
XLA Modules:
  0.0 313.5 jit_solution(14762552130366874943)
XLA Ops:
  0.0 4.3 %dynamic-slice_bitcast_fusion = (f32[16,4,7168]{2,1,0:T(4,128)}, f32[16,4,7168]{2,1,0:T(4,128)}) fusion(f32[4,32,7168]{2,0,1:T(4,128)} %bitcast.97, s32[]{:T(128)S(6)} %select_n.191, s32[]{:T(128)S(6)} %select_n.190), kind=kLoop, calls=%fused_computation.27 | loop fusion | bytes 7340040 | tf_op jit(solution)/shard_map/dynamic_slice | solution.py:141
  4.3 5.1 %collective-permute-start.1 = (f32[64,7168]{1,0:T(8,128)S(1)}, f32[64,7168]{1,0:T(8,128)}, u32[]{:S(2)}, u32[]{:S(2)}) collective-permute-start(f32[64,7168]{1,0:T(8,128)S(1)} %bitcast.92), channel_id=1, source_target_pairs={{0,2},{1,3},{2,4},{3,5},{4,6},{5,7},{8,10},{9,11},{10,12},{11,13},... | collective-permute-start | bytes 5505032 | tf_op jit(solution)/shard_map/ppermute | solution.py:130
  10.6 7.5 %all-to-all-start = ((f32[16,4,7168]{2,1,0:T(4,128)}), f32[16,4,7168]{2,1,0:T(4,128)}, u32[]{:S(2)}, u32[]{:S(2)}) async-start(f32[16,4,7168]{2,1,0:T(4,128)} %get-tuple-element.50), calls=%async_computation | async-start | bytes 3670016 | tf_op jit(solution)/shard_map/all_to_all | solution.py:149
  18.1 6.4 %collective-permute-start = (f32[16,4,7168]{2,1,0:T(4,128)}, f32[16,4,7168]{2,1,0:T(4,128)}, u32[]{:S(2)}, u32[]{:S(2)}) collective-permute-start(f32[16,4,7168]{2,1,0:T(4,128)} %get-tuple-element.17), channel_id=1, source_target_pairs={{0,128},{8,136},{16,144},{24,152},{32,160},{40,168},{48,176},{56,1... | collective-permute-start | bytes 5505032 | tf_op jit(solution)/shard_map/ppermute | solution.py:144
  24.5 17.8 %all-to-all-done = f32[16,4,7168]{2,1,0:T(4,128)} async-done(((f32[16,4,7168]{2,1,0:T(4,128)}), f32[16,4,7168]{2,1,0:T(4,128)}, u32[]{:S(2)}, u32[]{:S(2)}) %all-to-all-start) | async-done | bytes 1835040 | tf_op jit(solution)/shard_map/all_to_all | solution.py:149
  42.2 2.9 reshape.29
  45.2 3.3 %collective-permute-done.1 = f32[64,7168]{1,0:T(8,128)} collective-permute-done((f32[64,7168]{1,0:T(8,128)S(1)}, f32[64,7168]{1,0:T(8,128)}, u32[]{:S(2)}, u32[]{:S(2)}) %collective-permute-start.1) | collective-permute-done | bytes 1835040 | tf_op jit(solution)/shard_map/ppermute | solution.py:130
  48.5 2.0 collective-permute-start.2
  50.5 5.2 %collective-permute-done.3 = f32[64,7168]{1,0:T(8,128)} collective-permute-done((f32[64,7168]{1,0:T(8,128)S(1)}, f32[64,7168]{1,0:T(8,128)}, u32[]{:S(2)}, u32[]{:S(2)}) %collective-permute-start.3) | collective-permute-done | bytes 1835040 | tf_op jit(solution)/shard_map/ppermute | solution.py:130
  57.0 2.9 constant_dynamic-update-slice_fusion.1
  59.8 3.7 %broadcast_select_fusion.3 = (f32[64,7168]{1,0:T(8,128)}, f32[64,7168]{1,0:T(8,128)}) fusion(f32[64,7168]{1,0:T(8,128)S(1)} %bitcast.95, f32[64,7168]{1,0:T(8,128)} %collective-permute-done.10, pred[]{:T(512)S(6)} %eq.21), kind=kLoop, calls=%fused_computation.36 | loop fusion | flops 917504 | bytes 7340033 | tf_op jit(solution)/shard_map/jit(_where)/select_n | solution.py:134
  63.5 32.0 %collective-permute-done = f32[16,4,7168]{2,1,0:T(4,128)} collective-permute-done((f32[16,4,7168]{2,1,0:T(4,128)}, f32[16,4,7168]{2,1,0:T(4,128)}, u32[]{:S(2)}, u32[]{:S(2)}) %collective-permute-start) | collective-permute-done | bytes 1835040 | tf_op jit(solution)/shard_map/ppermute | solution.py:144
  95.5 75.3 %collective-permute-done.4 = f32[64,7168]{1,0:T(8,128)} collective-permute-done((f32[64,7168]{1,0:T(8,128)}, f32[64,7168]{1,0:T(8,128)}, u32[]{:S(2)}, u32[]{:S(2)}) %collective-permute-start.4) | collective-permute-done | bytes 1835040 | tf_op jit(solution)/shard_map/ppermute | solution.py:130
  170.8 1.9 collective-permute-start.5
  173.9 3.5 %add.109 = f32[64,7168]{1,0:T(8,128)} add(f32[64,7168]{1,0:T(8,128)} %collective-permute-done.2, f32[64,7168]{1,0:T(8,128)} %collective-permute-done.4) | non-fusion elementwise | flops 458752 | bytes 5505024 | tf_op jit(solution)/shard_map/add | solution.py:162
  177.4 7.5 %all-to-all-start.1 = ((f32[16,4,7168]{2,1,0:T(4,128)}), f32[16,4,7168]{2,1,0:T(4,128)}, u32[]{:S(2)}, u32[]{:S(2)}) async-start(f32[16,4,7168]{2,1,0:T(4,128)} %collective-permute-done), calls=%async_computation.1 | async-start | bytes 3670016 | tf_op jit(solution)/shard_map/all_to_all | solution.py:149
  184.9 3.6 %broadcast_select_fusion.7 = (f32[64,7168]{1,0:T(8,128)S(1)}, f32[64,7168]{1,0:T(8,128)}) fusion(f32[64,7168]{1,0:T(8,128)} %collective-permute-done.1, f32[64,7168]{1,0:T(8,128)} %collective-permute-done.8, pred[]{:T(512)S(6)} %eq.21), kind=kLoop, calls=%fused_computation.40 | loop fusion | flops 917504 | bytes 7340033 | tf_op jit(solution)/shard_map/jit(_where)/select_n | solution.py:134
  188.6 4.9 %broadcast_select_fusion.9 = (f32[64,7168]{1,0:T(8,128)}, f32[64,7168]{1,0:T(8,128)}) fusion(f32[64,7168]{1,0:T(8,128)} %collective-permute-done.3, f32[64,7168]{1,0:T(8,128)} %collective-permute-done.7, pred[]{:T(512)S(6)} %eq.21), kind=kLoop, calls=%fused_computation.42 | loop fusion | flops 917504 | bytes 7340033 | tf_op jit(solution)/shard_map/jit(_where)/select_n | solution.py:134
  193.5 14.6 %all-to-all-done.1 = f32[16,4,7168]{2,1,0:T(4,128)} async-done(((f32[16,4,7168]{2,1,0:T(4,128)}), f32[16,4,7168]{2,1,0:T(4,128)}, u32[]{:S(2)}, u32[]{:S(2)}) %all-to-all-start.1) | async-done | bytes 1835040 | tf_op jit(solution)/shard_map/all_to_all | solution.py:149
  208.1 2.9 reshape.30
  211.1 3.0 constant_dynamic-update-slice_fusion.rows_ref
  214.1 3.9 %fusion.7 = f32[128,128]{1,0:T(8,128)S(1)} fusion(f32[128,7168]{1,0:T(8,128)} %constant_dynamic-update-slice_fusion.rows_ref, f32[64,7168]{1,0:T(8,128)S(1)} %copy-done.22, f32[64,7168]{1,0:T(8,128)S(1)} %copy-done.21), kind=kOutput, calls=%fused_computation.22 | convolution fusion | flops 705560576 | bytes 7405568 | tf_op jit(solution)/shard_map/dot_general | solution.py:41
  218.4 1.9 fusion.9
  220.2 1.8 fusion.8
  222.0 2.4 broadcast_select_fusion.5
  224.4 1.9 fusion.14
  227.2 4.7 %fusion.4 = f32[64,128]{1,0:T(8,128)S(1)} fusion(f32[64,7168]{1,0:T(8,128)S(1)} %copy-done.12, f32[64,7168]{1,0:T(8,128)S(1)} %get-tuple-element.47, f32[64,7168]{1,0:T(8,128)S(1)} %copy-done.16, f32[64,7168]{1,0:T(8,128)S(1)} %copy-done.14, f32[64,7168]{1,0:T(8,128)} %add.109, f32[64,7168]{1,0:T(8,128)S(1)} %bitcast.96, ...), kind=kOutput, calls=%fused_computation.19 | convolution fusion | flops 357826560 | bytes 16547843 | tf_op jit(solution)/shard_map/dot_general | solution.py:41
  232.0 2.2 add.111
  234.6 3.8 %collective-permute-done.11 = f32[64,7168]{1,0:T(8,128)} collective-permute-done((f32[64,7168]{1,0:T(8,128)S(1)}, f32[64,7168]{1,0:T(8,128)}, u32[]{:S(2)}, u32[]{:S(2)}) %collective-permute-start.11) | collective-permute-done | bytes 1835040 | tf_op jit(solution)/shard_map/ppermute | solution.py:130
  238.4 4.2 %fusion.57 = f32[128,64]{1,0:T(8,128)S(1)} fusion(f32[128,7168]{1,0:T(8,128)} %constant_dynamic-update-slice_fusion.rows_ref, f32[64,7168]{1,0:T(8,128)} %collective-permute-done.11), kind=kOutput, calls=%fused_computation.124 | convolution fusion | flops 352321536 | bytes 5537792 | tf_op jit(solution)/shard_map/dot_general | solution.py:41
  242.6 1.6 broadcast_select_fusion.11
  244.4 2.8 collective-permute-start.14
  247.3 1.6 collective-permute-start.12
  249.9 3.2 %collective-permute-done.13 = f32[144,128]{1,0:T(8,128)S(1)} collective-permute-done((f32[144,128]{1,0:T(8,128)S(1)}, f32[144,128]{1,0:T(8,128)S(1)}, u32[]{:S(2)}, u32[]{:S(2)}) %collective-permute-start.13) | collective-permute-done | bytes 73760 | tf_op jit(solution)/shard_map/ppermute | solution.py:51
  255.8 5.0 %fusion = (bf16[128,7168]{1,0:T(8,128)(2,1)}, bf16[128,7168]{1,0:T(8,128)(2,1)}, bf16[128,7168]{1,0:T(8,128)(2,1)}, bf16[128,7168]{1,0:T(8,128)(2,1)}) fusion(f32[64,7168]{1,0:T(8,128)} %get-tuple-element.42, f32[64,7168]{1,0:T(8,128)} %get-tuple-element.41, f32[64,7168]{1,0:T(8,128)} %copy-done.20, f32[64,7168]{1,0:T(8,128)S(1)} %copy-done.19), kind=kLoop, calls=%fused_computation.8 | loop fusion | flops 9175040 | bytes 14680064 | tf_op jit(solution)/shard_map/convert_element_type | solution.py:71
  260.9 6.4 %collective-permute-start.18 = (f32[144,128]{1,0:T(8,128)S(1)}, f32[144,128]{1,0:T(8,128)S(1)}, u32[]{:S(2)}, u32[]{:S(2)}) collective-permute-start(f32[144,128]{1,0:T(8,128)S(1)} %add_add_fusion), channel_id=1, source_target_pairs={{0,128},{8,136},{16,144},{24,152},{32,160},{40,168},{48,176},{56,1... | collective-permute-start | bytes 221192 | tf_op jit(solution)/shard_map/ppermute | solution.py:51
  267.3 1.9 broadcast_select_fusion.1
  270.8 3.2 %collective-permute-start.20 = (f32[144,128]{1,0:T(8,128)S(1)}, f32[144,128]{1,0:T(8,128)S(1)}, u32[]{:S(2)}, u32[]{:S(2)}) collective-permute-start(f32[144,128]{1,0:T(8,128)S(1)} %maximum_add_fusion), channel_id=1, source_target_pairs={{0,16},{8,24},{16,0},{24,8},{32,48},{40,56},{48,32},{56,40},{64,80... | collective-permute-start | bytes 221192 | tf_op jit(solution)/shard_map/ppermute | solution.py:51
  274.5 3.3 %fusion.3 = (bf16[128,7168]{1,0:T(8,128)(2,1)S(1)}, bf16[128,7168]{1,0:T(8,128)(2,1)}, bf16[128,7168]{1,0:T(8,128)(2,1)}, bf16[128,7168]{1,0:T(8,128)(2,1)}) fusion(f32[64,7168]{1,0:T(8,128)S(1)} %get-tuple-element.40, f32[64,7168]{1,0:T(8,128)S(1)} %get-tuple-element.39, pred[]{:T(512)S(6)} %eq.19, f32[64,7168]{1,0:T(8,128)S(1)} %copy-done.13, ...), kind=kLoop, calls=%fused_computation.11 | loop fusion | flops 13762560 | bytes 18350082 | tf_op jit(solution)/shard_map/convert_element_type | solution.py:71
  279.2 5.8 %all-to-all-start.2 = ((f32[8,64,128]{2,1,0:T(8,128)}), f32[8,64,128]{2,1,0:T(8,128)S(1)}, u32[]{:S(2)}, u32[]{:S(2)}) async-start(f32[8,64,128]{2,1,0:T(8,128)} %broadcast_in_dim.3), calls=%async_computation.2 | async-start | bytes 524288 | tf_op jit(solution)/shard_map/all_to_all | solution.py:191
  285.5 9.2 %all-to-all-done.2 = f32[8,64,128]{2,1,0:T(8,128)S(1)} async-done(((f32[8,64,128]{2,1,0:T(8,128)}), f32[8,64,128]{2,1,0:T(8,128)S(1)}, u32[]{:S(2)}, u32[]{:S(2)}) %all-to-all-start.2) | async-done | bytes 262176 | tf_op jit(solution)/shard_map/all_to_all | solution.py:191
  296.8 1.5 copy-done.3
  298.3 1.5 copy-done.4
  299.8 1.5 copy-done.5
  301.3 1.5 copy-done.6
  302.8 1.5 copy-done.7
  304.3 1.5 copy-done.8
  307.3 6.2 %shard_map.37 = f32[128,7168]{1,0:T(8,128)} custom-call(s32[1]{0:T(128)} %bitcast.half_ref, f32[128,7168]{1,0:T(8,128)S(1)} %copy-done.2, bf16[256,512]{1,0:T(8,128)(2,1)S(1)} %pad_maximum_fusion.15.scaled_ref, bf16[128,7168]{1,0:T(8,128)(2,1)S(1)} %copy-done.7, bf16[128,7168]{1,0:T(8,128)(2,1)S(1)} %copy-done.4, bf16[128,7168]{1,0:T(8,128)(2,1)S(1)} %copy-done.8, ...), custom_call_target="tpu_custom_call" | custom-call | flops 2818572288 | bytes 22020096 | tf_op jit(solution)/shard_map/pallas_call | solution.py:100
  (110 shorter events, 16.9 us)
Async XLA Ops:
  0.0 4.3 %copy-start.25 = (f32[7168,64]{0,1:T(8,128)S(1)}, f32[7168,64]{0,1:T(8,128)}, u32[]{:S(2)}) copy-start(f32[7168,64]{0,1:T(8,128)} %param.4) | copy-start | bytes 5505028
  4.3 44.2 %collective-permute-start.1 = (f32[64,7168]{1,0:T(8,128)S(1)}, f32[64,7168]{1,0:T(8,128)}, u32[]{:S(2)}, u32[]{:S(2)}) collective-permute-start(f32[64,7168]{1,0:T(8,128)S(1)} %bitcast.92), channel_id=1, source_target_pairs={{0,2},{1,3},{2,4},{3,5},{4,6},{5,7},{8,10},{9,11},{10,12},{11,13},... | collective-permute-start | bytes 5505032 | tf_op jit(solution)/shard_map/ppermute | solution.py:130
  9.3 46.4 %collective-permute-start.3 = (f32[64,7168]{1,0:T(8,128)S(1)}, f32[64,7168]{1,0:T(8,128)}, u32[]{:S(2)}, u32[]{:S(2)}) collective-permute-start(f32[64,7168]{1,0:T(8,128)S(1)} %bitcast.93), channel_id=1, source_target_pairs={{2,0},{3,1},{4,2},{5,3},{6,4},{7,5},{10,8},{11,9},{12,10},{13,11},... | collective-permute-start | bytes 5505032 | tf_op jit(solution)/shard_map/ppermute | solution.py:130
  10.6 31.6 %all-to-all-start = ((f32[16,4,7168]{2,1,0:T(4,128)}), f32[16,4,7168]{2,1,0:T(4,128)}, u32[]{:S(2)}, u32[]{:S(2)}) async-start(f32[16,4,7168]{2,1,0:T(4,128)} %get-tuple-element.50), calls=%async_computation | async-start | bytes 3670016 | tf_op jit(solution)/shard_map/all_to_all | solution.py:149
  18.1 41.7 %collective-permute-start.10 = (f32[64,7168]{1,0:T(8,128)S(1)}, f32[64,7168]{1,0:T(8,128)}, u32[]{:S(2)}, u32[]{:S(2)}) collective-permute-start(f32[64,7168]{1,0:T(8,128)S(1)} %bitcast.94), channel_id=1, source_target_pairs={{0,1},{1,0},{2,3},{3,2},{4,5},{5,4},{6,7},{7,6},{8,9},{9,8},{10,11... | collective-permute-start | bytes 5505032 | tf_op jit(solution)/shard_map/ppermute | solution.py:130
  18.1 77.3 %collective-permute-start = (f32[16,4,7168]{2,1,0:T(4,128)}, f32[16,4,7168]{2,1,0:T(4,128)}, u32[]{:S(2)}, u32[]{:S(2)}) collective-permute-start(f32[16,4,7168]{2,1,0:T(4,128)} %get-tuple-element.17), channel_id=1, source_target_pairs={{0,128},{8,136},{16,144},{24,152},{32,160},{40,168},{48,176},{56,1... | collective-permute-start | bytes 5505032 | tf_op jit(solution)/shard_map/ppermute | solution.py:144
  48.5 47.0 %collective-permute-start.2 = (f32[64,7168]{1,0:T(8,128)}, f32[64,7168]{1,0:T(8,128)}, u32[]{:S(2)}, u32[]{:S(2)}) collective-permute-start(f32[64,7168]{1,0:T(8,128)} %collective-permute-done.1), channel_id=1, source_target_pairs={{2,4},{3,5},{4,6},{5,7},{10,12},{11,13},{12,14},{13,15},{18,20},{1... | collective-permute-start | bytes 5505032 | tf_op jit(solution)/shard_map/ppermute | solution.py:130
  50.5 134.4 %collective-permute-start.8 = (f32[64,7168]{1,0:T(8,128)}, f32[64,7168]{1,0:T(8,128)}, u32[]{:S(2)}, u32[]{:S(2)}) collective-permute-start(f32[64,7168]{1,0:T(8,128)} %collective-permute-done.1), channel_id=1, source_target_pairs={{0,1},{1,0},{2,3},{3,2},{4,5},{5,4},{6,7},{7,6},{8,9},{9,8},{10,11... | collective-permute-start | bytes 5505032 | tf_op jit(solution)/shard_map/ppermute | solution.py:130
  55.7 115.1 %collective-permute-start.4 = (f32[64,7168]{1,0:T(8,128)}, f32[64,7168]{1,0:T(8,128)}, u32[]{:S(2)}, u32[]{:S(2)}) collective-permute-start(f32[64,7168]{1,0:T(8,128)} %collective-permute-done.3), channel_id=1, source_target_pairs={{2,0},{3,1},{4,2},{5,3},{10,8},{11,9},{12,10},{13,11},{18,16},{19,... | collective-permute-start | bytes 5505032 | tf_op jit(solution)/shard_map/ppermute | solution.py:130
  59.8 128.7 %collective-permute-start.7 = (f32[64,7168]{1,0:T(8,128)}, f32[64,7168]{1,0:T(8,128)}, u32[]{:S(2)}, u32[]{:S(2)}) collective-permute-start(f32[64,7168]{1,0:T(8,128)} %collective-permute-done.3), channel_id=1, source_target_pairs={{0,1},{1,0},{2,3},{3,2},{4,5},{5,4},{6,7},{7,6},{8,9},{9,8},{10,11... | collective-permute-start | bytes 5505032 | tf_op jit(solution)/shard_map/ppermute | solution.py:130
  170.8 61.2 %collective-permute-start.5 = (f32[64,7168]{1,0:T(8,128)}, f32[64,7168]{1,0:T(8,128)}, u32[]{:S(2)}, u32[]{:S(2)}) collective-permute-start(f32[64,7168]{1,0:T(8,128)} %collective-permute-done.2), channel_id=1, source_target_pairs={{4,6},{5,7},{12,14},{13,15},{20,22},{21,23},{28,30},{29,31},{36,38... | collective-permute-start | bytes 5505032 | tf_op jit(solution)/shard_map/ppermute | solution.py:130
  172.6 59.3 %collective-permute-start.6 = (f32[64,7168]{1,0:T(8,128)}, f32[64,7168]{1,0:T(8,128)}, u32[]{:S(2)}, u32[]{:S(2)}) collective-permute-start(f32[64,7168]{1,0:T(8,128)} %collective-permute-done.4), channel_id=1, source_target_pairs={{2,0},{3,1},{10,8},{11,9},{18,16},{19,17},{26,24},{27,25},{34,32},... | collective-permute-start | bytes 5505032 | tf_op jit(solution)/shard_map/ppermute | solution.py:130
  177.4 30.7 %all-to-all-start.1 = ((f32[16,4,7168]{2,1,0:T(4,128)}), f32[16,4,7168]{2,1,0:T(4,128)}, u32[]{:S(2)}, u32[]{:S(2)}) async-start(f32[16,4,7168]{2,1,0:T(4,128)} %collective-permute-done), calls=%async_computation.1 | async-start | bytes 3670016 | tf_op jit(solution)/shard_map/all_to_all | solution.py:149
  184.9 37.1 %collective-permute-start.9 = (f32[64,7168]{1,0:T(8,128)}, f32[64,7168]{1,0:T(8,128)}, u32[]{:S(2)}, u32[]{:S(2)}) collective-permute-start(f32[64,7168]{1,0:T(8,128)} %add.109), channel_id=1, source_target_pairs={{0,1},{1,0},{2,3},{3,2},{4,5},{5,4},{6,7},{7,6},{8,9},{9,8},{10,11... | collective-permute-start | bytes 5505032 | tf_op jit(solution)/shard_map/ppermute | solution.py:130
  188.6 37.7 %copy-start.10 = (f32[64,7168]{1,0:T(8,128)}, f32[64,7168]{1,0:T(8,128)S(1)}, u32[]{:S(2)}) copy-start(f32[64,7168]{1,0:T(8,128)S(1)} %get-tuple-element.47) | copy-start | bytes 5505028
  211.1 3.0 copy-start.21
  211.1 3.0 copy-start.22
  214.1 3.9 %copy-start = (f32[128,7168]{1,0:T(8,128)S(1)}, f32[128,7168]{1,0:T(8,128)}, u32[]{:S(2)}) copy-start(f32[128,7168]{1,0:T(8,128)} %constant_dynamic-update-slice_fusion.rows_ref) | copy-start | bytes 11010052
  214.1 3.9 %copy-start.14 = (f32[64,7168]{1,0:T(8,128)S(1)}, f32[64,7168]{1,0:T(8,128)}, u32[]{:S(2)}) copy-start(f32[64,7168]{1,0:T(8,128)} %get-tuple-element.45) | copy-start | bytes 5505028
  214.1 4.3 %copy-start.16 = (f32[64,7168]{1,0:T(8,128)S(1)}, f32[64,7168]{1,0:T(8,128)}, u32[]{:S(2)}) copy-start(f32[64,7168]{1,0:T(8,128)} %get-tuple-element.46) | copy-start | bytes 5505028
  218.3 1.9 copy-start.12
  224.4 1.9 copy-start.18
  224.4 1.9 copy-start.20
  224.4 2.8 copy-start.26
  234.2 8.4 %copy-start.23 = (f32[64,7168]{1,0:T(8,128)}, f32[64,7168]{1,0:T(8,128)S(1)}, u32[]{:S(2)}) copy-start(f32[64,7168]{1,0:T(8,128)S(1)} %add.111) | copy-start | bytes 5505028
  234.2 4.2 %collective-permute-start.11 = (f32[64,7168]{1,0:T(8,128)S(1)}, f32[64,7168]{1,0:T(8,128)}, u32[]{:S(2)}, u32[]{:S(2)}) collective-permute-start(f32[64,7168]{1,0:T(8,128)S(1)} %add.111), channel_id=1, source_target_pairs={{0,1},{1,0},{2,3},{3,2},{4,5},{5,4},{6,7},{7,6},{8,9},{9,8},{10,11... | collective-permute-start | bytes 5505032 | tf_op jit(solution)/shard_map/ppermute | solution.py:130
  234.6 8.0 %copy-start.1 = (f32[128,7168]{1,0:T(8,128)S(1)}, f32[128,7168]{1,0:T(8,128)}, u32[]{:S(2)}) copy-start(f32[128,7168]{1,0:T(8,128)} %constant_dynamic-update-slice_fusion.rows_ref) | copy-start | bytes 11010052
  244.3 11.5 %copy-start.19 = (f32[64,7168]{1,0:T(8,128)S(1)}, f32[64,7168]{1,0:T(8,128)}, u32[]{:S(2)}) copy-start(f32[64,7168]{1,0:T(8,128)} %copy-done.18) | copy-start | bytes 5505028
  244.4 5.5 %collective-permute-start.14 = (f32[144,128]{1,0:T(8,128)S(1)}, f32[144,128]{1,0:T(8,128)S(1)}, u32[]{:S(2)}, u32[]{:S(2)}) collective-permute-start(f32[144,128]{1,0:T(8,128)S(1)} %get-tuple-element.56), channel_id=1, source_target_pairs={{0,24},{8,0},{16,8},{24,16},{32,56},{40,32},{48,40},{56,48},{64,88... | collective-permute-start | bytes 221192 | tf_op jit(solution)/shard_map/ppermute | solution.py:51
  247.3 5.9 %collective-permute-start.13 = (f32[144,128]{1,0:T(8,128)S(1)}, f32[144,128]{1,0:T(8,128)S(1)}, u32[]{:S(2)}, u32[]{:S(2)}) collective-permute-start(f32[144,128]{1,0:T(8,128)S(1)} %get-tuple-element.57), channel_id=1, source_target_pairs={{0,16},{8,24},{16,0},{24,8},{32,48},{40,56},{48,32},{56,40},{64,80... | collective-permute-start | bytes 221192 | tf_op jit(solution)/shard_map/ppermute | solution.py:51
  247.3 5.9 %collective-permute-start.12 = (f32[144,128]{1,0:T(8,128)S(1)}, f32[144,128]{1,0:T(8,128)S(1)}, u32[]{:S(2)}, u32[]{:S(2)}) collective-permute-start(f32[144,128]{1,0:T(8,128)S(1)} %get-tuple-element.55), channel_id=1, source_target_pairs={{0,8},{8,16},{16,24},{24,0},{32,40},{40,48},{48,56},{56,32},{64,72... | collective-permute-start | bytes 221192 | tf_op jit(solution)/shard_map/ppermute | solution.py:51
  253.2 14.1 %copy-start.24 = (f32[64,7168]{1,0:T(8,128)S(1)}, f32[64,7168]{1,0:T(8,128)}, u32[]{:S(2)}) copy-start(f32[64,7168]{1,0:T(8,128)} %copy-done.23) | copy-start | bytes 5505028
  253.2 7.6 %collective-permute-start.17 = (f32[144,128]{1,0:T(8,128)S(1)}, f32[144,128]{1,0:T(8,128)S(1)}, u32[]{:S(2)}, u32[]{:S(2)}) collective-permute-start(f32[144,128]{1,0:T(8,128)S(1)} %fusion.36), channel_id=1, source_target_pairs={{0,96},{8,104},{16,112},{24,120},{32,0},{40,8},{48,16},{56,24},{64... | collective-permute-start | bytes 221192 | tf_op jit(solution)/shard_map/ppermute | solution.py:51
  254.0 6.8 %collective-permute-start.16 = (f32[144,128]{1,0:T(8,128)S(1)}, f32[144,128]{1,0:T(8,128)S(1)}, u32[]{:S(2)}, u32[]{:S(2)}) collective-permute-start(f32[144,128]{1,0:T(8,128)S(1)} %fusion.36), channel_id=1, source_target_pairs={{0,64},{8,72},{16,80},{24,88},{32,96},{40,104},{48,112},{56,120},{... | collective-permute-start | bytes 221192 | tf_op jit(solution)/shard_map/ppermute | solution.py:51
  254.9 5.9 %collective-permute-start.15 = (f32[144,128]{1,0:T(8,128)S(1)}, f32[144,128]{1,0:T(8,128)S(1)}, u32[]{:S(2)}, u32[]{:S(2)}) collective-permute-start(f32[144,128]{1,0:T(8,128)S(1)} %fusion.36), channel_id=1, source_target_pairs={{0,32},{8,40},{16,48},{24,56},{32,64},{40,72},{48,80},{56,88},{64,... | collective-permute-start | bytes 221192 | tf_op jit(solution)/shard_map/ppermute | solution.py:51
  260.8 13.6 %copy-start.11 = (f32[64,7168]{1,0:T(8,128)S(1)}, f32[64,7168]{1,0:T(8,128)}, u32[]{:S(2)}) copy-start(f32[64,7168]{1,0:T(8,128)} %copy-done.10) | copy-start | bytes 5505028
  260.9 13.6 %copy-start.13 = (f32[64,7168]{1,0:T(8,128)S(1)}, f32[64,7168]{1,0:T(8,128)}, u32[]{:S(2)}) copy-start(f32[64,7168]{1,0:T(8,128)} %get-tuple-element.48) | copy-start | bytes 5505028
  260.9 13.6 %copy-start.15 = (f32[64,7168]{1,0:T(8,128)S(1)}, f32[64,7168]{1,0:T(8,128)}, u32[]{:S(2)}) copy-start(f32[64,7168]{1,0:T(8,128)} %get-tuple-element.45) | copy-start | bytes 5505028
  260.9 13.6 %copy-start.17 = (f32[64,7168]{1,0:T(8,128)S(1)}, f32[64,7168]{1,0:T(8,128)}, u32[]{:S(2)}) copy-start(f32[64,7168]{1,0:T(8,128)} %get-tuple-element.46) | copy-start | bytes 5505028
  260.9 8.7 %collective-permute-start.18 = (f32[144,128]{1,0:T(8,128)S(1)}, f32[144,128]{1,0:T(8,128)S(1)}, u32[]{:S(2)}, u32[]{:S(2)}) collective-permute-start(f32[144,128]{1,0:T(8,128)S(1)} %add_add_fusion), channel_id=1, source_target_pairs={{0,128},{8,136},{16,144},{24,152},{32,160},{40,168},{48,176},{56,1... | collective-permute-start | bytes 221192 | tf_op jit(solution)/shard_map/ppermute | solution.py:51
  269.6 8.1 %collective-permute-start.21 = (f32[144,128]{1,0:T(8,128)S(1)}, f32[144,128]{1,0:T(8,128)S(1)}, u32[]{:S(2)}, u32[]{:S(2)}) collective-permute-start(f32[144,128]{1,0:T(8,128)S(1)} %maximum_add_fusion), channel_id=1, source_target_pairs={{0,8},{8,16},{16,24},{24,0},{32,40},{40,48},{48,56},{56,32},{64,72... | collective-permute-start | bytes 221192 | tf_op jit(solution)/shard_map/ppermute | solution.py:51
  270.8 6.9 %collective-permute-start.20 = (f32[144,128]{1,0:T(8,128)S(1)}, f32[144,128]{1,0:T(8,128)S(1)}, u32[]{:S(2)}, u32[]{:S(2)}) collective-permute-start(f32[144,128]{1,0:T(8,128)S(1)} %maximum_add_fusion), channel_id=1, source_target_pairs={{0,16},{8,24},{16,0},{24,8},{32,48},{40,56},{48,32},{56,40},{64,80... | collective-permute-start | bytes 221192 | tf_op jit(solution)/shard_map/ppermute | solution.py:51
  274.0 4.4 %collective-permute-start.19 = (f32[144,128]{1,0:T(8,128)S(1)}, f32[144,128]{1,0:T(8,128)S(1)}, u32[]{:S(2)}, u32[]{:S(2)}) collective-permute-start(f32[144,128]{1,0:T(8,128)S(1)} %maximum_add_fusion), channel_id=1, source_target_pairs={{0,24},{8,0},{16,8},{24,16},{32,56},{40,32},{48,40},{56,48},{64,88... | collective-permute-start | bytes 221192 | tf_op jit(solution)/shard_map/ppermute | solution.py:51
  277.7 7.3 %copy-start.27 = (f32[2,256,256]{2,1,0:T(8,128)S(1)}, f32[2,256,256]{2,1,0:T(8,128)}, u32[]{:S(2)}) copy-start(f32[2,256,256]{2,1,0:T(8,128)} %param.5) | copy-start | bytes 1572868
  279.2 15.5 %all-to-all-start.2 = ((f32[8,64,128]{2,1,0:T(8,128)}), f32[8,64,128]{2,1,0:T(8,128)S(1)}, u32[]{:S(2)}, u32[]{:S(2)}) async-start(f32[8,64,128]{2,1,0:T(8,128)} %broadcast_in_dim.3), calls=%async_computation.2 | async-start | bytes 524288 | tf_op jit(solution)/shard_map/all_to_all | solution.py:191
  294.7 2.0 copy-start.2
  296.8 1.5 copy-start.3
  298.3 1.5 copy-start.4
  (5 other events, 7.5 us)
where the time goes:
time: 315 us; the launch traced here: 314 us
  waiting for transfers between devices  167 us (53%)
  starting transfers between devices  58.4 us (19%)
  other arithmetic  30.8 us (10%)
  local copies, waits for them, and re-layouts  29.8 us (9%)
  matrix products  20.9 us (7%)
  Pallas kernels  6.22 us (2%)
    ppermute x11, waiting for transfers between devices, send(): return lax.ppermute(value, 'pcol', pairs)  87.7 us
    all_to_all x2, waiting for transfers between devices, over_plane(): lax.all_to_all(value, 'prow', split_axis=0, concat_axis=0, tiled=True, ax...  32.4 us
    ppermute x1, waiting for transfers between devices, body(): arriving = lax.ppermute(leaving, 'prow', FAR)  32 us
    dot_general x7, matrix products, matmul_nt(): lax.dot_general(left, right, (((1,), (1,)), ((), ())), precision=lax.Prec...  19.9 us
    ppermute x10, starting transfers between devices, send(): return lax.ppermute(value, 'prow', pairs)  18.2 us
    select_n x5, other arithmetic, ordered(): jnp.where(core == 0, piece, other)  16.5 us
    unnamed x64, local copies, waits for them, and re-layouts  15.9 us
    all_to_all x2, starting transfers between devices, over_plane(): lax.all_to_all(value, 'prow', split_axis=0, concat_axis=0, tiled=True, ax...  15 us
  transfers between devices with their start and end apart: 25, of which 12 were waited for; matrix products, arithmetic and copies ran while one was open for 17% of the time, Pallas kernels for 0%

commit v1 on v0

v1 whole, which is shorter than its diff:
```python
import functools

import jax
import jax.numpy as jnp
from jax import lax
from jax.experimental import pallas as pl
from jax.experimental.pallas import tpu as pltpu
from jax.sharding import PartitionSpec as P

UP_ONE = [(c, c + 2) for c in range(6)]
DOWN_ONE = [(c, c - 2) for c in range(2, 8)]
UP_TWO = [(c, c + 2) for c in range(2, 6)]
DOWN_TWO = [(c, c - 2) for c in range(2, 6)]
UP_END = [(4, 6), (5, 7)]
DOWN_END = [(2, 0), (3, 1)]
SIBLING = [(c, c ^ 1) for c in range(8)]
FAR = [(r, (r + 16) % 32) for r in range(32)]
PLANES = [list(range(16)), list(range(16, 32))]


IN_X = [[4 * q + x for x in range(4)] for q in range(8)]
IN_Y = [[16 * z + 4 * y + x for y in range(4)] for z in range(2) for x in range(4)]
SLOTS, WIDE = 4, 128
CHUNKS, CHAINS = 4, 2


def upper_part(square):
    width = square.shape[0]
    rows = lax.broadcasted_iota(jnp.int32, (width, width), 0)
    cols = lax.broadcasted_iota(jnp.int32, (width, width), 1)
    return jnp.where(cols >= rows, square, jnp.zeros_like(square))


def matmul(left, right, precision=lax.Precision.HIGHEST):
    return jnp.dot(left, right, precision=precision, preferred_element_type=jnp.float32)


def matmul_nt(left, right):
    return lax.dot_general(
        left, right, (((1,), (1,)), ((), ())),
        precision=lax.Precision.HIGH, preferred_element_type=jnp.float32,
    )


def exchange(value, groups):
    return lax.all_to_all(
        value, "prow", split_axis=0, concat_axis=0, tiled=True, axis_index_groups=groups
    )


def gather(value, groups):
    return exchange(jnp.broadcast_to(value, (4, *value.shape)), groups)


def sum_over_plane(values):
    return jnp.sum(gather(jnp.sum(exchange(values, IN_X), axis=0), IN_Y), axis=0)


def far(value):
    return lax.ppermute(value, "prow", FAR)


def turned(parts, start):
    return lax.dynamic_slice_in_dim(jnp.concatenate([parts, parts], axis=0), start % 4, 4, 0)


def split(value):
    high = lax.reduce_precision(value, 8, 7)
    return high.astype(jnp.bfloat16), (value - high).astype(jnp.bfloat16)


def dot_nn(left, right):
    return jnp.dot(left, right, preferred_element_type=jnp.float32)


def dot_nt(left, right):
    return lax.dot_general(
        left, right, (((1,), (1,)), ((), ())), preferred_element_type=jnp.float32
    )


def two_slots(refs, pair):
    return jnp.concatenate([refs[2 * pair][...], refs[2 * pair + 1][...]], axis=0)


def project_kernel(rows_ref, *refs):
    high_refs, low_refs, out_ref = refs[:SLOTS], refs[SLOTS : 2 * SLOTS], refs[-1]

    @pl.when(pl.program_id(0) == 0)
    def _():
        out_ref[...] = jnp.zeros_like(out_ref)

    rows = rows_ref[...].reshape(-1, rows_ref.shape[-1])
    count = rows.shape[0]
    high = rows.astype(jnp.bfloat16)
    low = (rows - high.astype(jnp.float32)).astype(jnp.bfloat16)
    left = jnp.concatenate([high, low], axis=0)
    for pair in range(SLOTS // 2):
        both = dot_nt(left, two_slots(high_refs, pair))
        part = both[:count] + both[count:] + dot_nt(high, two_slots(low_refs, pair))
        out_ref[2 * pair] += part[:, :WIDE]
        out_ref[2 * pair + 1] += part[:, WIDE:]


def project(rows, high, low, start=0, tile=896):
    peers, count, length = rows.shape
    block = pl.BlockSpec((WIDE, tile), lambda i: (0, i + start // tile))
    return pl.pallas_call(
        project_kernel,
        out_shape=jax.ShapeDtypeStruct((SLOTS, peers * count, WIDE), jnp.float32),
        grid=(length // tile,),
        in_specs=[pl.BlockSpec((peers, count, tile), lambda i: (0, 0, i)), *[block] * 8],
        out_specs=pl.BlockSpec((SLOTS, peers * count, WIDE), lambda i: (0, 0, 0)),
        compiler_params=pltpu.CompilerParams(vmem_limit_bytes=60 * 1024 * 1024),
        cost_estimate=pl.CostEstimate(
            flops=6 * peers * count * 512 * length,
            bytes_accessed=length * (512 + peers * count) * 4,
            transcendentals=0,
        ),
    )(rows, *high, *low)


def update_kernel(half_ref, near_ref, scaled_ref, *refs):
    high_refs, low_refs, out_ref = refs[:SLOTS], refs[SLOTS : 2 * SLOTS], refs[-1]
    far_refs = refs[2 * SLOTS : -1]
    per = pl.num_programs(0) // len(far_refs)
    count, mid = out_ref.shape[0], out_ref.shape[0] // 2
    change = None
    for pair in range(SLOTS // 2):
        left = scaled_ref[:, slice(2 * WIDE * pair, 2 * WIDE * (pair + 1))]
        both = dot_nn(left, two_slots(high_refs, pair))
        part = both[:count] + both[count:] + dot_nn(left[:count], two_slots(low_refs, pair))
        change = part if change is None else change + part
    here = pl.multiple_of(half_ref[0] * mid, mid)
    there = pl.multiple_of((1 - half_ref[0]) * mid, mid)
    out_ref[pl.ds(here, mid), :] = near_ref[...].reshape(mid, -1) - change[:mid]
    for chunk, far_ref in enumerate(far_refs):

        @pl.when(pl.program_id(0) // per == chunk)
        def _():
            out_ref[pl.ds(there, mid), :] = far_ref[...].reshape(mid, -1) - change[mid:]


def update(half, near, others, scaled, high, low, tile=896):
    peers, each, length = near.shape
    count = 2 * peers * each
    per = length // tile // len(others)

    def rows(first, last):
        return pl.BlockSpec(
            (peers, each, tile), lambda i, h: (0, 0, jnp.clip(i, first, last) - first)
        )

    block = pl.BlockSpec((WIDE, tile), lambda i, h: (0, i))
    return pl.pallas_call(
        update_kernel,
        out_shape=jax.ShapeDtypeStruct((count, length), jnp.float32),
        grid_spec=pltpu.PrefetchScalarGridSpec(
            num_scalar_prefetch=1,
            grid=(length // tile,),
            in_specs=[
                rows(0, length // tile - 1),
                pl.BlockSpec(scaled.shape, lambda i, h: (0, 0)),
                *[block] * 8,
                *[rows(k * per, k * per + per - 1) for k in range(len(others))],
            ],
            out_specs=pl.BlockSpec((count, tile), lambda i, h: (0, i)),
        ),
        compiler_params=pltpu.CompilerParams(vmem_limit_bytes=60 * 1024 * 1024),
        cost_estimate=pl.CostEstimate(
            flops=6 * count * 512 * length,
            bytes_accessed=length * (512 * 4 + count * 8),
            transcendentals=0,
        ),
    )(half.reshape(1), near, scaled, *high, *low, *others)


def body(eigen_rows, reflectors, tfactors):
    count = eigen_rows.shape[0]
    half = lax.axis_index("prow") // 16
    column = lax.axis_index("pcol")
    chip, core = column // 2, column % 2
    length = reflectors.shape[0]
    mine = reflectors.T

    def send(value, pairs):
        return lax.ppermute(value, "pcol", pairs)

    def both_cores(piece):
        other = send(piece, SIBLING)
        return jnp.concatenate(
            [jnp.where(core == 0, piece, other), jnp.where(core == 0, other, piece)], axis=0
        )

    below = send(mine, UP_ONE)
    above = send(mine, DOWN_ONE)
    blocks = eigen_rows.reshape(count, 32, length).transpose(1, 0, 2)
    leaving = exchange(lax.dynamic_slice_in_dim(blocks, (1 - half) * 16, 16, 0), PLANES)
    near = exchange(lax.dynamic_slice_in_dim(blocks, half * 16, 16, 0), PLANES)
    below_two = send(below, UP_TWO)
    above_two = send(above, DOWN_TWO)
    leaving, below_two, above_two = lax.optimization_barrier((leaving, below_two, above_two))
    span = length // CHUNKS
    others = [leaving[:, :, k * span : (k + 1) * span] for k in range(CHUNKS)]
    for k in range(CHUNKS):
        if k >= CHAINS:
            others[k], others[k - CHAINS] = lax.optimization_barrier(
                (others[k], others[k - CHAINS])
            )
        others[k] = far(others[k])
    below_end = send(below_two, UP_END)
    above_end = send(above_two, DOWN_END)
    two = below_two + above_two
    all_mine, all_below, all_above, all_two = (
        both_cores(piece) for piece in (mine, below, above, two)
    )

    left = jnp.where(chip == 0, two, jnp.where(chip == 3, mine, above))
    right = jnp.where(chip == 0, all_above, jnp.where(chip == 1, all_below, all_two))
    cross = sum_over_plane(matmul_nt(left, right).reshape(4, 16, WIDE))
    cross = gather(cross + far(cross), IN_X).reshape(64, WIDE)
    cross = lax.all_to_all(
        jnp.broadcast_to(cross, (8, *cross.shape)), "pcol", split_axis=0, concat_axis=0, tiled=True
    ).reshape(4, WIDE, WIDE)
    cross = jnp.concatenate(
        [
            jnp.concatenate([cross[1], cross[0]], axis=1),
            jnp.concatenate([cross[2], cross[3]], axis=1),
        ],
        axis=0,
    )

    all_last = both_cores(below_end + above_end)
    zero = jnp.zeros_like(all_last)
    at_above = all_above + jnp.where(chip == 3, all_last, zero)
    at_below = all_below + jnp.where(chip == 0, all_last, zero)
    high, low = zip(*(split(piece) for piece in (all_mine, at_above, all_two, at_below)))

    near_sum = sum_over_plane(project(near, high, low))
    near_elsewhere = far(near_sum)
    early = sum(
        (project(others[k], high, low, k * span) for k in range(1, CHUNKS - 1)),
        project(others[0], high, low),
    )
    last_rows, early, near_sum, near_elsewhere, cross, high, low = lax.optimization_barrier(
        (others[-1], early, near_sum, near_elsewhere, cross, high, low)
    )
    others[-1] = last_rows
    other_sum = sum_over_plane(early + project(last_rows, high, low, length - span))
    near_sum = near_sum + far(other_sum)
    other_sum = other_sum + near_elsewhere
    slots = gather(jnp.concatenate([near_sum, other_sum], axis=0), IN_X)

    projected = turned(slots, 4 - chip)
    first = jnp.concatenate([projected[0], projected[1]], axis=1)
    second = jnp.concatenate([projected[2], projected[3]], axis=1)
    scaled_second = matmul(second, upper_part(tfactors[1]).T)
    scaled_first = matmul(first - matmul(scaled_second, cross), upper_part(tfactors[0]).T)
    scaled = jnp.stack(
        [
            scaled_first[:, :WIDE],
            scaled_first[:, WIDE:],
            scaled_second[:, :WIDE],
            scaled_second[:, WIDE:],
        ]
    )
    scaled = turned(scaled, chip)
    scaled = jnp.concatenate([scaled[j] for j in range(SLOTS)], axis=1)
    scaled = jnp.concatenate(split(scaled), axis=0)
    return update(half, near, others, scaled, high, low)


def solution(mesh):
    return jax.shard_map(
        body,
        mesh=mesh,
        in_specs=(P(("pcol", "prow"), None), P("prow", "pcol"), P()),
        out_specs=P("pcol", "prow"),
        check_vma=False,
    )
```

time: 315 us -> 384 us (1.22)
  starting transfers between devices: 58.4 us -> 123 us
  Pallas kernels: 6.22 us -> 37.8 us
  blocking collectives: 0 us -> 18.9 us
  waiting for transfers between devices: 167 us -> 149 us
  local copies, waits for them, and re-layouts: 29.8 us -> 13.5 us
  matrix products: 20.9 us -> 6.46 us
    pallas_call x1 -> x6, Pallas kernels: 6.22 us -> 37.8 us  [the longest x5 25.9 us: project(): pl.pallas_call(project_kernel, out_shape=jax.ShapeDtypeStruct((SLOTS, pee...]
    all_to_all x1, starting transfers between devices: 5.77 us -> 36.7 us  [body(): lax.all_to_all(jnp.broadcast_to(cross, (8, *cross.shape)), 'pcol', split_...]
    ppermute x11 -> x7, waiting for transfers between devices: 37.3 us -> 6.79 us  [far(): return lax.ppermute(value, 'prow', FAR)]
    all_to_all x2 -> x8, starting transfers between devices: 15 us -> 44.8 us  [exchange(): lax.all_to_all(value, 'prow', split_axis=0, concat_axis=0, tiled=True, ax...]
    all_to_all x2 -> x8, waiting for transfers between devices: 32.4 us -> 53.7 us  [exchange(): lax.all_to_all(value, 'prow', split_axis=0, concat_axis=0, tiled=True, ax...]
    all_to_all x0 -> x2, blocking collectives: none -> 18.9 us  [exchange(): lax.all_to_all(value, 'prow', split_axis=0, concat_axis=0, tiled=True, ax...]
    dot_general x7 -> x1, matrix products: 19.9 us -> 5.38 us  [matmul_nt(): lax.dot_general(left, right, (((1,), (1,)), ((), ())), precision=lax.Prec...]
    unnamed x64 -> x39, local copies, waits for them, and re-layouts: 15.9 us -> 3.24 us
  transfers between devices with their start and end apart: 25 -> 27, of which waited for: 12 -> 12; matrix products, arithmetic and copies ran while one was open for 17% -> 12% of each run, Pallas kernels for 0% -> 6%
where the time goes in v1:
time: 384 us; the launch traced here: 382 us
  waiting for transfers between devices  149 us (39%)
  starting transfers between devices  123 us (32%)
  Pallas kernels  37.8 us (10%)
  other arithmetic  33.5 us (9%)
  blocking collectives  18.9 us (5%)
  local copies, waits for them, and re-layouts  13.5 us (4%)
  matrix products  6.46 us (2%)
    ppermute x11, waiting for transfers between devices, send(): return lax.ppermute(value, 'pcol', pairs)  79 us
    all_to_all x8, waiting for transfers between devices, exchange(): lax.all_to_all(value, 'prow', split_axis=0, concat_axis=0, tiled=True, ax...  53.7 us
    all_to_all x8, starting transfers between devices, exchange(): lax.all_to_all(value, 'prow', split_axis=0, concat_axis=0, tiled=True, ax...  44.8 us
    all_to_all x1, starting transfers between devices, body(): lax.all_to_all(jnp.broadcast_to(cross, (8, *cross.shape)), 'pcol', split_...  36.7 us
    ppermute x7, starting transfers between devices, far(): return lax.ppermute(value, 'prow', FAR)  27 us
    pallas_call x5, Pallas kernels, project(): pl.pallas_call(project_kernel, out_shape=jax.ShapeDtypeStruct((SLOTS, pee...  25.9 us
    all_to_all x2, blocking collectives, exchange(): lax.all_to_all(value, 'prow', split_axis=0, concat_axis=0, tiled=True, ax...  18.9 us
    ppermute x11, starting transfers between devices, send(): return lax.ppermute(value, 'pcol', pairs)  14.2 us
  transfers between devices with their start and end apart: 27, of which 12 were waited for; matrix products, arithmetic and copies ran while one was open for 12% of the time, Pallas kernels for 6%

profile of v1, /device:TPU:2, one launch (start us, length us, event | category | flops | bytes accessed | tf_op | source)
XLA Modules:
  0.0 382.1 jit_solution(136500177671856209)
XLA Ops:
  1.3 5.8 %collective-permute-start = (f32[64,7168]{1,0:T(8,128)}, f32[64,7168]{1,0:T(8,128)}, u32[]{:S(2)}, u32[]{:S(2)}) collective-permute-start(f32[64,7168]{1,0:T(8,128)} %bitcast.4), channel_id=1, source_target_pairs={{0,2},{1,3},{2,4},{3,5},{4,6},{5,7},{8,10},{9,11},{10,12},{11,13},... | collective-permute-start | bytes 5505032 | tf_op jit(solution)/shard_map/ppermute | solution.py:187
  7.1 36.9 %collective-permute-done.2 = f32[64,7168]{1,0:T(8,128)S(1)} collective-permute-done((f32[64,7168]{1,0:T(8,128)}, f32[64,7168]{1,0:T(8,128)S(1)}, u32[]{:S(2)}, u32[]{:S(2)}) %collective-permute-start.2) | collective-permute-done | bytes 1835040 | tf_op jit(solution)/shard_map/ppermute | solution.py:187
  44.0 1.3 collective-permute-start.3
  45.4 1.9 collective-permute-start.1
  47.3 4.2 %dynamic-slice_bitcast_fusion = (f32[16,4,7168]{2,1,0:T(4,128)}, f32[16,4,7168]{2,1,0:T(4,128)}) fusion(f32[4,32,7168]{2,0,1:T(4,128)} %bitcast.68, s32[]{:T(128)S(6)} %select_n.123, s32[]{:T(128)S(6)} %select_n.122), kind=kLoop, calls=%fused_computation.24 | loop fusion | bytes 7340040 | tf_op jit(solution)/shard_map/dynamic_slice | solution.py:198
  51.5 7.5 %all-to-all-start.1 = ((f32[16,4,7168]{2,1,0:T(4,128)}), f32[16,4,7168]{2,1,0:T(4,128)}, u32[]{:S(2)}, u32[]{:S(2)}) async-start(f32[16,4,7168]{2,1,0:T(4,128)} %get-tuple-element.65), calls=%async_computation.1 | async-start | bytes 3670016 | tf_op jit(solution)/shard_map/all_to_all | solution.py:46
  59.5 24.8 %all-to-all-done.1 = f32[16,4,7168]{2,1,0:T(4,128)} async-done(((f32[16,4,7168]{2,1,0:T(4,128)}), f32[16,4,7168]{2,1,0:T(4,128)}, u32[]{:S(2)}, u32[]{:S(2)}) %all-to-all-start.1) | async-done | bytes 1835040 | tf_op jit(solution)/shard_map/all_to_all | solution.py:46
  84.4 3.0 collective-permute-done.3
  87.4 2.2 add.59
  89.8 1.8 broadcast_select_fusion.7
  91.6 3.0 broadcast_select_fusion.1
  96.4 5.4 %fusion.4 = f32[64,128]{1,0:T(8,128)} fusion(f32[64,7168]{1,0:T(8,128)S(1)} %get-tuple-element.56, f32[64,7168]{1,0:T(8,128)S(1)} %get-tuple-element.55, f32[64,7168]{1,0:T(8,128)S(1)} %get-tuple-element.60, f32[64,7168]{1,0:T(8,128)S(1)} %get-tuple-element.59, f32[64,7168]{1,0:T(8,128)S(1)} %get-tuple-element.58, f32[64,7168]{1,0:T(8,128)S(1)} %get-tuple-element.57, ...), kind=kOutput, calls=%fused_computation.17 | convolution fusion | flops 357826560 | bytes 16547843 | tf_op jit(solution)/shard_map/dot_general | solution.py:39
  101.8 5.7 %all-to-all-start.4 = ((f32[4,16,128]{2,1,0:T(8,128)}), f32[4,16,128]{2,1,0:T(8,128)S(1)}, u32[]{:S(2)}, u32[]{:S(2)}) async-start(f32[4,16,128]{2,1,0:T(8,128)} %bitcast.5), calls=%async_computation.4 | async-start | bytes 65536 | tf_op jit(solution)/shard_map/all_to_all | solution.py:46
  108.9 1.9 collective-permute-start.9
  112.2 3.5 all-to-all-start.5
  115.7 4.3 %broadcast_select_fusion.9 = (f32[64,7168]{1,0:T(8,128)}, f32[64,7168]{1,0:T(8,128)}) fusion(f32[64,7168]{1,0:T(8,128)} %collective-permute-done.7, pred[]{:T(512)S(6)} %eq.12, f32[7168,64]{0,1:T(8,128)} %param.4), kind=kLoop, calls=%fused_computation.40 | loop fusion | flops 917504 | bytes 7340033 | tf_op jit(solution)/shard_map/jit(_where)/select_n | solution.py:192
  121.2 6.7 %collective-permute-start.16 = (f32[16,128]{1,0:T(8,128)S(1)}, f32[16,128]{1,0:T(8,128)S(1)}, u32[]{:S(2)}, u32[]{:S(2)}) collective-permute-start(f32[16,128]{1,0:T(8,128)S(1)} %reduce_sum.57), channel_id=1, source_target_pairs={{0,128},{8,136},{16,144},{24,152},{32,160},{40,168},{48,176},{56,1... | collective-permute-start | bytes 24584 | tf_op jit(solution)/shard_map/ppermute | solution.py:60
  127.9 2.6 fusion.37
  130.5 5.9 %collective-permute-start.6 = (f32[16,4,1792]{2,1,0:T(4,128)S(1)}, f32[16,4,1792]{2,1,0:T(4,128)S(1)}, u32[]{:S(2)}, u32[]{:S(2)}) collective-permute-start(f32[16,4,1792]{2,1,0:T(4,128)S(1)} %get-tuple-element.67), channel_id=1, source_target_pairs={{0,128},{8,136},{16,144},{24,152},{32,160},{40,168},{48,176},{56,1... | collective-permute-start | bytes 1376264 | tf_op jit(solution)/shard_map/ppermute | solution.py:60
  136.4 39.0 %collective-permute-done.10 = f32[64,7168]{1,0:T(8,128)} collective-permute-done((f32[64,7168]{1,0:T(8,128)}, f32[64,7168]{1,0:T(8,128)}, u32[]{:S(2)}, u32[]{:S(2)}) %collective-permute-start.10) | collective-permute-done | bytes 1835040 | tf_op jit(solution)/shard_map/ppermute | solution.py:187
  175.5 3.5 add.57
  179.6 4.8 %all-to-all-start.6 = ((f32[4,16,128]{2,1,0:T(8,128)}), f32[4,16,128]{2,1,0:T(8,128)S(1)}, u32[]{:S(2)}, u32[]{:S(2)}) async-start(f32[4,16,128]{2,1,0:T(8,128)} %broadcast_in_dim.24), calls=%async_computation.6 | async-start | bytes 65536 | tf_op jit(solution)/shard_map/all_to_all | solution.py:46
  184.4 4.5 %fusion = (bf16[128,7168]{1,0:T(8,128)(2,1)}, bf16[128,7168]{1,0:T(8,128)(2,1)}) fusion(f32[64,7168]{1,0:T(8,128)} %get-tuple-element.64, f32[64,7168]{1,0:T(8,128)} %get-tuple-element.63), kind=kLoop, calls=%fused_computation.8 | loop fusion | flops 4587520 | bytes 7340032 | tf_op jit(solution)/shard_map/convert_element_type | solution.py:69
  188.9 6.2 %collective-permute-start.14 = (f32[16,4,1792]{2,1,0:T(4,128)}, f32[16,4,1792]{2,1,0:T(4,128)S(1)}, u32[]{:S(2)}, u32[]{:S(2)}) collective-permute-start(f32[16,4,1792]{2,1,0:T(4,128)} %get-tuple-element.31), channel_id=1, source_target_pairs={{0,128},{8,136},{16,144},{24,152},{32,160},{40,168},{48,176},{56,1... | collective-permute-start | bytes 1376264 | tf_op jit(solution)/shard_map/ppermute | solution.py:60
  196.0 36.7 %all-to-all-start.7 = ((f32[8,64,128]{2,1,0:T(8,128)}), f32[8,64,128]{2,1,0:T(8,128)S(1)}, u32[]{:S(2)}, u32[]{:S(2)}) async-start(f32[8,64,128]{2,1,0:T(8,128)} %broadcast_in_dim.25), calls=%async_computation.7 | async-start | bytes 524288 | tf_op jit(solution)/shard_map/all_to_all | solution.py:222
  232.6 4.6 %fusion.2 = (bf16[128,7168]{1,0:T(8,128)(2,1)}, bf16[128,7168]{1,0:T(8,128)(2,1)}) fusion(f32[64,7168]{1,0:T(8,128)} %copy-done.7, f32[64,7168]{1,0:T(8,128)} %copy-done.6), kind=kLoop, calls=%fused_computation.10 | loop fusion | flops 4587520 | bytes 7340032 | tf_op jit(solution)/shard_map/convert_element_type | solution.py:69
  237.2 9.2 %all-to-all-done.7 = f32[8,64,128]{2,1,0:T(8,128)S(1)} async-done(((f32[8,64,128]{2,1,0:T(8,128)}), f32[8,64,128]{2,1,0:T(8,128)S(1)}, u32[]{:S(2)}, u32[]{:S(2)}) %all-to-all-start.7) | async-done | bytes 262176 | tf_op jit(solution)/shard_map/all_to_all | solution.py:222
  246.4 7.6 %all-to-all-start = ((f32[16,4,7168]{2,1,0:T(4,128)}), f32[16,4,7168]{2,1,0:T(4,128)}, u32[]{:S(2)}, u32[]{:S(2)}) async-start(f32[16,4,7168]{2,1,0:T(4,128)} %get-tuple-element.66), calls=%async_computation | async-start | bytes 3670016 | tf_op jit(solution)/shard_map/all_to_all | solution.py:46
  254.1 2.6 broadcast_select_fusion.5
  257.8 3.7 fusion.3
  261.5 17.2 %all-to-all-done.rows_ref.near_ref = f32[16,4,7168]{2,1,0:T(4,128)} async-done(((f32[16,4,7168]{2,1,0:T(4,128)}), f32[16,4,7168]{2,1,0:T(4,128)}, u32[]{:S(2)}, u32[]{:S(2)}) %all-to-all-start) | async-done | bytes 1835040 | tf_op jit(solution)/shard_map/all_to_all | solution.py:46
  278.7 10.9 %shard_map.40 = f32[4,64,128]{2,1,0:T(8,128)} custom-call(f32[16,4,7168]{2,1,0:T(4,128)} %all-to-all-done.rows_ref.near_ref, bf16[128,7168]{1,0:T(8,128)(2,1)} %get-tuple-element.35.refs_0_, bf16[128,7168]{1,0:T(8,128)(2,1)} %get-tuple-element.36.refs_1_, bf16[128,7168]{1,0:T(8,128)(2,1)} %get-tuple-element.37.refs_2_, ...), custom_call_target="tpu_custom_call" | custom-call | flops 1409286144 | bytes 16515072 | tf_op jit(solution)/shard_map/pallas_call | solution.py:108
  289.6 7.5 %all-to-all-start.2 = ((f32[4,64,128]{2,1,0:T(8,128)}), f32[4,64,128]{2,1,0:T(8,128)S(1)}, u32[]{:S(2)}, u32[]{:S(2)}) async-start(f32[4,64,128]{2,1,0:T(8,128)} %shard_map.40), calls=%async_computation.2 | async-start | bytes 262144 | tf_op jit(solution)/shard_map/all_to_all | solution.py:46
  297.1 4.5 %all-to-all-done.2 = f32[4,64,128]{2,1,0:T(8,128)S(1)} async-done(((f32[4,64,128]{2,1,0:T(8,128)}), f32[4,64,128]{2,1,0:T(8,128)S(1)}, u32[]{:S(2)}, u32[]{:S(2)}) %all-to-all-start.2) | async-done | bytes 131104 | tf_op jit(solution)/shard_map/all_to_all | solution.py:46
  302.2 3.3 all-to-all-start.3
  305.6 3.8 shard_map.38
  309.3 3.8 shard_map.37
  313.9 3.7 shard_map.39
  317.6 4.0 %collective-permute-start.15 = (f32[64,128]{1,0:T(8,128)S(1)}, f32[64,128]{1,0:T(8,128)S(1)}, u32[]{:S(2)}, u32[]{:S(2)}) collective-permute-start(f32[64,128]{1,0:T(8,128)S(1)} %reduce_sum.55), channel_id=1, source_target_pairs={{0,128},{8,136},{16,144},{24,152},{32,160},{40,168},{48,176},{56,1... | collective-permute-start | bytes 98312 | tf_op jit(solution)/shard_map/ppermute | solution.py:60
  322.6 2.9 collective-permute-done.15
  325.5 3.7 shard_map.41
  330.3 8.4 %all_to_all.55 = f32[4,64,128]{2,1,0:T(8,128)S(1)} all-to-all(f32[4,64,128]{2,1,0:T(8,128)S(1)} %add.64), channel_id=1, replica_groups={{0,8,16,24},{32,40,48,56},{64,72,80,88},{96,104,112,120},{128,136,144,1..., dimensions={0} | all-to-all | bytes 262144 | tf_op jit(solution)/shard_map/all_to_all | solution.py:46
  338.7 10.5 %all_to_all.56 = f32[4,64,128]{2,1,0:T(8,128)S(1)} all-to-all(f32[4,64,128]{2,1,0:T(8,128)S(1)} %broadcast_in_dim.26), channel_id=1, replica_groups={{0,32,64,96},{8,40,72,104},{16,48,80,112},{24,56,88,120},{128,160,192,2..., dimensions={0} | all-to-all | bytes 262144 | tf_op jit(solution)/shard_map/all_to_all | solution.py:46
  349.2 4.1 %collective-permute-start.17 = (f32[64,128]{1,0:T(8,128)S(1)}, f32[64,128]{1,0:T(8,128)S(1)}, u32[]{:S(2)}, u32[]{:S(2)}) collective-permute-start(f32[64,128]{1,0:T(8,128)S(1)} %reduce_sum.59), channel_id=1, source_target_pairs={{0,128},{8,136},{16,144},{24,152},{32,160},{40,168},{48,176},{56,1... | collective-permute-start | bytes 98312 | tf_op jit(solution)/shard_map/ppermute | solution.py:60
  353.3 3.8 %collective-permute-done.17 = f32[64,128]{1,0:T(8,128)S(1)} collective-permute-done((f32[64,128]{1,0:T(8,128)S(1)}, f32[64,128]{1,0:T(8,128)S(1)}, u32[]{:S(2)}, u32[]{:S(2)}) %collective-permute-start.17) | collective-permute-done | bytes 32800 | tf_op jit(solution)/shard_map/ppermute | solution.py:60
  357.8 4.8 %all-to-all-start.10 = ((f32[4,128,128]{2,1,0:T(8,128)}), f32[4,128,128]{2,1,0:T(8,128)S(1)}, u32[]{:S(2)}, u32[]{:S(2)}) async-start(f32[4,128,128]{2,1,0:T(8,128)} %broadcast_in_dim.27), calls=%async_computation.10 | async-start | bytes 524288 | tf_op jit(solution)/shard_map/all_to_all | solution.py:46
  362.7 5.2 %all-to-all-done.10 = f32[4,128,128]{2,1,0:T(8,128)S(1)} async-done(((f32[4,128,128]{2,1,0:T(8,128)}), f32[4,128,128]{2,1,0:T(8,128)S(1)}, u32[]{:S(2)}, u32[]{:S(2)}) %all-to-all-start.10) | async-done | bytes 262176 | tf_op jit(solution)/shard_map/all_to_all | solution.py:46
  370.0 11.9 %shard_map.42 = f32[128,7168]{1,0:T(8,128)} custom-call(s32[1]{0:T(128)} %bitcast.half_ref, f32[16,4,7168]{2,1,0:T(4,128)} %all-to-all-done.rows_ref.near_ref, bf16[256,512]{1,0:T(8,128)(2,1)} %pad_maximum_fusion.9.scaled_ref, bf16[128,7168]{1,0:T(8,128)(2,1)} %get-tuple-element.35.refs_0_, bf16[128,7168]{1,0:T(8,128)(2,1)} %get-tuple-element.36.refs_1_, ...), custom_call_target="tpu_custom_call" | custom-call | flops 2818572288 | bytes 22020096 | tf_op jit(solution)/shard_map/pallas_call | solution.py:155
  (95 shorter events, 16.3 us)
Async XLA Ops:
  0.0 44.0 %collective-permute-start.2 = (f32[64,7168]{1,0:T(8,128)}, f32[64,7168]{1,0:T(8,128)S(1)}, u32[]{:S(2)}, u32[]{:S(2)}) collective-permute-start(f32[64,7168]{1,0:T(8,128)} %bitcast.4), channel_id=1, source_target_pairs={{2,0},{3,1},{4,2},{5,3},{6,4},{7,5},{10,8},{11,9},{12,10},{13,11},... | collective-permute-start | bytes 5505032 | tf_op jit(solution)/shard_map/ppermute | solution.py:187
  1.3 44.1 %collective-permute-start = (f32[64,7168]{1,0:T(8,128)}, f32[64,7168]{1,0:T(8,128)}, u32[]{:S(2)}, u32[]{:S(2)}) collective-permute-start(f32[64,7168]{1,0:T(8,128)} %bitcast.4), channel_id=1, source_target_pairs={{0,2},{1,3},{2,4},{3,5},{4,6},{5,7},{8,10},{9,11},{10,12},{11,13},... | collective-permute-start | bytes 5505032 | tf_op jit(solution)/shard_map/ppermute | solution.py:187
  44.0 7.5 %copy-start.8 = (f32[64,7168]{1,0:T(8,128)}, f32[64,7168]{1,0:T(8,128)S(1)}, u32[]{:S(2)}) copy-start(f32[64,7168]{1,0:T(8,128)S(1)} %collective-permute-done.2) | copy-start | bytes 5505028
  44.0 43.4 %collective-permute-start.3 = (f32[64,7168]{1,0:T(8,128)S(1)}, f32[64,7168]{1,0:T(8,128)}, u32[]{:S(2)}, u32[]{:S(2)}) collective-permute-start(f32[64,7168]{1,0:T(8,128)S(1)} %collective-permute-done.2), channel_id=1, source_target_pairs={{2,0},{3,1},{4,2},{5,3},{10,8},{11,9},{12,10},{13,11},{18,16},{19,... | collective-permute-start | bytes 5505032 | tf_op jit(solution)/shard_map/ppermute | solution.py:187
  45.3 44.4 %collective-permute-start.8 = (f32[64,7168]{1,0:T(8,128)S(1)}, f32[64,7168]{1,0:T(8,128)}, u32[]{:S(2)}, u32[]{:S(2)}) collective-permute-start(f32[64,7168]{1,0:T(8,128)S(1)} %collective-permute-done.2), channel_id=1, source_target_pairs={{0,1},{1,0},{2,3},{3,2},{4,5},{5,4},{6,7},{7,6},{8,9},{9,8},{10,11... | collective-permute-start | bytes 5505032 | tf_op jit(solution)/shard_map/ppermute | solution.py:187
  45.4 42.0 %collective-permute-start.1 = (f32[64,7168]{1,0:T(8,128)}, f32[64,7168]{1,0:T(8,128)}, u32[]{:S(2)}, u32[]{:S(2)}) collective-permute-start(f32[64,7168]{1,0:T(8,128)} %collective-permute-done), channel_id=1, source_target_pairs={{2,4},{3,5},{4,6},{5,7},{10,12},{11,13},{12,14},{13,15},{18,20},{1... | collective-permute-start | bytes 5505032 | tf_op jit(solution)/shard_map/ppermute | solution.py:187
  51.5 32.8 %all-to-all-start.1 = ((f32[16,4,7168]{2,1,0:T(4,128)}), f32[16,4,7168]{2,1,0:T(4,128)}, u32[]{:S(2)}, u32[]{:S(2)}) async-start(f32[16,4,7168]{2,1,0:T(4,128)} %get-tuple-element.65), calls=%async_computation.1 | async-start | bytes 3670016 | tf_op jit(solution)/shard_map/all_to_all | solution.py:46
  59.0 32.6 %collective-permute-start.13 = (f32[64,7168]{1,0:T(8,128)}, f32[64,7168]{1,0:T(8,128)}, u32[]{:S(2)}, u32[]{:S(2)}) collective-permute-start(f32[64,7168]{1,0:T(8,128)} %collective-permute-done), channel_id=1, source_target_pairs={{0,1},{1,0},{2,3},{3,2},{4,5},{5,4},{6,7},{7,6},{8,9},{9,8},{10,11... | collective-permute-start | bytes 5505032 | tf_op jit(solution)/shard_map/ppermute | solution.py:187
  59.0 56.7 %collective-permute-start.7 = (f32[64,7168]{1,0:T(8,128)}, f32[64,7168]{1,0:T(8,128)}, u32[]{:S(2)}, u32[]{:S(2)}) collective-permute-start(f32[64,7168]{1,0:T(8,128)} %bitcast.4), channel_id=1, source_target_pairs={{0,1},{1,0},{2,3},{3,2},{4,5},{5,4},{6,7},{7,6},{8,9},{9,8},{10,11... | collective-permute-start | bytes 5505032 | tf_op jit(solution)/shard_map/ppermute | solution.py:187
  84.4 5.4 %copy-start.9 = (f32[64,7168]{1,0:T(8,128)S(1)}, f32[64,7168]{1,0:T(8,128)}, u32[]{:S(2)}) copy-start(f32[64,7168]{1,0:T(8,128)} %copy-done.8) | copy-start | bytes 5505028
  89.6 5.0 %collective-permute-start.12 = (f32[64,7168]{1,0:T(8,128)S(1)}, f32[64,7168]{1,0:T(8,128)S(1)}, u32[]{:S(2)}, u32[]{:S(2)}) collective-permute-start(f32[64,7168]{1,0:T(8,128)S(1)} %add.59), channel_id=1, source_target_pairs={{0,1},{1,0},{2,3},{3,2},{4,5},{5,4},{6,7},{7,6},{8,9},{9,8},{10,11... | collective-permute-start | bytes 5505032 | tf_op jit(solution)/shard_map/ppermute | solution.py:187
  91.6 3.5 copy-start
  94.7 1.2 copy-start.2
  94.7 1.8 copy-start.4
  95.0 6.8 %copy-start.6 = (f32[64,7168]{1,0:T(8,128)}, f32[64,7168]{1,0:T(8,128)S(1)}, u32[]{:S(2)}) copy-start(f32[64,7168]{1,0:T(8,128)S(1)} %get-tuple-element.57) | copy-start | bytes 5505028
  95.1 6.8 %copy-start.7 = (f32[64,7168]{1,0:T(8,128)}, f32[64,7168]{1,0:T(8,128)S(1)}, u32[]{:S(2)}) copy-start(f32[64,7168]{1,0:T(8,128)S(1)} %get-tuple-element.58) | copy-start | bytes 5505028
  101.8 9.7 %all-to-all-start.4 = ((f32[4,16,128]{2,1,0:T(8,128)}), f32[4,16,128]{2,1,0:T(8,128)S(1)}, u32[]{:S(2)}, u32[]{:S(2)}) async-start(f32[4,16,128]{2,1,0:T(8,128)} %bitcast.5), calls=%async_computation.4 | async-start | bytes 65536 | tf_op jit(solution)/shard_map/all_to_all | solution.py:46
  107.6 67.9 %collective-permute-start.10 = (f32[64,7168]{1,0:T(8,128)}, f32[64,7168]{1,0:T(8,128)}, u32[]{:S(2)}, u32[]{:S(2)}) collective-permute-start(f32[64,7168]{1,0:T(8,128)} %collective-permute-done.3), channel_id=1, source_target_pairs={{2,0},{3,1},{10,8},{11,9},{18,16},{19,17},{26,24},{27,25},{34,32},... | collective-permute-start | bytes 5505032 | tf_op jit(solution)/shard_map/ppermute | solution.py:187
  108.9 66.6 %collective-permute-start.9 = (f32[64,7168]{1,0:T(8,128)}, f32[64,7168]{1,0:T(8,128)}, u32[]{:S(2)}, u32[]{:S(2)}) collective-permute-start(f32[64,7168]{1,0:T(8,128)} %collective-permute-done.1), channel_id=1, source_target_pairs={{4,6},{5,7},{12,14},{13,15},{20,22},{21,23},{28,30},{29,31},{36,38... | collective-permute-start | bytes 5505032 | tf_op jit(solution)/shard_map/ppermute | solution.py:187
  112.2 9.0 %all-to-all-start.5 = ((f32[4,16,128]{2,1,0:T(8,128)}), f32[4,16,128]{2,1,0:T(8,128)S(1)}, u32[]{:S(2)}, u32[]{:S(2)}) async-start(f32[4,16,128]{2,1,0:T(8,128)} %broadcast_in_dim.23), calls=%async_computation.5 | async-start | bytes 65536 | tf_op jit(solution)/shard_map/all_to_all | solution.py:46
  121.2 57.8 %collective-permute-start.16 = (f32[16,128]{1,0:T(8,128)S(1)}, f32[16,128]{1,0:T(8,128)S(1)}, u32[]{:S(2)}, u32[]{:S(2)}) collective-permute-start(f32[16,128]{1,0:T(8,128)S(1)} %reduce_sum.57), channel_id=1, source_target_pairs={{0,128},{8,136},{16,144},{24,152},{32,160},{40,168},{48,176},{56,1... | collective-permute-start | bytes 24584 | tf_op jit(solution)/shard_map/ppermute | solution.py:60
  130.5 58.4 %collective-permute-start.4 = (f32[16,4,1792]{2,1,0:T(4,128)}, f32[16,4,1792]{2,1,0:T(4,128)S(1)}, u32[]{:S(2)}, u32[]{:S(2)}) collective-permute-start(f32[16,4,1792]{2,1,0:T(4,128)} %get-tuple-element.69), channel_id=1, source_target_pairs={{0,128},{8,136},{16,144},{24,152},{32,160},{40,168},{48,176},{56,1... | collective-permute-start | bytes 1376264 | tf_op jit(solution)/shard_map/ppermute | solution.py:60
  130.5 58.4 %collective-permute-start.6 = (f32[16,4,1792]{2,1,0:T(4,128)S(1)}, f32[16,4,1792]{2,1,0:T(4,128)S(1)}, u32[]{:S(2)}, u32[]{:S(2)}) collective-permute-start(f32[16,4,1792]{2,1,0:T(4,128)S(1)} %get-tuple-element.67), channel_id=1, source_target_pairs={{0,128},{8,136},{16,144},{24,152},{32,160},{40,168},{48,176},{56,1... | collective-permute-start | bytes 1376264 | tf_op jit(solution)/shard_map/ppermute | solution.py:60
  178.9 75.1 %collective-permute-start.11 = (f32[64,7168]{1,0:T(8,128)}, f32[64,7168]{1,0:T(8,128)}, u32[]{:S(2)}, u32[]{:S(2)}) collective-permute-start(f32[64,7168]{1,0:T(8,128)} %add.57), channel_id=1, source_target_pairs={{0,1},{1,0},{2,3},{3,2},{4,5},{5,4},{6,7},{7,6},{8,9},{9,8},{10,11... | collective-permute-start | bytes 5505032 | tf_op jit(solution)/shard_map/ppermute | solution.py:187
  179.6 15.7 %all-to-all-start.6 = ((f32[4,16,128]{2,1,0:T(8,128)}), f32[4,16,128]{2,1,0:T(8,128)S(1)}, u32[]{:S(2)}, u32[]{:S(2)}) async-start(f32[4,16,128]{2,1,0:T(8,128)} %broadcast_in_dim.24), calls=%async_computation.6 | async-start | bytes 65536 | tf_op jit(solution)/shard_map/all_to_all | solution.py:46
  188.9 48.3 %copy-start.10 = (f32[16,4,1792]{2,1,0:T(4,128)}, f32[16,4,1792]{2,1,0:T(4,128)S(1)}, u32[]{:S(2)}) copy-start(f32[16,4,1792]{2,1,0:T(4,128)S(1)} %collective-permute-done.4.rows_ref.refs_9_) | copy-start | bytes 1376260
  188.9 48.3 %copy-start.11 = (f32[16,4,1792]{2,1,0:T(4,128)}, f32[16,4,1792]{2,1,0:T(4,128)S(1)}, u32[]{:S(2)}) copy-start(f32[16,4,1792]{2,1,0:T(4,128)S(1)} %collective-permute-done.6.rows_ref.refs_8_) | copy-start | bytes 1376260
  188.9 124.2 %collective-permute-start.14 = (f32[16,4,1792]{2,1,0:T(4,128)}, f32[16,4,1792]{2,1,0:T(4,128)S(1)}, u32[]{:S(2)}, u32[]{:S(2)}) collective-permute-start(f32[16,4,1792]{2,1,0:T(4,128)} %get-tuple-element.31), channel_id=1, source_target_pairs={{0,128},{8,136},{16,144},{24,152},{32,160},{40,168},{48,176},{56,1... | collective-permute-start | bytes 1376264 | tf_op jit(solution)/shard_map/ppermute | solution.py:60
  195.1 127.5 %collective-permute-start.5 = (f32[16,4,1792]{2,1,0:T(4,128)}, f32[16,4,1792]{2,1,0:T(4,128)}, u32[]{:S(2)}, u32[]{:S(2)}) collective-permute-start(f32[16,4,1792]{2,1,0:T(4,128)} %get-tuple-element.26), channel_id=1, source_target_pairs={{0,128},{8,136},{16,144},{24,152},{32,160},{40,168},{48,176},{56,1... | collective-permute-start | bytes 1376264 | tf_op jit(solution)/shard_map/ppermute | solution.py:60
  196.0 50.5 %all-to-all-start.7 = ((f32[8,64,128]{2,1,0:T(8,128)}), f32[8,64,128]{2,1,0:T(8,128)S(1)}, u32[]{:S(2)}, u32[]{:S(2)}) async-start(f32[8,64,128]{2,1,0:T(8,128)} %broadcast_in_dim.25), calls=%async_computation.7 | async-start | bytes 524288 | tf_op jit(solution)/shard_map/all_to_all | solution.py:222
  246.4 32.3 %all-to-all-start = ((f32[16,4,7168]{2,1,0:T(4,128)}), f32[16,4,7168]{2,1,0:T(4,128)}, u32[]{:S(2)}, u32[]{:S(2)}) async-start(f32[16,4,7168]{2,1,0:T(4,128)} %get-tuple-element.66), calls=%async_computation | async-start | bytes 3670016 | tf_op jit(solution)/shard_map/all_to_all | solution.py:46
  254.1 2.7 copy-start.1
  254.1 3.1 copy-start.3
  254.1 3.7 copy-start.5
  289.6 12.0 %all-to-all-start.2 = ((f32[4,64,128]{2,1,0:T(8,128)}), f32[4,64,128]{2,1,0:T(8,128)S(1)}, u32[]{:S(2)}, u32[]{:S(2)}) async-start(f32[4,64,128]{2,1,0:T(8,128)} %shard_map.40), calls=%async_computation.2 | async-start | bytes 262144 | tf_op jit(solution)/shard_map/all_to_all | solution.py:46
  302.2 15.4 %all-to-all-start.3 = ((f32[4,64,128]{2,1,0:T(8,128)}), f32[4,64,128]{2,1,0:T(8,128)S(1)}, u32[]{:S(2)}, u32[]{:S(2)}) async-start(f32[4,64,128]{2,1,0:T(8,128)} %broadcast_in_dim.22), calls=%async_computation.3 | async-start | bytes 262144 | tf_op jit(solution)/shard_map/all_to_all | solution.py:46
  313.1 8.6 %copy-start.13 = (f32[4,64,128]{2,1,0:T(8,128)S(1)}, f32[4,64,128]{2,1,0:T(8,128)}, u32[]{:S(2)}) copy-start(f32[4,64,128]{2,1,0:T(8,128)} %shard_map.38) | copy-start | bytes 393220
  313.1 8.6 %copy-start.14 = (f32[4,64,128]{2,1,0:T(8,128)S(1)}, f32[4,64,128]{2,1,0:T(8,128)}, u32[]{:S(2)}) copy-start(f32[4,64,128]{2,1,0:T(8,128)} %shard_map.37) | copy-start | bytes 393220
  313.1 0.8 copy-start.12
  317.6 7.9 %collective-permute-start.15 = (f32[64,128]{1,0:T(8,128)S(1)}, f32[64,128]{1,0:T(8,128)S(1)}, u32[]{:S(2)}, u32[]{:S(2)}) collective-permute-start(f32[64,128]{1,0:T(8,128)S(1)} %reduce_sum.55), channel_id=1, source_target_pairs={{0,128},{8,136},{16,144},{24,152},{32,160},{40,168},{48,176},{56,1... | collective-permute-start | bytes 98312 | tf_op jit(solution)/shard_map/ppermute | solution.py:60
  329.3 38.7 %copy-start.15 = (f32[2,256,256]{2,1,0:T(8,128)S(1)}, f32[2,256,256]{2,1,0:T(8,128)}, u32[]{:S(2)}) copy-start(f32[2,256,256]{2,1,0:T(8,128)} %param.5) | copy-start | bytes 1572868
  349.2 7.9 %collective-permute-start.17 = (f32[64,128]{1,0:T(8,128)S(1)}, f32[64,128]{1,0:T(8,128)S(1)}, u32[]{:S(2)}, u32[]{:S(2)}) collective-permute-start(f32[64,128]{1,0:T(8,128)S(1)} %reduce_sum.59), channel_id=1, source_target_pairs={{0,128},{8,136},{16,144},{24,152},{32,160},{40,168},{48,176},{56,1... | collective-permute-start | bytes 98312 | tf_op jit(solution)/shard_map/ppermute | solution.py:60
  357.8 10.1 %all-to-all-start.10 = ((f32[4,128,128]{2,1,0:T(8,128)}), f32[4,128,128]{2,1,0:T(8,128)S(1)}, u32[]{:S(2)}, u32[]{:S(2)}) async-start(f32[4,128,128]{2,1,0:T(8,128)} %broadcast_in_dim.27), calls=%async_computation.10 | async-start | bytes 524288 | tf_op jit(solution)/shard_map/all_to_all | solution.py:46

commit v2 on v0

v2 whole, which is shorter than its diff:
```python
import functools

import jax
import jax.numpy as jnp
from jax import lax
from jax.experimental import pallas as pl
from jax.experimental.pallas import tpu as pltpu
from jax.sharding import PartitionSpec as P

UP_ONE = [(c, c + 2) for c in range(6)]
DOWN_ONE = [(c, c - 2) for c in range(2, 8)]
UP_TWO = [(c, c + 2) for c in range(2, 6)]
DOWN_TWO = [(c, c - 2) for c in range(2, 6)]
TO_ENDS = [(4, 6), (5, 7), (2, 0), (3, 1)]
SIBLING = [(c, c ^ 1) for c in range(8)]
FAR = [(r, (r + 16) % 32) for r in range(32)]
PLANES = [list(range(16)), list(range(16, 32))]


def along_x(step):
    return [(r, r // 4 * 4 + (r + step) % 4) for r in range(32)]


def along_y(step):
    return [(r, r // 16 * 16 + (r + 4 * step) % 16) for r in range(32)]


def upper_part(square):
    width = square.shape[0]
    rows = lax.broadcasted_iota(jnp.int32, (width, width), 0)
    cols = lax.broadcasted_iota(jnp.int32, (width, width), 1)
    return jnp.where(cols >= rows, square, jnp.zeros_like(square))


def matmul(left, right, precision=lax.Precision.HIGHEST):
    return jnp.dot(left, right, precision=precision, preferred_element_type=jnp.float32)


def matmul_nt(left, right):
    return lax.dot_general(
        left, right, (((1,), (1,)), ((), ())),
        precision=lax.Precision.HIGH, preferred_element_type=jnp.float32,
    )


def sum_over_prow(quarters, block):
    x = lax.axis_index("prow") % 4
    count = quarters.shape[1]

    def send(value, pairs):
        return lax.ppermute(value, "prow", pairs)

    def packed(step):
        part = lax.dynamic_index_in_dim(quarters, (x + step) % 4, 0, keepdims=False)
        return jnp.concatenate([part, block], axis=0)

    total = packed(0)
    for step in (1, 2, 3):
        total = total + send(packed(step), along_x(step))
    total = total + send(total, along_y(1)) + send(total, along_y(2)) + send(total, along_y(3))
    far = send(total, FAR)
    mid = count // 2
    total = total + jnp.concatenate([far[mid:count], far[:mid], far[count:]], axis=0)
    part = total[:count]
    return jnp.stack([part, *(send(part, along_x(4 - step)) for step in (1, 2, 3))]), total[count:]


def turned(parts, start):
    return lax.dynamic_slice_in_dim(jnp.concatenate([parts, parts], axis=0), start % 4, 4, 0)


def split(value):
    high = lax.reduce_precision(value, 8, 7)
    return high.astype(jnp.bfloat16), (value - high).astype(jnp.bfloat16)


def update_kernel(where_ref, rows_ref, scaled_ref, *refs):
    out_ref = refs[-1]
    count, mid = rows_ref.shape[0], rows_ref.shape[0] // 2
    mine, above, two, below, last = (
        jnp.concatenate([refs[j][...], refs[j + 1][...]], axis=0) for j in range(0, 10, 2)
    )
    above = jnp.where(where_ref[2] == 0, last, above)
    below = jnp.where(where_ref[3] == 0, last, below)
    dot = functools.partial(jnp.dot, preferred_element_type=jnp.float32)
    change = None
    for pair, slots in enumerate(((mine, above), (two, below))):
        vectors = jnp.concatenate(slots, axis=0)
        high = vectors.astype(jnp.bfloat16)
        low = (vectors - high.astype(jnp.float32)).astype(jnp.bfloat16)
        left = scaled_ref[:, slice(256 * pair, 256 * pair + 256)]
        both = dot(left, high)
        part = both[:count] + both[count:] + dot(left[:count], low)
        change = part if change is None else change + part
    result = rows_ref[...] - change
    place = pl.multiple_of(where_ref[0] * mid, mid)
    other = pl.multiple_of((1 - where_ref[0]) * mid, mid)
    out_ref[pl.ds(place, mid), :] = result[:mid]
    out_ref[pl.ds(other, mid), :] = result[mid:]


def update(half, chip, rows, scaled, pieces, tile=1024):
    count, length = rows.shape
    where = jnp.stack(
        [half, chip, (chip != 3) * 1, (chip != 0) * 1, ((chip == 0) | (chip == 3)) * 1]
    ).astype(jnp.int32)
    streams = (None, 2, None, 3, 4)

    def piece(flag):
        if flag is None:
            return pl.BlockSpec((64, tile), lambda i, w: (0, i))
        return pl.BlockSpec((64, tile), lambda i, w: (0, i * w[flag]))

    return pl.pallas_call(
        update_kernel,
        out_shape=jax.ShapeDtypeStruct(rows.shape, jnp.float32),
        grid_spec=pltpu.PrefetchScalarGridSpec(
            num_scalar_prefetch=1,
            grid=(length // tile,),
            in_specs=[
                pl.BlockSpec((count, tile), lambda i, w: (0, i)),
                pl.BlockSpec(scaled.shape, lambda i, w: (0, 0)),
                *[piece(flag) for flag in streams for _ in range(2)],
            ],
            out_specs=pl.BlockSpec((count, tile), lambda i, w: (0, i)),
        ),
        compiler_params=pltpu.CompilerParams(vmem_limit_bytes=60 * 1024 * 1024),
        cost_estimate=pl.CostEstimate(
            flops=6 * count * 512 * length,
            bytes_accessed=length * (count * 8 + 512 * 4),
            transcendentals=0,
        ),
    )(where, rows, scaled, *pieces)


def body(eigen_rows, reflectors, tfactors):
    count = eigen_rows.shape[0]
    prow = lax.axis_index("prow")
    x, half = prow % 4, prow // 16
    column = lax.axis_index("pcol")
    chip, core = column // 2, column % 2
    length = reflectors.shape[0]
    mine = reflectors.T

    def send(value, pairs):
        return lax.ppermute(value, "pcol", pairs)

    def ordered(piece, other, axis):
        return jnp.concatenate(
            [jnp.where(core == 0, piece, other), jnp.where(core == 0, other, piece)], axis=axis
        )

    blocks = eigen_rows.reshape(count, 32, length).transpose(1, 0, 2)
    leaving = lax.dynamic_slice_in_dim(blocks, (1 - half) * 16, 16, 0)
    staying = lax.dynamic_slice_in_dim(blocks, half * 16, 16, 0)
    mine, leaving = lax.optimization_barrier((mine, leaving))
    arriving = lax.ppermute(leaving, "prow", FAR)
    below = send(mine, UP_ONE)
    above = send(mine, DOWN_ONE)

    def over_plane(value):
        value = lax.all_to_all(
            value, "prow", split_axis=0, concat_axis=0, tiled=True, axis_index_groups=PLANES
        )
        return value.reshape(16 * count, length)

    staying = over_plane(staying)
    below_two = send(below, UP_TWO)
    above_two = send(above, DOWN_TWO)
    arriving = over_plane(arriving)
    arriving, below_two, above_two = lax.optimization_barrier((arriving, below_two, above_two))
    last = send(jnp.where(chip == 2, below_two, above_two), TO_ENDS)
    rows = jnp.concatenate([staying, arriving], axis=0)
    two = below_two + above_two

    pieces = (mine, above, two, below)
    swapped = [send(piece, SIBLING) for piece in pieces]
    all_mine, all_above, all_two, all_below = (
        ordered(piece, other, 0) for piece, other in zip(pieces, swapped)
    )

    left = jnp.where(chip == 0, two, jnp.where(chip == 3, mine, above))
    right = jnp.where(chip == 0, all_above, jnp.where(chip == 1, all_below, all_two))
    cross = matmul_nt(left, right)
    on_mine, on_two = matmul_nt(rows, all_mine), matmul_nt(rows, all_two)
    on_above, on_below = matmul_nt(rows, all_above), matmul_nt(rows, all_below)
    last, cross, on_mine, on_two, on_above, on_below = lax.optimization_barrier(
        (last, cross, on_mine, on_two, on_above, on_below)
    )

    last_other = send(last, SIBLING)
    zero = jnp.zeros_like
    last_other, on_last = lax.optimization_barrier((last_other, matmul_nt(rows, last)))
    on_last = ordered(on_last, matmul_nt(rows, last_other), 1)
    slots = jnp.stack(
        [
            on_mine,
            on_above + jnp.where(chip == 3, on_last, zero(on_last)),
            on_two,
            on_below + jnp.where(chip == 0, on_last, zero(on_last)),
        ]
    )
    projected, cross = sum_over_prow(slots, cross)
    cross = lax.all_to_all(
        jnp.broadcast_to(cross, (8, *cross.shape)), "pcol", split_axis=0, concat_axis=0, tiled=True
    ).reshape(4, 128, 128)
    cross = jnp.concatenate(
        [
            jnp.concatenate([cross[1], cross[0]], axis=1),
            jnp.concatenate([cross[2], cross[3]], axis=1),
        ],
        axis=0,
    )
    projected = turned(projected, 8 - chip - x)
    first = jnp.concatenate([projected[0], projected[1]], axis=1)
    second = jnp.concatenate([projected[2], projected[3]], axis=1)
    scaled_second = matmul(second, upper_part(tfactors[1]).T)
    scaled_first = matmul(first - matmul(scaled_second, cross), upper_part(tfactors[0]).T)
    scaled = jnp.stack(
        [scaled_first[:, :128], scaled_first[:, 128:], scaled_second[:, :128], scaled_second[:, 128:]]
    )
    scaled = turned(scaled, chip)
    scaled = jnp.where(core == 0, scaled, jnp.roll(scaled, 64, axis=2))
    scaled = jnp.concatenate([scaled[j] for j in range(4)], axis=1)
    scaled = jnp.concatenate(split(scaled), axis=0)

    pieces, swapped = (*pieces, last), (*swapped, last_other)
    return update(half, chip, rows, scaled, [v for pair in zip(pieces, swapped) for v in pair])


def solution(mesh):
    return jax.shard_map(
        body,
        mesh=mesh,
        in_specs=(P(("pcol", "prow"), None), P("prow", "pcol"), P()),
        out_specs=P("pcol", "prow"),
        check_vma=False,
    )
```

time: 315 us -> 293 us (0.930)
  other arithmetic: 30.8 us -> 13.5 us
  local copies, waits for them, and re-layouts: 29.8 us -> 16 us
  Pallas kernels: 6.22 us -> 12.5 us
    ppermute x11 -> x10, waiting for transfers between devices: 87.7 us -> 61.8 us  [send(): return lax.ppermute(value, 'pcol', pairs)]
    unnamed x64 -> x37, local copies, waits for them, and re-layouts: 15.9 us -> 4.02 us
    ppermute x10, waiting for transfers between devices: 5.39 us -> 16.8 us  [send(): return lax.ppermute(value, 'prow', pairs)]
    ppermute x1, waiting for transfers between devices: 32 us -> 42.3 us  [body(): arriving = lax.ppermute(leaving, 'prow', FAR)]
    convert_element_type x3 -> x1, other arithmetic: 8.32 us -> 0.03 us  [split(): return (high.astype(jnp.bfloat16), (value - high).astype(jnp.bfloat16))]
    select_n x5, other arithmetic: 16.5 us -> 10 us  [ordered(): jnp.where(core == 0, piece, other)]
    all_to_all x2, waiting for transfers between devices: 32.4 us -> 38.7 us  [over_plane(): lax.all_to_all(value, 'prow', split_axis=0, concat_axis=0, tiled=True, ax...]
    pallas_call x1, Pallas kernels: 6.22 us -> 12.5 us  [update(): pl.pallas_call(update_kernel, out_shape=jax.ShapeDtypeStruct(rows.shape,...]
  transfers between devices with their start and end apart: 25 -> 24, of which waited for: 12 -> 15; matrix products, arithmetic and copies ran while one was open for 17% -> 13% of each run, Pallas kernels for 0% -> 0%
where the time goes in v2:
time: 293 us; the launch traced here: 292 us
  waiting for transfers between devices  169 us (58%)
  starting transfers between devices  59.6 us (20%)
  matrix products  21.2 us (7%)
  local copies, waits for them, and re-layouts  16 us (5%)
  other arithmetic  13.5 us (5%)
  Pallas kernels  12.5 us (4%)
    ppermute x10, waiting for transfers between devices, send(): return lax.ppermute(value, 'pcol', pairs)  61.8 us
    ppermute x1, waiting for transfers between devices, body(): arriving = lax.ppermute(leaving, 'prow', FAR)  42.3 us
    all_to_all x2, waiting for transfers between devices, over_plane(): lax.all_to_all(value, 'prow', split_axis=0, concat_axis=0, tiled=True, ax...  38.7 us
    dot_general x7, matrix products, matmul_nt(): lax.dot_general(left, right, (((1,), (1,)), ((), ())), precision=lax.Prec...  20.1 us
    ppermute x10, starting transfers between devices, send(): return lax.ppermute(value, 'prow', pairs)  19.2 us
    ppermute x10, waiting for transfers between devices, send(): return lax.ppermute(value, 'prow', pairs)  16.8 us
    all_to_all x2, starting transfers between devices, over_plane(): lax.all_to_all(value, 'prow', split_axis=0, concat_axis=0, tiled=True, ax...  15 us
    pallas_call x1, Pallas kernels, update(): pl.pallas_call(update_kernel, out_shape=jax.ShapeDtypeStruct(rows.shape,...  12.5 us
  transfers between devices with their start and end apart: 24, of which 15 were waited for; matrix products, arithmetic and copies ran while one was open for 13% of the time, Pallas kernels for 0%

profile of v2, /device:TPU:2, one launch (start us, length us, event | category | flops | bytes accessed | tf_op | source)
XLA Modules:
  0.0 291.9 jit_solution(7616954956642196462)
XLA Ops:
  0.0 4.3 %dynamic-slice_bitcast_fusion = (f32[16,4,7168]{2,1,0:T(4,128)}, f32[16,4,7168]{2,1,0:T(4,128)}) fusion(f32[4,32,7168]{2,0,1:T(4,128)} %bitcast.104, s32[]{:T(128)S(6)} %select_n.181, s32[]{:T(128)S(6)} %select_n.180), kind=kLoop, calls=%fused_computation.15 | loop fusion | bytes 7340040 | tf_op jit(solution)/shard_map/dynamic_slice | solution.py:154
  4.3 1.3 collective-permute-start.3
  5.6 5.8 %collective-permute-start.1 = (f32[64,7168]{1,0:T(8,128)S(1)}, f32[64,7168]{1,0:T(8,128)}, u32[]{:S(2)}, u32[]{:S(2)}) collective-permute-start(f32[64,7168]{1,0:T(8,128)S(1)} %bitcast.100), channel_id=1, source_target_pairs={{0,2},{1,3},{2,4},{3,5},{4,6},{5,7},{8,10},{9,11},{10,12},{11,13},... | collective-permute-start | bytes 5505032 | tf_op jit(solution)/shard_map/ppermute | solution.py:146
  11.4 7.5 %all-to-all-start = ((f32[16,4,7168]{2,1,0:T(4,128)}), f32[16,4,7168]{2,1,0:T(4,128)}, u32[]{:S(2)}, u32[]{:S(2)}) async-start(f32[16,4,7168]{2,1,0:T(4,128)} %get-tuple-element.42), calls=%async_computation | async-start | bytes 3670016 | tf_op jit(solution)/shard_map/all_to_all | solution.py:162
  18.8 7.2 %collective-permute-start = (f32[16,4,7168]{2,1,0:T(4,128)}, f32[16,4,7168]{2,1,0:T(4,128)}, u32[]{:S(2)}, u32[]{:S(2)}) collective-permute-start(f32[16,4,7168]{2,1,0:T(4,128)} %get-tuple-element.18), channel_id=1, source_target_pairs={{0,128},{8,136},{16,144},{24,152},{32,160},{40,168},{48,176},{56,1... | collective-permute-start | bytes 5505032 | tf_op jit(solution)/shard_map/ppermute | solution.py:157
  26.0 16.9 %all-to-all-done = f32[16,4,7168]{2,1,0:T(4,128)} async-done(((f32[16,4,7168]{2,1,0:T(4,128)}), f32[16,4,7168]{2,1,0:T(4,128)}, u32[]{:S(2)}, u32[]{:S(2)}) %all-to-all-start) | async-done | bytes 1835040 | tf_op jit(solution)/shard_map/all_to_all | solution.py:162
  42.9 3.0 %reshape.19 = f32[64,7168]{1,0:T(8,128)} reshape(f32[16,4,7168]{2,1,0:T(4,128)} %all-to-all-done) | data formatting | bytes 3670016 | tf_op jit(solution)/shard_map/reshape | solution.py:165
  45.9 3.3 %collective-permute-done.3.refs_2_ = f32[64,7168]{1,0:T(8,128)} collective-permute-done((f32[64,7168]{1,0:T(8,128)S(1)}, f32[64,7168]{1,0:T(8,128)}, u32[]{:S(2)}, u32[]{:S(2)}) %collective-permute-start.3) | collective-permute-done | bytes 1835040 | tf_op jit(solution)/shard_map/ppermute | solution.py:146
  49.1 1.3 collective-permute-start.4
  50.5 1.9 collective-permute-start.2
  52.4 2.9 constant_dynamic-update-slice_fusion.1
  55.3 42.3 %collective-permute-done = f32[16,4,7168]{2,1,0:T(4,128)} collective-permute-done((f32[16,4,7168]{2,1,0:T(4,128)}, f32[16,4,7168]{2,1,0:T(4,128)}, u32[]{:S(2)}, u32[]{:S(2)}) %collective-permute-start) | collective-permute-done | bytes 1835040 | tf_op jit(solution)/shard_map/ppermute | solution.py:157
  97.5 7.5 %all-to-all-start.1 = ((f32[16,4,7168]{2,1,0:T(4,128)}), f32[16,4,7168]{2,1,0:T(4,128)}, u32[]{:S(2)}, u32[]{:S(2)}) async-start(f32[16,4,7168]{2,1,0:T(4,128)} %collective-permute-done), calls=%async_computation.1 | async-start | bytes 3670016 | tf_op jit(solution)/shard_map/all_to_all | solution.py:162
  105.0 3.6 %broadcast_select_fusion.1 = (f32[64,7168]{1,0:T(8,128)}, f32[64,7168]{1,0:T(8,128)}) fusion(f32[64,7168]{1,0:T(8,128)S(1)} %bitcast.102, f32[64,7168]{1,0:T(8,128)} %collective-permute-done.9.refs_1_, pred[]{:T(512)S(6)} %eq.42), kind=kLoop, calls=%fused_computation.21 | loop fusion | flops 917504 | bytes 7340033 | tf_op jit(solution)/shard_map/jit(_where)/select_n | solution.py:150
  108.6 21.8 %all-to-all-done.1 = f32[16,4,7168]{2,1,0:T(4,128)} async-done(((f32[16,4,7168]{2,1,0:T(4,128)}), f32[16,4,7168]{2,1,0:T(4,128)}, u32[]{:S(2)}, u32[]{:S(2)}) %all-to-all-start.1) | async-done | bytes 1835040 | tf_op jit(solution)/shard_map/all_to_all | solution.py:162
  130.5 2.9 %reshape.20 = f32[64,7168]{1,0:T(8,128)} reshape(f32[16,4,7168]{2,1,0:T(4,128)} %all-to-all-done.1) | data formatting | bytes 3670016 | tf_op jit(solution)/shard_map/reshape | solution.py:165
  133.4 32.8 %collective-permute-done.4 = f32[64,7168]{1,0:T(8,128)} collective-permute-done((f32[64,7168]{1,0:T(8,128)}, f32[64,7168]{1,0:T(8,128)}, u32[]{:S(2)}, u32[]{:S(2)}) %collective-permute-start.4) | collective-permute-done | bytes 1835040 | tf_op jit(solution)/shard_map/ppermute | solution.py:146
  166.2 2.4 fusion.53
  168.6 1.3 collective-permute-start.5
  170.3 3.7 %broadcast_select_fusion.5 = (f32[64,7168]{1,0:T(8,128)S(1)}, f32[64,7168]{1,0:T(8,128)S(1)}) fusion(f32[64,7168]{1,0:T(8,128)} %collective-permute-done.1.refs_6_, f32[64,7168]{1,0:T(8,128)} %collective-permute-done.7.refs_7_, pred[]{:T(512)S(6)} %eq.42), kind=kLoop, calls=%fused_computation.25 | loop fusion | flops 917504 | bytes 7340033 | tf_op jit(solution)/shard_map/jit(_where)/select_n | solution.py:150
  174.0 1.9 fusion.8
  175.9 2.4 broadcast_select_fusion.7
  178.3 1.9 fusion.9
  180.3 1.7 fusion
  182.4 0.9 copy-done.5
  183.3 1.9 fusion.7
  185.2 4.1 %fusion.4 = f32[64,128]{1,0:T(8,128)S(1)} fusion(f32[64,7168]{1,0:T(8,128)S(1)} %get-tuple-element.38, f32[64,7168]{1,0:T(8,128)S(1)} %get-tuple-element.37, f32[64,7168]{1,0:T(8,128)S(1)} %get-tuple-element.36, f32[64,7168]{1,0:T(8,128)S(1)} %get-tuple-element.35, f32[64,7168]{1,0:T(8,128)S(1)} %get-tuple-element.34, f32[64,7168]{1,0:T(8,128)S(1)} %get-tuple-element.33, ...), kind=kOutput, calls=%fused_computation.7 | convolution fusion | flops 357826560 | bytes 16547843 | tf_op jit(solution)/shard_map/dot_general | solution.py:40
  189.2 25.7 %collective-permute-done.5.refs_8_ = f32[64,7168]{1,0:T(8,128)} collective-permute-done((f32[64,7168]{1,0:T(8,128)S(1)}, f32[64,7168]{1,0:T(8,128)}, u32[]{:S(2)}, u32[]{:S(2)}) %collective-permute-start.5) | collective-permute-done | bytes 1835040 | tf_op jit(solution)/shard_map/ppermute | solution.py:146
  214.9 4.6 %fusion.56 = f32[128,64]{0,1:T(8,128)S(1)} fusion(f32[128,7168]{1,0:T(8,128)} %copy-done.1, f32[64,7168]{1,0:T(8,128)} %collective-permute-done.5.refs_8_), kind=kOutput, calls=%fused_computation.119 | convolution fusion | flops 352321536 | bytes 5537792 | tf_op jit(solution)/shard_map/dot_general | solution.py:40
  219.6 4.2 %fusion.57 = f32[128,64]{1,0:T(8,128)S(1)} fusion(f32[128,7168]{1,0:T(8,128)} %copy-done.1, f32[64,7168]{1,0:T(8,128)S(1)} %collective-permute-done.10.refs_9_), kind=kOutput, calls=%fused_computation.120 | convolution fusion | flops 352321536 | bytes 5537792 | tf_op jit(solution)/shard_map/dot_general | solution.py:40
  224.0 1.7 collective-permute-start.11
  225.8 5.4 %collective-permute-start.12 = (f32[192,128]{1,0:T(8,128)S(1)}, f32[192,128]{1,0:T(8,128)S(1)}, u32[]{:S(2)}, u32[]{:S(2)}) collective-permute-start(f32[192,128]{1,0:T(8,128)S(1)} %get-tuple-element.71), channel_id=1, source_target_pairs={{0,16},{8,24},{16,0},{24,8},{32,48},{40,56},{48,32},{56,40},{64,80... | collective-permute-start | bytes 294920 | tf_op jit(solution)/shard_map/ppermute | solution.py:51
  231.2 1.6 collective-permute-done.11
  232.7 2.0 collective-permute-done.12
  234.7 1.7 collective-permute-done.13
  236.5 1.6 collective-permute-start.16
  238.1 1.3 collective-permute-start.15
  239.4 2.6 collective-permute-done.16
  242.1 2.7 collective-permute-done.15
  244.7 1.0 collective-permute-done.14
  245.8 3.0 %collective-permute-start.17 = (f32[192,128]{1,0:T(8,128)S(1)}, f32[192,128]{1,0:T(8,128)S(1)}, u32[]{:S(2)}, u32[]{:S(2)}) collective-permute-start(f32[192,128]{1,0:T(8,128)S(1)} %add_add_fusion), channel_id=1, source_target_pairs={{0,128},{8,136},{16,144},{24,152},{32,160},{40,168},{48,176},{56,1... | collective-permute-start | bytes 294920 | tf_op jit(solution)/shard_map/ppermute | solution.py:51
  249.3 5.1 %collective-permute-done.17 = f32[192,128]{1,0:T(8,128)S(1)} collective-permute-done((f32[192,128]{1,0:T(8,128)S(1)}, f32[192,128]{1,0:T(8,128)S(1)}, u32[]{:S(2)}, u32[]{:S(2)}) %collective-permute-start.17) | collective-permute-done | bytes 98336 | tf_op jit(solution)/shard_map/ppermute | solution.py:51
  254.5 4.1 %collective-permute-start.19 = (f32[128,128]{1,0:T(8,128)S(1)}, f32[128,128]{1,0:T(8,128)S(1)}, u32[]{:S(2)}, u32[]{:S(2)}) collective-permute-start(f32[128,128]{1,0:T(8,128)S(1)} %slice.109), channel_id=1, source_target_pairs={{0,16},{8,24},{16,0},{24,8},{32,48},{40,56},{48,32},{56,40},{64,80... | collective-permute-start | bytes 196616 | tf_op jit(solution)/shard_map/ppermute | solution.py:51
  258.7 2.0 collective-permute-start.20
  260.7 0.7 broadcast_in_dim.3
  261.4 6.4 %all-to-all-start.2 = ((f32[8,64,128]{2,1,0:T(8,128)}), f32[8,64,128]{2,1,0:T(8,128)S(1)}, u32[]{:S(2)}, u32[]{:S(2)}) async-start(f32[8,64,128]{2,1,0:T(8,128)} %broadcast_in_dim.3), calls=%async_computation.2 | async-start | bytes 524288 | tf_op jit(solution)/shard_map/all_to_all | solution.py:204
  268.4 9.2 %all-to-all-done.2 = f32[8,64,128]{2,1,0:T(8,128)S(1)} async-done(((f32[8,64,128]{2,1,0:T(8,128)}), f32[8,64,128]{2,1,0:T(8,128)S(1)}, u32[]{:S(2)}, u32[]{:S(2)}) %all-to-all-start.2) | async-done | bytes 262176 | tf_op jit(solution)/shard_map/all_to_all | solution.py:204
  279.5 12.5 %shard_map.37 = f32[128,7168]{1,0:T(8,128)} custom-call(s32[5]{0:T(128)} %stack.76.where_ref, f32[128,7168]{1,0:T(8,128)} %copy-done.1, bf16[256,512]{1,0:T(8,128)(2,1)} %pad_maximum_fusion.11.scaled_ref, f32[64,7168]{1,0:T(8,128)} %bitcast.98, f32[64,7168]{1,0:T(8,128)} %collective-permute-done.9.refs_1_, f32[64,7168]{1,0:T(8,128)} %collective-permute-done.3.refs_2_, ...), custom_call_target="tpu_custom_call" | custom-call | flops 2818572288 | bytes 22020096 | tf_op jit(solution)/shard_map/pallas_call | solution.py:114
  (80 shorter events, 4.3 us)
Async XLA Ops:
  0.0 4.3 %copy-start.3 = (f32[7168,64]{0,1:T(8,128)S(1)}, f32[7168,64]{0,1:T(8,128)}, u32[]{:S(2)}) copy-start(f32[7168,64]{0,1:T(8,128)} %param.4) | copy-start | bytes 5505028
  4.3 44.9 %collective-permute-start.3 = (f32[64,7168]{1,0:T(8,128)S(1)}, f32[64,7168]{1,0:T(8,128)}, u32[]{:S(2)}, u32[]{:S(2)}) collective-permute-start(f32[64,7168]{1,0:T(8,128)S(1)} %bitcast.99), channel_id=1, source_target_pairs={{2,0},{3,1},{4,2},{5,3},{6,4},{7,5},{10,8},{11,9},{12,10},{13,11},... | collective-permute-start | bytes 5505032 | tf_op jit(solution)/shard_map/ppermute | solution.py:146
  5.6 45.0 %collective-permute-start.1 = (f32[64,7168]{1,0:T(8,128)S(1)}, f32[64,7168]{1,0:T(8,128)}, u32[]{:S(2)}, u32[]{:S(2)}) collective-permute-start(f32[64,7168]{1,0:T(8,128)S(1)} %bitcast.100), channel_id=1, source_target_pairs={{0,2},{1,3},{2,4},{3,5},{4,6},{5,7},{8,10},{9,11},{10,12},{11,13},... | collective-permute-start | bytes 5505032 | tf_op jit(solution)/shard_map/ppermute | solution.py:146
  11.4 31.5 %all-to-all-start = ((f32[16,4,7168]{2,1,0:T(4,128)}), f32[16,4,7168]{2,1,0:T(4,128)}, u32[]{:S(2)}, u32[]{:S(2)}) async-start(f32[16,4,7168]{2,1,0:T(4,128)} %get-tuple-element.42), calls=%async_computation | async-start | bytes 3670016 | tf_op jit(solution)/shard_map/all_to_all | solution.py:162
  18.8 78.7 %collective-permute-start = (f32[16,4,7168]{2,1,0:T(4,128)}, f32[16,4,7168]{2,1,0:T(4,128)}, u32[]{:S(2)}, u32[]{:S(2)}) collective-permute-start(f32[16,4,7168]{2,1,0:T(4,128)} %get-tuple-element.18), channel_id=1, source_target_pairs={{0,128},{8,136},{16,144},{24,152},{32,160},{40,168},{48,176},{56,1... | collective-permute-start | bytes 5505032 | tf_op jit(solution)/shard_map/ppermute | solution.py:157
  26.0 79.0 %collective-permute-start.9 = (f32[64,7168]{1,0:T(8,128)S(1)}, f32[64,7168]{1,0:T(8,128)}, u32[]{:S(2)}, u32[]{:S(2)}) collective-permute-start(f32[64,7168]{1,0:T(8,128)S(1)} %bitcast.101), channel_id=1, source_target_pairs={{0,1},{1,0},{2,3},{3,2},{4,5},{5,4},{6,7},{7,6},{8,9},{9,8},{10,11... | collective-permute-start | bytes 5505032 | tf_op jit(solution)/shard_map/ppermute | solution.py:146
  49.1 117.0 %collective-permute-start.4 = (f32[64,7168]{1,0:T(8,128)}, f32[64,7168]{1,0:T(8,128)}, u32[]{:S(2)}, u32[]{:S(2)}) collective-permute-start(f32[64,7168]{1,0:T(8,128)} %collective-permute-done.3.refs_2_), channel_id=1, source_target_pairs={{2,0},{3,1},{4,2},{5,3},{10,8},{11,9},{12,10},{13,11},{18,16},{19,... | collective-permute-start | bytes 5505032 | tf_op jit(solution)/shard_map/ppermute | solution.py:146
  50.5 115.6 %collective-permute-start.2 = (f32[64,7168]{1,0:T(8,128)}, f32[64,7168]{1,0:T(8,128)}, u32[]{:S(2)}, u32[]{:S(2)}) collective-permute-start(f32[64,7168]{1,0:T(8,128)} %collective-permute-done.1.refs_6_), channel_id=1, source_target_pairs={{2,4},{3,5},{4,6},{5,7},{10,12},{11,13},{12,14},{13,15},{18,20},{1... | collective-permute-start | bytes 5505032 | tf_op jit(solution)/shard_map/ppermute | solution.py:146
  55.3 120.6 %collective-permute-start.6 = (f32[64,7168]{1,0:T(8,128)}, f32[64,7168]{1,0:T(8,128)}, u32[]{:S(2)}, u32[]{:S(2)}) collective-permute-start(f32[64,7168]{1,0:T(8,128)} %collective-permute-done.3.refs_2_), channel_id=1, source_target_pairs={{0,1},{1,0},{2,3},{3,2},{4,5},{5,4},{6,7},{7,6},{8,9},{9,8},{10,11... | collective-permute-start | bytes 5505032 | tf_op jit(solution)/shard_map/ppermute | solution.py:146
  97.5 72.8 %collective-permute-start.7 = (f32[64,7168]{1,0:T(8,128)}, f32[64,7168]{1,0:T(8,128)}, u32[]{:S(2)}, u32[]{:S(2)}) collective-permute-start(f32[64,7168]{1,0:T(8,128)} %collective-permute-done.1.refs_6_), channel_id=1, source_target_pairs={{0,1},{1,0},{2,3},{3,2},{4,5},{5,4},{6,7},{7,6},{8,9},{9,8},{10,11... | collective-permute-start | bytes 5505032 | tf_op jit(solution)/shard_map/ppermute | solution.py:146
  97.5 32.9 %all-to-all-start.1 = ((f32[16,4,7168]{2,1,0:T(4,128)}), f32[16,4,7168]{2,1,0:T(4,128)}, u32[]{:S(2)}, u32[]{:S(2)}) async-start(f32[16,4,7168]{2,1,0:T(4,128)} %collective-permute-done), calls=%async_computation.1 | async-start | bytes 3670016 | tf_op jit(solution)/shard_map/all_to_all | solution.py:162
  133.4 36.8 %copy-start = (f32[128,7168]{1,0:T(8,128)S(1)}, f32[128,7168]{1,0:T(8,128)}, u32[]{:S(2)}) copy-start(f32[128,7168]{1,0:T(8,128)} %constant_dynamic-update-slice_fusion.1) | copy-start | bytes 11010052
  133.4 36.8 %copy-start.7 = (f32[64,7168]{1,0:T(8,128)S(1)}, f32[64,7168]{1,0:T(8,128)}, u32[]{:S(2)}) copy-start(f32[64,7168]{1,0:T(8,128)} %reshape.20) | copy-start | bytes 5505028
  168.6 16.6 %copy-start.2 = (f32[64,7168]{1,0:T(8,128)}, f32[64,7168]{1,0:T(8,128)S(1)}, u32[]{:S(2)}) copy-start(f32[64,7168]{1,0:T(8,128)S(1)} %get-tuple-element.39.refs_4_) | copy-start | bytes 5505028
  168.6 46.3 %collective-permute-start.5 = (f32[64,7168]{1,0:T(8,128)S(1)}, f32[64,7168]{1,0:T(8,128)}, u32[]{:S(2)}, u32[]{:S(2)}) collective-permute-start(f32[64,7168]{1,0:T(8,128)S(1)} %get-tuple-element.40), channel_id=1, source_target_pairs={{4,6},{5,7},{2,0},{3,1},{12,14},{13,15},{10,8},{11,9},{20,22},{21,... | collective-permute-start | bytes 5505032 | tf_op jit(solution)/shard_map/ppermute | solution.py:146
  169.9 12.1 %collective-permute-start.8 = (f32[64,7168]{1,0:T(8,128)S(1)}, f32[64,7168]{1,0:T(8,128)S(1)}, u32[]{:S(2)}, u32[]{:S(2)}) collective-permute-start(f32[64,7168]{1,0:T(8,128)S(1)} %get-tuple-element.39.refs_4_), channel_id=1, source_target_pairs={{0,1},{1,0},{2,3},{3,2},{4,5},{5,4},{6,7},{7,6},{8,9},{9,8},{10,11... | collective-permute-start | bytes 5505032 | tf_op jit(solution)/shard_map/ppermute | solution.py:146
  170.3 13.0 %copy-start.1 = (f32[128,7168]{1,0:T(8,128)}, f32[128,7168]{1,0:T(8,128)S(1)}, u32[]{:S(2)}) copy-start(f32[128,7168]{1,0:T(8,128)S(1)} %constant_dynamic-update-slice_fusion.rows_ref) | copy-start | bytes 11010052
  178.3 1.9 copy-start.8
  178.3 2.0 copy-start.9
  182.0 1.2 copy-start.5
  183.3 1.9 copy-start.4
  214.9 4.6 %collective-permute-start.10 = (f32[64,7168]{1,0:T(8,128)}, f32[64,7168]{1,0:T(8,128)S(1)}, u32[]{:S(2)}, u32[]{:S(2)}) collective-permute-start(f32[64,7168]{1,0:T(8,128)} %collective-permute-done.5.refs_8_), channel_id=1, source_target_pairs={{0,1},{1,0},{2,3},{3,2},{4,5},{5,4},{6,7},{7,6},{8,9},{9,8},{10,11... | collective-permute-start | bytes 5505032 | tf_op jit(solution)/shard_map/ppermute | solution.py:146
  219.5 4.3 %copy-start.6 = (f32[64,7168]{1,0:T(8,128)}, f32[64,7168]{1,0:T(8,128)S(1)}, u32[]{:S(2)}) copy-start(f32[64,7168]{1,0:T(8,128)S(1)} %collective-permute-done.10.refs_9_) | copy-start | bytes 5505028
  224.0 8.7 %collective-permute-start.11 = (f32[192,128]{1,0:T(8,128)S(1)}, f32[192,128]{1,0:T(8,128)S(1)}, u32[]{:S(2)}, u32[]{:S(2)}) collective-permute-start(f32[192,128]{1,0:T(8,128)S(1)} %get-tuple-element.70), channel_id=1, source_target_pairs={{0,8},{8,16},{16,24},{24,0},{32,40},{40,48},{48,56},{56,32},{64,72... | collective-permute-start | bytes 294920 | tf_op jit(solution)/shard_map/ppermute | solution.py:51
  225.8 8.9 %collective-permute-start.12 = (f32[192,128]{1,0:T(8,128)S(1)}, f32[192,128]{1,0:T(8,128)S(1)}, u32[]{:S(2)}, u32[]{:S(2)}) collective-permute-start(f32[192,128]{1,0:T(8,128)S(1)} %get-tuple-element.71), channel_id=1, source_target_pairs={{0,16},{8,24},{16,0},{24,8},{32,48},{40,56},{48,32},{56,40},{64,80... | collective-permute-start | bytes 294920 | tf_op jit(solution)/shard_map/ppermute | solution.py:51
  231.2 5.3 %collective-permute-start.13 = (f32[192,128]{1,0:T(8,128)S(1)}, f32[192,128]{1,0:T(8,128)S(1)}, u32[]{:S(2)}, u32[]{:S(2)}) collective-permute-start(f32[192,128]{1,0:T(8,128)S(1)} %get-tuple-element.72), channel_id=1, source_target_pairs={{0,24},{8,0},{16,8},{24,16},{32,56},{40,32},{48,40},{56,48},{64,88... | collective-permute-start | bytes 294920 | tf_op jit(solution)/shard_map/ppermute | solution.py:51
  236.5 31.5 %copy-start.10 = (f32[2,256,256]{2,1,0:T(8,128)S(1)}, f32[2,256,256]{2,1,0:T(8,128)}, u32[]{:S(2)}) copy-start(f32[2,256,256]{2,1,0:T(8,128)} %param.5) | copy-start | bytes 1572868
  236.5 5.6 %collective-permute-start.16 = (f32[192,128]{1,0:T(8,128)S(1)}, f32[192,128]{1,0:T(8,128)S(1)}, u32[]{:S(2)}, u32[]{:S(2)}) collective-permute-start(f32[192,128]{1,0:T(8,128)S(1)} %fusion.35), channel_id=1, source_target_pairs={{0,96},{8,104},{16,112},{24,120},{32,0},{40,8},{48,16},{56,24},{64... | collective-permute-start | bytes 294920 | tf_op jit(solution)/shard_map/ppermute | solution.py:51
  238.1 6.7 %collective-permute-start.15 = (f32[192,128]{1,0:T(8,128)S(1)}, f32[192,128]{1,0:T(8,128)S(1)}, u32[]{:S(2)}, u32[]{:S(2)}) collective-permute-start(f32[192,128]{1,0:T(8,128)S(1)} %fusion.35), channel_id=1, source_target_pairs={{0,64},{8,72},{16,80},{24,88},{32,96},{40,104},{48,112},{56,120},{... | collective-permute-start | bytes 294920 | tf_op jit(solution)/shard_map/ppermute | solution.py:51
  239.4 6.3 %collective-permute-start.14 = (f32[192,128]{1,0:T(8,128)S(1)}, f32[192,128]{1,0:T(8,128)S(1)}, u32[]{:S(2)}, u32[]{:S(2)}) collective-permute-start(f32[192,128]{1,0:T(8,128)S(1)} %fusion.35), channel_id=1, source_target_pairs={{0,32},{8,40},{16,48},{24,56},{32,64},{40,72},{48,80},{56,88},{64,... | collective-permute-start | bytes 294920 | tf_op jit(solution)/shard_map/ppermute | solution.py:51
  245.8 8.7 %collective-permute-start.17 = (f32[192,128]{1,0:T(8,128)S(1)}, f32[192,128]{1,0:T(8,128)S(1)}, u32[]{:S(2)}, u32[]{:S(2)}) collective-permute-start(f32[192,128]{1,0:T(8,128)S(1)} %add_add_fusion), channel_id=1, source_target_pairs={{0,128},{8,136},{16,144},{24,152},{32,160},{40,168},{48,176},{56,1... | collective-permute-start | bytes 294920 | tf_op jit(solution)/shard_map/ppermute | solution.py:51
  254.5 13.3 %collective-permute-start.19 = (f32[128,128]{1,0:T(8,128)S(1)}, f32[128,128]{1,0:T(8,128)S(1)}, u32[]{:S(2)}, u32[]{:S(2)}) collective-permute-start(f32[128,128]{1,0:T(8,128)S(1)} %slice.109), channel_id=1, source_target_pairs={{0,16},{8,24},{16,0},{24,8},{32,48},{40,56},{48,32},{56,40},{64,80... | collective-permute-start | bytes 196616 | tf_op jit(solution)/shard_map/ppermute | solution.py:51
  258.7 9.2 %collective-permute-start.18 = (f32[128,128]{1,0:T(8,128)S(1)}, f32[128,128]{1,0:T(8,128)S(1)}, u32[]{:S(2)}, u32[]{:S(2)}) collective-permute-start(f32[128,128]{1,0:T(8,128)S(1)} %slice.109), channel_id=1, source_target_pairs={{0,24},{8,0},{16,8},{24,16},{32,56},{40,32},{48,40},{56,48},{64,88... | collective-permute-start | bytes 196616 | tf_op jit(solution)/shard_map/ppermute | solution.py:51
  258.7 9.2 %collective-permute-start.20 = (f32[128,128]{1,0:T(8,128)S(1)}, f32[128,128]{1,0:T(8,128)S(1)}, u32[]{:S(2)}, u32[]{:S(2)}) collective-permute-start(f32[128,128]{1,0:T(8,128)S(1)} %slice.109), channel_id=1, source_target_pairs={{0,8},{8,16},{16,24},{24,0},{32,40},{40,48},{48,56},{56,32},{64,72... | collective-permute-start | bytes 196616 | tf_op jit(solution)/shard_map/ppermute | solution.py:51
  261.4 16.1 %all-to-all-start.2 = ((f32[8,64,128]{2,1,0:T(8,128)}), f32[8,64,128]{2,1,0:T(8,128)S(1)}, u32[]{:S(2)}, u32[]{:S(2)}) async-start(f32[8,64,128]{2,1,0:T(8,128)} %broadcast_in_dim.3), calls=%async_computation.2 | async-start | bytes 524288 | tf_op jit(solution)/shard_map/all_to_all | solution.py:204

commit v3 on v2

--- a/solution.py
+++ b/solution.py
@@ -43,26 +43,22 @@
     )
 
 
-def sum_over_prow(quarters, block):
+def sum_over_prow(quarters):
     x = lax.axis_index("prow") % 4
-    count = quarters.shape[1]
 
     def send(value, pairs):
         return lax.ppermute(value, "prow", pairs)
 
-    def packed(step):
-        part = lax.dynamic_index_in_dim(quarters, (x + step) % 4, 0, keepdims=False)
-        return jnp.concatenate([part, block], axis=0)
-
-    total = packed(0)
+    def quarter(step):
+        return lax.dynamic_index_in_dim(quarters, (x + step) % 4, 0, keepdims=False)
+
+    total = quarter(0)
     for step in (1, 2, 3):
-        total = total + send(packed(step), along_x(step))
+        total = total + send(quarter(step), along_x(step))
     total = total + send(total, along_y(1)) + send(total, along_y(2)) + send(total, along_y(3))
     far = send(total, FAR)
-    mid = count // 2
-    total = total + jnp.concatenate([far[mid:count], far[:mid], far[count:]], axis=0)
-    part = total[:count]
-    return jnp.stack([part, *(send(part, along_x(4 - step)) for step in (1, 2, 3))]), total[count:]
+    total = total + jnp.concatenate([far[64:128], far[:64], far[128:]], axis=0)
+    return jnp.stack([total, *(send(total, along_x(4 - step)) for step in (1, 2, 3))])
 
 
 def turned(parts, start):
@@ -168,7 +164,7 @@
     below_two = send(below, UP_TWO)
     above_two = send(above, DOWN_TWO)
     arriving = over_plane(arriving)
-    arriving, below_two, above_two = lax.optimization_barrier((arriving, below_two, above_two))
+    arriving, _, _ = lax.optimization_barrier((arriving, below_two, above_two))
     last = send(jnp.where(chip == 2, below_two, above_two), TO_ENDS)
     rows = jnp.concatenate([staying, arriving], axis=0)
     two = below_two + above_two
@@ -181,37 +177,38 @@
 
     left = jnp.where(chip == 0, two, jnp.where(chip == 3, mine, above))
     right = jnp.where(chip == 0, all_above, jnp.where(chip == 1, all_below, all_two))
-    cross = matmul_nt(left, right)
+    cross = lax.all_to_all(
+        jnp.broadcast_to(matmul_nt(left, right), (8, 64, 128)),
+        "pcol", split_axis=0, concat_axis=0, tiled=True,
+    ).reshape(4, 128, 128)
+    cross = jnp.stack([cross[1], cross[0], cross[2], cross[3]])
     on_mine, on_two = matmul_nt(rows, all_mine), matmul_nt(rows, all_two)
     on_above, on_below = matmul_nt(rows, all_above), matmul_nt(rows, all_below)
     last, cross, on_mine, on_two, on_above, on_below = lax.optimization_barrier(
         (last, cross, on_mine, on_two, on_above, on_below)
     )
-
     last_other = send(last, SIBLING)
-    zero = jnp.zeros_like
-    last_other, on_last = lax.optimization_barrier((last_other, matmul_nt(rows, last)))
-    on_last = ordered(on_last, matmul_nt(rows, last_other), 1)
+    on_last = matmul_nt(rows, jnp.concatenate([last, last_other], axis=0))
+    on_last = jnp.where(core == 0, on_last, jnp.roll(on_last, 64, axis=1))
+    zero = jnp.zeros_like(on_last)
     slots = jnp.stack(
         [
             on_mine,
-            on_above + jnp.where(chip == 3, on_last, zero(on_last)),
+            on_above + jnp.where(chip == 3, on_last, zero),
             on_two,
-            on_below + jnp.where(chip == 0, on_last, zero(on_last)),
+            on_below + jnp.where(chip == 0, on_last, zero),
         ]
     )
-    projected, cross = sum_over_prow(slots, cross)
-    cross = lax.all_to_all(
-        jnp.broadcast_to(cross, (8, *cross.shape)), "pcol", split_axis=0, concat_axis=0, tiled=True
-    ).reshape(4, 128, 128)
+    summed = sum_over_prow(jnp.concatenate([slots, cross], axis=1))
+    cross = turned(summed[:, 128:], 4 - x)
     cross = jnp.concatenate(
         [
-            jnp.concatenate([cross[1], cross[0]], axis=1),
+            jnp.concatenate([cross[0], cross[1]], axis=1),
             jnp.concatenate([cross[2], cross[3]], axis=1),
         ],
         axis=0,
     )
-    projected = turned(projected, 8 - chip - x)
+    projected = turned(summed[:, :128], 8 - chip - x)
     first = jnp.concatenate([projected[0], projected[1]], axis=1)
     second = jnp.concatenate([projected[2], projected[3]], axis=1)
     scaled_second = matmul(second, upper_part(tfactors[1]).T)

time: 293 us -> 291 us (level)
  waiting for transfers between devices: 169 us -> 156 us
  starting transfers between devices: 59.6 us -> 65.2 us
    ppermute x10, waiting for transfers between devices: 61.8 us -> 40.1 us  [send(): return lax.ppermute(value, 'pcol', pairs)]
    all_to_all x1, starting transfers between devices: 6.4 us -> 11.8 us  [body(): lax.all_to_all(jnp.broadcast_to(matmul_nt(left, right), (8, 64, 128)), 'p...]
    ppermute x10, waiting for transfers between devices: 16.8 us -> 21.9 us  [send(): return lax.ppermute(value, 'prow', pairs)]
    all_to_all x1, waiting for transfers between devices: 9.15 us -> 13.2 us  [body(): lax.all_to_all(jnp.broadcast_to(matmul_nt(left, right), (8, 64, 128)), 'p...]
    dot_general x7 -> x6, matrix products: 20.1 us -> 19.2 us  [matmul_nt(): lax.dot_general(left, right, (((1,), (1,)), ((), ())), precision=lax.Prec...]
    select_n x5 -> x4, other arithmetic: 10 us -> 10.1 us  [ordered(): jnp.where(core == 0, piece, other)]
  transfers between devices with their start and end apart: 24 -> 24, of which waited for: 15 -> 16; matrix products, arithmetic and copies ran while one was open for 13% -> 13% of each run, Pallas kernels for 0% -> 0%
where the time goes in v3:
time: 291 us; the launch traced here: 287 us
  waiting for transfers between devices  156 us (54%)
  starting transfers between devices  65.2 us (22%)
  matrix products  20.3 us (7%)
  local copies, waits for them, and re-layouts  17.9 us (6%)
  other arithmetic  14.9 us (5%)
  Pallas kernels  12.5 us (4%)
    ppermute x1, waiting for transfers between devices, body(): arriving = lax.ppermute(leaving, 'prow', FAR)  42.2 us
    ppermute x10, waiting for transfers between devices, send(): return lax.ppermute(value, 'pcol', pairs)  40.1 us
    all_to_all x2, waiting for transfers between devices, over_plane(): lax.all_to_all(value, 'prow', split_axis=0, concat_axis=0, tiled=True, ax...  38.6 us
    ppermute x10, waiting for transfers between devices, send(): return lax.ppermute(value, 'prow', pairs)  21.9 us
    dot_general x6, matrix products, matmul_nt(): lax.dot_general(left, right, (((1,), (1,)), ((), ())), precision=lax.Prec...  19.2 us
    ppermute x10, starting transfers between devices, send(): return lax.ppermute(value, 'prow', pairs)  19.1 us
    all_to_all x2, starting transfers between devices, over_plane(): lax.all_to_all(value, 'prow', split_axis=0, concat_axis=0, tiled=True, ax...  15 us
    all_to_all x1, waiting for transfers between devices, body(): lax.all_to_all(jnp.broadcast_to(matmul_nt(left, right), (8, 64, 128)), 'p...  13.2 us
  transfers between devices with their start and end apart: 24, of which 16 were waited for; matrix products, arithmetic and copies ran while one was open for 13% of the time, Pallas kernels for 0%

profile of v3, /device:TPU:2, one launch (start us, length us, event | category | flops | bytes accessed | tf_op | source)
XLA Modules:
  0.0 287.4 jit_solution(11782438662630329267)
XLA Ops:
  0.0 4.3 %dynamic-slice_bitcast_fusion = (f32[16,4,7168]{2,1,0:T(4,128)}, f32[16,4,7168]{2,1,0:T(4,128)}) fusion(f32[4,32,7168]{2,0,1:T(4,128)} %bitcast.105, s32[]{:T(128)S(6)} %select_n.182, s32[]{:T(128)S(6)} %select_n.181), kind=kLoop, calls=%fused_computation.19 | loop fusion | bytes 7340040 | tf_op jit(solution)/shard_map/dynamic_slice | solution.py:150
  4.3 1.3 collective-permute-start.3
  5.6 5.8 %collective-permute-start.1 = (f32[64,7168]{1,0:T(8,128)S(1)}, f32[64,7168]{1,0:T(8,128)}, u32[]{:S(2)}, u32[]{:S(2)}) collective-permute-start(f32[64,7168]{1,0:T(8,128)S(1)} %bitcast.101), channel_id=1, source_target_pairs={{0,2},{1,3},{2,4},{3,5},{4,6},{5,7},{8,10},{9,11},{10,12},{11,13},... | collective-permute-start | bytes 5505032 | tf_op jit(solution)/shard_map/ppermute | solution.py:142
  11.4 7.5 %all-to-all-start = ((f32[16,4,7168]{2,1,0:T(4,128)}), f32[16,4,7168]{2,1,0:T(4,128)}, u32[]{:S(2)}, u32[]{:S(2)}) async-start(f32[16,4,7168]{2,1,0:T(4,128)} %get-tuple-element.36), calls=%async_computation | async-start | bytes 3670016 | tf_op jit(solution)/shard_map/all_to_all | solution.py:158
  18.8 7.2 %collective-permute-start = (f32[16,4,7168]{2,1,0:T(4,128)}, f32[16,4,7168]{2,1,0:T(4,128)}, u32[]{:S(2)}, u32[]{:S(2)}) collective-permute-start(f32[16,4,7168]{2,1,0:T(4,128)} %get-tuple-element.14), channel_id=1, source_target_pairs={{0,128},{8,136},{16,144},{24,152},{32,160},{40,168},{48,176},{56,1... | collective-permute-start | bytes 5505032 | tf_op jit(solution)/shard_map/ppermute | solution.py:153
  26.0 16.9 %all-to-all-done = f32[16,4,7168]{2,1,0:T(4,128)} async-done(((f32[16,4,7168]{2,1,0:T(4,128)}), f32[16,4,7168]{2,1,0:T(4,128)}, u32[]{:S(2)}, u32[]{:S(2)}) %all-to-all-start) | async-done | bytes 1835040 | tf_op jit(solution)/shard_map/all_to_all | solution.py:158
  42.9 3.0 %reshape.15 = f32[64,7168]{1,0:T(8,128)} reshape(f32[16,4,7168]{2,1,0:T(4,128)} %all-to-all-done) | data formatting | bytes 3670016 | tf_op jit(solution)/shard_map/reshape | solution.py:161
  45.9 3.2 %collective-permute-done.3.refs_2_ = f32[64,7168]{1,0:T(8,128)} collective-permute-done((f32[64,7168]{1,0:T(8,128)S(1)}, f32[64,7168]{1,0:T(8,128)}, u32[]{:S(2)}, u32[]{:S(2)}) %collective-permute-start.3) | collective-permute-done | bytes 1835040 | tf_op jit(solution)/shard_map/ppermute | solution.py:142
  49.1 1.3 collective-permute-start.4
  50.5 1.9 collective-permute-start.2
  52.4 2.9 constant_dynamic-update-slice_fusion.1
  55.3 42.2 %collective-permute-done = f32[16,4,7168]{2,1,0:T(4,128)} collective-permute-done((f32[16,4,7168]{2,1,0:T(4,128)}, f32[16,4,7168]{2,1,0:T(4,128)}, u32[]{:S(2)}, u32[]{:S(2)}) %collective-permute-start) | collective-permute-done | bytes 1835040 | tf_op jit(solution)/shard_map/ppermute | solution.py:153
  97.5 7.5 %all-to-all-start.1 = ((f32[16,4,7168]{2,1,0:T(4,128)}), f32[16,4,7168]{2,1,0:T(4,128)}, u32[]{:S(2)}, u32[]{:S(2)}) async-start(f32[16,4,7168]{2,1,0:T(4,128)} %collective-permute-done), calls=%async_computation.1 | async-start | bytes 3670016 | tf_op jit(solution)/shard_map/all_to_all | solution.py:158
  105.0 3.7 %broadcast_select_fusion.1 = (f32[64,7168]{1,0:T(8,128)}, f32[64,7168]{1,0:T(8,128)}) fusion(f32[64,7168]{1,0:T(8,128)S(1)} %bitcast.103, f32[64,7168]{1,0:T(8,128)} %collective-permute-done.9.refs_1_, pred[]{:T(512)S(6)} %eq.42), kind=kLoop, calls=%fused_computation.25 | loop fusion | flops 917504 | bytes 7340033 | tf_op jit(solution)/shard_map/jit(_where)/select_n | solution.py:146
  108.7 21.7 %all-to-all-done.1 = f32[16,4,7168]{2,1,0:T(4,128)} async-done(((f32[16,4,7168]{2,1,0:T(4,128)}), f32[16,4,7168]{2,1,0:T(4,128)}, u32[]{:S(2)}, u32[]{:S(2)}) %all-to-all-start.1) | async-done | bytes 1835040 | tf_op jit(solution)/shard_map/all_to_all | solution.py:158
  130.4 2.9 %reshape.16 = f32[64,7168]{1,0:T(8,128)} reshape(f32[16,4,7168]{2,1,0:T(4,128)} %all-to-all-done.1) | data formatting | bytes 3670016 | tf_op jit(solution)/shard_map/reshape | solution.py:161
  133.3 32.8 %collective-permute-done.4 = f32[64,7168]{1,0:T(8,128)} collective-permute-done((f32[64,7168]{1,0:T(8,128)}, f32[64,7168]{1,0:T(8,128)}, u32[]{:S(2)}, u32[]{:S(2)}) %collective-permute-start.4) | collective-permute-done | bytes 1835040 | tf_op jit(solution)/shard_map/ppermute | solution.py:142
  166.2 3.6 %fusion.59 = (f32[64,7168]{1,0:T(8,128)S(1)}, f32[64,7168]{1,0:T(8,128)}) fusion(f32[64,7168]{1,0:T(8,128)} %collective-permute-done.2, f32[64,7168]{1,0:T(8,128)} %collective-permute-done.4, pred[]{:T(512)S(6)} %eq.43), kind=kLoop, calls=%fused_computation.118 | loop fusion | flops 917504 | bytes 7340033 | tf_op jit(solution)/shard_map/add | solution.py:170
  169.7 1.3 collective-permute-start.5
  171.5 3.7 %broadcast_select_fusion.5 = (f32[64,7168]{1,0:T(8,128)S(1)}, f32[64,7168]{1,0:T(8,128)S(1)}) fusion(f32[64,7168]{1,0:T(8,128)} %collective-permute-done.1.refs_6_, f32[64,7168]{1,0:T(8,128)} %collective-permute-done.7.refs_7_, pred[]{:T(512)S(6)} %eq.42), kind=kLoop, calls=%fused_computation.29 | loop fusion | flops 917504 | bytes 7340033 | tf_op jit(solution)/shard_map/jit(_where)/select_n | solution.py:146
  175.2 1.9 fusion.12
  177.0 2.4 broadcast_select_fusion.7
  179.4 1.9 fusion.13
  181.7 0.9 copy-done.11
  182.6 0.9 copy-done.5
  183.4 4.5 %fusion.8 = f32[64,128]{1,0:T(8,128)S(1)} fusion(f32[64,7168]{1,0:T(8,128)S(1)} %get-tuple-element.32, f32[64,7168]{1,0:T(8,128)S(1)} %get-tuple-element.31, f32[64,7168]{1,0:T(8,128)S(1)} %get-tuple-element.30, f32[64,7168]{1,0:T(8,128)S(1)} %get-tuple-element.29, f32[64,7168]{1,0:T(8,128)S(1)} %get-tuple-element.28, ...), kind=kOutput, calls=%fused_computation.11 | convolution fusion | flops 357826560 | bytes 16547843 | tf_op jit(solution)/shard_map/dot_general | solution.py:40
  188.6 11.8 %all-to-all-start.2 = ((f32[8,64,128]{2,1,0:T(8,128)}), f32[8,64,128]{2,1,0:T(8,128)S(1)}, u32[]{:S(2)}, u32[]{:S(2)}) async-start(f32[8,64,128]{2,1,0:T(8,128)} %broadcast_in_dim.6), calls=%async_computation.2 | async-start | bytes 524288 | tf_op jit(solution)/shard_map/all_to_all | solution.py:180
  200.5 4.4 %fusion = f32[128,128]{1,0:T(8,128)S(1)} fusion(f32[128,7168]{1,0:T(8,128)} %copy-done.1, f32[64,7168]{1,0:T(8,128)} %get-tuple-element.26, f32[64,7168]{1,0:T(8,128)S(1)} %copy-done.13), kind=kOutput, calls=%fused_computation.3 | convolution fusion | flops 705560576 | bytes 7405568 | tf_op jit(solution)/shard_map/dot_general | solution.py:40
  205.3 1.7 fusion.11
  207.0 13.2 %all-to-all-done.2 = f32[8,64,128]{2,1,0:T(8,128)S(1)} async-done(((f32[8,64,128]{2,1,0:T(8,128)}), f32[8,64,128]{2,1,0:T(8,128)S(1)}, u32[]{:S(2)}, u32[]{:S(2)}) %all-to-all-start.2) | async-done | bytes 262176 | tf_op jit(solution)/shard_map/all_to_all | solution.py:180
  220.6 3.9 %collective-permute-done.10.refs_9_ = f32[64,7168]{1,0:T(8,128)S(1)} collective-permute-done((f32[64,7168]{1,0:T(8,128)}, f32[64,7168]{1,0:T(8,128)S(1)}, u32[]{:S(2)}, u32[]{:S(2)}) %collective-permute-start.10) | collective-permute-done | bytes 1835040 | tf_op jit(solution)/shard_map/ppermute | solution.py:142
  224.5 4.9 %fusion.4 = f32[128,128]{1,0:T(8,128)S(1)} fusion(f32[128,7168]{1,0:T(8,128)} %copy-done.1, f32[64,7168]{1,0:T(8,128)S(1)} %collective-permute-done.10.refs_9_, f32[64,7168]{1,0:T(8,128)} %collective-permute-done.5.refs_8_), kind=kOutput, calls=%fused_computation.7 | convolution fusion | flops 705560576 | bytes 7405568 | tf_op jit(solution)/shard_map/dot_general | solution.py:40
  229.8 1.7 collective-permute-start.11
  231.5 3.4 %collective-permute-start.13 = (f32[256,128]{1,0:T(8,128)S(1)}, f32[256,128]{1,0:T(8,128)S(1)}, u32[]{:S(2)}, u32[]{:S(2)}) collective-permute-start(f32[256,128]{1,0:T(8,128)S(1)} %get-tuple-element.42), channel_id=1, source_target_pairs={{0,24},{8,0},{16,8},{24,16},{32,56},{40,32},{48,40},{56,48},{64,88... | collective-permute-start | bytes 393224 | tf_op jit(solution)/shard_map/ppermute | solution.py:50
  234.9 2.0 collective-permute-start.12
  236.9 1.8 collective-permute-done.11
  238.8 4.4 %collective-permute-done.12 = f32[256,128]{1,0:T(8,128)S(1)} collective-permute-done((f32[256,128]{1,0:T(8,128)S(1)}, f32[256,128]{1,0:T(8,128)S(1)}, u32[]{:S(2)}, u32[]{:S(2)}) %collective-permute-start.12) | collective-permute-done | bytes 131104 | tf_op jit(solution)/shard_map/ppermute | solution.py:50
  243.3 1.5 collective-permute-start.16
  245.8 3.6 %collective-permute-done.16 = f32[256,128]{1,0:T(8,128)S(1)} collective-permute-done((f32[256,128]{1,0:T(8,128)S(1)}, f32[256,128]{1,0:T(8,128)S(1)}, u32[]{:S(2)}, u32[]{:S(2)}) %collective-permute-start.16) | collective-permute-done | bytes 131104 | tf_op jit(solution)/shard_map/ppermute | solution.py:50
  249.5 2.7 collective-permute-done.15
  252.1 1.3 collective-permute-done.14
  253.5 3.0 %collective-permute-start.17 = (f32[256,128]{1,0:T(8,128)S(1)}, f32[256,128]{1,0:T(8,128)S(1)}, u32[]{:S(2)}, u32[]{:S(2)}) collective-permute-start(f32[256,128]{1,0:T(8,128)S(1)} %add_add_fusion), channel_id=1, source_target_pairs={{0,128},{8,136},{16,144},{24,152},{32,160},{40,168},{48,176},{56,1... | collective-permute-start | bytes 393224 | tf_op jit(solution)/shard_map/ppermute | solution.py:50
  256.5 6.0 %collective-permute-done.17 = f32[256,128]{1,0:T(8,128)S(1)} collective-permute-done((f32[256,128]{1,0:T(8,128)S(1)}, f32[256,128]{1,0:T(8,128)S(1)}, u32[]{:S(2)}, u32[]{:S(2)}) %collective-permute-start.17) | collective-permute-done | bytes 131104 | tf_op jit(solution)/shard_map/ppermute | solution.py:50
  263.1 3.4 %collective-permute-start.19 = (f32[256,128]{1,0:T(8,128)S(1)}, f32[256,128]{1,0:T(8,128)S(1)}, u32[]{:S(2)}, u32[]{:S(2)}) collective-permute-start(f32[256,128]{1,0:T(8,128)S(1)} %maximum_add_fusion), channel_id=1, source_target_pairs={{0,16},{8,24},{16,0},{24,8},{32,48},{40,56},{48,32},{56,40},{64,80... | collective-permute-start | bytes 393224 | tf_op jit(solution)/shard_map/ppermute | solution.py:50
  266.5 2.5 collective-permute-start.18
  269.7 1.9 collective-permute-done.18
  271.8 0.8 copy-done.14
  275.0 12.5 %shard_map.37 = f32[128,7168]{1,0:T(8,128)} custom-call(s32[5]{0:T(128)} %stack.81.where_ref, f32[128,7168]{1,0:T(8,128)} %copy-done.1, bf16[256,512]{1,0:T(8,128)(2,1)} %pad_maximum_fusion.13.scaled_ref, f32[64,7168]{1,0:T(8,128)} %bitcast.99, f32[64,7168]{1,0:T(8,128)} %collective-permute-done.9.refs_1_, f32[64,7168]{1,0:T(8,128)} %collective-permute-done.3.refs_2_, ...), custom_call_target="tpu_custom_call" | custom-call | flops 2818572288 | bytes 22020096 | tf_op jit(solution)/shard_map/pallas_call | solution.py:110
  (82 shorter events, 7.4 us)
Async XLA Ops:
  0.0 4.3 %copy-start.4 = (f32[7168,64]{0,1:T(8,128)S(1)}, f32[7168,64]{0,1:T(8,128)}, u32[]{:S(2)}) copy-start(f32[7168,64]{0,1:T(8,128)} %param.4) | copy-start | bytes 5505028
  4.3 44.9 %collective-permute-start.3 = (f32[64,7168]{1,0:T(8,128)S(1)}, f32[64,7168]{1,0:T(8,128)}, u32[]{:S(2)}, u32[]{:S(2)}) collective-permute-start(f32[64,7168]{1,0:T(8,128)S(1)} %bitcast.100), channel_id=1, source_target_pairs={{2,0},{3,1},{4,2},{5,3},{6,4},{7,5},{10,8},{11,9},{12,10},{13,11},... | collective-permute-start | bytes 5505032 | tf_op jit(solution)/shard_map/ppermute | solution.py:142
  5.6 45.0 %collective-permute-start.1 = (f32[64,7168]{1,0:T(8,128)S(1)}, f32[64,7168]{1,0:T(8,128)}, u32[]{:S(2)}, u32[]{:S(2)}) collective-permute-start(f32[64,7168]{1,0:T(8,128)S(1)} %bitcast.101), channel_id=1, source_target_pairs={{0,2},{1,3},{2,4},{3,5},{4,6},{5,7},{8,10},{9,11},{10,12},{11,13},... | collective-permute-start | bytes 5505032 | tf_op jit(solution)/shard_map/ppermute | solution.py:142
  11.4 31.5 %all-to-all-start = ((f32[16,4,7168]{2,1,0:T(4,128)}), f32[16,4,7168]{2,1,0:T(4,128)}, u32[]{:S(2)}, u32[]{:S(2)}) async-start(f32[16,4,7168]{2,1,0:T(4,128)} %get-tuple-element.36), calls=%async_computation | async-start | bytes 3670016 | tf_op jit(solution)/shard_map/all_to_all | solution.py:158
  18.8 78.7 %collective-permute-start = (f32[16,4,7168]{2,1,0:T(4,128)}, f32[16,4,7168]{2,1,0:T(4,128)}, u32[]{:S(2)}, u32[]{:S(2)}) collective-permute-start(f32[16,4,7168]{2,1,0:T(4,128)} %get-tuple-element.14), channel_id=1, source_target_pairs={{0,128},{8,136},{16,144},{24,152},{32,160},{40,168},{48,176},{56,1... | collective-permute-start | bytes 5505032 | tf_op jit(solution)/shard_map/ppermute | solution.py:153
  26.0 79.0 %collective-permute-start.9 = (f32[64,7168]{1,0:T(8,128)S(1)}, f32[64,7168]{1,0:T(8,128)}, u32[]{:S(2)}, u32[]{:S(2)}) collective-permute-start(f32[64,7168]{1,0:T(8,128)S(1)} %bitcast.102), channel_id=1, source_target_pairs={{0,1},{1,0},{2,3},{3,2},{4,5},{5,4},{6,7},{7,6},{8,9},{9,8},{10,11... | collective-permute-start | bytes 5505032 | tf_op jit(solution)/shard_map/ppermute | solution.py:142
  49.1 117.0 %collective-permute-start.4 = (f32[64,7168]{1,0:T(8,128)}, f32[64,7168]{1,0:T(8,128)}, u32[]{:S(2)}, u32[]{:S(2)}) collective-permute-start(f32[64,7168]{1,0:T(8,128)} %collective-permute-done.3.refs_2_), channel_id=1, source_target_pairs={{2,0},{3,1},{4,2},{5,3},{10,8},{11,9},{12,10},{13,11},{18,16},{19,... | collective-permute-start | bytes 5505032 | tf_op jit(solution)/shard_map/ppermute | solution.py:142
  50.5 115.6 %collective-permute-start.2 = (f32[64,7168]{1,0:T(8,128)}, f32[64,7168]{1,0:T(8,128)}, u32[]{:S(2)}, u32[]{:S(2)}) collective-permute-start(f32[64,7168]{1,0:T(8,128)} %collective-permute-done.1.refs_6_), channel_id=1, source_target_pairs={{2,4},{3,5},{4,6},{5,7},{10,12},{11,13},{12,14},{13,15},{18,20},{1... | collective-permute-start | bytes 5505032 | tf_op jit(solution)/shard_map/ppermute | solution.py:142
  55.3 121.8 %collective-permute-start.6 = (f32[64,7168]{1,0:T(8,128)}, f32[64,7168]{1,0:T(8,128)}, u32[]{:S(2)}, u32[]{:S(2)}) collective-permute-start(f32[64,7168]{1,0:T(8,128)} %collective-permute-done.3.refs_2_), channel_id=1, source_target_pairs={{0,1},{1,0},{2,3},{3,2},{4,5},{5,4},{6,7},{7,6},{8,9},{9,8},{10,11... | collective-permute-start | bytes 5505032 | tf_op jit(solution)/shard_map/ppermute | solution.py:142
  97.5 73.9 %collective-permute-start.7 = (f32[64,7168]{1,0:T(8,128)}, f32[64,7168]{1,0:T(8,128)}, u32[]{:S(2)}, u32[]{:S(2)}) collective-permute-start(f32[64,7168]{1,0:T(8,128)} %collective-permute-done.1.refs_6_), channel_id=1, source_target_pairs={{0,1},{1,0},{2,3},{3,2},{4,5},{5,4},{6,7},{7,6},{8,9},{9,8},{10,11... | collective-permute-start | bytes 5505032 | tf_op jit(solution)/shard_map/ppermute | solution.py:142
  97.5 32.9 %all-to-all-start.1 = ((f32[16,4,7168]{2,1,0:T(4,128)}), f32[16,4,7168]{2,1,0:T(4,128)}, u32[]{:S(2)}, u32[]{:S(2)}) async-start(f32[16,4,7168]{2,1,0:T(4,128)} %collective-permute-done), calls=%async_computation.1 | async-start | bytes 3670016 | tf_op jit(solution)/shard_map/all_to_all | solution.py:158
  133.3 38.0 %copy-start = (f32[128,7168]{1,0:T(8,128)S(1)}, f32[128,7168]{1,0:T(8,128)}, u32[]{:S(2)}) copy-start(f32[128,7168]{1,0:T(8,128)} %constant_dynamic-update-slice_fusion.1) | copy-start | bytes 11010052
  133.3 38.0 %copy-start.12 = (f32[64,7168]{1,0:T(8,128)S(1)}, f32[64,7168]{1,0:T(8,128)}, u32[]{:S(2)}) copy-start(f32[64,7168]{1,0:T(8,128)} %reshape.16) | copy-start | bytes 5505028
  169.7 12.8 %copy-start.3 = (f32[64,7168]{1,0:T(8,128)}, f32[64,7168]{1,0:T(8,128)S(1)}, u32[]{:S(2)}) copy-start(f32[64,7168]{1,0:T(8,128)S(1)} %get-tuple-element.33.refs_4_) | copy-start | bytes 5505028
  169.7 50.5 %collective-permute-start.5 = (f32[64,7168]{1,0:T(8,128)}, f32[64,7168]{1,0:T(8,128)}, u32[]{:S(2)}, u32[]{:S(2)}) collective-permute-start(f32[64,7168]{1,0:T(8,128)} %get-tuple-element.34), channel_id=1, source_target_pairs={{4,6},{5,7},{2,0},{3,1},{12,14},{13,15},{10,8},{11,9},{20,22},{21,... | collective-permute-start | bytes 5505032 | tf_op jit(solution)/shard_map/ppermute | solution.py:142
  171.0 10.3 %collective-permute-start.8 = (f32[64,7168]{1,0:T(8,128)S(1)}, f32[64,7168]{1,0:T(8,128)S(1)}, u32[]{:S(2)}, u32[]{:S(2)}) collective-permute-start(f32[64,7168]{1,0:T(8,128)S(1)} %get-tuple-element.33.refs_4_), channel_id=1, source_target_pairs={{0,1},{1,0},{2,3},{3,2},{4,5},{5,4},{6,7},{7,6},{8,9},{9,8},{10,11... | collective-permute-start | bytes 5505032 | tf_op jit(solution)/shard_map/ppermute | solution.py:142
  171.5 8.0 %copy-start.1 = (f32[128,7168]{1,0:T(8,128)}, f32[128,7168]{1,0:T(8,128)S(1)}, u32[]{:S(2)}) copy-start(f32[128,7168]{1,0:T(8,128)S(1)} %constant_dynamic-update-slice_fusion.rows_ref) | copy-start | bytes 11010052
  181.3 2.2 copy-start.5
  181.3 1.3 copy-start.11
  182.6 5.3 %copy-start.6 = (f32[64,7168]{1,0:T(8,128)}, f32[64,7168]{1,0:T(8,128)S(1)}, u32[]{:S(2)}) copy-start(f32[64,7168]{1,0:T(8,128)S(1)} %get-tuple-element.31) | copy-start | bytes 5505028
  182.6 5.4 %copy-start.8 = (f32[64,7168]{1,0:T(8,128)}, f32[64,7168]{1,0:T(8,128)S(1)}, u32[]{:S(2)}) copy-start(f32[64,7168]{1,0:T(8,128)S(1)} %get-tuple-element.32) | copy-start | bytes 5505028
  183.4 17.0 %copy-start.13 = (f32[64,7168]{1,0:T(8,128)S(1)}, f32[64,7168]{1,0:T(8,128)}, u32[]{:S(2)}) copy-start(f32[64,7168]{1,0:T(8,128)} %get-tuple-element.25) | copy-start | bytes 5505028
  188.6 31.5 %all-to-all-start.2 = ((f32[8,64,128]{2,1,0:T(8,128)}), f32[8,64,128]{2,1,0:T(8,128)S(1)}, u32[]{:S(2)}, u32[]{:S(2)}) async-start(f32[8,64,128]{2,1,0:T(8,128)} %broadcast_in_dim.6), calls=%async_computation.2 | async-start | bytes 524288 | tf_op jit(solution)/shard_map/all_to_all | solution.py:180
  200.5 4.5 %copy-start.2 = (f32[128,7168]{1,0:T(8,128)S(1)}, f32[128,7168]{1,0:T(8,128)}, u32[]{:S(2)}) copy-start(f32[128,7168]{1,0:T(8,128)} %copy-done.1) | copy-start | bytes 11010052
  200.5 4.5 %copy-start.7 = (f32[64,7168]{1,0:T(8,128)S(1)}, f32[64,7168]{1,0:T(8,128)}, u32[]{:S(2)}) copy-start(f32[64,7168]{1,0:T(8,128)} %copy-done.6) | copy-start | bytes 5505028
  200.5 4.8 %copy-start.9 = (f32[64,7168]{1,0:T(8,128)S(1)}, f32[64,7168]{1,0:T(8,128)}, u32[]{:S(2)}) copy-start(f32[64,7168]{1,0:T(8,128)} %copy-done.8) | copy-start | bytes 5505028
  220.2 4.3 %collective-permute-start.10 = (f32[64,7168]{1,0:T(8,128)}, f32[64,7168]{1,0:T(8,128)S(1)}, u32[]{:S(2)}, u32[]{:S(2)}) collective-permute-start(f32[64,7168]{1,0:T(8,128)} %collective-permute-done.5.refs_8_), channel_id=1, source_target_pairs={{0,1},{1,0},{2,3},{3,2},{4,5},{5,4},{6,7},{7,6},{8,9},{9,8},{10,11... | collective-permute-start | bytes 5505032 | tf_op jit(solution)/shard_map/ppermute | solution.py:142
  224.5 5.0 %copy-start.10 = (f32[64,7168]{1,0:T(8,128)}, f32[64,7168]{1,0:T(8,128)S(1)}, u32[]{:S(2)}) copy-start(f32[64,7168]{1,0:T(8,128)S(1)} %collective-permute-done.10.refs_9_) | copy-start | bytes 5505028
  229.8 8.9 %collective-permute-start.11 = (f32[256,128]{1,0:T(8,128)S(1)}, f32[256,128]{1,0:T(8,128)S(1)}, u32[]{:S(2)}, u32[]{:S(2)}) collective-permute-start(f32[256,128]{1,0:T(8,128)S(1)} %get-tuple-element.41), channel_id=1, source_target_pairs={{0,8},{8,16},{16,24},{24,0},{32,40},{40,48},{48,56},{56,32},{64,72... | collective-permute-start | bytes 393224 | tf_op jit(solution)/shard_map/ppermute | solution.py:50
  231.5 7.3 %collective-permute-start.13 = (f32[256,128]{1,0:T(8,128)S(1)}, f32[256,128]{1,0:T(8,128)S(1)}, u32[]{:S(2)}, u32[]{:S(2)}) collective-permute-start(f32[256,128]{1,0:T(8,128)S(1)} %get-tuple-element.42), channel_id=1, source_target_pairs={{0,24},{8,0},{16,8},{24,16},{32,56},{40,32},{48,40},{56,48},{64,88... | collective-permute-start | bytes 393224 | tf_op jit(solution)/shard_map/ppermute | solution.py:50
  234.9 8.3 %collective-permute-start.12 = (f32[256,128]{1,0:T(8,128)S(1)}, f32[256,128]{1,0:T(8,128)S(1)}, u32[]{:S(2)}, u32[]{:S(2)}) collective-permute-start(f32[256,128]{1,0:T(8,128)S(1)} %get-tuple-element.43), channel_id=1, source_target_pairs={{0,16},{8,24},{16,0},{24,8},{32,48},{40,56},{48,32},{56,40},{64,80... | collective-permute-start | bytes 393224 | tf_op jit(solution)/shard_map/ppermute | solution.py:50
  243.3 6.2 %collective-permute-start.16 = (f32[256,128]{1,0:T(8,128)S(1)}, f32[256,128]{1,0:T(8,128)S(1)}, u32[]{:S(2)}, u32[]{:S(2)}) collective-permute-start(f32[256,128]{1,0:T(8,128)S(1)} %fusion.38), channel_id=1, source_target_pairs={{0,96},{8,104},{16,112},{24,120},{32,0},{40,8},{48,16},{56,24},{64... | collective-permute-start | bytes 393224 | tf_op jit(solution)/shard_map/ppermute | solution.py:50
  244.7 7.4 %collective-permute-start.15 = (f32[256,128]{1,0:T(8,128)S(1)}, f32[256,128]{1,0:T(8,128)S(1)}, u32[]{:S(2)}, u32[]{:S(2)}) collective-permute-start(f32[256,128]{1,0:T(8,128)S(1)} %fusion.38), channel_id=1, source_target_pairs={{0,64},{8,72},{16,80},{24,88},{32,96},{40,104},{48,112},{56,120},{... | collective-permute-start | bytes 393224 | tf_op jit(solution)/shard_map/ppermute | solution.py:50
  245.5 7.9 %collective-permute-start.14 = (f32[256,128]{1,0:T(8,128)S(1)}, f32[256,128]{1,0:T(8,128)S(1)}, u32[]{:S(2)}, u32[]{:S(2)}) collective-permute-start(f32[256,128]{1,0:T(8,128)S(1)} %fusion.38), channel_id=1, source_target_pairs={{0,32},{8,40},{16,48},{24,56},{32,64},{40,72},{48,80},{56,88},{64,... | collective-permute-start | bytes 393224 | tf_op jit(solution)/shard_map/ppermute | solution.py:50
  253.5 9.1 %collective-permute-start.17 = (f32[256,128]{1,0:T(8,128)S(1)}, f32[256,128]{1,0:T(8,128)S(1)}, u32[]{:S(2)}, u32[]{:S(2)}) collective-permute-start(f32[256,128]{1,0:T(8,128)S(1)} %add_add_fusion), channel_id=1, source_target_pairs={{0,128},{8,136},{16,144},{24,152},{32,160},{40,168},{48,176},{56,1... | collective-permute-start | bytes 393224 | tf_op jit(solution)/shard_map/ppermute | solution.py:50
  262.6 7.0 %collective-permute-start.20 = (f32[256,128]{1,0:T(8,128)S(1)}, f32[256,128]{1,0:T(8,128)S(1)}, u32[]{:S(2)}, u32[]{:S(2)}) collective-permute-start(f32[256,128]{1,0:T(8,128)S(1)} %maximum_add_fusion), channel_id=1, source_target_pairs={{0,8},{8,16},{16,24},{24,0},{32,40},{40,48},{48,56},{56,32},{64,72... | collective-permute-start | bytes 393224 | tf_op jit(solution)/shard_map/ppermute | solution.py:50
  263.1 6.5 %collective-permute-start.19 = (f32[256,128]{1,0:T(8,128)S(1)}, f32[256,128]{1,0:T(8,128)S(1)}, u32[]{:S(2)}, u32[]{:S(2)}) collective-permute-start(f32[256,128]{1,0:T(8,128)S(1)} %maximum_add_fusion), channel_id=1, source_target_pairs={{0,16},{8,24},{16,0},{24,8},{32,48},{40,56},{48,32},{56,40},{64,80... | collective-permute-start | bytes 393224 | tf_op jit(solution)/shard_map/ppermute | solution.py:50
  266.5 5.1 %collective-permute-start.18 = (f32[256,128]{1,0:T(8,128)S(1)}, f32[256,128]{1,0:T(8,128)S(1)}, u32[]{:S(2)}, u32[]{:S(2)}) collective-permute-start(f32[256,128]{1,0:T(8,128)S(1)} %maximum_add_fusion), channel_id=1, source_target_pairs={{0,24},{8,0},{16,8},{24,16},{32,56},{40,32},{48,40},{56,48},{64,88... | collective-permute-start | bytes 393224 | tf_op jit(solution)/shard_map/ppermute | solution.py:50
  271.6 1.0 copy-start.14

commit v4 on v3

--- a/solution.py
+++ b/solution.py
@@ -95,7 +95,7 @@
     out_ref[pl.ds(other, mid), :] = result[mid:]
 
 
-def update(half, chip, rows, scaled, pieces, tile=1024):
+def update(half, chip, rows, scaled, pieces, tile=1792):
     count, length = rows.shape
     where = jnp.stack(
         [half, chip, (chip != 3) * 1, (chip != 0) * 1, ((chip == 0) | (chip == 3)) * 1]
@@ -177,10 +177,15 @@
 
     left = jnp.where(chip == 0, two, jnp.where(chip == 3, mine, above))
     right = jnp.where(chip == 0, all_above, jnp.where(chip == 1, all_below, all_two))
-    cross = lax.all_to_all(
-        jnp.broadcast_to(matmul_nt(left, right), (8, 64, 128)),
-        "pcol", split_axis=0, concat_axis=0, tiled=True,
-    ).reshape(4, 128, 128)
+    cross = matmul_nt(left, right)
+    cross = ordered(cross, send(cross, SIBLING), 0)
+    cross = turned(
+        jnp.stack(
+            [cross]
+            + [send(cross, [(c, (c + 2 * (4 - step)) % 8) for c in range(8)]) for step in (1, 2, 3)]
+        ),
+        4 - chip,
+    )
     cross = jnp.stack([cross[1], cross[0], cross[2], cross[3]])
     on_mine, on_two = matmul_nt(rows, all_mine), matmul_nt(rows, all_two)
     on_above, on_below = matmul_nt(rows, all_above), matmul_nt(rows, all_below)
@@ -188,7 +193,8 @@
         (last, cross, on_mine, on_two, on_above, on_below)
     )
     last_other = send(last, SIBLING)
-    on_last = matmul_nt(rows, jnp.concatenate([last, last_other], axis=0))
+    both = lax.optimization_barrier(jnp.concatenate([last, last_other], axis=0))
+    on_last = matmul_nt(rows, both)
     on_last = jnp.where(core == 0, on_last, jnp.roll(on_last, 64, axis=1))
     zero = jnp.zeros_like(on_last)
     slots = jnp.stack(

time: 291 us -> 294 us (1.010)
  waiting for transfers between devices: 156 us -> 171 us
  starting transfers between devices: 65.2 us -> 58 us
  matrix products: 20.3 us -> 14.1 us
    ppermute x10 -> x14, waiting for transfers between devices: 40.1 us -> 73.5 us  [send(): return lax.ppermute(value, 'pcol', pairs)]
    all_to_all x1 -> x0, waiting for transfers between devices: 13.2 us -> none  [body(): lax.all_to_all(jnp.broadcast_to(matmul_nt(left, right), (8, 64, 128)), 'p...]
    all_to_all x1 -> x0, starting transfers between devices: 11.8 us -> none  [body(): lax.all_to_all(jnp.broadcast_to(matmul_nt(left, right), (8, 64, 128)), 'p...]
    ppermute x1, waiting for transfers between devices: 42.2 us -> 35.6 us  [body(): arriving = lax.ppermute(leaving, 'prow', FAR)]
    ppermute x10 -> x14, starting transfers between devices: 12.1 us -> 18.8 us  [send(): return lax.ppermute(value, 'pcol', pairs)]
    dot_general x6, matrix products: 19.2 us -> 13 us  [matmul_nt(): lax.dot_general(left, right, (((1,), (1,)), ((), ())), precision=lax.Prec...]
    unnamed x38 -> x37, local copies, waits for them, and re-layouts: 5.83 us -> 6.48 us
    select_n x4 -> x5, other arithmetic: 10.1 us -> 10 us  [ordered(): jnp.where(core == 0, piece, other)]
  transfers between devices with their start and end apart: 24 -> 27, of which waited for: 16 -> 16; matrix products, arithmetic and copies ran while one was open for 13% -> 12% of each run, Pallas kernels for 0% -> 0%
where the time goes in v4:
time: 294 us; the launch traced here: 289 us
  waiting for transfers between devices  171 us (58%)
  starting transfers between devices  58 us (20%)
  local copies, waits for them, and re-layouts  17.8 us (6%)
  other arithmetic  16.2 us (6%)
  matrix products  14.1 us (5%)
  Pallas kernels  11.1 us (4%)
    ppermute x14, waiting for transfers between devices, send(): return lax.ppermute(value, 'pcol', pairs)  73.5 us
    all_to_all x2, waiting for transfers between devices, over_plane(): lax.all_to_all(value, 'prow', split_axis=0, concat_axis=0, tiled=True, ax...  39.6 us
    ppermute x1, waiting for transfers between devices, body(): arriving = lax.ppermute(leaving, 'prow', FAR)  35.6 us
    ppermute x10, waiting for transfers between devices, send(): return lax.ppermute(value, 'prow', pairs)  22.6 us
    ppermute x14, starting transfers between devices, send(): return lax.ppermute(value, 'pcol', pairs)  18.8 us
    ppermute x10, starting transfers between devices, send(): return lax.ppermute(value, 'prow', pairs)  17.9 us
    all_to_all x2, starting transfers between devices, over_plane(): lax.all_to_all(value, 'prow', split_axis=0, concat_axis=0, tiled=True, ax...  15 us
    dot_general x6, matrix products, matmul_nt(): lax.dot_general(left, right, (((1,), (1,)), ((), ())), precision=lax.Prec...  13 us
  transfers between devices with their start and end apart: 27, of which 16 were waited for; matrix products, arithmetic and copies ran while one was open for 12% of the time, Pallas kernels for 0%

profile of v4, /device:TPU:2, one launch (start us, length us, event | category | flops | bytes accessed | tf_op | source)
XLA Modules:
  0.0 289.1 jit_solution(14040687105742480495)
XLA Ops:
  0.0 4.3 %dynamic-slice_bitcast_fusion = (f32[16,4,7168]{2,1,0:T(4,128)}, f32[16,4,7168]{2,1,0:T(4,128)}) fusion(f32[4,32,7168]{2,0,1:T(4,128)} %bitcast.114, s32[]{:T(128)S(6)} %select_n.201, s32[]{:T(128)S(6)} %select_n.200), kind=kLoop, calls=%fused_computation.16 | loop fusion | bytes 7340040 | tf_op jit(solution)/shard_map/dynamic_slice | solution.py:150
  4.3 5.1 %collective-permute-start.1 = (f32[64,7168]{1,0:T(8,128)S(1)}, f32[64,7168]{1,0:T(8,128)}, u32[]{:S(2)}, u32[]{:S(2)}) collective-permute-start(f32[64,7168]{1,0:T(8,128)S(1)} %bitcast.109), channel_id=1, source_target_pairs={{0,2},{1,3},{2,4},{3,5},{4,6},{5,7},{8,10},{9,11},{10,12},{11,13},... | collective-permute-start | bytes 5505032 | tf_op jit(solution)/shard_map/ppermute | solution.py:142
  9.3 1.3 collective-permute-start.3
  10.6 7.5 %all-to-all-start = ((f32[16,4,7168]{2,1,0:T(4,128)}), f32[16,4,7168]{2,1,0:T(4,128)}, u32[]{:S(2)}, u32[]{:S(2)}) async-start(f32[16,4,7168]{2,1,0:T(4,128)} %get-tuple-element.36), calls=%async_computation | async-start | bytes 3670016 | tf_op jit(solution)/shard_map/all_to_all | solution.py:158
  18.1 6.3 %collective-permute-start = (f32[16,4,7168]{2,1,0:T(4,128)}, f32[16,4,7168]{2,1,0:T(4,128)}, u32[]{:S(2)}, u32[]{:S(2)}) collective-permute-start(f32[16,4,7168]{2,1,0:T(4,128)} %get-tuple-element.14), channel_id=1, source_target_pairs={{0,128},{8,136},{16,144},{24,152},{32,160},{40,168},{48,176},{56,1... | collective-permute-start | bytes 5505032 | tf_op jit(solution)/shard_map/ppermute | solution.py:153
  24.4 17.9 %all-to-all-done = f32[16,4,7168]{2,1,0:T(4,128)} async-done(((f32[16,4,7168]{2,1,0:T(4,128)}), f32[16,4,7168]{2,1,0:T(4,128)}, u32[]{:S(2)}, u32[]{:S(2)}) %all-to-all-start) | async-done | bytes 1835040 | tf_op jit(solution)/shard_map/all_to_all | solution.py:158
  42.3 3.0 %reshape.10 = f32[64,7168]{1,0:T(8,128)} reshape(f32[16,4,7168]{2,1,0:T(4,128)} %all-to-all-done) | data formatting | bytes 3670016 | tf_op jit(solution)/shard_map/reshape | solution.py:161
  45.3 3.2 %collective-permute-done.1.refs_6_ = f32[64,7168]{1,0:T(8,128)} collective-permute-done((f32[64,7168]{1,0:T(8,128)S(1)}, f32[64,7168]{1,0:T(8,128)}, u32[]{:S(2)}, u32[]{:S(2)}) %collective-permute-start.1) | collective-permute-done | bytes 1835040 | tf_op jit(solution)/shard_map/ppermute | solution.py:142
  48.5 1.9 collective-permute-start.2
  50.4 5.3 %collective-permute-done.3.refs_2_ = f32[64,7168]{1,0:T(8,128)} collective-permute-done((f32[64,7168]{1,0:T(8,128)S(1)}, f32[64,7168]{1,0:T(8,128)}, u32[]{:S(2)}, u32[]{:S(2)}) %collective-permute-start.3) | collective-permute-done | bytes 1835040 | tf_op jit(solution)/shard_map/ppermute | solution.py:142
  55.7 1.3 collective-permute-start.4
  57.0 2.9 constant_dynamic-update-slice_fusion.1
  59.9 35.6 %collective-permute-done = f32[16,4,7168]{2,1,0:T(4,128)} collective-permute-done((f32[16,4,7168]{2,1,0:T(4,128)}, f32[16,4,7168]{2,1,0:T(4,128)}, u32[]{:S(2)}, u32[]{:S(2)}) %collective-permute-start) | collective-permute-done | bytes 1835040 | tf_op jit(solution)/shard_map/ppermute | solution.py:153
  95.5 7.5 %all-to-all-start.1 = ((f32[16,4,7168]{2,1,0:T(4,128)}), f32[16,4,7168]{2,1,0:T(4,128)}, u32[]{:S(2)}, u32[]{:S(2)}) async-start(f32[16,4,7168]{2,1,0:T(4,128)} %collective-permute-done), calls=%async_computation.1 | async-start | bytes 3670016 | tf_op jit(solution)/shard_map/all_to_all | solution.py:158
  102.9 3.6 %broadcast_select_fusion.1 = (f32[64,7168]{1,0:T(8,128)}, f32[64,7168]{1,0:T(8,128)}) fusion(f32[64,7168]{1,0:T(8,128)S(1)} %bitcast.112, f32[64,7168]{1,0:T(8,128)} %collective-permute-done.13.refs_1_, pred[]{:T(512)S(6)} %eq.45), kind=kLoop, calls=%fused_computation.22 | loop fusion | flops 917504 | bytes 7340033 | tf_op jit(solution)/shard_map/jit(_where)/select_n | solution.py:146
  106.6 21.8 %all-to-all-done.1 = f32[16,4,7168]{2,1,0:T(4,128)} async-done(((f32[16,4,7168]{2,1,0:T(4,128)}), f32[16,4,7168]{2,1,0:T(4,128)}, u32[]{:S(2)}, u32[]{:S(2)}) %all-to-all-start.1) | async-done | bytes 1835040 | tf_op jit(solution)/shard_map/all_to_all | solution.py:158
  128.4 2.9 %reshape.11 = f32[64,7168]{1,0:T(8,128)} reshape(f32[16,4,7168]{2,1,0:T(4,128)} %all-to-all-done.1) | data formatting | bytes 3670016 | tf_op jit(solution)/shard_map/reshape | solution.py:161
  131.3 39.4 %collective-permute-done.4 = f32[64,7168]{1,0:T(8,128)} collective-permute-done((f32[64,7168]{1,0:T(8,128)}, f32[64,7168]{1,0:T(8,128)}, u32[]{:S(2)}, u32[]{:S(2)}) %collective-permute-start.4) | collective-permute-done | bytes 1835040 | tf_op jit(solution)/shard_map/ppermute | solution.py:142
  170.8 2.4 fusion.54
  173.3 1.5 collective-permute-start.5
  174.9 3.7 %broadcast_select_fusion.5 = (f32[64,7168]{1,0:T(8,128)S(1)}, f32[64,7168]{1,0:T(8,128)S(1)}) fusion(f32[64,7168]{1,0:T(8,128)} %collective-permute-done.1.refs_6_, f32[64,7168]{1,0:T(8,128)} %collective-permute-done.7.refs_7_, pred[]{:T(512)S(6)} %eq.45), kind=kLoop, calls=%fused_computation.26 | loop fusion | flops 917504 | bytes 7340033 | tf_op jit(solution)/shard_map/jit(_where)/select_n | solution.py:146
  178.6 1.8 fusion.8
  180.5 2.4 broadcast_select_fusion.7
  182.9 1.8 fusion.9
  184.9 1.8 fusion
  188.0 0.9 copy-done.5
  188.9 4.0 %fusion.4 = f32[64,128]{1,0:T(8,128)S(1)} fusion(f32[64,7168]{1,0:T(8,128)S(1)} %get-tuple-element.32, f32[64,7168]{1,0:T(8,128)S(1)} %get-tuple-element.31, f32[64,7168]{1,0:T(8,128)S(1)} %get-tuple-element.30, f32[64,7168]{1,0:T(8,128)S(1)} %get-tuple-element.29, f32[64,7168]{1,0:T(8,128)S(1)} %get-tuple-element.28, f32[64,7168]{1,0:T(8,128)S(1)} %get-tuple-element.27, ...), kind=kOutput, calls=%fused_computation.8 | convolution fusion | flops 357826560 | bytes 16547843 | tf_op jit(solution)/shard_map/dot_general | solution.py:40
  193.5 1.8 fusion.7
  195.8 6.6 %collective-permute-start.11 = (f32[128,128]{1,0:T(8,128)S(1)}, f32[128,128]{1,0:T(8,128)S(1)}, u32[]{:S(2)}, u32[]{:S(2)}) collective-permute-start(f32[128,128]{1,0:T(8,128)S(1)} %pad_maximum_fusion.15), channel_id=1, source_target_pairs={{0,4},{1,5},{2,6},{3,7},{4,0},{5,1},{6,2},{7,3},{8,12},{9,13},{10,... | collective-permute-start | bytes 196616 | tf_op jit(solution)/shard_map/ppermute | solution.py:142
  202.4 21.5 %collective-permute-done.10 = f32[128,128]{1,0:T(8,128)S(1)} collective-permute-done((f32[128,128]{1,0:T(8,128)S(1)}, f32[128,128]{1,0:T(8,128)S(1)}, u32[]{:S(2)}, u32[]{:S(2)}) %collective-permute-start.10) | collective-permute-done | bytes 65568 | tf_op jit(solution)/shard_map/ppermute | solution.py:142
  224.3 3.9 %collective-permute-done.14.refs_9_ = f32[64,7168]{1,0:T(8,128)S(1)} collective-permute-done((f32[64,7168]{1,0:T(8,128)}, f32[64,7168]{1,0:T(8,128)S(1)}, u32[]{:S(2)}, u32[]{:S(2)}) %collective-permute-start.14) | collective-permute-done | bytes 1835040 | tf_op jit(solution)/shard_map/ppermute | solution.py:142
  228.2 2.5 pad_maximum_fusion.3
  231.4 1.7 fusion.58
  233.4 1.8 collective-permute-start.15
  235.3 5.6 %collective-permute-start.16 = (f32[256,128]{1,0:T(8,128)S(1)}, f32[256,128]{1,0:T(8,128)S(1)}, u32[]{:S(2)}, u32[]{:S(2)}) collective-permute-start(f32[256,128]{1,0:T(8,128)S(1)} %get-tuple-element.43), channel_id=1, source_target_pairs={{0,16},{8,24},{16,0},{24,8},{32,48},{40,56},{48,32},{56,40},{64,80... | collective-permute-start | bytes 393224 | tf_op jit(solution)/shard_map/ppermute | solution.py:50
  240.9 2.2 collective-permute-done.15
  243.1 2.1 collective-permute-done.16
  245.2 2.0 collective-permute-done.17
  247.5 2.7 collective-permute-start.19
  250.7 5.7 %collective-permute-done.18 = f32[256,128]{1,0:T(8,128)S(1)} collective-permute-done((f32[256,128]{1,0:T(8,128)S(1)}, f32[256,128]{1,0:T(8,128)S(1)}, u32[]{:S(2)}, u32[]{:S(2)}) %collective-permute-start.18) | collective-permute-done | bytes 131104 | tf_op jit(solution)/shard_map/ppermute | solution.py:50
  257.0 1.3 collective-permute-start.21
  258.3 7.7 %collective-permute-done.21 = f32[256,128]{1,0:T(8,128)S(1)} collective-permute-done((f32[256,128]{1,0:T(8,128)S(1)}, f32[256,128]{1,0:T(8,128)S(1)}, u32[]{:S(2)}, u32[]{:S(2)}) %collective-permute-start.21) | collective-permute-done | bytes 131104 | tf_op jit(solution)/shard_map/ppermute | solution.py:50
  266.0 1.3 collective-permute-start.22
  267.3 2.0 collective-permute-start.23
  269.2 2.5 collective-permute-start.24
  272.4 1.4 collective-permute-done.23
  273.8 0.9 collective-permute-done.24
  278.0 11.1 %shard_map.37 = f32[128,7168]{1,0:T(8,128)} custom-call(s32[5]{0:T(128)} %stack.95.where_ref, f32[128,7168]{1,0:T(8,128)} %copy-done.1, bf16[256,512]{1,0:T(8,128)(2,1)} %pad_maximum_fusion.14.scaled_ref, f32[64,7168]{1,0:T(8,128)} %bitcast.108, f32[64,7168]{1,0:T(8,128)} %collective-permute-done.13.refs_1_, f32[64,7168]{1,0:T(8,128)} %collective-permute-done.3.refs_2_, ...), custom_call_target="tpu_custom_call" | custom-call | flops 2818572288 | bytes 22020096 | tf_op jit(solution)/shard_map/pallas_call | solution.py:110
  (93 shorter events, 9.2 us)
Async XLA Ops:
  0.0 4.3 %copy-start.4 = (f32[7168,64]{0,1:T(8,128)S(1)}, f32[7168,64]{0,1:T(8,128)}, u32[]{:S(2)}) copy-start(f32[7168,64]{0,1:T(8,128)} %param.4) | copy-start | bytes 5505028
  4.3 44.2 %collective-permute-start.1 = (f32[64,7168]{1,0:T(8,128)S(1)}, f32[64,7168]{1,0:T(8,128)}, u32[]{:S(2)}, u32[]{:S(2)}) collective-permute-start(f32[64,7168]{1,0:T(8,128)S(1)} %bitcast.109), channel_id=1, source_target_pairs={{0,2},{1,3},{2,4},{3,5},{4,6},{5,7},{8,10},{9,11},{10,12},{11,13},... | collective-permute-start | bytes 5505032 | tf_op jit(solution)/shard_map/ppermute | solution.py:142
  9.3 46.4 %collective-permute-start.3 = (f32[64,7168]{1,0:T(8,128)S(1)}, f32[64,7168]{1,0:T(8,128)}, u32[]{:S(2)}, u32[]{:S(2)}) collective-permute-start(f32[64,7168]{1,0:T(8,128)S(1)} %bitcast.110), channel_id=1, source_target_pairs={{2,0},{3,1},{4,2},{5,3},{6,4},{7,5},{10,8},{11,9},{12,10},{13,11},... | collective-permute-start | bytes 5505032 | tf_op jit(solution)/shard_map/ppermute | solution.py:142
  10.6 31.6 %all-to-all-start = ((f32[16,4,7168]{2,1,0:T(4,128)}), f32[16,4,7168]{2,1,0:T(4,128)}, u32[]{:S(2)}, u32[]{:S(2)}) async-start(f32[16,4,7168]{2,1,0:T(4,128)} %get-tuple-element.36), calls=%async_computation | async-start | bytes 3670016 | tf_op jit(solution)/shard_map/all_to_all | solution.py:158
  18.1 77.3 %collective-permute-start = (f32[16,4,7168]{2,1,0:T(4,128)}, f32[16,4,7168]{2,1,0:T(4,128)}, u32[]{:S(2)}, u32[]{:S(2)}) collective-permute-start(f32[16,4,7168]{2,1,0:T(4,128)} %get-tuple-element.14), channel_id=1, source_target_pairs={{0,128},{8,136},{16,144},{24,152},{32,160},{40,168},{48,176},{56,1... | collective-permute-start | bytes 5505032 | tf_op jit(solution)/shard_map/ppermute | solution.py:153
  24.4 78.5 %collective-permute-start.13 = (f32[64,7168]{1,0:T(8,128)S(1)}, f32[64,7168]{1,0:T(8,128)}, u32[]{:S(2)}, u32[]{:S(2)}) collective-permute-start(f32[64,7168]{1,0:T(8,128)S(1)} %bitcast.111), channel_id=1, source_target_pairs={{0,1},{1,0},{2,3},{3,2},{4,5},{5,4},{6,7},{7,6},{8,9},{9,8},{10,11... | collective-permute-start | bytes 5505032 | tf_op jit(solution)/shard_map/ppermute | solution.py:142
  48.5 82.8 %collective-permute-start.2 = (f32[64,7168]{1,0:T(8,128)}, f32[64,7168]{1,0:T(8,128)}, u32[]{:S(2)}, u32[]{:S(2)}) collective-permute-start(f32[64,7168]{1,0:T(8,128)} %collective-permute-done.1.refs_6_), channel_id=1, source_target_pairs={{2,4},{3,5},{4,6},{5,7},{10,12},{11,13},{12,14},{13,15},{18,20},{1... | collective-permute-start | bytes 5505032 | tf_op jit(solution)/shard_map/ppermute | solution.py:142
  55.7 115.1 %collective-permute-start.4 = (f32[64,7168]{1,0:T(8,128)}, f32[64,7168]{1,0:T(8,128)}, u32[]{:S(2)}, u32[]{:S(2)}) collective-permute-start(f32[64,7168]{1,0:T(8,128)} %collective-permute-done.3.refs_2_), channel_id=1, source_target_pairs={{2,0},{3,1},{4,2},{5,3},{10,8},{11,9},{12,10},{13,11},{18,16},{19,... | collective-permute-start | bytes 5505032 | tf_op jit(solution)/shard_map/ppermute | solution.py:142
  59.9 115.1 %collective-permute-start.7 = (f32[64,7168]{1,0:T(8,128)}, f32[64,7168]{1,0:T(8,128)}, u32[]{:S(2)}, u32[]{:S(2)}) collective-permute-start(f32[64,7168]{1,0:T(8,128)} %collective-permute-done.1.refs_6_), channel_id=1, source_target_pairs={{0,1},{1,0},{2,3},{3,2},{4,5},{5,4},{6,7},{7,6},{8,9},{9,8},{10,11... | collective-permute-start | bytes 5505032 | tf_op jit(solution)/shard_map/ppermute | solution.py:142
  95.5 85.0 %collective-permute-start.6 = (f32[64,7168]{1,0:T(8,128)}, f32[64,7168]{1,0:T(8,128)}, u32[]{:S(2)}, u32[]{:S(2)}) collective-permute-start(f32[64,7168]{1,0:T(8,128)} %collective-permute-done.3.refs_2_), channel_id=1, source_target_pairs={{0,1},{1,0},{2,3},{3,2},{4,5},{5,4},{6,7},{7,6},{8,9},{9,8},{10,11... | collective-permute-start | bytes 5505032 | tf_op jit(solution)/shard_map/ppermute | solution.py:142
  95.5 32.9 %all-to-all-start.1 = ((f32[16,4,7168]{2,1,0:T(4,128)}), f32[16,4,7168]{2,1,0:T(4,128)}, u32[]{:S(2)}, u32[]{:S(2)}) async-start(f32[16,4,7168]{2,1,0:T(4,128)} %collective-permute-done), calls=%async_computation.1 | async-start | bytes 3670016 | tf_op jit(solution)/shard_map/all_to_all | solution.py:158
  131.3 43.5 %copy-start = (f32[128,7168]{1,0:T(8,128)S(1)}, f32[128,7168]{1,0:T(8,128)}, u32[]{:S(2)}) copy-start(f32[128,7168]{1,0:T(8,128)} %constant_dynamic-update-slice_fusion.1) | copy-start | bytes 11010052
  131.3 43.5 %copy-start.8 = (f32[64,7168]{1,0:T(8,128)S(1)}, f32[64,7168]{1,0:T(8,128)}, u32[]{:S(2)}) copy-start(f32[64,7168]{1,0:T(8,128)} %reshape.11) | copy-start | bytes 5505028
  173.2 14.8 %copy-start.3 = (f32[64,7168]{1,0:T(8,128)}, f32[64,7168]{1,0:T(8,128)S(1)}, u32[]{:S(2)}) copy-start(f32[64,7168]{1,0:T(8,128)S(1)} %get-tuple-element.33.refs_4_) | copy-start | bytes 5505028
  173.2 13.5 %collective-permute-start.8 = (f32[64,7168]{1,0:T(8,128)S(1)}, f32[64,7168]{1,0:T(8,128)S(1)}, u32[]{:S(2)}, u32[]{:S(2)}) collective-permute-start(f32[64,7168]{1,0:T(8,128)S(1)} %get-tuple-element.33.refs_4_), channel_id=1, source_target_pairs={{0,1},{1,0},{2,3},{3,2},{4,5},{5,4},{6,7},{7,6},{8,9},{9,8},{10,11... | collective-permute-start | bytes 5505032 | tf_op jit(solution)/shard_map/ppermute | solution.py:142
  173.3 50.8 %collective-permute-start.5 = (f32[64,7168]{1,0:T(8,128)S(1)}, f32[64,7168]{1,0:T(8,128)}, u32[]{:S(2)}, u32[]{:S(2)}) collective-permute-start(f32[64,7168]{1,0:T(8,128)S(1)} %get-tuple-element.34), channel_id=1, source_target_pairs={{4,6},{5,7},{2,0},{3,1},{12,14},{13,15},{10,8},{11,9},{20,22},{21,... | collective-permute-start | bytes 5505032 | tf_op jit(solution)/shard_map/ppermute | solution.py:142
  174.9 18.6 %copy-start.1 = (f32[128,7168]{1,0:T(8,128)}, f32[128,7168]{1,0:T(8,128)S(1)}, u32[]{:S(2)}) copy-start(f32[128,7168]{1,0:T(8,128)S(1)} %constant_dynamic-update-slice_fusion.rows_ref) | copy-start | bytes 11010052
  182.8 1.9 copy-start.9
  182.9 2.0 copy-start.10
  186.7 2.2 copy-start.5
  186.7 1.3 copy-start.7
  192.9 2.4 collective-permute-start.9
  195.4 28.5 %collective-permute-start.10 = (f32[128,128]{1,0:T(8,128)S(1)}, f32[128,128]{1,0:T(8,128)S(1)}, u32[]{:S(2)}, u32[]{:S(2)}) collective-permute-start(f32[128,128]{1,0:T(8,128)S(1)} %pad_maximum_fusion.15), channel_id=1, source_target_pairs={{0,6},{1,7},{2,0},{3,1},{4,2},{5,3},{6,4},{7,5},{8,14},{9,15},{10,... | collective-permute-start | bytes 196616 | tf_op jit(solution)/shard_map/ppermute | solution.py:142
  195.8 28.1 %collective-permute-start.11 = (f32[128,128]{1,0:T(8,128)S(1)}, f32[128,128]{1,0:T(8,128)S(1)}, u32[]{:S(2)}, u32[]{:S(2)}) collective-permute-start(f32[128,128]{1,0:T(8,128)S(1)} %pad_maximum_fusion.15), channel_id=1, source_target_pairs={{0,4},{1,5},{2,6},{3,7},{4,0},{5,1},{6,2},{7,3},{8,12},{9,13},{10,... | collective-permute-start | bytes 196616 | tf_op jit(solution)/shard_map/ppermute | solution.py:142
  202.4 21.5 %collective-permute-start.12 = (f32[128,128]{1,0:T(8,128)S(1)}, f32[128,128]{1,0:T(8,128)S(1)}, u32[]{:S(2)}, u32[]{:S(2)}) collective-permute-start(f32[128,128]{1,0:T(8,128)S(1)} %pad_maximum_fusion.15), channel_id=1, source_target_pairs={{0,2},{1,3},{2,4},{3,5},{4,6},{5,7},{6,0},{7,1},{8,10},{9,11},{10,... | collective-permute-start | bytes 196616 | tf_op jit(solution)/shard_map/ppermute | solution.py:142
  224.1 4.1 %collective-permute-start.14 = (f32[64,7168]{1,0:T(8,128)}, f32[64,7168]{1,0:T(8,128)S(1)}, u32[]{:S(2)}, u32[]{:S(2)}) collective-permute-start(f32[64,7168]{1,0:T(8,128)} %collective-permute-done.5.refs_8_), channel_id=1, source_target_pairs={{0,1},{1,0},{2,3},{3,2},{4,5},{5,4},{6,7},{7,6},{8,9},{9,8},{10,11... | collective-permute-start | bytes 5505032 | tf_op jit(solution)/shard_map/ppermute | solution.py:142
  228.2 2.5 copy-start.6
  228.2 3.3 %copy-start.2 = (f32[128,7168]{1,0:T(8,128)S(1)}, f32[128,7168]{1,0:T(8,128)}, u32[]{:S(2)}) copy-start(f32[128,7168]{1,0:T(8,128)} %copy-done.1) | copy-start | bytes 11010052
  233.4 9.7 %collective-permute-start.15 = (f32[256,128]{1,0:T(8,128)S(1)}, f32[256,128]{1,0:T(8,128)S(1)}, u32[]{:S(2)}, u32[]{:S(2)}) collective-permute-start(f32[256,128]{1,0:T(8,128)S(1)} %get-tuple-element.41), channel_id=1, source_target_pairs={{0,8},{8,16},{16,24},{24,0},{32,40},{40,48},{48,56},{56,32},{64,72... | collective-permute-start | bytes 393224 | tf_op jit(solution)/shard_map/ppermute | solution.py:50
  235.3 10.0 %collective-permute-start.16 = (f32[256,128]{1,0:T(8,128)S(1)}, f32[256,128]{1,0:T(8,128)S(1)}, u32[]{:S(2)}, u32[]{:S(2)}) collective-permute-start(f32[256,128]{1,0:T(8,128)S(1)} %get-tuple-element.43), channel_id=1, source_target_pairs={{0,16},{8,24},{16,0},{24,8},{32,48},{40,56},{48,32},{56,40},{64,80... | collective-permute-start | bytes 393224 | tf_op jit(solution)/shard_map/ppermute | solution.py:50
  240.9 6.3 %collective-permute-start.17 = (f32[256,128]{1,0:T(8,128)S(1)}, f32[256,128]{1,0:T(8,128)S(1)}, u32[]{:S(2)}, u32[]{:S(2)}) collective-permute-start(f32[256,128]{1,0:T(8,128)S(1)} %get-tuple-element.42), channel_id=1, source_target_pairs={{0,24},{8,0},{16,8},{24,16},{32,56},{40,32},{48,40},{56,48},{64,88... | collective-permute-start | bytes 393224 | tf_op jit(solution)/shard_map/ppermute | solution.py:50
  247.2 9.1 %collective-permute-start.18 = (f32[256,128]{1,0:T(8,128)S(1)}, f32[256,128]{1,0:T(8,128)S(1)}, u32[]{:S(2)}, u32[]{:S(2)}) collective-permute-start(f32[256,128]{1,0:T(8,128)S(1)} %fusion.34), channel_id=1, source_target_pairs={{0,32},{8,40},{16,48},{24,56},{32,64},{40,72},{48,80},{56,88},{64,... | collective-permute-start | bytes 393224 | tf_op jit(solution)/shard_map/ppermute | solution.py:50
  247.5 8.9 %collective-permute-start.19 = (f32[256,128]{1,0:T(8,128)S(1)}, f32[256,128]{1,0:T(8,128)S(1)}, u32[]{:S(2)}, u32[]{:S(2)}) collective-permute-start(f32[256,128]{1,0:T(8,128)S(1)} %fusion.34), channel_id=1, source_target_pairs={{0,64},{8,72},{16,80},{24,88},{32,96},{40,104},{48,112},{56,120},{... | collective-permute-start | bytes 393224 | tf_op jit(solution)/shard_map/ppermute | solution.py:50
  250.2 6.8 %collective-permute-start.20 = (f32[256,128]{1,0:T(8,128)S(1)}, f32[256,128]{1,0:T(8,128)S(1)}, u32[]{:S(2)}, u32[]{:S(2)}) collective-permute-start(f32[256,128]{1,0:T(8,128)S(1)} %fusion.34), channel_id=1, source_target_pairs={{0,96},{8,104},{16,112},{24,120},{32,0},{40,8},{48,16},{56,24},{64... | collective-permute-start | bytes 393224 | tf_op jit(solution)/shard_map/ppermute | solution.py:50
  257.0 9.0 %collective-permute-start.21 = (f32[256,128]{1,0:T(8,128)S(1)}, f32[256,128]{1,0:T(8,128)S(1)}, u32[]{:S(2)}, u32[]{:S(2)}) collective-permute-start(f32[256,128]{1,0:T(8,128)S(1)} %add_add_fusion), channel_id=1, source_target_pairs={{0,128},{8,136},{16,144},{24,152},{32,160},{40,168},{48,176},{56,1... | collective-permute-start | bytes 393224 | tf_op jit(solution)/shard_map/ppermute | solution.py:50
  266.0 6.4 %collective-permute-start.22 = (f32[256,128]{1,0:T(8,128)S(1)}, f32[256,128]{1,0:T(8,128)S(1)}, u32[]{:S(2)}, u32[]{:S(2)}) collective-permute-start(f32[256,128]{1,0:T(8,128)S(1)} %maximum_add_fusion), channel_id=1, source_target_pairs={{0,24},{8,0},{16,8},{24,16},{32,56},{40,32},{48,40},{56,48},{64,88... | collective-permute-start | bytes 393224 | tf_op jit(solution)/shard_map/ppermute | solution.py:50
  267.3 6.5 %collective-permute-start.23 = (f32[256,128]{1,0:T(8,128)S(1)}, f32[256,128]{1,0:T(8,128)S(1)}, u32[]{:S(2)}, u32[]{:S(2)}) collective-permute-start(f32[256,128]{1,0:T(8,128)S(1)} %maximum_add_fusion), channel_id=1, source_target_pairs={{0,16},{8,24},{16,0},{24,8},{32,48},{40,56},{48,32},{56,40},{64,80... | collective-permute-start | bytes 393224 | tf_op jit(solution)/shard_map/ppermute | solution.py:50
  269.2 5.4 %collective-permute-start.24 = (f32[256,128]{1,0:T(8,128)S(1)}, f32[256,128]{1,0:T(8,128)S(1)}, u32[]{:S(2)}, u32[]{:S(2)}) collective-permute-start(f32[256,128]{1,0:T(8,128)S(1)} %maximum_add_fusion), channel_id=1, source_target_pairs={{0,8},{8,16},{16,24},{24,0},{32,40},{40,48},{48,56},{56,32},{64,72... | collective-permute-start | bytes 393224 | tf_op jit(solution)/shard_map/ppermute | solution.py:50
  274.7 1.0 copy-start.11

commit v5 on v2

--- a/solution.py
+++ b/solution.py
@@ -99,7 +99,7 @@
     out_ref[pl.ds(other, mid), :] = result[mid:]
 
 
-def update(half, chip, rows, scaled, pieces, tile=1024):
+def update(half, chip, rows, scaled, pieces, tile=1792):
     count, length = rows.shape
     where = jnp.stack(
         [half, chip, (chip != 3) * 1, (chip != 0) * 1, ((chip == 0) | (chip == 3)) * 1]
@@ -168,7 +168,6 @@
     below_two = send(below, UP_TWO)
     above_two = send(above, DOWN_TWO)
     arriving = over_plane(arriving)
-    arriving, below_two, above_two = lax.optimization_barrier((arriving, below_two, above_two))
     last = send(jnp.where(chip == 2, below_two, above_two), TO_ENDS)
     rows = jnp.concatenate([staying, arriving], axis=0)
     two = below_two + above_two
@@ -187,23 +186,28 @@
     last, cross, on_mine, on_two, on_above, on_below = lax.optimization_barrier(
         (last, cross, on_mine, on_two, on_above, on_below)
     )
-
     last_other = send(last, SIBLING)
-    zero = jnp.zeros_like
-    last_other, on_last = lax.optimization_barrier((last_other, matmul_nt(rows, last)))
-    on_last = ordered(on_last, matmul_nt(rows, last_other), 1)
+    both = lax.optimization_barrier(jnp.concatenate([last, last_other], axis=0))
+    on_last = matmul_nt(rows, both)
+    on_last = jnp.where(core == 0, on_last, jnp.roll(on_last, 64, axis=1))
+    zero = jnp.zeros_like(on_last)
     slots = jnp.stack(
         [
             on_mine,
-            on_above + jnp.where(chip == 3, on_last, zero(on_last)),
+            on_above + jnp.where(chip == 3, on_last, zero),
             on_two,
-            on_below + jnp.where(chip == 0, on_last, zero(on_last)),
+            on_below + jnp.where(chip == 0, on_last, zero),
         ]
     )
     projected, cross = sum_over_prow(slots, cross)
-    cross = lax.all_to_all(
-        jnp.broadcast_to(cross, (8, *cross.shape)), "pcol", split_axis=0, concat_axis=0, tiled=True
-    ).reshape(4, 128, 128)
+    cross = ordered(cross, send(cross, SIBLING), 0)
+    cross = turned(
+        jnp.stack(
+            [cross]
+            + [send(cross, [(c, (c + 2 * (4 - step)) % 8) for c in range(8)]) for step in (1, 2, 3)]
+        ),
+        4 - chip,
+    )
     cross = jnp.concatenate(
         [
             jnp.concatenate([cross[1], cross[0]], axis=1),

time: 293 us -> 299 us (1.020)
  waiting for transfers between devices: 169 us -> 186 us
  starting transfers between devices: 59.6 us -> 51.5 us
  matrix products: 21.2 us -> 16.1 us
    ppermute x10 -> x14, waiting for transfers between devices: 61.8 us -> 98 us  [send(): return lax.ppermute(value, 'pcol', pairs)]
    all_to_all x1 -> x0, waiting for transfers between devices: 9.15 us -> none  [body(): lax.all_to_all(jnp.broadcast_to(cross, (8, *cross.shape)), 'pcol', split_...]
    all_to_all x1 -> x0, starting transfers between devices: 6.4 us -> none  [body(): lax.all_to_all(jnp.broadcast_to(cross, (8, *cross.shape)), 'pcol', split_...]
    ppermute x1, waiting for transfers between devices: 42.3 us -> 36.7 us  [body(): arriving = lax.ppermute(leaving, 'prow', FAR)]
    all_to_all x2, waiting for transfers between devices: 38.7 us -> 33.4 us  [over_plane(): lax.all_to_all(value, 'prow', split_axis=0, concat_axis=0, tiled=True, ax...]
    dot_general x7 -> x6, matrix products: 20.1 us -> 15 us  [matmul_nt(): lax.dot_general(left, right, (((1,), (1,)), ((), ())), precision=lax.Prec...]
    unnamed x37 -> x40, local copies, waits for them, and re-layouts: 4.02 us -> 6.66 us
    ppermute x10 -> x14, starting transfers between devices: 11.8 us -> 13.4 us  [send(): return lax.ppermute(value, 'pcol', pairs)]
  transfers between devices with their start and end apart: 24 -> 27, of which waited for: 15 -> 17; matrix products, arithmetic and copies ran while one was open for 13% -> 12% of each run, Pallas kernels for 0% -> 0%
where the time goes in v5:
time: 299 us; the launch traced here: 298 us
  waiting for transfers between devices  186 us (62%)
  starting transfers between devices  51.5 us (17%)
  local copies, waits for them, and re-layouts  18 us (6%)
  matrix products  16.1 us (5%)
  other arithmetic  14.9 us (5%)
  Pallas kernels  11.1 us (4%)
    ppermute x14, waiting for transfers between devices, send(): return lax.ppermute(value, 'pcol', pairs)  98 us
    ppermute x1, waiting for transfers between devices, body(): arriving = lax.ppermute(leaving, 'prow', FAR)  36.7 us
    all_to_all x2, waiting for transfers between devices, over_plane(): lax.all_to_all(value, 'prow', split_axis=0, concat_axis=0, tiled=True, ax...  33.4 us
    ppermute x10, waiting for transfers between devices, send(): return lax.ppermute(value, 'prow', pairs)  17.5 us
    ppermute x10, starting transfers between devices, send(): return lax.ppermute(value, 'prow', pairs)  16.9 us
    dot_general x6, matrix products, matmul_nt(): lax.dot_general(left, right, (((1,), (1,)), ((), ())), precision=lax.Prec...  15 us
    all_to_all x2, starting transfers between devices, over_plane(): lax.all_to_all(value, 'prow', split_axis=0, concat_axis=0, tiled=True, ax...  14.8 us
    ppermute x14, starting transfers between devices, send(): return lax.ppermute(value, 'pcol', pairs)  13.4 us
  transfers between devices with their start and end apart: 27, of which 17 were waited for; matrix products, arithmetic and copies ran while one was open for 12% of the time, Pallas kernels for 0%

profile of v5, /device:TPU:2, one launch (start us, length us, event | category | flops | bytes accessed | tf_op | source)
XLA Modules:
  0.0 297.9 jit_solution(5334260987528323797)
XLA Ops:
  0.0 4.1 %dynamic-slice_bitcast_fusion = (f32[16,4,7168]{2,1,0:T(4,128)}, f32[16,4,7168]{2,1,0:T(4,128)}) fusion(f32[4,32,7168]{2,0,1:T(4,128)} %bitcast.118, s32[]{:T(128)S(6)} %select_n.194, s32[]{:T(128)S(6)} %select_n.193), kind=kLoop, calls=%fused_computation.16 | loop fusion | bytes 7340040 | tf_op jit(solution)/shard_map/dynamic_slice | solution.py:154
  4.1 7.6 %all-to-all-start = ((f32[16,4,7168]{2,1,0:T(4,128)}), f32[16,4,7168]{2,1,0:T(4,128)}, u32[]{:S(2)}, u32[]{:S(2)}) async-start(f32[16,4,7168]{2,1,0:T(4,128)} %get-tuple-element.34), calls=%async_computation | async-start | bytes 3670016 | tf_op jit(solution)/shard_map/all_to_all | solution.py:162
  11.7 5.1 %collective-permute-start.1 = (f32[64,7168]{1,0:T(8,128)S(1)}, f32[64,7168]{1,0:T(8,128)}, u32[]{:S(2)}, u32[]{:S(2)}) collective-permute-start(f32[64,7168]{1,0:T(8,128)S(1)} %bitcast.113), channel_id=1, source_target_pairs={{0,2},{1,3},{2,4},{3,5},{4,6},{5,7},{8,10},{9,11},{10,12},{11,13},... | collective-permute-start | bytes 5505032 | tf_op jit(solution)/shard_map/ppermute | solution.py:146
  16.8 1.3 collective-permute-start.3
  18.1 6.4 %collective-permute-start = (f32[16,4,7168]{2,1,0:T(4,128)}, f32[16,4,7168]{2,1,0:T(4,128)}, u32[]{:S(2)}, u32[]{:S(2)}) collective-permute-start(f32[16,4,7168]{2,1,0:T(4,128)} %get-tuple-element.13), channel_id=1, source_target_pairs={{0,128},{8,136},{16,144},{24,152},{32,160},{40,168},{48,176},{56,1... | collective-permute-start | bytes 5505032 | tf_op jit(solution)/shard_map/ppermute | solution.py:157
  24.5 11.7 %all-to-all-done = f32[16,4,7168]{2,1,0:T(4,128)} async-done(((f32[16,4,7168]{2,1,0:T(4,128)}), f32[16,4,7168]{2,1,0:T(4,128)}, u32[]{:S(2)}, u32[]{:S(2)}) %all-to-all-start) | async-done | bytes 1835040 | tf_op jit(solution)/shard_map/all_to_all | solution.py:162
  36.2 2.9 reshape.10
  39.1 2.9 constant_dynamic-update-slice_fusion.1
  42.0 14.1 %collective-permute-done.1.refs_6_ = f32[64,7168]{1,0:T(8,128)} collective-permute-done((f32[64,7168]{1,0:T(8,128)S(1)}, f32[64,7168]{1,0:T(8,128)}, u32[]{:S(2)}, u32[]{:S(2)}) %collective-permute-start.1) | collective-permute-done | bytes 1835040 | tf_op jit(solution)/shard_map/ppermute | solution.py:146
  56.0 1.9 collective-permute-start.2
  57.9 7.1 %collective-permute-done.3.refs_2_ = f32[64,7168]{1,0:T(8,128)} collective-permute-done((f32[64,7168]{1,0:T(8,128)S(1)}, f32[64,7168]{1,0:T(8,128)}, u32[]{:S(2)}, u32[]{:S(2)}) %collective-permute-start.3) | collective-permute-done | bytes 1835040 | tf_op jit(solution)/shard_map/ppermute | solution.py:146
  65.0 1.3 collective-permute-start.4
  66.3 36.7 %collective-permute-done = f32[16,4,7168]{2,1,0:T(4,128)} collective-permute-done((f32[16,4,7168]{2,1,0:T(4,128)}, f32[16,4,7168]{2,1,0:T(4,128)}, u32[]{:S(2)}, u32[]{:S(2)}) %collective-permute-start) | collective-permute-done | bytes 1835040 | tf_op jit(solution)/shard_map/ppermute | solution.py:157
  103.0 7.2 %all-to-all-start.1 = ((f32[16,4,7168]{2,1,0:T(4,128)}), f32[16,4,7168]{2,1,0:T(4,128)}, u32[]{:S(2)}, u32[]{:S(2)}) async-start(f32[16,4,7168]{2,1,0:T(4,128)} %collective-permute-done), calls=%async_computation.1 | async-start | bytes 3670016 | tf_op jit(solution)/shard_map/all_to_all | solution.py:162
  110.2 3.7 %broadcast_select_fusion.1 = (f32[64,7168]{1,0:T(8,128)}, f32[64,7168]{1,0:T(8,128)}) fusion(f32[64,7168]{1,0:T(8,128)S(1)} %bitcast.116, f32[64,7168]{1,0:T(8,128)} %collective-permute-done.9.refs_1_, pred[]{:T(512)S(6)} %eq.44), kind=kLoop, calls=%fused_computation.22 | loop fusion | flops 917504 | bytes 7340033 | tf_op jit(solution)/shard_map/jit(_where)/select_n | solution.py:150
  113.9 21.8 %all-to-all-done.1 = f32[16,4,7168]{2,1,0:T(4,128)} async-done(((f32[16,4,7168]{2,1,0:T(4,128)}), f32[16,4,7168]{2,1,0:T(4,128)}, u32[]{:S(2)}, u32[]{:S(2)}) %all-to-all-start.1) | async-done | bytes 1835040 | tf_op jit(solution)/shard_map/all_to_all | solution.py:162
  135.6 1.9 reshape.11
  137.6 1.3 constant_dynamic-update-slice_fusion.rows_ref
  140.3 3.7 %fusion = f32[128,128]{1,0:T(8,128)S(1)} fusion(f32[128,7168]{1,0:T(8,128)} %constant_dynamic-update-slice_fusion.rows_ref, f32[64,7168]{1,0:T(8,128)S(1)} %copy-done.8, f32[64,7168]{1,0:T(8,128)S(1)} %copy-done.7), kind=kOutput, calls=%fused_computation.3 | convolution fusion | flops 705560576 | bytes 7405568 | tf_op jit(solution)/shard_map/dot_general | solution.py:40
  144.0 33.7 %collective-permute-done.4 = f32[64,7168]{1,0:T(8,128)} collective-permute-done((f32[64,7168]{1,0:T(8,128)}, f32[64,7168]{1,0:T(8,128)}, u32[]{:S(2)}, u32[]{:S(2)}) %collective-permute-start.4) | collective-permute-done | bytes 1835040 | tf_op jit(solution)/shard_map/ppermute | solution.py:146
  177.7 2.4 fusion.53
  180.2 1.5 collective-permute-start.5
  181.7 2.5 broadcast_select_fusion.5
  184.8 1.9 fusion.8
  186.7 2.4 broadcast_select_fusion.7
  189.1 1.9 fusion.9
  192.2 1.9 fusion.7
  194.1 4.1 %fusion.4 = f32[64,128]{1,0:T(8,128)S(1)} fusion(f32[64,7168]{1,0:T(8,128)S(1)} %get-tuple-element.30, f32[64,7168]{1,0:T(8,128)S(1)} %get-tuple-element.29, f32[64,7168]{1,0:T(8,128)S(1)} %get-tuple-element.28, f32[64,7168]{1,0:T(8,128)S(1)} %get-tuple-element.27, f32[64,7168]{1,0:T(8,128)S(1)} %get-tuple-element.26, f32[64,7168]{1,0:T(8,128)S(1)} %get-tuple-element.25, ...), kind=kOutput, calls=%fused_computation.8 | convolution fusion | flops 357826560 | bytes 16547843 | tf_op jit(solution)/shard_map/dot_general | solution.py:40
  198.2 34.2 %collective-permute-done.5.refs_8_ = f32[64,7168]{1,0:T(8,128)} collective-permute-done((f32[64,7168]{1,0:T(8,128)S(1)}, f32[64,7168]{1,0:T(8,128)}, u32[]{:S(2)}, u32[]{:S(2)}) %collective-permute-start.5) | collective-permute-done | bytes 1835040 | tf_op jit(solution)/shard_map/ppermute | solution.py:146
  232.3 4.0 %collective-permute-done.10.refs_9_ = f32[64,7168]{1,0:T(8,128)S(1)} collective-permute-done((f32[64,7168]{1,0:T(8,128)}, f32[64,7168]{1,0:T(8,128)S(1)}, u32[]{:S(2)}, u32[]{:S(2)}) %collective-permute-start.10) | collective-permute-done | bytes 1835040 | tf_op jit(solution)/shard_map/ppermute | solution.py:146
  236.3 2.5 pad_maximum_fusion.3
  239.6 1.7 fusion.56
  241.6 1.8 collective-permute-start.11
  243.4 5.6 %collective-permute-start.12 = (f32[192,128]{1,0:T(8,128)S(1)}, f32[192,128]{1,0:T(8,128)S(1)}, u32[]{:S(2)}, u32[]{:S(2)}) collective-permute-start(f32[192,128]{1,0:T(8,128)S(1)} %get-tuple-element.63), channel_id=1, source_target_pairs={{0,16},{8,24},{16,0},{24,8},{32,48},{40,56},{48,32},{56,40},{64,80... | collective-permute-start | bytes 294920 | tf_op jit(solution)/shard_map/ppermute | solution.py:51
  249.0 1.5 collective-permute-done.11
  250.6 2.1 collective-permute-done.12
  252.7 1.4 collective-permute-done.13
  254.4 2.6 collective-permute-start.15
  257.5 4.0 %collective-permute-done.14 = f32[192,128]{1,0:T(8,128)S(1)} collective-permute-done((f32[192,128]{1,0:T(8,128)S(1)}, f32[192,128]{1,0:T(8,128)S(1)}, u32[]{:S(2)}, u32[]{:S(2)}) %collective-permute-start.14) | collective-permute-done | bytes 98336 | tf_op jit(solution)/shard_map/ppermute | solution.py:51
  263.0 7.8 %collective-permute-done.17 = f32[192,128]{1,0:T(8,128)S(1)} collective-permute-done((f32[192,128]{1,0:T(8,128)S(1)}, f32[192,128]{1,0:T(8,128)S(1)}, u32[]{:S(2)}, u32[]{:S(2)}) %collective-permute-start.17) | collective-permute-done | bytes 98336 | tf_op jit(solution)/shard_map/ppermute | solution.py:51
  271.0 1.6 collective-permute-start.18
  272.5 1.8 collective-permute-start.19
  274.4 2.5 collective-permute-start.20
  277.0 1.1 collective-permute-start.23
  278.2 1.0 collective-permute-start.24
  279.8 2.0 collective-permute-done.22
  281.8 3.0 %collective-permute-done.23 = f32[128,128]{1,0:T(8,128)S(1)} collective-permute-done((f32[128,128]{1,0:T(8,128)S(1)}, f32[128,128]{1,0:T(8,128)S(1)}, u32[]{:S(2)}, u32[]{:S(2)}) %collective-permute-start.23) | collective-permute-done | bytes 65568 | tf_op jit(solution)/shard_map/ppermute | solution.py:146
  286.9 11.1 %shard_map.37 = f32[128,7168]{1,0:T(8,128)} custom-call(s32[5]{0:T(128)} %stack.89.where_ref, f32[128,7168]{1,0:T(8,128)} %constant_dynamic-update-slice_fusion.rows_ref, bf16[256,512]{1,0:T(8,128)(2,1)} %pad_maximum_fusion.12.scaled_ref, f32[64,7168]{1,0:T(8,128)} %bitcast.112, f32[64,7168]{1,0:T(8,128)} %collective-permute-done.9.refs_1_, ...), custom_call_target="tpu_custom_call" | custom-call | flops 2818572288 | bytes 22020096 | tf_op jit(solution)/shard_map/pallas_call | solution.py:114
  (93 shorter events, 9.4 us)
Async XLA Ops:
  4.1 7.6 %copy-start.3 = (f32[7168,64]{0,1:T(8,128)S(1)}, f32[7168,64]{0,1:T(8,128)}, u32[]{:S(2)}) copy-start(f32[7168,64]{0,1:T(8,128)} %param.4) | copy-start | bytes 5505028
  4.1 32.0 %all-to-all-start = ((f32[16,4,7168]{2,1,0:T(4,128)}), f32[16,4,7168]{2,1,0:T(4,128)}, u32[]{:S(2)}, u32[]{:S(2)}) async-start(f32[16,4,7168]{2,1,0:T(4,128)} %get-tuple-element.34), calls=%async_computation | async-start | bytes 3670016 | tf_op jit(solution)/shard_map/all_to_all | solution.py:162
  11.7 44.3 %collective-permute-start.1 = (f32[64,7168]{1,0:T(8,128)S(1)}, f32[64,7168]{1,0:T(8,128)}, u32[]{:S(2)}, u32[]{:S(2)}) collective-permute-start(f32[64,7168]{1,0:T(8,128)S(1)} %bitcast.113), channel_id=1, source_target_pairs={{0,2},{1,3},{2,4},{3,5},{4,6},{5,7},{8,10},{9,11},{10,12},{11,13},... | collective-permute-start | bytes 5505032 | tf_op jit(solution)/shard_map/ppermute | solution.py:146
  16.8 48.2 %collective-permute-start.3 = (f32[64,7168]{1,0:T(8,128)S(1)}, f32[64,7168]{1,0:T(8,128)}, u32[]{:S(2)}, u32[]{:S(2)}) collective-permute-start(f32[64,7168]{1,0:T(8,128)S(1)} %bitcast.114), channel_id=1, source_target_pairs={{2,0},{3,1},{4,2},{5,3},{6,4},{7,5},{10,8},{11,9},{12,10},{13,11},... | collective-permute-start | bytes 5505032 | tf_op jit(solution)/shard_map/ppermute | solution.py:146
  18.1 84.9 %collective-permute-start = (f32[16,4,7168]{2,1,0:T(4,128)}, f32[16,4,7168]{2,1,0:T(4,128)}, u32[]{:S(2)}, u32[]{:S(2)}) collective-permute-start(f32[16,4,7168]{2,1,0:T(4,128)} %get-tuple-element.13), channel_id=1, source_target_pairs={{0,128},{8,136},{16,144},{24,152},{32,160},{40,168},{48,176},{56,1... | collective-permute-start | bytes 5505032 | tf_op jit(solution)/shard_map/ppermute | solution.py:157
  24.5 85.7 %collective-permute-start.9 = (f32[64,7168]{1,0:T(8,128)S(1)}, f32[64,7168]{1,0:T(8,128)}, u32[]{:S(2)}, u32[]{:S(2)}) collective-permute-start(f32[64,7168]{1,0:T(8,128)S(1)} %bitcast.115), channel_id=1, source_target_pairs={{0,1},{1,0},{2,3},{3,2},{4,5},{5,4},{6,7},{7,6},{8,9},{9,8},{10,11... | collective-permute-start | bytes 5505032 | tf_op jit(solution)/shard_map/ppermute | solution.py:146
  56.0 88.0 %collective-permute-start.2 = (f32[64,7168]{1,0:T(8,128)}, f32[64,7168]{1,0:T(8,128)}, u32[]{:S(2)}, u32[]{:S(2)}) collective-permute-start(f32[64,7168]{1,0:T(8,128)} %collective-permute-done.1.refs_6_), channel_id=1, source_target_pairs={{2,4},{3,5},{4,6},{5,7},{10,12},{11,13},{12,14},{13,15},{18,20},{1... | collective-permute-start | bytes 5505032 | tf_op jit(solution)/shard_map/ppermute | solution.py:146
  57.9 123.8 %collective-permute-start.7 = (f32[64,7168]{1,0:T(8,128)}, f32[64,7168]{1,0:T(8,128)}, u32[]{:S(2)}, u32[]{:S(2)}) collective-permute-start(f32[64,7168]{1,0:T(8,128)} %collective-permute-done.1.refs_6_), channel_id=1, source_target_pairs={{0,1},{1,0},{2,3},{3,2},{4,5},{5,4},{6,7},{7,6},{8,9},{9,8},{10,11... | collective-permute-start | bytes 5505032 | tf_op jit(solution)/shard_map/ppermute | solution.py:146
  65.0 112.7 %collective-permute-start.4 = (f32[64,7168]{1,0:T(8,128)}, f32[64,7168]{1,0:T(8,128)}, u32[]{:S(2)}, u32[]{:S(2)}) collective-permute-start(f32[64,7168]{1,0:T(8,128)} %collective-permute-done.3.refs_2_), channel_id=1, source_target_pairs={{2,0},{3,1},{4,2},{5,3},{10,8},{11,9},{12,10},{13,11},{18,16},{19,... | collective-permute-start | bytes 5505032 | tf_op jit(solution)/shard_map/ppermute | solution.py:146
  103.0 83.7 %collective-permute-start.6 = (f32[64,7168]{1,0:T(8,128)}, f32[64,7168]{1,0:T(8,128)}, u32[]{:S(2)}, u32[]{:S(2)}) collective-permute-start(f32[64,7168]{1,0:T(8,128)} %collective-permute-done.3.refs_2_), channel_id=1, source_target_pairs={{0,1},{1,0},{2,3},{3,2},{4,5},{5,4},{6,7},{7,6},{8,9},{9,8},{10,11... | collective-permute-start | bytes 5505032 | tf_op jit(solution)/shard_map/ppermute | solution.py:146
  103.0 32.7 %all-to-all-start.1 = ((f32[16,4,7168]{2,1,0:T(4,128)}), f32[16,4,7168]{2,1,0:T(4,128)}, u32[]{:S(2)}, u32[]{:S(2)}) async-start(f32[16,4,7168]{2,1,0:T(4,128)} %collective-permute-done), calls=%async_computation.1 | async-start | bytes 3670016 | tf_op jit(solution)/shard_map/all_to_all | solution.py:162
  137.6 2.2 copy-start.7
  137.6 2.7 copy-start.8
  180.1 14.0 %copy-start.2 = (f32[64,7168]{1,0:T(8,128)}, f32[64,7168]{1,0:T(8,128)S(1)}, u32[]{:S(2)}) copy-start(f32[64,7168]{1,0:T(8,128)S(1)} %get-tuple-element.31.refs_4_) | copy-start | bytes 5505028
  180.1 10.8 %collective-permute-start.8 = (f32[64,7168]{1,0:T(8,128)S(1)}, f32[64,7168]{1,0:T(8,128)S(1)}, u32[]{:S(2)}, u32[]{:S(2)}) collective-permute-start(f32[64,7168]{1,0:T(8,128)S(1)} %get-tuple-element.31.refs_4_), channel_id=1, source_target_pairs={{0,1},{1,0},{2,3},{3,2},{4,5},{5,4},{6,7},{7,6},{8,9},{9,8},{10,11... | collective-permute-start | bytes 5505032 | tf_op jit(solution)/shard_map/ppermute | solution.py:146
  180.2 52.1 %collective-permute-start.5 = (f32[64,7168]{1,0:T(8,128)S(1)}, f32[64,7168]{1,0:T(8,128)}, u32[]{:S(2)}, u32[]{:S(2)}) collective-permute-start(f32[64,7168]{1,0:T(8,128)S(1)} %get-tuple-element.32), channel_id=1, source_target_pairs={{4,6},{5,7},{2,0},{3,1},{12,14},{13,15},{10,8},{11,9},{20,22},{21,... | collective-permute-start | bytes 5505032 | tf_op jit(solution)/shard_map/ppermute | solution.py:146
  181.7 3.1 %copy-start = (f32[128,7168]{1,0:T(8,128)S(1)}, f32[128,7168]{1,0:T(8,128)}, u32[]{:S(2)}) copy-start(f32[128,7168]{1,0:T(8,128)} %constant_dynamic-update-slice_fusion.rows_ref) | copy-start | bytes 11010052
  191.0 1.2 copy-start.6
  192.2 1.9 copy-start.4
  232.3 4.0 %collective-permute-start.10 = (f32[64,7168]{1,0:T(8,128)}, f32[64,7168]{1,0:T(8,128)S(1)}, u32[]{:S(2)}, u32[]{:S(2)}) collective-permute-start(f32[64,7168]{1,0:T(8,128)} %collective-permute-done.5.refs_8_), channel_id=1, source_target_pairs={{0,1},{1,0},{2,3},{3,2},{4,5},{5,4},{6,7},{7,6},{8,9},{9,8},{10,11... | collective-permute-start | bytes 5505032 | tf_op jit(solution)/shard_map/ppermute | solution.py:146
  236.3 2.5 copy-start.5
  236.3 3.3 %copy-start.1 = (f32[128,7168]{1,0:T(8,128)S(1)}, f32[128,7168]{1,0:T(8,128)}, u32[]{:S(2)}) copy-start(f32[128,7168]{1,0:T(8,128)} %constant_dynamic-update-slice_fusion.rows_ref) | copy-start | bytes 11010052
  241.6 9.0 %collective-permute-start.11 = (f32[192,128]{1,0:T(8,128)S(1)}, f32[192,128]{1,0:T(8,128)S(1)}, u32[]{:S(2)}, u32[]{:S(2)}) collective-permute-start(f32[192,128]{1,0:T(8,128)S(1)} %get-tuple-element.62), channel_id=1, source_target_pairs={{0,8},{8,16},{16,24},{24,0},{32,40},{40,48},{48,56},{56,32},{64,72... | collective-permute-start | bytes 294920 | tf_op jit(solution)/shard_map/ppermute | solution.py:51
  243.4 9.2 %collective-permute-start.12 = (f32[192,128]{1,0:T(8,128)S(1)}, f32[192,128]{1,0:T(8,128)S(1)}, u32[]{:S(2)}, u32[]{:S(2)}) collective-permute-start(f32[192,128]{1,0:T(8,128)S(1)} %get-tuple-element.63), channel_id=1, source_target_pairs={{0,16},{8,24},{16,0},{24,8},{32,48},{40,56},{48,32},{56,40},{64,80... | collective-permute-start | bytes 294920 | tf_op jit(solution)/shard_map/ppermute | solution.py:51
  249.0 5.0 %collective-permute-start.13 = (f32[192,128]{1,0:T(8,128)S(1)}, f32[192,128]{1,0:T(8,128)S(1)}, u32[]{:S(2)}, u32[]{:S(2)}) collective-permute-start(f32[192,128]{1,0:T(8,128)S(1)} %get-tuple-element.64), channel_id=1, source_target_pairs={{0,24},{8,0},{16,8},{24,16},{32,56},{40,32},{48,40},{56,48},{64,88... | collective-permute-start | bytes 294920 | tf_op jit(solution)/shard_map/ppermute | solution.py:51
  254.0 25.4 %copy-start.9 = (f32[2,256,256]{2,1,0:T(8,128)S(1)}, f32[2,256,256]{2,1,0:T(8,128)}, u32[]{:S(2)}) copy-start(f32[2,256,256]{2,1,0:T(8,128)} %param.5) | copy-start | bytes 1572868
  254.1 7.5 %collective-permute-start.14 = (f32[192,128]{1,0:T(8,128)S(1)}, f32[192,128]{1,0:T(8,128)S(1)}, u32[]{:S(2)}, u32[]{:S(2)}) collective-permute-start(f32[192,128]{1,0:T(8,128)S(1)} %fusion.35), channel_id=1, source_target_pairs={{0,32},{8,40},{16,48},{24,56},{32,64},{40,72},{48,80},{56,88},{64,... | collective-permute-start | bytes 294920 | tf_op jit(solution)/shard_map/ppermute | solution.py:51
  254.4 7.1 %collective-permute-start.15 = (f32[192,128]{1,0:T(8,128)S(1)}, f32[192,128]{1,0:T(8,128)S(1)}, u32[]{:S(2)}, u32[]{:S(2)}) collective-permute-start(f32[192,128]{1,0:T(8,128)S(1)} %fusion.35), channel_id=1, source_target_pairs={{0,64},{8,72},{16,80},{24,88},{32,96},{40,104},{48,112},{56,120},{... | collective-permute-start | bytes 294920 | tf_op jit(solution)/shard_map/ppermute | solution.py:51
  257.0 5.2 %collective-permute-start.16 = (f32[192,128]{1,0:T(8,128)S(1)}, f32[192,128]{1,0:T(8,128)S(1)}, u32[]{:S(2)}, u32[]{:S(2)}) collective-permute-start(f32[192,128]{1,0:T(8,128)S(1)} %fusion.35), channel_id=1, source_target_pairs={{0,96},{8,104},{16,112},{24,120},{32,0},{40,8},{48,16},{56,24},{64... | collective-permute-start | bytes 294920 | tf_op jit(solution)/shard_map/ppermute | solution.py:51
  262.2 8.6 %collective-permute-start.17 = (f32[192,128]{1,0:T(8,128)S(1)}, f32[192,128]{1,0:T(8,128)S(1)}, u32[]{:S(2)}, u32[]{:S(2)}) collective-permute-start(f32[192,128]{1,0:T(8,128)S(1)} %add_add_fusion), channel_id=1, source_target_pairs={{0,128},{8,136},{16,144},{24,152},{32,160},{40,168},{48,176},{56,1... | collective-permute-start | bytes 294920 | tf_op jit(solution)/shard_map/ppermute | solution.py:51
  270.8 6.1 %collective-permute-start.21 = (f32[64,128]{1,0:T(8,128)S(1)}, f32[64,128]{1,0:T(8,128)S(1)}, u32[]{:S(2)}, u32[]{:S(2)}) collective-permute-start(f32[64,128]{1,0:T(8,128)S(1)} %slice.118), channel_id=1, source_target_pairs={{0,1},{1,0},{2,3},{3,2},{4,5},{5,4},{6,7},{7,6},{8,9},{9,8},{10,11... | collective-permute-start | bytes 98312 | tf_op jit(solution)/shard_map/ppermute | solution.py:146
  271.0 7.2 %collective-permute-start.18 = (f32[128,128]{1,0:T(8,128)S(1)}, f32[128,128]{1,0:T(8,128)S(1)}, u32[]{:S(2)}, u32[]{:S(2)}) collective-permute-start(f32[128,128]{1,0:T(8,128)S(1)} %slice.117), channel_id=1, source_target_pairs={{0,24},{8,0},{16,8},{24,16},{32,56},{40,32},{48,40},{56,48},{64,88... | collective-permute-start | bytes 196616 | tf_op jit(solution)/shard_map/ppermute | solution.py:51
  272.5 6.6 %collective-permute-start.19 = (f32[128,128]{1,0:T(8,128)S(1)}, f32[128,128]{1,0:T(8,128)S(1)}, u32[]{:S(2)}, u32[]{:S(2)}) collective-permute-start(f32[128,128]{1,0:T(8,128)S(1)} %slice.117), channel_id=1, source_target_pairs={{0,16},{8,24},{16,0},{24,8},{32,48},{40,56},{48,32},{56,40},{64,80... | collective-permute-start | bytes 196616 | tf_op jit(solution)/shard_map/ppermute | solution.py:51
  274.4 4.9 %collective-permute-start.20 = (f32[128,128]{1,0:T(8,128)S(1)}, f32[128,128]{1,0:T(8,128)S(1)}, u32[]{:S(2)}, u32[]{:S(2)}) collective-permute-start(f32[128,128]{1,0:T(8,128)S(1)} %slice.117), channel_id=1, source_target_pairs={{0,8},{8,16},{16,24},{24,0},{32,40},{40,48},{48,56},{56,32},{64,72... | collective-permute-start | bytes 196616 | tf_op jit(solution)/shard_map/ppermute | solution.py:51
  276.9 4.9 %collective-permute-start.22 = (f32[128,128]{1,0:T(8,128)S(1)}, f32[128,128]{1,0:T(8,128)S(1)}, u32[]{:S(2)}, u32[]{:S(2)}) collective-permute-start(f32[128,128]{1,0:T(8,128)S(1)} %pad_maximum_fusion.17), channel_id=1, source_target_pairs={{0,6},{1,7},{2,0},{3,1},{4,2},{5,3},{6,4},{7,5},{8,14},{9,15},{10,... | collective-permute-start | bytes 196616 | tf_op jit(solution)/shard_map/ppermute | solution.py:146
  277.0 7.8 %collective-permute-start.23 = (f32[128,128]{1,0:T(8,128)S(1)}, f32[128,128]{1,0:T(8,128)S(1)}, u32[]{:S(2)}, u32[]{:S(2)}) collective-permute-start(f32[128,128]{1,0:T(8,128)S(1)} %pad_maximum_fusion.17), channel_id=1, source_target_pairs={{0,4},{1,5},{2,6},{3,7},{4,0},{5,1},{6,2},{7,3},{8,12},{9,13},{10,... | collective-permute-start | bytes 196616 | tf_op jit(solution)/shard_map/ppermute | solution.py:146
  278.2 6.7 %collective-permute-start.24 = (f32[128,128]{1,0:T(8,128)S(1)}, f32[128,128]{1,0:T(8,128)S(1)}, u32[]{:S(2)}, u32[]{:S(2)}) collective-permute-start(f32[128,128]{1,0:T(8,128)S(1)} %pad_maximum_fusion.17), channel_id=1, source_target_pairs={{0,2},{1,3},{2,4},{3,5},{4,6},{5,7},{6,0},{7,1},{8,10},{9,11},{10,... | collective-permute-start | bytes 196616 | tf_op jit(solution)/shard_map/ppermute | solution.py:146

commit v6 on v5

--- a/solution.py
+++ b/solution.py
@@ -151,12 +151,9 @@
         )
 
     blocks = eigen_rows.reshape(count, 32, length).transpose(1, 0, 2)
-    leaving = lax.dynamic_slice_in_dim(blocks, (1 - half) * 16, 16, 0)
-    staying = lax.dynamic_slice_in_dim(blocks, half * 16, 16, 0)
-    mine, leaving = lax.optimization_barrier((mine, leaving))
-    arriving = lax.ppermute(leaving, "prow", FAR)
-    below = send(mine, UP_ONE)
-    above = send(mine, DOWN_ONE)
+
+    def zero_from(*values):
+        return sum(jnp.minimum(jnp.abs(value[0, 0]), 0.0) for value in values).astype(jnp.int32)
 
     def over_plane(value):
         value = lax.all_to_all(
@@ -164,16 +161,27 @@
         )
         return value.reshape(16 * count, length)
 
-    staying = over_plane(staying)
+    below = send(mine, UP_ONE)
+    above = send(mine, DOWN_ONE)
+    mine_other = send(mine, SIBLING)
+    leaving = lax.dynamic_slice_in_dim(blocks, (1 - half) * 16, 16, 0)
+    arriving = over_plane(lax.ppermute(leaving, "prow", FAR))
+    staying = over_plane(
+        lax.dynamic_slice_in_dim(blocks, half * 16 + zero_from(leaving[0]), 16, 0)
+    )
     below_two = send(below, UP_TWO)
     above_two = send(above, DOWN_TWO)
-    arriving = over_plane(arriving)
     last = send(jnp.where(chip == 2, below_two, above_two), TO_ENDS)
-    rows = jnp.concatenate([staying, arriving], axis=0)
+    rows = lax.dynamic_update_slice_in_dim(
+        jnp.pad(staying, ((0, 16 * count), (0, 0))),
+        arriving,
+        16 * count + zero_from(below_two, above_two),
+        0,
+    )
     two = below_two + above_two
 
     pieces = (mine, above, two, below)
-    swapped = [send(piece, SIBLING) for piece in pieces]
+    swapped = [mine_other, *(send(piece, SIBLING) for piece in pieces[1:])]
     all_mine, all_above, all_two, all_below = (
         ordered(piece, other, 0) for piece, other in zip(pieces, swapped)
     )

time: 299 us -> 287 us (0.960)
  waiting for transfers between devices: 186 us -> 156 us
  starting transfers between devices: 51.5 us -> 60.7 us
  local copies, waits for them, and re-layouts: 18 us -> 24.8 us
    ppermute x14, waiting for transfers between devices: 98 us -> 79.6 us  [send(): return lax.ppermute(value, 'pcol', pairs)]
    all_to_all x2, waiting for transfers between devices: 33.4 us -> 27.4 us  [over_plane(): lax.all_to_all(value, 'prow', split_axis=0, concat_axis=0, tiled=True, ax...]
    ppermute x14, starting transfers between devices: 13.4 us -> 18.7 us  [send(): return lax.ppermute(value, 'pcol', pairs)]
    unnamed x40 -> x37, local copies, waits for them, and re-layouts: 6.66 us -> 1.69 us
    dynamic_update_slice x0 -> x1, local copies, waits for them, and re-layouts: none -> 4.3 us  [body(): lax.dynamic_update_slice_in_dim(jnp.pad(staying, ((0, 16 * count), (0, 0)...]
    pad x0 -> x1, local copies, waits for them, and re-layouts: none -> 3.58 us  [body(): jnp.pad(staying, ((0, 16 * count), (0, 0)))]
  transfers between devices with their start and end apart: 27 -> 27, of which waited for: 17 -> 17; matrix products, arithmetic and copies ran while one was open for 12% -> 17% of each run, Pallas kernels for 0% -> 0%
where the time goes in v6:
time: 287 us
  waiting for transfers between devices  156 us (54%)
  starting transfers between devices  60.7 us (21%)
  local copies, waits for them, and re-layouts  24.8 us (9%)
  other arithmetic  17.7 us (6%)
  matrix products  14.1 us (5%)
  Pallas kernels  11.1 us (4%)
    ppermute x14, waiting for transfers between devices, send(): return lax.ppermute(value, 'pcol', pairs)  79.6 us
    ppermute x1, waiting for transfers between devices, body(): arriving = over_plane(lax.ppermute(leaving, 'prow', FAR))  33.9 us
    all_to_all x2, waiting for transfers between devices, over_plane(): lax.all_to_all(value, 'prow', split_axis=0, concat_axis=0, tiled=True, ax...  27.4 us
    ppermute x10, starting transfers between devices, send(): return lax.ppermute(value, 'prow', pairs)  19.9 us
    ppermute x14, starting transfers between devices, send(): return lax.ppermute(value, 'pcol', pairs)  18.7 us
    all_to_all x2, starting transfers between devices, over_plane(): lax.all_to_all(value, 'prow', split_axis=0, concat_axis=0, tiled=True, ax...  15 us
    ppermute x10, waiting for transfers between devices, send(): return lax.ppermute(value, 'prow', pairs)  15 us
    dot_general x6, matrix products, matmul_nt(): lax.dot_general(left, right, (((1,), (1,)), ((), ())), precision=lax.Prec...  13.1 us
  transfers between devices with their start and end apart: 27, of which 17 were waited for; matrix products, arithmetic and copies ran while one was open for 17% of the time, Pallas kernels for 0%

profile of v6, /device:TPU:2, one launch (start us, length us, event | category | flops | bytes accessed | tf_op | source)
XLA Modules:
  0.0 286.6 jit_solution(9150668673888014691)
XLA Ops:
  0.0 1.3 collective-permute-start.3
  1.3 5.8 %collective-permute-start.1 = (f32[64,7168]{1,0:T(8,128)}, f32[64,7168]{1,0:T(8,128)}, u32[]{:S(2)}, u32[]{:S(2)}) collective-permute-start(f32[64,7168]{1,0:T(8,128)} %bitcast.123), channel_id=1, source_target_pairs={{0,2},{1,3},{2,4},{3,5},{4,6},{5,7},{8,10},{9,11},{10,12},{11,13},... | collective-permute-start | bytes 5505032 | tf_op jit(solution)/shard_map/ppermute | solution.py:146
  7.1 2.9 dynamic-slice_bitcast_fusion.1
  10.0 7.2 %collective-permute-start = (f32[16,4,7168]{2,1,0:T(4,128)}, f32[16,4,7168]{2,1,0:T(4,128)}, u32[]{:S(2)}, u32[]{:S(2)}) collective-permute-start(f32[16,4,7168]{2,1,0:T(4,128)} %dynamic-slice_bitcast_fusion.1), channel_id=1, source_target_pairs={{0,128},{8,136},{16,144},{24,152},{32,160},{40,168},{48,176},{56,1... | collective-permute-start | bytes 5505032 | tf_op jit(solution)/shard_map/ppermute | solution.py:168
  19.2 2.9 dynamic-slice_bitcast_fusion
  22.0 7.5 %all-to-all-start = ((f32[16,4,7168]{2,1,0:T(4,128)}), f32[16,4,7168]{2,1,0:T(4,128)S(1)}, u32[]{:S(2)}, u32[]{:S(2)}) async-start(f32[16,4,7168]{2,1,0:T(4,128)} %dynamic-slice_bitcast_fusion), calls=%async_computation | async-start | bytes 3670016 | tf_op jit(solution)/shard_map/all_to_all | solution.py:159
  29.5 15.6 %collective-permute-done.3.refs_2_ = f32[64,7168]{1,0:T(8,128)} collective-permute-done((f32[64,7168]{1,0:T(8,128)}, f32[64,7168]{1,0:T(8,128)}, u32[]{:S(2)}, u32[]{:S(2)}) %collective-permute-start.3) | collective-permute-done | bytes 1835040 | tf_op jit(solution)/shard_map/ppermute | solution.py:146
  45.1 1.3 collective-permute-start.4
  46.6 1.9 collective-permute-start.2
  48.5 5.7 %all-to-all-done = f32[16,4,7168]{2,1,0:T(4,128)S(1)} async-done(((f32[16,4,7168]{2,1,0:T(4,128)}), f32[16,4,7168]{2,1,0:T(4,128)S(1)}, u32[]{:S(2)}, u32[]{:S(2)}) %all-to-all-start) | async-done | bytes 1835040 | tf_op jit(solution)/shard_map/all_to_all | solution.py:159
  54.2 1.8 reshape.22
  56.0 3.6 %pad.4 = f32[128,7168]{1,0:T(8,128)} pad(f32[64,7168]{1,0:T(8,128)} %reshape.22, f32[]{:T(128)} %constant.110.clone.1), padding=0_64x0_0 | pad | bytes 5505028 | tf_op jit(solution)/shard_map/jit(_pad)/pad | solution.py:176
  59.6 33.9 %collective-permute-done = f32[16,4,7168]{2,1,0:T(4,128)} collective-permute-done((f32[16,4,7168]{2,1,0:T(4,128)}, f32[16,4,7168]{2,1,0:T(4,128)}, u32[]{:S(2)}, u32[]{:S(2)}) %collective-permute-start) | collective-permute-done | bytes 1835040 | tf_op jit(solution)/shard_map/ppermute | solution.py:168
  93.5 7.5 %all-to-all-start.1 = ((f32[16,4,7168]{2,1,0:T(4,128)}), f32[16,4,7168]{2,1,0:T(4,128)}, u32[]{:S(2)}, u32[]{:S(2)}) async-start(f32[16,4,7168]{2,1,0:T(4,128)} %collective-permute-done), calls=%async_computation.1 | async-start | bytes 3670016 | tf_op jit(solution)/shard_map/all_to_all | solution.py:159
  101.0 3.7 %broadcast_select_fusion.1 = (f32[64,7168]{1,0:T(8,128)}, f32[64,7168]{1,0:T(8,128)}) fusion(f32[64,7168]{1,0:T(8,128)} %collective-permute-done.9.refs_1_, pred[]{:T(512)S(6)} %eq.44, f32[7168,64]{0,1:T(8,128)S(1)} %copy-done.3), kind=kLoop, calls=%fused_computation.22 | loop fusion | flops 917504 | bytes 7340033 | tf_op jit(solution)/shard_map/jit(_where)/select_n | solution.py:150
  104.7 21.7 %all-to-all-done.1 = f32[16,4,7168]{2,1,0:T(4,128)} async-done(((f32[16,4,7168]{2,1,0:T(4,128)}), f32[16,4,7168]{2,1,0:T(4,128)}, u32[]{:S(2)}, u32[]{:S(2)}) %all-to-all-start.1) | async-done | bytes 1835040 | tf_op jit(solution)/shard_map/all_to_all | solution.py:159
  126.4 2.9 %reshape.23 = f32[64,7168]{1,0:T(8,128)} reshape(f32[16,4,7168]{2,1,0:T(4,128)} %all-to-all-done.1) | data formatting | bytes 3670016 | tf_op jit(solution)/shard_map/reshape | solution.py:162
  129.3 32.8 %collective-permute-done.4 = f32[64,7168]{1,0:T(8,128)} collective-permute-done((f32[64,7168]{1,0:T(8,128)}, f32[64,7168]{1,0:T(8,128)}, u32[]{:S(2)}, u32[]{:S(2)}) %collective-permute-start.4) | collective-permute-done | bytes 1835040 | tf_op jit(solution)/shard_map/ppermute | solution.py:146
  162.1 3.7 %fusion.54 = (f32[64,7168]{1,0:T(8,128)S(1)}, f32[64,7168]{1,0:T(8,128)}) fusion(f32[64,7168]{1,0:T(8,128)} %collective-permute-done.2, f32[64,7168]{1,0:T(8,128)} %collective-permute-done.4, pred[]{:T(512)S(6)} %eq.45), kind=kLoop, calls=%fused_computation.130 | loop fusion | flops 917504 | bytes 7340033 | tf_op jit(solution)/shard_map/add | solution.py:181
  165.9 1.2 slice.131
  169.5 1.5 collective-permute-start.5
  171.0 4.3 %dynamic_update_slice.3.rows_ref = f32[128,7168]{1,0:T(8,128)} dynamic-update-slice(f32[128,7168]{1,0:T(8,128)} %pad.4, f32[64,7168]{1,0:T(8,128)} %reshape.23, s32[]{:T(128)S(6)} %select_n.198, s32[]{:T(128)} %constant.101.clone.1) | dynamic-update-slice | bytes 3670020 | tf_op jit(solution)/shard_map/dynamic_update_slice | solution.py:175
  175.3 2.5 broadcast_select_fusion.5
  178.4 1.9 fusion.8
  180.3 2.4 broadcast_select_fusion.7
  182.7 1.9 fusion.9
  184.7 1.7 fusion
  186.4 1.8 broadcast_select_fusion.3
  188.3 1.9 fusion.7
  190.2 4.1 %fusion.4 = f32[64,128]{1,0:T(8,128)S(1)} fusion(f32[64,7168]{1,0:T(8,128)S(1)} %get-tuple-element.26, f32[64,7168]{1,0:T(8,128)S(1)} %get-tuple-element.25, f32[64,7168]{1,0:T(8,128)S(1)} %get-tuple-element.24, f32[64,7168]{1,0:T(8,128)S(1)} %get-tuple-element.23, f32[64,7168]{1,0:T(8,128)S(1)} %get-tuple-element.22, f32[64,7168]{1,0:T(8,128)S(1)} %get-tuple-element.21, ...), kind=kOutput, calls=%fused_computation.8 | convolution fusion | flops 357826560 | bytes 16547843 | tf_op jit(solution)/shard_map/dot_general | solution.py:40
  194.3 22.1 %collective-permute-done.5.refs_8_ = f32[64,7168]{1,0:T(8,128)} collective-permute-done((f32[64,7168]{1,0:T(8,128)}, f32[64,7168]{1,0:T(8,128)}, u32[]{:S(2)}, u32[]{:S(2)}) %collective-permute-start.5) | collective-permute-done | bytes 1835040 | tf_op jit(solution)/shard_map/ppermute | solution.py:146
  216.4 4.0 %collective-permute-done.10.refs_9_ = f32[64,7168]{1,0:T(8,128)S(1)} collective-permute-done((f32[64,7168]{1,0:T(8,128)}, f32[64,7168]{1,0:T(8,128)S(1)}, u32[]{:S(2)}, u32[]{:S(2)}) %collective-permute-start.10) | collective-permute-done | bytes 1835040 | tf_op jit(solution)/shard_map/ppermute | solution.py:146
  220.4 2.5 pad_maximum_fusion.3
  223.6 1.7 fusion.57
  225.6 1.8 collective-permute-start.11
  227.5 5.6 %collective-permute-start.12 = (f32[192,128]{1,0:T(8,128)S(1)}, f32[192,128]{1,0:T(8,128)S(1)}, u32[]{:S(2)}, u32[]{:S(2)}) collective-permute-start(f32[192,128]{1,0:T(8,128)S(1)} %get-tuple-element.57), channel_id=1, source_target_pairs={{0,16},{8,24},{16,0},{24,8},{32,48},{40,56},{48,32},{56,40},{64,80... | collective-permute-start | bytes 294920 | tf_op jit(solution)/shard_map/ppermute | solution.py:51
  233.1 1.5 collective-permute-done.11
  234.6 2.1 collective-permute-done.12
  236.7 1.4 collective-permute-done.13
  238.5 2.6 collective-permute-start.15
  241.6 4.0 %collective-permute-done.14 = f32[192,128]{1,0:T(8,128)S(1)} collective-permute-done((f32[192,128]{1,0:T(8,128)S(1)}, f32[192,128]{1,0:T(8,128)S(1)}, u32[]{:S(2)}, u32[]{:S(2)}) %collective-permute-start.14) | collective-permute-done | bytes 98336 | tf_op jit(solution)/shard_map/ppermute | solution.py:51
  246.2 2.8 collective-permute-start.17
  249.6 5.3 %collective-permute-done.17 = f32[192,128]{1,0:T(8,128)S(1)} collective-permute-done((f32[192,128]{1,0:T(8,128)S(1)}, f32[192,128]{1,0:T(8,128)S(1)}, u32[]{:S(2)}, u32[]{:S(2)}) %collective-permute-start.17) | collective-permute-done | bytes 98336 | tf_op jit(solution)/shard_map/ppermute | solution.py:51
  255.1 2.5 collective-permute-start.18
  258.7 2.5 collective-permute-start.20
  261.3 5.9 %collective-permute-start.22 = (f32[128,128]{1,0:T(8,128)S(1)}, f32[128,128]{1,0:T(8,128)S(1)}, u32[]{:S(2)}, u32[]{:S(2)}) collective-permute-start(f32[128,128]{1,0:T(8,128)S(1)} %pad_maximum_fusion.17), channel_id=1, source_target_pairs={{0,6},{1,7},{2,0},{3,1},{4,2},{5,3},{6,4},{7,5},{8,14},{9,15},{10,... | collective-permute-start | bytes 196616 | tf_op jit(solution)/shard_map/ppermute | solution.py:146
  269.7 3.0 %collective-permute-done.23 = f32[128,128]{1,0:T(8,128)S(1)} collective-permute-done((f32[128,128]{1,0:T(8,128)S(1)}, f32[128,128]{1,0:T(8,128)S(1)}, u32[]{:S(2)}, u32[]{:S(2)}) %collective-permute-start.23) | collective-permute-done | bytes 65568 | tf_op jit(solution)/shard_map/ppermute | solution.py:146
  275.6 11.1 %shard_map.37 = f32[128,7168]{1,0:T(8,128)} custom-call(s32[5]{0:T(128)} %stack.89.where_ref, f32[128,7168]{1,0:T(8,128)} %dynamic_update_slice.3.rows_ref, bf16[256,512]{1,0:T(8,128)(2,1)} %pad_maximum_fusion.12.scaled_ref, f32[64,7168]{1,0:T(8,128)} %bitcast.125, f32[64,7168]{1,0:T(8,128)} %collective-permute-done.9.refs_1_, ...), custom_call_target="tpu_custom_call" | custom-call | flops 2818572288 | bytes 22020096 | tf_op jit(solution)/shard_map/pallas_call | solution.py:114
  (96 shorter events, 13.2 us)
Async XLA Ops:
  0.0 45.1 %collective-permute-start.3 = (f32[64,7168]{1,0:T(8,128)}, f32[64,7168]{1,0:T(8,128)}, u32[]{:S(2)}, u32[]{:S(2)}) collective-permute-start(f32[64,7168]{1,0:T(8,128)} %bitcast.122), channel_id=1, source_target_pairs={{2,0},{3,1},{4,2},{5,3},{6,4},{7,5},{10,8},{11,9},{12,10},{13,11},... | collective-permute-start | bytes 5505032 | tf_op jit(solution)/shard_map/ppermute | solution.py:146
  1.3 45.3 %collective-permute-start.1 = (f32[64,7168]{1,0:T(8,128)}, f32[64,7168]{1,0:T(8,128)}, u32[]{:S(2)}, u32[]{:S(2)}) collective-permute-start(f32[64,7168]{1,0:T(8,128)} %bitcast.123), channel_id=1, source_target_pairs={{0,2},{1,3},{2,4},{3,5},{4,6},{5,7},{8,10},{9,11},{10,12},{11,13},... | collective-permute-start | bytes 5505032 | tf_op jit(solution)/shard_map/ppermute | solution.py:146
  7.1 93.9 %collective-permute-start.9 = (f32[64,7168]{1,0:T(8,128)}, f32[64,7168]{1,0:T(8,128)}, u32[]{:S(2)}, u32[]{:S(2)}) collective-permute-start(f32[64,7168]{1,0:T(8,128)} %bitcast.124), channel_id=1, source_target_pairs={{0,1},{1,0},{2,3},{3,2},{4,5},{5,4},{6,7},{7,6},{8,9},{9,8},{10,11... | collective-permute-start | bytes 5505032 | tf_op jit(solution)/shard_map/ppermute | solution.py:146
  10.0 83.5 %collective-permute-start = (f32[16,4,7168]{2,1,0:T(4,128)}, f32[16,4,7168]{2,1,0:T(4,128)}, u32[]{:S(2)}, u32[]{:S(2)}) collective-permute-start(f32[16,4,7168]{2,1,0:T(4,128)} %dynamic-slice_bitcast_fusion.1), channel_id=1, source_target_pairs={{0,128},{8,136},{16,144},{24,152},{32,160},{40,168},{48,176},{56,1... | collective-permute-start | bytes 5505032 | tf_op jit(solution)/shard_map/ppermute | solution.py:168
  22.0 32.2 %all-to-all-start = ((f32[16,4,7168]{2,1,0:T(4,128)}), f32[16,4,7168]{2,1,0:T(4,128)S(1)}, u32[]{:S(2)}, u32[]{:S(2)}) async-start(f32[16,4,7168]{2,1,0:T(4,128)} %dynamic-slice_bitcast_fusion), calls=%async_computation | async-start | bytes 3670016 | tf_op jit(solution)/shard_map/all_to_all | solution.py:159
  45.1 117.0 %collective-permute-start.4 = (f32[64,7168]{1,0:T(8,128)}, f32[64,7168]{1,0:T(8,128)}, u32[]{:S(2)}, u32[]{:S(2)}) collective-permute-start(f32[64,7168]{1,0:T(8,128)} %collective-permute-done.3.refs_2_), channel_id=1, source_target_pairs={{2,0},{3,1},{4,2},{5,3},{10,8},{11,9},{12,10},{13,11},{18,16},{19,... | collective-permute-start | bytes 5505032 | tf_op jit(solution)/shard_map/ppermute | solution.py:146
  46.6 115.5 %collective-permute-start.2 = (f32[64,7168]{1,0:T(8,128)}, f32[64,7168]{1,0:T(8,128)}, u32[]{:S(2)}, u32[]{:S(2)}) collective-permute-start(f32[64,7168]{1,0:T(8,128)} %collective-permute-done.1.refs_6_), channel_id=1, source_target_pairs={{2,4},{3,5},{4,6},{5,7},{10,12},{11,13},{12,14},{13,15},{18,20},{1... | collective-permute-start | bytes 5505032 | tf_op jit(solution)/shard_map/ppermute | solution.py:146
  59.6 41.3 %copy-start.3 = (f32[7168,64]{0,1:T(8,128)S(1)}, f32[7168,64]{0,1:T(8,128)}, u32[]{:S(2)}) copy-start(f32[7168,64]{0,1:T(8,128)} %param.4) | copy-start | bytes 5505028
  59.6 120.7 %collective-permute-start.6 = (f32[64,7168]{1,0:T(8,128)}, f32[64,7168]{1,0:T(8,128)}, u32[]{:S(2)}, u32[]{:S(2)}) collective-permute-start(f32[64,7168]{1,0:T(8,128)} %collective-permute-done.3.refs_2_), channel_id=1, source_target_pairs={{0,1},{1,0},{2,3},{3,2},{4,5},{5,4},{6,7},{7,6},{8,9},{9,8},{10,11... | collective-permute-start | bytes 5505032 | tf_op jit(solution)/shard_map/ppermute | solution.py:146
  93.5 81.8 %collective-permute-start.7 = (f32[64,7168]{1,0:T(8,128)}, f32[64,7168]{1,0:T(8,128)}, u32[]{:S(2)}, u32[]{:S(2)}) collective-permute-start(f32[64,7168]{1,0:T(8,128)} %collective-permute-done.1.refs_6_), channel_id=1, source_target_pairs={{0,1},{1,0},{2,3},{3,2},{4,5},{5,4},{6,7},{7,6},{8,9},{9,8},{10,11... | collective-permute-start | bytes 5505032 | tf_op jit(solution)/shard_map/ppermute | solution.py:146
  93.5 32.9 %all-to-all-start.1 = ((f32[16,4,7168]{2,1,0:T(4,128)}), f32[16,4,7168]{2,1,0:T(4,128)}, u32[]{:S(2)}, u32[]{:S(2)}) async-start(f32[16,4,7168]{2,1,0:T(4,128)} %collective-permute-done), calls=%async_computation.1 | async-start | bytes 3670016 | tf_op jit(solution)/shard_map/all_to_all | solution.py:159
  165.9 24.3 %copy-start.2 = (f32[64,7168]{1,0:T(8,128)}, f32[64,7168]{1,0:T(8,128)S(1)}, u32[]{:S(2)}) copy-start(f32[64,7168]{1,0:T(8,128)S(1)} %get-tuple-element.27.refs_4_) | copy-start | bytes 5505028
  165.9 20.6 %collective-permute-start.8 = (f32[64,7168]{1,0:T(8,128)S(1)}, f32[64,7168]{1,0:T(8,128)}, u32[]{:S(2)}, u32[]{:S(2)}) collective-permute-start(f32[64,7168]{1,0:T(8,128)S(1)} %get-tuple-element.27.refs_4_), channel_id=1, source_target_pairs={{0,1},{1,0},{2,3},{3,2},{4,5},{5,4},{6,7},{7,6},{8,9},{9,8},{10,11... | collective-permute-start | bytes 5505032 | tf_op jit(solution)/shard_map/ppermute | solution.py:146
  169.5 46.9 %collective-permute-start.5 = (f32[64,7168]{1,0:T(8,128)}, f32[64,7168]{1,0:T(8,128)}, u32[]{:S(2)}, u32[]{:S(2)}) collective-permute-start(f32[64,7168]{1,0:T(8,128)} %get-tuple-element.28), channel_id=1, source_target_pairs={{4,6},{5,7},{2,0},{3,1},{12,14},{13,15},{10,8},{11,9},{20,22},{21,... | collective-permute-start | bytes 5505032 | tf_op jit(solution)/shard_map/ppermute | solution.py:146
  175.3 3.1 %copy-start = (f32[128,7168]{1,0:T(8,128)S(1)}, f32[128,7168]{1,0:T(8,128)}, u32[]{:S(2)}) copy-start(f32[128,7168]{1,0:T(8,128)} %dynamic_update_slice.3.rows_ref) | copy-start | bytes 11010052
  182.7 1.9 copy-start.6
  182.7 2.0 copy-start.7
  188.3 1.9 copy-start.4
  216.4 4.0 %collective-permute-start.10 = (f32[64,7168]{1,0:T(8,128)}, f32[64,7168]{1,0:T(8,128)S(1)}, u32[]{:S(2)}, u32[]{:S(2)}) collective-permute-start(f32[64,7168]{1,0:T(8,128)} %collective-permute-done.5.refs_8_), channel_id=1, source_target_pairs={{0,1},{1,0},{2,3},{3,2},{4,5},{5,4},{6,7},{7,6},{8,9},{9,8},{10,11... | collective-permute-start | bytes 5505032 | tf_op jit(solution)/shard_map/ppermute | solution.py:146
  220.4 2.5 copy-start.5
  220.4 3.3 %copy-start.1 = (f32[128,7168]{1,0:T(8,128)S(1)}, f32[128,7168]{1,0:T(8,128)}, u32[]{:S(2)}) copy-start(f32[128,7168]{1,0:T(8,128)} %dynamic_update_slice.3.rows_ref) | copy-start | bytes 11010052
  225.6 9.0 %collective-permute-start.11 = (f32[192,128]{1,0:T(8,128)S(1)}, f32[192,128]{1,0:T(8,128)S(1)}, u32[]{:S(2)}, u32[]{:S(2)}) collective-permute-start(f32[192,128]{1,0:T(8,128)S(1)} %get-tuple-element.56), channel_id=1, source_target_pairs={{0,8},{8,16},{16,24},{24,0},{32,40},{40,48},{48,56},{56,32},{64,72... | collective-permute-start | bytes 294920 | tf_op jit(solution)/shard_map/ppermute | solution.py:51
  227.5 9.3 %collective-permute-start.12 = (f32[192,128]{1,0:T(8,128)S(1)}, f32[192,128]{1,0:T(8,128)S(1)}, u32[]{:S(2)}, u32[]{:S(2)}) collective-permute-start(f32[192,128]{1,0:T(8,128)S(1)} %get-tuple-element.57), channel_id=1, source_target_pairs={{0,16},{8,24},{16,0},{24,8},{32,48},{40,56},{48,32},{56,40},{64,80... | collective-permute-start | bytes 294920 | tf_op jit(solution)/shard_map/ppermute | solution.py:51
  233.1 5.0 %collective-permute-start.13 = (f32[192,128]{1,0:T(8,128)S(1)}, f32[192,128]{1,0:T(8,128)S(1)}, u32[]{:S(2)}, u32[]{:S(2)}) collective-permute-start(f32[192,128]{1,0:T(8,128)S(1)} %get-tuple-element.58), channel_id=1, source_target_pairs={{0,24},{8,0},{16,8},{24,16},{32,56},{40,32},{48,40},{56,48},{64,88... | collective-permute-start | bytes 294920 | tf_op jit(solution)/shard_map/ppermute | solution.py:51
  238.1 30.2 %copy-start.8 = (f32[2,256,256]{2,1,0:T(8,128)S(1)}, f32[2,256,256]{2,1,0:T(8,128)}, u32[]{:S(2)}) copy-start(f32[2,256,256]{2,1,0:T(8,128)} %param.5) | copy-start | bytes 1572868
  238.1 7.5 %collective-permute-start.14 = (f32[192,128]{1,0:T(8,128)S(1)}, f32[192,128]{1,0:T(8,128)S(1)}, u32[]{:S(2)}, u32[]{:S(2)}) collective-permute-start(f32[192,128]{1,0:T(8,128)S(1)} %fusion.35), channel_id=1, source_target_pairs={{0,32},{8,40},{16,48},{24,56},{32,64},{40,72},{48,80},{56,88},{64,... | collective-permute-start | bytes 294920 | tf_op jit(solution)/shard_map/ppermute | solution.py:51
  238.5 7.1 %collective-permute-start.15 = (f32[192,128]{1,0:T(8,128)S(1)}, f32[192,128]{1,0:T(8,128)S(1)}, u32[]{:S(2)}, u32[]{:S(2)}) collective-permute-start(f32[192,128]{1,0:T(8,128)S(1)} %fusion.35), channel_id=1, source_target_pairs={{0,64},{8,72},{16,80},{24,88},{32,96},{40,104},{48,112},{56,120},{... | collective-permute-start | bytes 294920 | tf_op jit(solution)/shard_map/ppermute | solution.py:51
  241.0 5.2 %collective-permute-start.16 = (f32[192,128]{1,0:T(8,128)S(1)}, f32[192,128]{1,0:T(8,128)S(1)}, u32[]{:S(2)}, u32[]{:S(2)}) collective-permute-start(f32[192,128]{1,0:T(8,128)S(1)} %fusion.35), channel_id=1, source_target_pairs={{0,96},{8,104},{16,112},{24,120},{32,0},{40,8},{48,16},{56,24},{64... | collective-permute-start | bytes 294920 | tf_op jit(solution)/shard_map/ppermute | solution.py:51
  246.2 8.7 %collective-permute-start.17 = (f32[192,128]{1,0:T(8,128)S(1)}, f32[192,128]{1,0:T(8,128)S(1)}, u32[]{:S(2)}, u32[]{:S(2)}) collective-permute-start(f32[192,128]{1,0:T(8,128)S(1)} %add_add_fusion), channel_id=1, source_target_pairs={{0,128},{8,136},{16,144},{24,152},{32,160},{40,168},{48,176},{56,1... | collective-permute-start | bytes 294920 | tf_op jit(solution)/shard_map/ppermute | solution.py:51
  255.0 6.3 %collective-permute-start.21 = (f32[64,128]{1,0:T(8,128)S(1)}, f32[64,128]{1,0:T(8,128)S(1)}, u32[]{:S(2)}, u32[]{:S(2)}) collective-permute-start(f32[64,128]{1,0:T(8,128)S(1)} %slice.138), channel_id=1, source_target_pairs={{0,1},{1,0},{2,3},{3,2},{4,5},{5,4},{6,7},{7,6},{8,9},{9,8},{10,11... | collective-permute-start | bytes 98312 | tf_op jit(solution)/shard_map/ppermute | solution.py:146
  255.1 12.1 %collective-permute-start.18 = (f32[128,128]{1,0:T(8,128)S(1)}, f32[128,128]{1,0:T(8,128)S(1)}, u32[]{:S(2)}, u32[]{:S(2)}) collective-permute-start(f32[128,128]{1,0:T(8,128)S(1)} %slice.137), channel_id=1, source_target_pairs={{0,24},{8,0},{16,8},{24,16},{32,56},{40,32},{48,40},{56,48},{64,88... | collective-permute-start | bytes 196616 | tf_op jit(solution)/shard_map/ppermute | solution.py:51
  257.6 10.6 %collective-permute-start.19 = (f32[128,128]{1,0:T(8,128)S(1)}, f32[128,128]{1,0:T(8,128)S(1)}, u32[]{:S(2)}, u32[]{:S(2)}) collective-permute-start(f32[128,128]{1,0:T(8,128)S(1)} %slice.137), channel_id=1, source_target_pairs={{0,16},{8,24},{16,0},{24,8},{32,48},{40,56},{48,32},{56,40},{64,80... | collective-permute-start | bytes 196616 | tf_op jit(solution)/shard_map/ppermute | solution.py:51
  258.7 9.5 %collective-permute-start.20 = (f32[128,128]{1,0:T(8,128)S(1)}, f32[128,128]{1,0:T(8,128)S(1)}, u32[]{:S(2)}, u32[]{:S(2)}) collective-permute-start(f32[128,128]{1,0:T(8,128)S(1)} %slice.137), channel_id=1, source_target_pairs={{0,8},{8,16},{16,24},{24,0},{32,40},{40,48},{48,56},{56,32},{64,72... | collective-permute-start | bytes 196616 | tf_op jit(solution)/shard_map/ppermute | solution.py:51
  261.3 8.4 %collective-permute-start.22 = (f32[128,128]{1,0:T(8,128)S(1)}, f32[128,128]{1,0:T(8,128)S(1)}, u32[]{:S(2)}, u32[]{:S(2)}) collective-permute-start(f32[128,128]{1,0:T(8,128)S(1)} %pad_maximum_fusion.17), channel_id=1, source_target_pairs={{0,6},{1,7},{2,0},{3,1},{4,2},{5,3},{6,4},{7,5},{8,14},{9,15},{10,... | collective-permute-start | bytes 196616 | tf_op jit(solution)/shard_map/ppermute | solution.py:146
  267.2 5.5 %collective-permute-start.23 = (f32[128,128]{1,0:T(8,128)S(1)}, f32[128,128]{1,0:T(8,128)S(1)}, u32[]{:S(2)}, u32[]{:S(2)}) collective-permute-start(f32[128,128]{1,0:T(8,128)S(1)} %pad_maximum_fusion.17), channel_id=1, source_target_pairs={{0,4},{1,5},{2,6},{3,7},{4,0},{5,1},{6,2},{7,3},{8,12},{9,13},{10,... | collective-permute-start | bytes 196616 | tf_op jit(solution)/shard_map/ppermute | solution.py:146
  267.2 6.4 %collective-permute-start.24 = (f32[128,128]{1,0:T(8,128)S(1)}, f32[128,128]{1,0:T(8,128)S(1)}, u32[]{:S(2)}, u32[]{:S(2)}) collective-permute-start(f32[128,128]{1,0:T(8,128)S(1)} %pad_maximum_fusion.17), channel_id=1, source_target_pairs={{0,2},{1,3},{2,4},{3,5},{4,6},{5,7},{6,0},{7,1},{8,10},{9,11},{10,... | collective-permute-start | bytes 196616 | tf_op jit(solution)/shard_map/ppermute | solution.py:146

commit v7 on v6

--- a/solution.py
+++ b/solution.py
@@ -156,10 +156,9 @@
         return sum(jnp.minimum(jnp.abs(value[0, 0]), 0.0) for value in values).astype(jnp.int32)
 
     def over_plane(value):
-        value = lax.all_to_all(
+        return lax.all_to_all(
             value, "prow", split_axis=0, concat_axis=0, tiled=True, axis_index_groups=PLANES
         )
-        return value.reshape(16 * count, length)
 
     below = send(mine, UP_ONE)
     above = send(mine, DOWN_ONE)
@@ -171,14 +170,11 @@
     )
     below_two = send(below, UP_TWO)
     above_two = send(above, DOWN_TWO)
-    last = send(jnp.where(chip == 2, below_two, above_two), TO_ENDS)
+    two = jnp.where(chip >= 2, below_two, above_two)
+    last = send(two, TO_ENDS)
     rows = lax.dynamic_update_slice_in_dim(
-        jnp.pad(staying, ((0, 16 * count), (0, 0))),
-        arriving,
-        16 * count + zero_from(below_two, above_two),
-        0,
-    )
-    two = below_two + above_two
+        jnp.pad(staying, ((0, 16), (0, 0), (0, 0))), arriving, 16 + zero_from(two), 0
+    ).reshape(32 * count, length)
 
     pieces = (mine, above, two, below)
     swapped = [mine_other, *(send(piece, SIBLING) for piece in pieces[1:])]

time: 287 us -> 277 us (0.965)
  waiting for transfers between devices: 156 us -> 150 us
  local copies, waits for them, and re-layouts: 24.8 us -> 21.2 us
    all_to_all x2, waiting for transfers between devices: 27.4 us -> 5.85 us  [over_plane(): lax.all_to_all(value, 'prow', split_axis=0, concat_axis=0, tiled=True, ax...]
    ppermute x14, waiting for transfers between devices: 79.6 us -> 97.8 us  [send(): return lax.ppermute(value, 'pcol', pairs)]
    ppermute x10, waiting for transfers between devices: 15 us -> 9.48 us  [send(): return lax.ppermute(value, 'prow', pairs)]
    add x1 -> x0, other arithmetic: 3.74 us -> none  [body(): two = below_two + above_two]
  transfers between devices with their start and end apart: 27 -> 27, of which waited for: 17 -> 17; matrix products, arithmetic and copies ran while one was open for 17% -> 16% of each run, Pallas kernels for 0% -> 0%
where the time goes in v7:
time: 277 us
  waiting for transfers between devices  150 us (54%)
  starting transfers between devices  63 us (23%)
  local copies, waits for them, and re-layouts  21.2 us (8%)
  other arithmetic  15.7 us (6%)
  matrix products  14.1 us (5%)
  Pallas kernels  11.1 us (4%)
    ppermute x14, waiting for transfers between devices, send(): return lax.ppermute(value, 'pcol', pairs)  97.8 us
    ppermute x1, waiting for transfers between devices, body(): arriving = over_plane(lax.ppermute(leaving, 'prow', FAR))  36.6 us
    ppermute x10, starting transfers between devices, send(): return lax.ppermute(value, 'prow', pairs)  22 us
    ppermute x14, starting transfers between devices, send(): return lax.ppermute(value, 'pcol', pairs)  18.9 us
    all_to_all x2, starting transfers between devices, over_plane(): lax.all_to_all(value, 'prow', split_axis=0, concat_axis=0, tiled=True, ax...  15 us
    dot_general x6, matrix products, matmul_nt(): lax.dot_general(left, right, (((1,), (1,)), ((), ())), precision=lax.Prec...  13.1 us
    pallas_call x1, Pallas kernels, update(): pl.pallas_call(update_kernel, out_shape=jax.ShapeDtypeStruct(rows.shape,...  11.1 us
    select_n x5, other arithmetic, ordered(): jnp.where(core == 0, piece, other)  10.4 us
  transfers between devices with their start and end apart: 27, of which 17 were waited for; matrix products, arithmetic and copies ran while one was open for 16% of the time, Pallas kernels for 0%

profile of v7, /device:TPU:2, one launch (start us, length us, event | category | flops | bytes accessed | tf_op | source)
XLA Modules:
  0.0 276.8 jit_solution(4752859820916796920)
XLA Ops:
  0.0 1.3 collective-permute-start.3
  1.3 5.8 %collective-permute-start.1 = (f32[64,7168]{1,0:T(8,128)}, f32[64,7168]{1,0:T(8,128)}, u32[]{:S(2)}, u32[]{:S(2)}) collective-permute-start(f32[64,7168]{1,0:T(8,128)} %bitcast.123), channel_id=1, source_target_pairs={{0,2},{1,3},{2,4},{3,5},{4,6},{5,7},{8,10},{9,11},{10,12},{11,13},... | collective-permute-start | bytes 5505032 | tf_op jit(solution)/shard_map/ppermute | solution.py:146
  7.1 2.9 %dynamic-slice_bitcast_fusion.1 = f32[16,4,7168]{2,1,0:T(4,128)} fusion(f32[4,32,7168]{2,0,1:T(4,128)} %bitcast.126, s32[]{:T(128)S(6)} %select_n.196), kind=kLoop, calls=%fused_computation.17 | loop fusion | bytes 3670020 | tf_op jit(solution)/shard_map/dynamic_slice | solution.py:166
  10.0 7.2 %collective-permute-start = (f32[16,4,7168]{2,1,0:T(4,128)}, f32[16,4,7168]{2,1,0:T(4,128)}, u32[]{:S(2)}, u32[]{:S(2)}) collective-permute-start(f32[16,4,7168]{2,1,0:T(4,128)} %dynamic-slice_bitcast_fusion.1), channel_id=1, source_target_pairs={{0,128},{8,136},{16,144},{24,152},{32,160},{40,168},{48,176},{56,1... | collective-permute-start | bytes 5505032 | tf_op jit(solution)/shard_map/ppermute | solution.py:167
  19.3 2.9 %dynamic-slice_bitcast_fusion = f32[16,4,7168]{2,1,0:T(4,128)} fusion(f32[4,32,7168]{2,0,1:T(4,128)} %bitcast.127, s32[]{:T(128)S(6)} %select_n.197), kind=kLoop, calls=%fused_computation.16 | loop fusion | bytes 3670020 | tf_op jit(solution)/shard_map/dynamic_slice | solution.py:169
  22.1 7.5 %all-to-all-start = ((f32[16,4,7168]{2,1,0:T(4,128)}), f32[16,4,7168]{2,1,0:T(4,128)S(1)}, u32[]{:S(2)}, u32[]{:S(2)}) async-start(f32[16,4,7168]{2,1,0:T(4,128)} %dynamic-slice_bitcast_fusion), calls=%async_computation | async-start | bytes 3670016 | tf_op jit(solution)/shard_map/all_to_all | solution.py:159
  29.6 15.5 %collective-permute-done.3.refs_2_ = f32[64,7168]{1,0:T(8,128)} collective-permute-done((f32[64,7168]{1,0:T(8,128)}, f32[64,7168]{1,0:T(8,128)}, u32[]{:S(2)}, u32[]{:S(2)}) %collective-permute-start.3) | collective-permute-done | bytes 1835040 | tf_op jit(solution)/shard_map/ppermute | solution.py:146
  45.1 1.3 collective-permute-start.4
  46.6 1.9 collective-permute-start.2
  48.5 5.9 %all-to-all-done = f32[16,4,7168]{2,1,0:T(4,128)S(1)} async-done(((f32[16,4,7168]{2,1,0:T(4,128)}), f32[16,4,7168]{2,1,0:T(4,128)S(1)}, u32[]{:S(2)}, u32[]{:S(2)}) %all-to-all-start) | async-done | bytes 1835040 | tf_op jit(solution)/shard_map/all_to_all | solution.py:159
  54.3 2.6 pad.4
  56.9 36.6 %collective-permute-done = f32[16,4,7168]{2,1,0:T(4,128)} collective-permute-done((f32[16,4,7168]{2,1,0:T(4,128)}, f32[16,4,7168]{2,1,0:T(4,128)}, u32[]{:S(2)}, u32[]{:S(2)}) %collective-permute-start) | collective-permute-done | bytes 1835040 | tf_op jit(solution)/shard_map/ppermute | solution.py:167
  93.5 7.5 %all-to-all-start.1 = ((f32[16,4,7168]{2,1,0:T(4,128)}), f32[16,4,7168]{2,1,0:T(4,128)}, u32[]{:S(2)}, u32[]{:S(2)}) async-start(f32[16,4,7168]{2,1,0:T(4,128)} %collective-permute-done), calls=%async_computation.1 | async-start | bytes 3670016 | tf_op jit(solution)/shard_map/all_to_all | solution.py:159
  101.0 3.7 %broadcast_select_fusion.1 = (f32[64,7168]{1,0:T(8,128)}, f32[64,7168]{1,0:T(8,128)}) fusion(f32[64,7168]{1,0:T(8,128)} %collective-permute-done.9.refs_1_, pred[]{:T(512)S(6)} %eq.21, f32[7168,64]{0,1:T(8,128)S(1)} %copy-done.3), kind=kLoop, calls=%fused_computation.22 | loop fusion | flops 917504 | bytes 7340033 | tf_op jit(solution)/shard_map/jit(_where)/select_n | solution.py:150
  104.7 57.4 %collective-permute-done.4 = f32[64,7168]{1,0:T(8,128)} collective-permute-done((f32[64,7168]{1,0:T(8,128)}, f32[64,7168]{1,0:T(8,128)}, u32[]{:S(2)}, u32[]{:S(2)}) %collective-permute-start.4) | collective-permute-done | bytes 1835040 | tf_op jit(solution)/shard_map/ppermute | solution.py:146
  162.1 1.7 broadcast_select_fusion.8.refs_4_
  164.5 1.5 collective-permute-start.5
  166.6 2.9 %constant_dynamic-update-slice_fusion = f32[32,4,7168]{2,1,0:T(4,128)} fusion(f32[32,4,7168]{2,1,0:T(4,128)} %pad.4, f32[16,4,7168]{2,1,0:T(4,128)} %all-to-all-done.1, s32[]{:T(128)S(6)} %select_n.200), kind=kLoop, calls=%fused_computation.120 | loop fusion | bytes 3670020 | tf_op jit(solution)/shard_map/dynamic_update_slice | solution.py:175
  169.5 5.3 %reshape.19.rows_ref = f32[128,7168]{1,0:T(8,128)} reshape(f32[32,4,7168]{2,1,0:T(4,128)} %constant_dynamic-update-slice_fusion) | data formatting | bytes 7340032 | tf_op jit(solution)/shard_map/reshape | solution.py:177
  174.8 2.5 broadcast_select_fusion.5
  177.9 1.9 fusion.8
  179.8 2.4 broadcast_select_fusion.7
  182.2 1.9 fusion.9
  184.2 1.7 fusion
  185.9 1.8 broadcast_select_fusion.3
  187.8 1.9 fusion.7
  189.7 4.1 %fusion.4 = f32[64,128]{1,0:T(8,128)S(1)} fusion(f32[64,7168]{1,0:T(8,128)S(1)} %get-tuple-element.26, f32[64,7168]{1,0:T(8,128)S(1)} %get-tuple-element.25, f32[64,7168]{1,0:T(8,128)S(1)} %get-tuple-element.24, f32[64,7168]{1,0:T(8,128)S(1)} %get-tuple-element.23, f32[64,7168]{1,0:T(8,128)S(1)} %get-tuple-element.22, f32[64,7168]{1,0:T(8,128)S(1)} %get-tuple-element.21, ...), kind=kOutput, calls=%fused_computation.8 | convolution fusion | flops 357826560 | bytes 16547843 | tf_op jit(solution)/shard_map/dot_general | solution.py:40
  193.7 15.9 %collective-permute-done.5.refs_8_ = f32[64,7168]{1,0:T(8,128)} collective-permute-done((f32[64,7168]{1,0:T(8,128)S(1)}, f32[64,7168]{1,0:T(8,128)}, u32[]{:S(2)}, u32[]{:S(2)}) %collective-permute-start.5) | collective-permute-done | bytes 1835040 | tf_op jit(solution)/shard_map/ppermute | solution.py:146
  209.6 4.0 %collective-permute-done.10.refs_9_ = f32[64,7168]{1,0:T(8,128)S(1)} collective-permute-done((f32[64,7168]{1,0:T(8,128)}, f32[64,7168]{1,0:T(8,128)S(1)}, u32[]{:S(2)}, u32[]{:S(2)}) %collective-permute-start.10) | collective-permute-done | bytes 1835040 | tf_op jit(solution)/shard_map/ppermute | solution.py:146
  213.6 2.5 pad_maximum_fusion.3
  216.9 1.7 fusion.56
  218.9 1.6 collective-permute-start.11
  220.5 1.1 collective-permute-start.12
  221.6 2.2 collective-permute-start.13
  223.8 3.8 %collective-permute-done.12 = f32[192,128]{1,0:T(8,128)S(1)} collective-permute-done((f32[192,128]{1,0:T(8,128)S(1)}, f32[192,128]{1,0:T(8,128)S(1)}, u32[]{:S(2)}, u32[]{:S(2)}) %collective-permute-start.12) | collective-permute-done | bytes 98336 | tf_op jit(solution)/shard_map/ppermute | solution.py:51
  228.0 1.7 collective-permute-start.14
  229.6 2.9 %collective-permute-start.15 = (f32[192,128]{1,0:T(8,128)S(1)}, f32[192,128]{1,0:T(8,128)S(1)}, u32[]{:S(2)}, u32[]{:S(2)}) collective-permute-start(f32[192,128]{1,0:T(8,128)S(1)} %fusion.35), channel_id=1, source_target_pairs={{0,64},{8,72},{16,80},{24,88},{32,96},{40,104},{48,112},{56,120},{... | collective-permute-start | bytes 294920 | tf_op jit(solution)/shard_map/ppermute | solution.py:51
  232.5 1.3 collective-permute-start.16
  233.9 1.1 collective-permute-done.14
  234.9 1.2 collective-permute-done.15
  237.2 6.6 %collective-permute-start.17 = (f32[192,128]{1,0:T(8,128)S(1)}, f32[192,128]{1,0:T(8,128)S(1)}, u32[]{:S(2)}, u32[]{:S(2)}) collective-permute-start(f32[192,128]{1,0:T(8,128)S(1)} %add_add_fusion), channel_id=1, source_target_pairs={{0,128},{8,136},{16,144},{24,152},{32,160},{40,168},{48,176},{56,1... | collective-permute-start | bytes 294920 | tf_op jit(solution)/shard_map/ppermute | solution.py:51
  244.4 2.0 collective-permute-done.17
  246.6 1.7 collective-permute-start.18
  248.3 1.1 collective-permute-start.19
  249.4 1.8 collective-permute-start.20
  251.2 6.1 %collective-permute-start.22 = (f32[128,128]{1,0:T(8,128)S(1)}, f32[128,128]{1,0:T(8,128)S(1)}, u32[]{:S(2)}, u32[]{:S(2)}) collective-permute-start(f32[128,128]{1,0:T(8,128)S(1)} %pad_maximum_fusion.17), channel_id=1, source_target_pairs={{0,6},{1,7},{2,0},{3,1},{4,2},{5,3},{6,4},{7,5},{8,14},{9,15},{10,... | collective-permute-start | bytes 196616 | tf_op jit(solution)/shard_map/ppermute | solution.py:146
  259.8 3.0 %collective-permute-done.23 = f32[128,128]{1,0:T(8,128)S(1)} collective-permute-done((f32[128,128]{1,0:T(8,128)S(1)}, f32[128,128]{1,0:T(8,128)S(1)}, u32[]{:S(2)}, u32[]{:S(2)}) %collective-permute-start.23) | collective-permute-done | bytes 65568 | tf_op jit(solution)/shard_map/ppermute | solution.py:146
  265.7 11.1 %shard_map.37 = f32[128,7168]{1,0:T(8,128)} custom-call(s32[5]{0:T(128)} %stack.89.where_ref, f32[128,7168]{1,0:T(8,128)} %reshape.19.rows_ref, bf16[256,512]{1,0:T(8,128)(2,1)} %pad_maximum_fusion.12.scaled_ref, f32[64,7168]{1,0:T(8,128)} %bitcast.125, f32[64,7168]{1,0:T(8,128)} %collective-permute-done.9.refs_1_, ...), custom_call_target="tpu_custom_call" | custom-call | flops 2818572288 | bytes 22020096 | tf_op jit(solution)/shard_map/pallas_call | solution.py:114
  (94 shorter events, 11.5 us)
Async XLA Ops:
  0.0 45.1 %collective-permute-start.3 = (f32[64,7168]{1,0:T(8,128)}, f32[64,7168]{1,0:T(8,128)}, u32[]{:S(2)}, u32[]{:S(2)}) collective-permute-start(f32[64,7168]{1,0:T(8,128)} %bitcast.122), channel_id=1, source_target_pairs={{2,0},{3,1},{4,2},{5,3},{6,4},{7,5},{10,8},{11,9},{12,10},{13,11},... | collective-permute-start | bytes 5505032 | tf_op jit(solution)/shard_map/ppermute | solution.py:146
  1.3 45.3 %collective-permute-start.1 = (f32[64,7168]{1,0:T(8,128)}, f32[64,7168]{1,0:T(8,128)}, u32[]{:S(2)}, u32[]{:S(2)}) collective-permute-start(f32[64,7168]{1,0:T(8,128)} %bitcast.123), channel_id=1, source_target_pairs={{0,2},{1,3},{2,4},{3,5},{4,6},{5,7},{8,10},{9,11},{10,12},{11,13},... | collective-permute-start | bytes 5505032 | tf_op jit(solution)/shard_map/ppermute | solution.py:146
  7.1 93.9 %collective-permute-start.9 = (f32[64,7168]{1,0:T(8,128)}, f32[64,7168]{1,0:T(8,128)}, u32[]{:S(2)}, u32[]{:S(2)}) collective-permute-start(f32[64,7168]{1,0:T(8,128)} %bitcast.124), channel_id=1, source_target_pairs={{0,1},{1,0},{2,3},{3,2},{4,5},{5,4},{6,7},{7,6},{8,9},{9,8},{10,11... | collective-permute-start | bytes 5505032 | tf_op jit(solution)/shard_map/ppermute | solution.py:146
  10.0 83.5 %collective-permute-start = (f32[16,4,7168]{2,1,0:T(4,128)}, f32[16,4,7168]{2,1,0:T(4,128)}, u32[]{:S(2)}, u32[]{:S(2)}) collective-permute-start(f32[16,4,7168]{2,1,0:T(4,128)} %dynamic-slice_bitcast_fusion.1), channel_id=1, source_target_pairs={{0,128},{8,136},{16,144},{24,152},{32,160},{40,168},{48,176},{56,1... | collective-permute-start | bytes 5505032 | tf_op jit(solution)/shard_map/ppermute | solution.py:167
  22.1 32.2 %all-to-all-start = ((f32[16,4,7168]{2,1,0:T(4,128)}), f32[16,4,7168]{2,1,0:T(4,128)S(1)}, u32[]{:S(2)}, u32[]{:S(2)}) async-start(f32[16,4,7168]{2,1,0:T(4,128)} %dynamic-slice_bitcast_fusion), calls=%async_computation | async-start | bytes 3670016 | tf_op jit(solution)/shard_map/all_to_all | solution.py:159
  45.1 117.0 %collective-permute-start.4 = (f32[64,7168]{1,0:T(8,128)}, f32[64,7168]{1,0:T(8,128)}, u32[]{:S(2)}, u32[]{:S(2)}) collective-permute-start(f32[64,7168]{1,0:T(8,128)} %collective-permute-done.3.refs_2_), channel_id=1, source_target_pairs={{2,0},{3,1},{4,2},{5,3},{10,8},{11,9},{12,10},{13,11},{18,16},{19,... | collective-permute-start | bytes 5505032 | tf_op jit(solution)/shard_map/ppermute | solution.py:146
  46.6 115.5 %collective-permute-start.2 = (f32[64,7168]{1,0:T(8,128)}, f32[64,7168]{1,0:T(8,128)}, u32[]{:S(2)}, u32[]{:S(2)}) collective-permute-start(f32[64,7168]{1,0:T(8,128)} %collective-permute-done.1.refs_6_), channel_id=1, source_target_pairs={{2,4},{3,5},{4,6},{5,7},{10,12},{11,13},{12,14},{13,15},{18,20},{1... | collective-permute-start | bytes 5505032 | tf_op jit(solution)/shard_map/ppermute | solution.py:146
  56.9 44.1 %copy-start.3 = (f32[7168,64]{0,1:T(8,128)S(1)}, f32[7168,64]{0,1:T(8,128)}, u32[]{:S(2)}) copy-start(f32[7168,64]{0,1:T(8,128)} %param.4) | copy-start | bytes 5505028
  56.9 117.9 %collective-permute-start.7 = (f32[64,7168]{1,0:T(8,128)}, f32[64,7168]{1,0:T(8,128)}, u32[]{:S(2)}, u32[]{:S(2)}) collective-permute-start(f32[64,7168]{1,0:T(8,128)} %collective-permute-done.1.refs_6_), channel_id=1, source_target_pairs={{0,1},{1,0},{2,3},{3,2},{4,5},{5,4},{6,7},{7,6},{8,9},{9,8},{10,11... | collective-permute-start | bytes 5505032 | tf_op jit(solution)/shard_map/ppermute | solution.py:146
  93.5 86.3 %collective-permute-start.6 = (f32[64,7168]{1,0:T(8,128)}, f32[64,7168]{1,0:T(8,128)}, u32[]{:S(2)}, u32[]{:S(2)}) collective-permute-start(f32[64,7168]{1,0:T(8,128)} %collective-permute-done.3.refs_2_), channel_id=1, source_target_pairs={{0,1},{1,0},{2,3},{3,2},{4,5},{5,4},{6,7},{7,6},{8,9},{9,8},{10,11... | collective-permute-start | bytes 5505032 | tf_op jit(solution)/shard_map/ppermute | solution.py:146
  93.5 73.1 %all-to-all-start.1 = ((f32[16,4,7168]{2,1,0:T(4,128)}), f32[16,4,7168]{2,1,0:T(4,128)}, u32[]{:S(2)}, u32[]{:S(2)}) async-start(f32[16,4,7168]{2,1,0:T(4,128)} %collective-permute-done), calls=%async_computation.1 | async-start | bytes 3670016 | tf_op jit(solution)/shard_map/all_to_all | solution.py:159
  163.8 25.8 %copy-start.2 = (f32[64,7168]{1,0:T(8,128)}, f32[64,7168]{1,0:T(8,128)S(1)}, u32[]{:S(2)}) copy-start(f32[64,7168]{1,0:T(8,128)S(1)} %broadcast_select_fusion.8.refs_4_) | copy-start | bytes 5505028
  164.5 21.4 %collective-permute-start.8 = (f32[64,7168]{1,0:T(8,128)S(1)}, f32[64,7168]{1,0:T(8,128)}, u32[]{:S(2)}, u32[]{:S(2)}) collective-permute-start(f32[64,7168]{1,0:T(8,128)S(1)} %broadcast_select_fusion.8.refs_4_), channel_id=1, source_target_pairs={{0,1},{1,0},{2,3},{3,2},{4,5},{5,4},{6,7},{7,6},{8,9},{9,8},{10,11... | collective-permute-start | bytes 5505032 | tf_op jit(solution)/shard_map/ppermute | solution.py:146
  164.5 45.2 %collective-permute-start.5 = (f32[64,7168]{1,0:T(8,128)S(1)}, f32[64,7168]{1,0:T(8,128)}, u32[]{:S(2)}, u32[]{:S(2)}) collective-permute-start(f32[64,7168]{1,0:T(8,128)S(1)} %broadcast_select_fusion.8.refs_4_), channel_id=1, source_target_pairs={{4,6},{5,7},{2,0},{3,1},{12,14},{13,15},{10,8},{11,9},{20,22},{21,... | collective-permute-start | bytes 5505032 | tf_op jit(solution)/shard_map/ppermute | solution.py:146
  174.8 3.1 %copy-start = (f32[128,7168]{1,0:T(8,128)S(1)}, f32[128,7168]{1,0:T(8,128)}, u32[]{:S(2)}) copy-start(f32[128,7168]{1,0:T(8,128)} %reshape.19.rows_ref) | copy-start | bytes 11010052
  182.1 1.9 copy-start.6
  182.2 2.0 copy-start.7
  187.7 1.9 copy-start.4
  209.6 4.0 %collective-permute-start.10 = (f32[64,7168]{1,0:T(8,128)}, f32[64,7168]{1,0:T(8,128)S(1)}, u32[]{:S(2)}, u32[]{:S(2)}) collective-permute-start(f32[64,7168]{1,0:T(8,128)} %collective-permute-done.5.refs_8_), channel_id=1, source_target_pairs={{0,1},{1,0},{2,3},{3,2},{4,5},{5,4},{6,7},{7,6},{8,9},{9,8},{10,11... | collective-permute-start | bytes 5505032 | tf_op jit(solution)/shard_map/ppermute | solution.py:146
  213.6 2.5 copy-start.5
  213.6 3.3 %copy-start.1 = (f32[128,7168]{1,0:T(8,128)S(1)}, f32[128,7168]{1,0:T(8,128)}, u32[]{:S(2)}) copy-start(f32[128,7168]{1,0:T(8,128)} %reshape.19.rows_ref) | copy-start | bytes 11010052
  218.9 4.9 %collective-permute-start.11 = (f32[192,128]{1,0:T(8,128)S(1)}, f32[192,128]{1,0:T(8,128)S(1)}, u32[]{:S(2)}, u32[]{:S(2)}) collective-permute-start(f32[192,128]{1,0:T(8,128)S(1)} %get-tuple-element.54), channel_id=1, source_target_pairs={{0,8},{8,16},{16,24},{24,0},{32,40},{40,48},{48,56},{56,32},{64,72... | collective-permute-start | bytes 294920 | tf_op jit(solution)/shard_map/ppermute | solution.py:51
  220.5 7.2 %collective-permute-start.12 = (f32[192,128]{1,0:T(8,128)S(1)}, f32[192,128]{1,0:T(8,128)S(1)}, u32[]{:S(2)}, u32[]{:S(2)}) collective-permute-start(f32[192,128]{1,0:T(8,128)S(1)} %get-tuple-element.55), channel_id=1, source_target_pairs={{0,16},{8,24},{16,0},{24,8},{32,48},{40,56},{48,32},{56,40},{64,80... | collective-permute-start | bytes 294920 | tf_op jit(solution)/shard_map/ppermute | solution.py:51
  221.6 6.4 %collective-permute-start.13 = (f32[192,128]{1,0:T(8,128)S(1)}, f32[192,128]{1,0:T(8,128)S(1)}, u32[]{:S(2)}, u32[]{:S(2)}) collective-permute-start(f32[192,128]{1,0:T(8,128)S(1)} %get-tuple-element.56), channel_id=1, source_target_pairs={{0,24},{8,0},{16,8},{24,16},{32,56},{40,32},{48,40},{56,48},{64,88... | collective-permute-start | bytes 294920 | tf_op jit(solution)/shard_map/ppermute | solution.py:51
  228.0 30.5 %copy-start.8 = (f32[2,256,256]{2,1,0:T(8,128)S(1)}, f32[2,256,256]{2,1,0:T(8,128)}, u32[]{:S(2)}) copy-start(f32[2,256,256]{2,1,0:T(8,128)} %param.5) | copy-start | bytes 1572868
  228.0 7.0 %collective-permute-start.14 = (f32[192,128]{1,0:T(8,128)S(1)}, f32[192,128]{1,0:T(8,128)S(1)}, u32[]{:S(2)}, u32[]{:S(2)}) collective-permute-start(f32[192,128]{1,0:T(8,128)S(1)} %fusion.35), channel_id=1, source_target_pairs={{0,32},{8,40},{16,48},{24,56},{32,64},{40,72},{48,80},{56,88},{64,... | collective-permute-start | bytes 294920 | tf_op jit(solution)/shard_map/ppermute | solution.py:51
  229.6 6.5 %collective-permute-start.15 = (f32[192,128]{1,0:T(8,128)S(1)}, f32[192,128]{1,0:T(8,128)S(1)}, u32[]{:S(2)}, u32[]{:S(2)}) collective-permute-start(f32[192,128]{1,0:T(8,128)S(1)} %fusion.35), channel_id=1, source_target_pairs={{0,64},{8,72},{16,80},{24,88},{32,96},{40,104},{48,112},{56,120},{... | collective-permute-start | bytes 294920 | tf_op jit(solution)/shard_map/ppermute | solution.py:51
  232.5 4.6 %collective-permute-start.16 = (f32[192,128]{1,0:T(8,128)S(1)}, f32[192,128]{1,0:T(8,128)S(1)}, u32[]{:S(2)}, u32[]{:S(2)}) collective-permute-start(f32[192,128]{1,0:T(8,128)S(1)} %fusion.35), channel_id=1, source_target_pairs={{0,96},{8,104},{16,112},{24,120},{32,0},{40,8},{48,16},{56,24},{64... | collective-permute-start | bytes 294920 | tf_op jit(solution)/shard_map/ppermute | solution.py:51
  237.2 9.2 %collective-permute-start.17 = (f32[192,128]{1,0:T(8,128)S(1)}, f32[192,128]{1,0:T(8,128)S(1)}, u32[]{:S(2)}, u32[]{:S(2)}) collective-permute-start(f32[192,128]{1,0:T(8,128)S(1)} %add_add_fusion), channel_id=1, source_target_pairs={{0,128},{8,136},{16,144},{24,152},{32,160},{40,168},{48,176},{56,1... | collective-permute-start | bytes 294920 | tf_op jit(solution)/shard_map/ppermute | solution.py:51
  246.5 4.7 %collective-permute-start.21 = (f32[64,128]{1,0:T(8,128)S(1)}, f32[64,128]{1,0:T(8,128)S(1)}, u32[]{:S(2)}, u32[]{:S(2)}) collective-permute-start(f32[64,128]{1,0:T(8,128)S(1)} %slice.133), channel_id=1, source_target_pairs={{0,1},{1,0},{2,3},{3,2},{4,5},{5,4},{6,7},{7,6},{8,9},{9,8},{10,11... | collective-permute-start | bytes 98312 | tf_op jit(solution)/shard_map/ppermute | solution.py:146
  246.6 10.7 %collective-permute-start.18 = (f32[128,128]{1,0:T(8,128)S(1)}, f32[128,128]{1,0:T(8,128)S(1)}, u32[]{:S(2)}, u32[]{:S(2)}) collective-permute-start(f32[128,128]{1,0:T(8,128)S(1)} %slice.132), channel_id=1, source_target_pairs={{0,24},{8,0},{16,8},{24,16},{32,56},{40,32},{48,40},{56,48},{64,88... | collective-permute-start | bytes 196616 | tf_op jit(solution)/shard_map/ppermute | solution.py:51
  248.3 10.0 %collective-permute-start.19 = (f32[128,128]{1,0:T(8,128)S(1)}, f32[128,128]{1,0:T(8,128)S(1)}, u32[]{:S(2)}, u32[]{:S(2)}) collective-permute-start(f32[128,128]{1,0:T(8,128)S(1)} %slice.132), channel_id=1, source_target_pairs={{0,16},{8,24},{16,0},{24,8},{32,48},{40,56},{48,32},{56,40},{64,80... | collective-permute-start | bytes 196616 | tf_op jit(solution)/shard_map/ppermute | solution.py:51
  249.4 8.9 %collective-permute-start.20 = (f32[128,128]{1,0:T(8,128)S(1)}, f32[128,128]{1,0:T(8,128)S(1)}, u32[]{:S(2)}, u32[]{:S(2)}) collective-permute-start(f32[128,128]{1,0:T(8,128)S(1)} %slice.132), channel_id=1, source_target_pairs={{0,8},{8,16},{16,24},{24,0},{32,40},{40,48},{48,56},{56,32},{64,72... | collective-permute-start | bytes 196616 | tf_op jit(solution)/shard_map/ppermute | solution.py:51
  251.2 8.6 %collective-permute-start.22 = (f32[128,128]{1,0:T(8,128)S(1)}, f32[128,128]{1,0:T(8,128)S(1)}, u32[]{:S(2)}, u32[]{:S(2)}) collective-permute-start(f32[128,128]{1,0:T(8,128)S(1)} %pad_maximum_fusion.17), channel_id=1, source_target_pairs={{0,6},{1,7},{2,0},{3,1},{4,2},{5,3},{6,4},{7,5},{8,14},{9,15},{10,... | collective-permute-start | bytes 196616 | tf_op jit(solution)/shard_map/ppermute | solution.py:146
  257.3 5.5 %collective-permute-start.23 = (f32[128,128]{1,0:T(8,128)S(1)}, f32[128,128]{1,0:T(8,128)S(1)}, u32[]{:S(2)}, u32[]{:S(2)}) collective-permute-start(f32[128,128]{1,0:T(8,128)S(1)} %pad_maximum_fusion.17), channel_id=1, source_target_pairs={{0,4},{1,5},{2,6},{3,7},{4,0},{5,1},{6,2},{7,3},{8,12},{9,13},{10,... | collective-permute-start | bytes 196616 | tf_op jit(solution)/shard_map/ppermute | solution.py:146
  257.3 6.4 %collective-permute-start.24 = (f32[128,128]{1,0:T(8,128)S(1)}, f32[128,128]{1,0:T(8,128)S(1)}, u32[]{:S(2)}, u32[]{:S(2)}) collective-permute-start(f32[128,128]{1,0:T(8,128)S(1)} %pad_maximum_fusion.17), channel_id=1, source_target_pairs={{0,2},{1,3},{2,4},{3,5},{4,6},{5,7},{6,0},{7,1},{8,10},{9,11},{10,... | collective-permute-start | bytes 196616 | tf_op jit(solution)/shard_map/ppermute | solution.py:146

commit v8 on v7

--- a/solution.py
+++ b/solution.py
@@ -43,26 +43,41 @@
     )
 
 
-def sum_over_prow(quarters, block):
+def over_prow(value, pairs):
+    return lax.ppermute(value, "prow", pairs)
+
+
+def sum_over_plane(quarters, block=None):
     x = lax.axis_index("prow") % 4
-    count = quarters.shape[1]
-
-    def send(value, pairs):
-        return lax.ppermute(value, "prow", pairs)
 
     def packed(step):
         part = lax.dynamic_index_in_dim(quarters, (x + step) % 4, 0, keepdims=False)
-        return jnp.concatenate([part, block], axis=0)
+        return part if block is None else jnp.concatenate([part, block], axis=0)
 
     total = packed(0)
     for step in (1, 2, 3):
-        total = total + send(packed(step), along_x(step))
-    total = total + send(total, along_y(1)) + send(total, along_y(2)) + send(total, along_y(3))
-    far = send(total, FAR)
-    mid = count // 2
-    total = total + jnp.concatenate([far[mid:count], far[:mid], far[count:]], axis=0)
-    part = total[:count]
-    return jnp.stack([part, *(send(part, along_x(4 - step)) for step in (1, 2, 3))]), total[count:]
+        total = total + over_prow(packed(step), along_x(step))
+    return total + sum(
+        (over_prow(total, along_y(step)) for step in (2, 3)), over_prow(total, along_y(1))
+    )
+
+
+def in_quarters(*slots):
+    return jnp.concatenate(
+        [slot.reshape(2, 4, 16, 128).transpose(1, 0, 2, 3).reshape(4, 32, 128) for slot in slots],
+        axis=1,
+    )
+
+
+def finish_sum(parts):
+    x = lax.axis_index("prow") % 4
+    far = over_prow(parts, FAR)
+    swapped = far[:128].reshape(4, 2, 16, 128)[:, ::-1].reshape(128, 128)
+    parts = parts + jnp.concatenate([swapped, far[128:]], axis=0)
+    own = parts[:128]
+    ring = jnp.stack([own, *(over_prow(own, along_x(4 - step)) for step in (1, 2, 3))])
+    slots = turned(ring, 4 - x).reshape(4, 4, 2, 16, 128).transpose(1, 2, 0, 3, 4)
+    return slots.reshape(4, 128, 128), parts[128:]
 
 
 def turned(parts, start):
@@ -187,23 +202,26 @@
     cross = matmul_nt(left, right)
     on_mine, on_two = matmul_nt(rows, all_mine), matmul_nt(rows, all_two)
     on_above, on_below = matmul_nt(rows, all_above), matmul_nt(rows, all_below)
-    last, cross, on_mine, on_two, on_above, on_below = lax.optimization_barrier(
-        (last, cross, on_mine, on_two, on_above, on_below)
-    )
+    on_mine, on_two, on_above, on_below = lax.optimization_barrier(
+        (on_mine, on_two, on_above, on_below)
+    )
+    early = sum_over_plane(in_quarters(on_mine, on_two), cross)
+    last = lax.dynamic_update_slice(last, last[:8, :128], (zero_from(early), 0))
     last_other = send(last, SIBLING)
     both = lax.optimization_barrier(jnp.concatenate([last, last_other], axis=0))
-    on_last = matmul_nt(rows, both)
+    on_last = lax.optimization_barrier(matmul_nt(rows, both))
     on_last = jnp.where(core == 0, on_last, jnp.roll(on_last, 64, axis=1))
     zero = jnp.zeros_like(on_last)
-    slots = jnp.stack(
-        [
-            on_mine,
+    late = sum_over_plane(
+        in_quarters(
             on_above + jnp.where(chip == 3, on_last, zero),
-            on_two,
             on_below + jnp.where(chip == 0, on_last, zero),
-        ]
-    )
-    projected, cross = sum_over_prow(slots, cross)
+        )
+    )
+    (above_sum, below_sum, mine_sum, two_sum), cross = finish_sum(
+        jnp.concatenate([late, early], axis=0)
+    )
+    projected = jnp.stack([mine_sum, above_sum, two_sum, below_sum])
     cross = ordered(cross, send(cross, SIBLING), 0)
     cross = turned(
         jnp.stack(
@@ -219,7 +237,7 @@
         ],
         axis=0,
     )
-    projected = turned(projected, 8 - chip - x)
+    projected = turned(projected, 4 - chip)
     first = jnp.concatenate([projected[0], projected[1]], axis=1)
     second = jnp.concatenate([projected[2], projected[3]], axis=1)
     scaled_second = matmul(second, upper_part(tfactors[1]).T)

time: 277 us -> 285 us (1.029)
  starting transfers between devices: 63 us -> 71 us
  waiting for transfers between devices: 150 us -> 144 us
  local copies, waits for them, and re-layouts: 21.2 us -> 25.7 us
    ppermute x14, waiting for transfers between devices: 97.8 us -> 87.4 us  [send(): return lax.ppermute(value, 'pcol', pairs)]
    ppermute x10 -> x16, starting transfers between devices: 22 us -> 27.8 us  [over_prow(): return lax.ppermute(value, 'prow', pairs)]
    ppermute x10 -> x16, waiting for transfers between devices: 9.48 us -> 14 us  [over_prow(): return lax.ppermute(value, 'prow', pairs)]
  transfers between devices with their start and end apart: 27 -> 33, of which waited for: 17 -> 17; matrix products, arithmetic and copies ran while one was open for 16% -> 15% of each run, Pallas kernels for 0% -> 0%
where the time goes in v8:
time: 285 us; the launch traced here: 284 us
  waiting for transfers between devices  144 us (51%)
  starting transfers between devices  71 us (25%)
  local copies, waits for them, and re-layouts  25.7 us (9%)
  other arithmetic  15.7 us (6%)
  matrix products  14.1 us (5%)
  Pallas kernels  11.1 us (4%)
    ppermute x14, waiting for transfers between devices, send(): return lax.ppermute(value, 'pcol', pairs)  87.4 us
    ppermute x1, waiting for transfers between devices, body(): arriving = over_plane(lax.ppermute(leaving, 'prow', FAR))  37 us
    ppermute x16, starting transfers between devices, over_prow(): return lax.ppermute(value, 'prow', pairs)  27.8 us
    ppermute x14, starting transfers between devices, send(): return lax.ppermute(value, 'pcol', pairs)  21 us
    all_to_all x2, starting transfers between devices, over_plane(): lax.all_to_all(value, 'prow', split_axis=0, concat_axis=0, tiled=True, ax...  15 us
    ppermute x16, waiting for transfers between devices, over_prow(): return lax.ppermute(value, 'prow', pairs)  14 us
    dot_general x6, matrix products, matmul_nt(): lax.dot_general(left, right, (((1,), (1,)), ((), ())), precision=lax.Prec...  13 us
    pallas_call x1, Pallas kernels, update(): pl.pallas_call(update_kernel, out_shape=jax.ShapeDtypeStruct(rows.shape,...  11.1 us
  transfers between devices with their start and end apart: 33, of which 17 were waited for; matrix products, arithmetic and copies ran while one was open for 15% of the time, Pallas kernels for 0%

profile of v8, /device:TPU:2, one launch (start us, length us, event | category | flops | bytes accessed | tf_op | source)
XLA Modules:
  0.0 284.2 jit_solution(11565893564879309285)
XLA Ops:
  0.0 1.3 collective-permute-start.3
  1.3 5.8 %collective-permute-start.1 = (f32[64,7168]{1,0:T(8,128)}, f32[64,7168]{1,0:T(8,128)}, u32[]{:S(2)}, u32[]{:S(2)}) collective-permute-start(f32[64,7168]{1,0:T(8,128)} %bitcast.158), channel_id=1, source_target_pairs={{0,2},{1,3},{2,4},{3,5},{4,6},{5,7},{8,10},{9,11},{10,12},{11,13},... | collective-permute-start | bytes 5505032 | tf_op jit(solution)/shard_map/ppermute | solution.py:161
  7.1 2.8 %dynamic-slice_bitcast_fusion.1 = f32[16,4,7168]{2,1,0:T(4,128)} fusion(f32[4,32,7168]{2,0,1:T(4,128)} %bitcast.160, s32[]{:T(128)S(6)} %select_n.216), kind=kLoop, calls=%fused_computation.17 | loop fusion | bytes 3670020 | tf_op jit(solution)/shard_map/dynamic_slice | solution.py:181
  9.9 7.2 %collective-permute-start = (f32[16,4,7168]{2,1,0:T(4,128)}, f32[16,4,7168]{2,1,0:T(4,128)}, u32[]{:S(2)}, u32[]{:S(2)}) collective-permute-start(f32[16,4,7168]{2,1,0:T(4,128)} %dynamic-slice_bitcast_fusion.1), channel_id=1, source_target_pairs={{0,128},{8,136},{16,144},{24,152},{32,160},{40,168},{48,176},{56,1... | collective-permute-start | bytes 5505032 | tf_op jit(solution)/shard_map/ppermute | solution.py:182
  19.3 2.9 %dynamic-slice_bitcast_fusion = f32[16,4,7168]{2,1,0:T(4,128)} fusion(f32[4,32,7168]{2,0,1:T(4,128)} %bitcast.161, s32[]{:T(128)S(6)} %select_n.217), kind=kLoop, calls=%fused_computation.16 | loop fusion | bytes 3670020 | tf_op jit(solution)/shard_map/dynamic_slice | solution.py:184
  22.1 7.5 %all-to-all-start = ((f32[16,4,7168]{2,1,0:T(4,128)}), f32[16,4,7168]{2,1,0:T(4,128)S(1)}, u32[]{:S(2)}, u32[]{:S(2)}) async-start(f32[16,4,7168]{2,1,0:T(4,128)} %dynamic-slice_bitcast_fusion), calls=%async_computation | async-start | bytes 3670016 | tf_op jit(solution)/shard_map/all_to_all | solution.py:174
  29.6 15.5 %collective-permute-done.3.refs_2_ = f32[64,7168]{1,0:T(8,128)} collective-permute-done((f32[64,7168]{1,0:T(8,128)}, f32[64,7168]{1,0:T(8,128)}, u32[]{:S(2)}, u32[]{:S(2)}) %collective-permute-start.3) | collective-permute-done | bytes 1835040 | tf_op jit(solution)/shard_map/ppermute | solution.py:161
  45.1 1.3 collective-permute-start.4
  46.5 1.9 collective-permute-start.2
  48.4 5.4 %all-to-all-done = f32[16,4,7168]{2,1,0:T(4,128)S(1)} async-done(((f32[16,4,7168]{2,1,0:T(4,128)}), f32[16,4,7168]{2,1,0:T(4,128)S(1)}, u32[]{:S(2)}, u32[]{:S(2)}) %all-to-all-start) | async-done | bytes 1835040 | tf_op jit(solution)/shard_map/all_to_all | solution.py:174
  53.7 2.6 pad.4
  56.3 37.0 %collective-permute-done = f32[16,4,7168]{2,1,0:T(4,128)} collective-permute-done((f32[16,4,7168]{2,1,0:T(4,128)}, f32[16,4,7168]{2,1,0:T(4,128)}, u32[]{:S(2)}, u32[]{:S(2)}) %collective-permute-start) | collective-permute-done | bytes 1835040 | tf_op jit(solution)/shard_map/ppermute | solution.py:182
  93.4 7.5 %all-to-all-start.1 = ((f32[16,4,7168]{2,1,0:T(4,128)}), f32[16,4,7168]{2,1,0:T(4,128)}, u32[]{:S(2)}, u32[]{:S(2)}) async-start(f32[16,4,7168]{2,1,0:T(4,128)} %collective-permute-done), calls=%async_computation.1 | async-start | bytes 3670016 | tf_op jit(solution)/shard_map/all_to_all | solution.py:174
  100.9 3.6 %broadcast_select_fusion.7 = (f32[64,7168]{1,0:T(8,128)}, f32[64,7168]{1,0:T(8,128)}) fusion(f32[64,7168]{1,0:T(8,128)} %collective-permute-done.5.refs_1_, pred[]{:T(512)S(6)} %eq.47, f32[7168,64]{0,1:T(8,128)S(1)} %copy-done.3), kind=kLoop, calls=%fused_computation.30 | loop fusion | flops 917504 | bytes 7340033 | tf_op jit(solution)/shard_map/jit(_where)/select_n | solution.py:165
  104.5 58.3 %collective-permute-done.4 = f32[64,7168]{1,0:T(8,128)} collective-permute-done((f32[64,7168]{1,0:T(8,128)}, f32[64,7168]{1,0:T(8,128)}, u32[]{:S(2)}, u32[]{:S(2)}) %collective-permute-start.4) | collective-permute-done | bytes 1835040 | tf_op jit(solution)/shard_map/ppermute | solution.py:161
  162.8 1.7 broadcast_select_fusion.8.refs_4_
  167.3 2.9 %constant_dynamic-update-slice_fusion.32 = f32[32,4,7168]{2,1,0:T(4,128)} fusion(f32[32,4,7168]{2,1,0:T(4,128)} %pad.4, f32[16,4,7168]{2,1,0:T(4,128)} %all-to-all-done.1, s32[]{:T(128)S(6)} %select_n.220), kind=kLoop, calls=%fused_computation.161 | loop fusion | bytes 3670020 | tf_op jit(solution)/shard_map/dynamic_update_slice | solution.py:190
  170.2 5.2 %reshape.61.rows_ref = f32[128,7168]{1,0:T(8,128)} reshape(f32[32,4,7168]{2,1,0:T(4,128)} %constant_dynamic-update-slice_fusion.32) | data formatting | bytes 7340032 | tf_op jit(solution)/shard_map/reshape | solution.py:192
  175.4 2.5 broadcast_select_fusion.1
  178.6 1.9 fusion.7
  180.5 2.4 broadcast_select_fusion.3
  182.8 1.9 fusion.8
  184.9 1.7 fusion
  186.6 1.8 broadcast_select_fusion.5
  188.4 1.9 fusion.9
  190.4 4.1 %fusion.4 = f32[64,128]{1,0:T(8,128)S(1)} fusion(f32[64,7168]{1,0:T(8,128)S(1)} %get-tuple-element.22, f32[64,7168]{1,0:T(8,128)S(1)} %get-tuple-element.21, f32[64,7168]{1,0:T(8,128)S(1)} %get-tuple-element.20, f32[64,7168]{1,0:T(8,128)S(1)} %get-tuple-element.19, f32[64,7168]{1,0:T(8,128)S(1)} %get-tuple-element.18, f32[64,7168]{1,0:T(8,128)S(1)} %get-tuple-element.17, ...), kind=kOutput, calls=%fused_computation.8 | convolution fusion | flops 357826560 | bytes 16547843 | tf_op jit(solution)/shard_map/dot_general | solution.py:40
  194.5 1.6 collective-permute-start.10
  196.1 2.7 collective-permute-start.11
  199.4 3.1 %collective-permute-done.11 = f32[128,128]{1,0:T(8,128)S(1)} collective-permute-done((f32[128,128]{1,0:T(8,128)S(1)}, f32[128,128]{1,0:T(8,128)S(1)}, u32[]{:S(2)}, u32[]{:S(2)}) %collective-permute-start.11) | collective-permute-done | bytes 65568 | tf_op jit(solution)/shard_map/ppermute | solution.py:47
  203.3 2.3 collective-permute-start.15
  207.2 5.2 %collective-permute-done.9 = f32[64,7168]{1,0:T(8,128)} collective-permute-done((f32[64,7168]{1,0:T(8,128)S(1)}, f32[64,7168]{1,0:T(8,128)}, u32[]{:S(2)}, u32[]{:S(2)}) %collective-permute-start.9) | collective-permute-done | bytes 1835040 | tf_op jit(solution)/shard_map/ppermute | solution.py:161
  214.3 2.6 dynamic_update_slice.7.refs_8_
  216.9 4.0 %collective-permute-done.16.refs_9_ = f32[64,7168]{1,0:T(8,128)S(1)} collective-permute-done((f32[64,7168]{1,0:T(8,128)}, f32[64,7168]{1,0:T(8,128)S(1)}, u32[]{:S(2)}, u32[]{:S(2)}) %collective-permute-start.16) | collective-permute-done | bytes 1835040 | tf_op jit(solution)/shard_map/ppermute | solution.py:161
  220.9 2.6 pad_maximum_fusion.3
  224.1 1.7 fusion.67
  226.1 1.6 collective-permute-start.17
  228.4 2.5 collective-permute-start.19
  230.9 2.1 collective-permute-done.18
  233.1 3.1 %collective-permute-start.22 = (f32[64,128]{1,0:T(8,128)S(1)}, f32[64,128]{1,0:T(8,128)S(1)}, u32[]{:S(2)}, u32[]{:S(2)}) collective-permute-start(f32[64,128]{1,0:T(8,128)S(1)} %fusion.42), channel_id=1, source_target_pairs={{0,96},{8,104},{16,112},{24,120},{32,0},{40,8},{48,16},{56,24},{64... | collective-permute-start | bytes 98312 | tf_op jit(solution)/shard_map/ppermute | solution.py:47
  237.8 3.8 %collective-permute-done.21 = f32[64,128]{1,0:T(8,128)S(1)} collective-permute-done((f32[64,128]{1,0:T(8,128)S(1)}, f32[64,128]{1,0:T(8,128)S(1)}, u32[]{:S(2)}, u32[]{:S(2)}) %collective-permute-start.21) | collective-permute-done | bytes 32800 | tf_op jit(solution)/shard_map/ppermute | solution.py:47
  242.0 4.2 %collective-permute-start.23 = (f32[192,128]{1,0:T(8,128)S(1)}, f32[192,128]{1,0:T(8,128)S(1)}, u32[]{:S(2)}, u32[]{:S(2)}) collective-permute-start(f32[192,128]{1,0:T(8,128)S(1)} %pad_maximum_fusion.16), channel_id=1, source_target_pairs={{0,128},{8,136},{16,144},{24,152},{32,160},{40,168},{48,176},{56,1... | collective-permute-start | bytes 294920 | tf_op jit(solution)/shard_map/ppermute | solution.py:47
  246.9 3.7 %collective-permute-done.23 = f32[192,128]{1,0:T(8,128)S(1)} collective-permute-done((f32[192,128]{1,0:T(8,128)S(1)}, f32[192,128]{1,0:T(8,128)S(1)}, u32[]{:S(2)}, u32[]{:S(2)}) %collective-permute-start.23) | collective-permute-done | bytes 98336 | tf_op jit(solution)/shard_map/ppermute | solution.py:47
  250.7 3.3 %collective-permute-start.25 = (f32[128,128]{1,0:T(8,128)S(1)}, f32[128,128]{1,0:T(8,128)S(1)}, u32[]{:S(2)}, u32[]{:S(2)}) collective-permute-start(f32[128,128]{1,0:T(8,128)S(1)} %slice.141), channel_id=1, source_target_pairs={{0,16},{8,24},{16,0},{24,8},{32,48},{40,56},{48,32},{56,40},{64,80... | collective-permute-start | bytes 196616 | tf_op jit(solution)/shard_map/ppermute | solution.py:47
  254.0 2.0 collective-permute-start.26
  257.3 7.1 %collective-permute-start.29 = (f32[128,128]{1,0:T(8,128)S(1)}, f32[128,128]{1,0:T(8,128)S(1)}, u32[]{:S(2)}, u32[]{:S(2)}) collective-permute-start(f32[128,128]{1,0:T(8,128)S(1)} %pad_maximum_fusion.17), channel_id=1, source_target_pairs={{0,4},{1,5},{2,6},{3,7},{4,0},{5,1},{6,2},{7,3},{8,12},{9,13},{10,... | collective-permute-start | bytes 196616 | tf_op jit(solution)/shard_map/ppermute | solution.py:161
  265.0 1.5 collective-permute-start.30
  269.1 2.0 collective-permute-done.30
  273.1 11.1 %shard_map.37 = f32[128,7168]{1,0:T(8,128)} custom-call(s32[5]{0:T(128)} %stack.75.where_ref, f32[128,7168]{1,0:T(8,128)} %reshape.61.rows_ref, bf16[256,512]{1,0:T(8,128)(2,1)} %pad_maximum_fusion.11.scaled_ref, f32[64,7168]{1,0:T(8,128)} %bitcast.159, f32[64,7168]{1,0:T(8,128)} %collective-permute-done.5.refs_1_, ...), custom_call_target="tpu_custom_call" | custom-call | flops 2818572288 | bytes 22020096 | tf_op jit(solution)/shard_map/pallas_call | solution.py:129
  (132 shorter events, 19.4 us)
Async XLA Ops:
  0.0 100.9 %collective-permute-start.5 = (f32[64,7168]{1,0:T(8,128)}, f32[64,7168]{1,0:T(8,128)}, u32[]{:S(2)}, u32[]{:S(2)}) collective-permute-start(f32[64,7168]{1,0:T(8,128)} %bitcast.156), channel_id=1, source_target_pairs={{0,1},{1,0},{2,3},{3,2},{4,5},{5,4},{6,7},{7,6},{8,9},{9,8},{10,11... | collective-permute-start | bytes 5505032 | tf_op jit(solution)/shard_map/ppermute | solution.py:161
  0.0 45.1 %collective-permute-start.3 = (f32[64,7168]{1,0:T(8,128)}, f32[64,7168]{1,0:T(8,128)}, u32[]{:S(2)}, u32[]{:S(2)}) collective-permute-start(f32[64,7168]{1,0:T(8,128)} %bitcast.157), channel_id=1, source_target_pairs={{2,0},{3,1},{4,2},{5,3},{6,4},{7,5},{10,8},{11,9},{12,10},{13,11},... | collective-permute-start | bytes 5505032 | tf_op jit(solution)/shard_map/ppermute | solution.py:161
  1.3 45.2 %collective-permute-start.1 = (f32[64,7168]{1,0:T(8,128)}, f32[64,7168]{1,0:T(8,128)}, u32[]{:S(2)}, u32[]{:S(2)}) collective-permute-start(f32[64,7168]{1,0:T(8,128)} %bitcast.158), channel_id=1, source_target_pairs={{0,2},{1,3},{2,4},{3,5},{4,6},{5,7},{8,10},{9,11},{10,12},{11,13},... | collective-permute-start | bytes 5505032 | tf_op jit(solution)/shard_map/ppermute | solution.py:161
  9.9 83.4 %collective-permute-start = (f32[16,4,7168]{2,1,0:T(4,128)}, f32[16,4,7168]{2,1,0:T(4,128)}, u32[]{:S(2)}, u32[]{:S(2)}) collective-permute-start(f32[16,4,7168]{2,1,0:T(4,128)} %dynamic-slice_bitcast_fusion.1), channel_id=1, source_target_pairs={{0,128},{8,136},{16,144},{24,152},{32,160},{40,168},{48,176},{56,1... | collective-permute-start | bytes 5505032 | tf_op jit(solution)/shard_map/ppermute | solution.py:182
  22.1 31.6 %all-to-all-start = ((f32[16,4,7168]{2,1,0:T(4,128)}), f32[16,4,7168]{2,1,0:T(4,128)S(1)}, u32[]{:S(2)}, u32[]{:S(2)}) async-start(f32[16,4,7168]{2,1,0:T(4,128)} %dynamic-slice_bitcast_fusion), calls=%async_computation | async-start | bytes 3670016 | tf_op jit(solution)/shard_map/all_to_all | solution.py:174
  45.1 117.7 %collective-permute-start.4 = (f32[64,7168]{1,0:T(8,128)}, f32[64,7168]{1,0:T(8,128)}, u32[]{:S(2)}, u32[]{:S(2)}) collective-permute-start(f32[64,7168]{1,0:T(8,128)} %collective-permute-done.3.refs_2_), channel_id=1, source_target_pairs={{2,0},{3,1},{4,2},{5,3},{10,8},{11,9},{12,10},{13,11},{18,16},{19,... | collective-permute-start | bytes 5505032 | tf_op jit(solution)/shard_map/ppermute | solution.py:161
  46.5 116.3 %collective-permute-start.2 = (f32[64,7168]{1,0:T(8,128)}, f32[64,7168]{1,0:T(8,128)}, u32[]{:S(2)}, u32[]{:S(2)}) collective-permute-start(f32[64,7168]{1,0:T(8,128)} %collective-permute-done.1.refs_6_), channel_id=1, source_target_pairs={{2,4},{3,5},{4,6},{5,7},{10,12},{11,13},{12,14},{13,15},{18,20},{1... | collective-permute-start | bytes 5505032 | tf_op jit(solution)/shard_map/ppermute | solution.py:161
  56.3 44.5 %copy-start.3 = (f32[7168,64]{0,1:T(8,128)S(1)}, f32[7168,64]{0,1:T(8,128)}, u32[]{:S(2)}) copy-start(f32[7168,64]{0,1:T(8,128)} %param.4) | copy-start | bytes 5505028
  56.3 124.1 %collective-permute-start.7 = (f32[64,7168]{1,0:T(8,128)}, f32[64,7168]{1,0:T(8,128)}, u32[]{:S(2)}, u32[]{:S(2)}) collective-permute-start(f32[64,7168]{1,0:T(8,128)} %collective-permute-done.3.refs_2_), channel_id=1, source_target_pairs={{0,1},{1,0},{2,3},{3,2},{4,5},{5,4},{6,7},{7,6},{8,9},{9,8},{10,11... | collective-permute-start | bytes 5505032 | tf_op jit(solution)/shard_map/ppermute | solution.py:161
  93.4 82.1 %collective-permute-start.8 = (f32[64,7168]{1,0:T(8,128)}, f32[64,7168]{1,0:T(8,128)}, u32[]{:S(2)}, u32[]{:S(2)}) collective-permute-start(f32[64,7168]{1,0:T(8,128)} %collective-permute-done.1.refs_6_), channel_id=1, source_target_pairs={{0,1},{1,0},{2,3},{3,2},{4,5},{5,4},{6,7},{7,6},{8,9},{9,8},{10,11... | collective-permute-start | bytes 5505032 | tf_op jit(solution)/shard_map/ppermute | solution.py:161
  93.4 73.9 %all-to-all-start.1 = ((f32[16,4,7168]{2,1,0:T(4,128)}), f32[16,4,7168]{2,1,0:T(4,128)}, u32[]{:S(2)}, u32[]{:S(2)}) async-start(f32[16,4,7168]{2,1,0:T(4,128)} %collective-permute-done), calls=%async_computation.1 | async-start | bytes 3670016 | tf_op jit(solution)/shard_map/all_to_all | solution.py:174
  164.5 25.9 %copy-start.2 = (f32[64,7168]{1,0:T(8,128)}, f32[64,7168]{1,0:T(8,128)S(1)}, u32[]{:S(2)}) copy-start(f32[64,7168]{1,0:T(8,128)S(1)} %broadcast_select_fusion.8.refs_4_) | copy-start | bytes 5505028
  165.1 47.3 %collective-permute-start.9 = (f32[64,7168]{1,0:T(8,128)S(1)}, f32[64,7168]{1,0:T(8,128)}, u32[]{:S(2)}, u32[]{:S(2)}) collective-permute-start(f32[64,7168]{1,0:T(8,128)S(1)} %broadcast_select_fusion.8.refs_4_), channel_id=1, source_target_pairs={{4,6},{5,7},{2,0},{3,1},{12,14},{13,15},{10,8},{11,9},{20,22},{21,... | collective-permute-start | bytes 5505032 | tf_op jit(solution)/shard_map/ppermute | solution.py:161
  166.4 20.2 %collective-permute-start.6 = (f32[64,7168]{1,0:T(8,128)S(1)}, f32[64,7168]{1,0:T(8,128)}, u32[]{:S(2)}, u32[]{:S(2)}) collective-permute-start(f32[64,7168]{1,0:T(8,128)S(1)} %broadcast_select_fusion.8.refs_4_), channel_id=1, source_target_pairs={{0,1},{1,0},{2,3},{3,2},{4,5},{5,4},{6,7},{7,6},{8,9},{9,8},{10,11... | collective-permute-start | bytes 5505032 | tf_op jit(solution)/shard_map/ppermute | solution.py:161
  175.4 3.1 %copy-start = (f32[128,7168]{1,0:T(8,128)S(1)}, f32[128,7168]{1,0:T(8,128)}, u32[]{:S(2)}) copy-start(f32[128,7168]{1,0:T(8,128)} %reshape.61.rows_ref) | copy-start | bytes 11010052
  182.8 1.9 copy-start.6
  182.8 2.0 copy-start.7
  188.4 1.9 copy-start.4
  194.5 4.9 %collective-permute-start.10 = (f32[128,128]{1,0:T(8,128)S(1)}, f32[128,128]{1,0:T(8,128)S(1)}, u32[]{:S(2)}, u32[]{:S(2)}) collective-permute-start(f32[128,128]{1,0:T(8,128)S(1)} %get-tuple-element.54), channel_id=1, source_target_pairs={{0,8},{8,16},{16,24},{24,0},{32,40},{40,48},{48,56},{56,32},{64,72... | collective-permute-start | bytes 196616 | tf_op jit(solution)/shard_map/ppermute | solution.py:47
  196.1 6.4 %collective-permute-start.11 = (f32[128,128]{1,0:T(8,128)S(1)}, f32[128,128]{1,0:T(8,128)S(1)}, u32[]{:S(2)}, u32[]{:S(2)}) collective-permute-start(f32[128,128]{1,0:T(8,128)S(1)} %get-tuple-element.55), channel_id=1, source_target_pairs={{0,16},{8,24},{16,0},{24,8},{32,48},{40,56},{48,32},{56,40},{64,80... | collective-permute-start | bytes 196616 | tf_op jit(solution)/shard_map/ppermute | solution.py:47
  198.7 4.6 %collective-permute-start.12 = (f32[128,128]{1,0:T(8,128)S(1)}, f32[128,128]{1,0:T(8,128)S(1)}, u32[]{:S(2)}, u32[]{:S(2)}) collective-permute-start(f32[128,128]{1,0:T(8,128)S(1)} %get-tuple-element.56), channel_id=1, source_target_pairs={{0,24},{8,0},{16,8},{24,16},{32,56},{40,32},{48,40},{56,48},{64,88... | collective-permute-start | bytes 196616 | tf_op jit(solution)/shard_map/ppermute | solution.py:47
  203.3 9.8 %collective-permute-start.15 = (f32[128,128]{1,0:T(8,128)S(1)}, f32[128,128]{1,0:T(8,128)S(1)}, u32[]{:S(2)}, u32[]{:S(2)}) collective-permute-start(f32[128,128]{1,0:T(8,128)S(1)} %fusion.35), channel_id=1, source_target_pairs={{0,96},{8,104},{16,112},{24,120},{32,0},{40,8},{48,16},{56,24},{64... | collective-permute-start | bytes 196616 | tf_op jit(solution)/shard_map/ppermute | solution.py:47
  205.6 7.5 %collective-permute-start.14 = (f32[128,128]{1,0:T(8,128)S(1)}, f32[128,128]{1,0:T(8,128)S(1)}, u32[]{:S(2)}, u32[]{:S(2)}) collective-permute-start(f32[128,128]{1,0:T(8,128)S(1)} %fusion.35), channel_id=1, source_target_pairs={{0,64},{8,72},{16,80},{24,88},{32,96},{40,104},{48,112},{56,120},{... | collective-permute-start | bytes 196616 | tf_op jit(solution)/shard_map/ppermute | solution.py:47
  206.3 6.9 %collective-permute-start.13 = (f32[128,128]{1,0:T(8,128)S(1)}, f32[128,128]{1,0:T(8,128)S(1)}, u32[]{:S(2)}, u32[]{:S(2)}) collective-permute-start(f32[128,128]{1,0:T(8,128)S(1)} %fusion.35), channel_id=1, source_target_pairs={{0,32},{8,40},{16,48},{24,56},{32,64},{40,72},{48,80},{56,88},{64,... | collective-permute-start | bytes 196616 | tf_op jit(solution)/shard_map/ppermute | solution.py:47
  216.9 4.0 %collective-permute-start.16 = (f32[64,7168]{1,0:T(8,128)}, f32[64,7168]{1,0:T(8,128)S(1)}, u32[]{:S(2)}, u32[]{:S(2)}) collective-permute-start(f32[64,7168]{1,0:T(8,128)} %dynamic_update_slice.7.refs_8_), channel_id=1, source_target_pairs={{0,1},{1,0},{2,3},{3,2},{4,5},{5,4},{6,7},{7,6},{8,9},{9,8},{10,11... | collective-permute-start | bytes 5505032 | tf_op jit(solution)/shard_map/ppermute | solution.py:161
  220.9 2.6 copy-start.5
  220.9 3.3 %copy-start.1 = (f32[128,7168]{1,0:T(8,128)S(1)}, f32[128,7168]{1,0:T(8,128)}, u32[]{:S(2)}) copy-start(f32[128,7168]{1,0:T(8,128)} %reshape.61.rows_ref) | copy-start | bytes 11010052
  226.1 4.8 %collective-permute-start.17 = (f32[64,128]{1,0:T(8,128)S(1)}, f32[64,128]{1,0:T(8,128)S(1)}, u32[]{:S(2)}, u32[]{:S(2)}) collective-permute-start(f32[64,128]{1,0:T(8,128)S(1)} %get-tuple-element.45), channel_id=1, source_target_pairs={{0,8},{8,16},{16,24},{24,0},{32,40},{40,48},{48,56},{56,32},{64,72... | collective-permute-start | bytes 98312 | tf_op jit(solution)/shard_map/ppermute | solution.py:47
  227.7 5.4 %collective-permute-start.18 = (f32[64,128]{1,0:T(8,128)S(1)}, f32[64,128]{1,0:T(8,128)S(1)}, u32[]{:S(2)}, u32[]{:S(2)}) collective-permute-start(f32[64,128]{1,0:T(8,128)S(1)} %get-tuple-element.46), channel_id=1, source_target_pairs={{0,16},{8,24},{16,0},{24,8},{32,48},{40,56},{48,32},{56,40},{64,80... | collective-permute-start | bytes 98312 | tf_op jit(solution)/shard_map/ppermute | solution.py:47
  228.4 4.7 %collective-permute-start.19 = (f32[64,128]{1,0:T(8,128)S(1)}, f32[64,128]{1,0:T(8,128)S(1)}, u32[]{:S(2)}, u32[]{:S(2)}) collective-permute-start(f32[64,128]{1,0:T(8,128)S(1)} %get-tuple-element.47), channel_id=1, source_target_pairs={{0,24},{8,0},{16,8},{24,16},{32,56},{40,32},{48,40},{56,48},{64,88... | collective-permute-start | bytes 98312 | tf_op jit(solution)/shard_map/ppermute | solution.py:47
  233.1 4.7 %collective-permute-start.22 = (f32[64,128]{1,0:T(8,128)S(1)}, f32[64,128]{1,0:T(8,128)S(1)}, u32[]{:S(2)}, u32[]{:S(2)}) collective-permute-start(f32[64,128]{1,0:T(8,128)S(1)} %fusion.42), channel_id=1, source_target_pairs={{0,96},{8,104},{16,112},{24,120},{32,0},{40,8},{48,16},{56,24},{64... | collective-permute-start | bytes 98312 | tf_op jit(solution)/shard_map/ppermute | solution.py:47
  236.2 5.4 %collective-permute-start.21 = (f32[64,128]{1,0:T(8,128)S(1)}, f32[64,128]{1,0:T(8,128)S(1)}, u32[]{:S(2)}, u32[]{:S(2)}) collective-permute-start(f32[64,128]{1,0:T(8,128)S(1)} %fusion.42), channel_id=1, source_target_pairs={{0,64},{8,72},{16,80},{24,88},{32,96},{40,104},{48,112},{56,120},{... | collective-permute-start | bytes 98312 | tf_op jit(solution)/shard_map/ppermute | solution.py:47
  236.8 5.1 %collective-permute-start.20 = (f32[64,128]{1,0:T(8,128)S(1)}, f32[64,128]{1,0:T(8,128)S(1)}, u32[]{:S(2)}, u32[]{:S(2)}) collective-permute-start(f32[64,128]{1,0:T(8,128)S(1)} %fusion.42), channel_id=1, source_target_pairs={{0,32},{8,40},{16,48},{24,56},{32,64},{40,72},{48,80},{56,88},{64,... | collective-permute-start | bytes 98312 | tf_op jit(solution)/shard_map/ppermute | solution.py:47
  242.0 8.6 %collective-permute-start.23 = (f32[192,128]{1,0:T(8,128)S(1)}, f32[192,128]{1,0:T(8,128)S(1)}, u32[]{:S(2)}, u32[]{:S(2)}) collective-permute-start(f32[192,128]{1,0:T(8,128)S(1)} %pad_maximum_fusion.16), channel_id=1, source_target_pairs={{0,128},{8,136},{16,144},{24,152},{32,160},{40,168},{48,176},{56,1... | collective-permute-start | bytes 294920 | tf_op jit(solution)/shard_map/ppermute | solution.py:47
  250.7 15.8 %collective-permute-start.25 = (f32[128,128]{1,0:T(8,128)S(1)}, f32[128,128]{1,0:T(8,128)S(1)}, u32[]{:S(2)}, u32[]{:S(2)}) collective-permute-start(f32[128,128]{1,0:T(8,128)S(1)} %slice.141), channel_id=1, source_target_pairs={{0,16},{8,24},{16,0},{24,8},{32,48},{40,56},{48,32},{56,40},{64,80... | collective-permute-start | bytes 196616 | tf_op jit(solution)/shard_map/ppermute | solution.py:47
  254.0 11.0 %collective-permute-start.24 = (f32[128,128]{1,0:T(8,128)S(1)}, f32[128,128]{1,0:T(8,128)S(1)}, u32[]{:S(2)}, u32[]{:S(2)}) collective-permute-start(f32[128,128]{1,0:T(8,128)S(1)} %slice.141), channel_id=1, source_target_pairs={{0,24},{8,0},{16,8},{24,16},{32,56},{40,32},{48,40},{56,48},{64,88... | collective-permute-start | bytes 196616 | tf_op jit(solution)/shard_map/ppermute | solution.py:47
  254.0 12.5 %collective-permute-start.26 = (f32[128,128]{1,0:T(8,128)S(1)}, f32[128,128]{1,0:T(8,128)S(1)}, u32[]{:S(2)}, u32[]{:S(2)}) collective-permute-start(f32[128,128]{1,0:T(8,128)S(1)} %slice.141), channel_id=1, source_target_pairs={{0,8},{8,16},{16,24},{24,0},{32,40},{40,48},{48,56},{56,32},{64,72... | collective-permute-start | bytes 196616 | tf_op jit(solution)/shard_map/ppermute | solution.py:47
  256.0 1.2 collective-permute-start.27
  257.3 11.8 %collective-permute-start.29 = (f32[128,128]{1,0:T(8,128)S(1)}, f32[128,128]{1,0:T(8,128)S(1)}, u32[]{:S(2)}, u32[]{:S(2)}) collective-permute-start(f32[128,128]{1,0:T(8,128)S(1)} %pad_maximum_fusion.17), channel_id=1, source_target_pairs={{0,4},{1,5},{2,6},{3,7},{4,0},{5,1},{6,2},{7,3},{8,12},{9,13},{10,... | collective-permute-start | bytes 196616 | tf_op jit(solution)/shard_map/ppermute | solution.py:161
  264.4 4.7 %collective-permute-start.28 = (f32[128,128]{1,0:T(8,128)S(1)}, f32[128,128]{1,0:T(8,128)S(1)}, u32[]{:S(2)}, u32[]{:S(2)}) collective-permute-start(f32[128,128]{1,0:T(8,128)S(1)} %pad_maximum_fusion.17), channel_id=1, source_target_pairs={{0,6},{1,7},{2,0},{3,1},{4,2},{5,3},{6,4},{7,5},{8,14},{9,15},{10,... | collective-permute-start | bytes 196616 | tf_op jit(solution)/shard_map/ppermute | solution.py:161
  265.0 6.1 %collective-permute-start.30 = (f32[128,128]{1,0:T(8,128)S(1)}, f32[128,128]{1,0:T(8,128)S(1)}, u32[]{:S(2)}, u32[]{:S(2)}) collective-permute-start(f32[128,128]{1,0:T(8,128)S(1)} %pad_maximum_fusion.17), channel_id=1, source_target_pairs={{0,2},{1,3},{2,4},{3,5},{4,6},{5,7},{6,0},{7,1},{8,10},{9,11},{10,... | collective-permute-start | bytes 196616 | tf_op jit(solution)/shard_map/ppermute | solution.py:161
  266.5 1.0 copy-start.8

commit v9 on v7

--- a/solution.py
+++ b/solution.py
@@ -185,6 +185,7 @@
     left = jnp.where(chip == 0, two, jnp.where(chip == 3, mine, above))
     right = jnp.where(chip == 0, all_above, jnp.where(chip == 1, all_below, all_two))
     cross = matmul_nt(left, right)
+    cross = ordered(cross, send(cross, SIBLING), 0)
     on_mine, on_two = matmul_nt(rows, all_mine), matmul_nt(rows, all_two)
     on_above, on_below = matmul_nt(rows, all_above), matmul_nt(rows, all_below)
     last, cross, on_mine, on_two, on_above, on_below = lax.optimization_barrier(
@@ -204,7 +205,6 @@
         ]
     )
     projected, cross = sum_over_prow(slots, cross)
-    cross = ordered(cross, send(cross, SIBLING), 0)
     cross = turned(
         jnp.stack(
             [cross]

time: 277 us -> 281 us (1.014)
  waiting for transfers between devices: 150 us -> 154 us
    ppermute x10, waiting for transfers between devices: 9.48 us -> 13.9 us  [send(): return lax.ppermute(value, 'prow', pairs)]
  transfers between devices with their start and end apart: 27 -> 27, of which waited for: 17 -> 16; matrix products, arithmetic and copies ran while one was open for 16% -> 15% of each run, Pallas kernels for 0% -> 0%
where the time goes in v9:
time: 281 us; the launch traced here: 280 us
  waiting for transfers between devices  154 us (55%)
  starting transfers between devices  62.1 us (22%)
  local copies, waits for them, and re-layouts  21.1 us (8%)
  other arithmetic  15.8 us (6%)
  matrix products  14.2 us (5%)
  Pallas kernels  11.1 us (4%)
    ppermute x14, waiting for transfers between devices, send(): return lax.ppermute(value, 'pcol', pairs)  97.8 us
    ppermute x1, waiting for transfers between devices, body(): arriving = over_plane(lax.ppermute(leaving, 'prow', FAR))  36.6 us
    ppermute x10, starting transfers between devices, send(): return lax.ppermute(value, 'prow', pairs)  22 us
    ppermute x14, starting transfers between devices, send(): return lax.ppermute(value, 'pcol', pairs)  17.9 us
    all_to_all x2, starting transfers between devices, over_plane(): lax.all_to_all(value, 'prow', split_axis=0, concat_axis=0, tiled=True, ax...  15 us
    ppermute x10, waiting for transfers between devices, send(): return lax.ppermute(value, 'prow', pairs)  13.9 us
    dot_general x6, matrix products, matmul_nt(): lax.dot_general(left, right, (((1,), (1,)), ((), ())), precision=lax.Prec...  13.1 us
    pallas_call x1, Pallas kernels, update(): pl.pallas_call(update_kernel, out_shape=jax.ShapeDtypeStruct(rows.shape,...  11.1 us
  transfers between devices with their start and end apart: 27, of which 16 were waited for; matrix products, arithmetic and copies ran while one was open for 15% of the time, Pallas kernels for 0%

profile of v9, /device:TPU:2, one launch (start us, length us, event | category | flops | bytes accessed | tf_op | source)
XLA Modules:
  0.0 280.1 jit_solution(11512242403871321112)
XLA Ops:
  0.0 1.3 collective-permute-start.3
  1.3 5.8 %collective-permute-start.1 = (f32[64,7168]{1,0:T(8,128)}, f32[64,7168]{1,0:T(8,128)}, u32[]{:S(2)}, u32[]{:S(2)}) collective-permute-start(f32[64,7168]{1,0:T(8,128)} %bitcast.123), channel_id=1, source_target_pairs={{0,2},{1,3},{2,4},{3,5},{4,6},{5,7},{8,10},{9,11},{10,12},{11,13},... | collective-permute-start | bytes 5505032 | tf_op jit(solution)/shard_map/ppermute | solution.py:146
  7.1 2.9 %dynamic-slice_bitcast_fusion.1 = f32[16,4,7168]{2,1,0:T(4,128)} fusion(f32[4,32,7168]{2,0,1:T(4,128)} %bitcast.126, s32[]{:T(128)S(6)} %select_n.196), kind=kLoop, calls=%fused_computation.17 | loop fusion | bytes 3670020 | tf_op jit(solution)/shard_map/dynamic_slice | solution.py:166
  10.0 7.2 %collective-permute-start = (f32[16,4,7168]{2,1,0:T(4,128)}, f32[16,4,7168]{2,1,0:T(4,128)}, u32[]{:S(2)}, u32[]{:S(2)}) collective-permute-start(f32[16,4,7168]{2,1,0:T(4,128)} %dynamic-slice_bitcast_fusion.1), channel_id=1, source_target_pairs={{0,128},{8,136},{16,144},{24,152},{32,160},{40,168},{48,176},{56,1... | collective-permute-start | bytes 5505032 | tf_op jit(solution)/shard_map/ppermute | solution.py:167
  19.3 2.9 %dynamic-slice_bitcast_fusion = f32[16,4,7168]{2,1,0:T(4,128)} fusion(f32[4,32,7168]{2,0,1:T(4,128)} %bitcast.127, s32[]{:T(128)S(6)} %select_n.197), kind=kLoop, calls=%fused_computation.16 | loop fusion | bytes 3670020 | tf_op jit(solution)/shard_map/dynamic_slice | solution.py:169
  22.1 7.5 %all-to-all-start = ((f32[16,4,7168]{2,1,0:T(4,128)}), f32[16,4,7168]{2,1,0:T(4,128)S(1)}, u32[]{:S(2)}, u32[]{:S(2)}) async-start(f32[16,4,7168]{2,1,0:T(4,128)} %dynamic-slice_bitcast_fusion), calls=%async_computation | async-start | bytes 3670016 | tf_op jit(solution)/shard_map/all_to_all | solution.py:159
  29.6 15.5 %collective-permute-done.3.refs_2_ = f32[64,7168]{1,0:T(8,128)} collective-permute-done((f32[64,7168]{1,0:T(8,128)}, f32[64,7168]{1,0:T(8,128)}, u32[]{:S(2)}, u32[]{:S(2)}) %collective-permute-start.3) | collective-permute-done | bytes 1835040 | tf_op jit(solution)/shard_map/ppermute | solution.py:146
  45.1 1.3 collective-permute-start.4
  46.6 1.9 collective-permute-start.2
  48.5 5.9 %all-to-all-done = f32[16,4,7168]{2,1,0:T(4,128)S(1)} async-done(((f32[16,4,7168]{2,1,0:T(4,128)}), f32[16,4,7168]{2,1,0:T(4,128)S(1)}, u32[]{:S(2)}, u32[]{:S(2)}) %all-to-all-start) | async-done | bytes 1835040 | tf_op jit(solution)/shard_map/all_to_all | solution.py:159
  54.3 2.6 pad.4
  56.9 36.6 %collective-permute-done = f32[16,4,7168]{2,1,0:T(4,128)} collective-permute-done((f32[16,4,7168]{2,1,0:T(4,128)}, f32[16,4,7168]{2,1,0:T(4,128)}, u32[]{:S(2)}, u32[]{:S(2)}) %collective-permute-start) | collective-permute-done | bytes 1835040 | tf_op jit(solution)/shard_map/ppermute | solution.py:167
  93.5 7.5 %all-to-all-start.1 = ((f32[16,4,7168]{2,1,0:T(4,128)}), f32[16,4,7168]{2,1,0:T(4,128)}, u32[]{:S(2)}, u32[]{:S(2)}) async-start(f32[16,4,7168]{2,1,0:T(4,128)} %collective-permute-done), calls=%async_computation.1 | async-start | bytes 3670016 | tf_op jit(solution)/shard_map/all_to_all | solution.py:159
  101.0 3.7 %broadcast_select_fusion.1 = (f32[64,7168]{1,0:T(8,128)}, f32[64,7168]{1,0:T(8,128)}) fusion(f32[64,7168]{1,0:T(8,128)} %collective-permute-done.10.refs_1_, pred[]{:T(512)S(6)} %eq.21, f32[7168,64]{0,1:T(8,128)S(1)} %copy-done.3), kind=kLoop, calls=%fused_computation.22 | loop fusion | flops 917504 | bytes 7340033 | tf_op jit(solution)/shard_map/jit(_where)/select_n | solution.py:150
  104.7 57.4 %collective-permute-done.4 = f32[64,7168]{1,0:T(8,128)} collective-permute-done((f32[64,7168]{1,0:T(8,128)}, f32[64,7168]{1,0:T(8,128)}, u32[]{:S(2)}, u32[]{:S(2)}) %collective-permute-start.4) | collective-permute-done | bytes 1835040 | tf_op jit(solution)/shard_map/ppermute | solution.py:146
  162.1 1.7 broadcast_select_fusion.8.refs_4_
  164.3 1.5 collective-permute-start.5
  166.4 2.9 %constant_dynamic-update-slice_fusion = f32[32,4,7168]{2,1,0:T(4,128)} fusion(f32[32,4,7168]{2,1,0:T(4,128)} %pad.4, f32[16,4,7168]{2,1,0:T(4,128)} %all-to-all-done.1, s32[]{:T(128)S(6)} %select_n.200), kind=kLoop, calls=%fused_computation.120 | loop fusion | bytes 3670020 | tf_op jit(solution)/shard_map/dynamic_update_slice | solution.py:175
  169.2 5.3 %reshape.19.rows_ref = f32[128,7168]{1,0:T(8,128)} reshape(f32[32,4,7168]{2,1,0:T(4,128)} %constant_dynamic-update-slice_fusion) | data formatting | bytes 7340032 | tf_op jit(solution)/shard_map/reshape | solution.py:177
  174.5 2.5 broadcast_select_fusion.5
  177.6 1.8 fusion.8
  179.5 2.4 broadcast_select_fusion.7
  181.9 1.8 fusion.9
  183.9 1.8 fusion
  185.7 2.0 broadcast_select_fusion.3
  187.8 4.1 %fusion.4 = f32[64,128]{1,0:T(8,128)S(1)} fusion(f32[64,7168]{1,0:T(8,128)S(1)} %get-tuple-element.26, f32[64,7168]{1,0:T(8,128)S(1)} %get-tuple-element.25, f32[64,7168]{1,0:T(8,128)S(1)} %get-tuple-element.24, f32[64,7168]{1,0:T(8,128)S(1)} %get-tuple-element.23, f32[64,7168]{1,0:T(8,128)S(1)} %get-tuple-element.22, f32[64,7168]{1,0:T(8,128)S(1)} %get-tuple-element.21, ...), kind=kOutput, calls=%fused_computation.8 | convolution fusion | flops 357826560 | bytes 16547843 | tf_op jit(solution)/shard_map/dot_general | solution.py:40
  192.4 1.8 fusion.7
  194.3 15.2 %collective-permute-done.5.refs_8_ = f32[64,7168]{1,0:T(8,128)} collective-permute-done((f32[64,7168]{1,0:T(8,128)S(1)}, f32[64,7168]{1,0:T(8,128)}, u32[]{:S(2)}, u32[]{:S(2)}) %collective-permute-start.5) | collective-permute-done | bytes 1835040 | tf_op jit(solution)/shard_map/ppermute | solution.py:146
  209.5 4.0 %collective-permute-done.11.refs_9_ = f32[64,7168]{1,0:T(8,128)S(1)} collective-permute-done((f32[64,7168]{1,0:T(8,128)}, f32[64,7168]{1,0:T(8,128)S(1)}, u32[]{:S(2)}, u32[]{:S(2)}) %collective-permute-start.11) | collective-permute-done | bytes 1835040 | tf_op jit(solution)/shard_map/ppermute | solution.py:146
  213.5 2.5 pad_maximum_fusion.3
  216.8 1.7 fusion.57
  218.8 1.6 collective-permute-start.12
  220.3 1.1 collective-permute-start.13
  221.5 2.2 collective-permute-start.14
  224.7 3.5 %collective-permute-done.13 = f32[256,128]{1,0:T(8,128)S(1)} collective-permute-done((f32[256,128]{1,0:T(8,128)S(1)}, f32[256,128]{1,0:T(8,128)S(1)}, u32[]{:S(2)}, u32[]{:S(2)}) %collective-permute-start.13) | collective-permute-done | bytes 131104 | tf_op jit(solution)/shard_map/ppermute | solution.py:51
  229.3 1.7 collective-permute-start.15
  230.9 2.9 %collective-permute-start.16 = (f32[256,128]{1,0:T(8,128)S(1)}, f32[256,128]{1,0:T(8,128)S(1)}, u32[]{:S(2)}, u32[]{:S(2)}) collective-permute-start(f32[256,128]{1,0:T(8,128)S(1)} %fusion.30), channel_id=1, source_target_pairs={{0,64},{8,72},{16,80},{24,88},{32,96},{40,104},{48,112},{56,120},{... | collective-permute-start | bytes 393224 | tf_op jit(solution)/shard_map/ppermute | solution.py:51
  233.8 1.3 collective-permute-start.17
  235.2 1.1 collective-permute-done.15
  236.3 3.0 %collective-permute-done.16 = f32[256,128]{1,0:T(8,128)S(1)} collective-permute-done((f32[256,128]{1,0:T(8,128)S(1)}, f32[256,128]{1,0:T(8,128)S(1)}, u32[]{:S(2)}, u32[]{:S(2)}) %collective-permute-start.16) | collective-permute-done | bytes 131104 | tf_op jit(solution)/shard_map/ppermute | solution.py:51
  239.3 6.6 %collective-permute-start.18 = (f32[256,128]{1,0:T(8,128)S(1)}, f32[256,128]{1,0:T(8,128)S(1)}, u32[]{:S(2)}, u32[]{:S(2)}) collective-permute-start(f32[256,128]{1,0:T(8,128)S(1)} %add_add_fusion), channel_id=1, source_target_pairs={{0,128},{8,136},{16,144},{24,152},{32,160},{40,168},{48,176},{56,1... | collective-permute-start | bytes 393224 | tf_op jit(solution)/shard_map/ppermute | solution.py:51
  246.6 4.1 %collective-permute-done.18 = f32[256,128]{1,0:T(8,128)S(1)} collective-permute-done((f32[256,128]{1,0:T(8,128)S(1)}, f32[256,128]{1,0:T(8,128)S(1)}, u32[]{:S(2)}, u32[]{:S(2)}) %collective-permute-start.18) | collective-permute-done | bytes 131104 | tf_op jit(solution)/shard_map/ppermute | solution.py:51
  251.6 1.5 collective-permute-start.20
  253.1 2.4 collective-permute-start.21
  255.4 5.0 %collective-permute-start.22 = (f32[128,128]{1,0:T(8,128)S(1)}, f32[128,128]{1,0:T(8,128)S(1)}, u32[]{:S(2)}, u32[]{:S(2)}) collective-permute-start(f32[128,128]{1,0:T(8,128)S(1)} %get-tuple-element.49), channel_id=1, source_target_pairs={{0,6},{1,7},{2,0},{3,1},{4,2},{5,3},{6,4},{7,5},{8,14},{9,15},{10,... | collective-permute-start | bytes 196616 | tf_op jit(solution)/shard_map/ppermute | solution.py:146
  261.1 1.3 collective-permute-done.22
  262.4 3.3 %collective-permute-done.23 = f32[128,128]{1,0:T(8,128)S(1)} collective-permute-done((f32[128,128]{1,0:T(8,128)S(1)}, f32[128,128]{1,0:T(8,128)S(1)}, u32[]{:S(2)}, u32[]{:S(2)}) %collective-permute-start.23) | collective-permute-done | bytes 65568 | tf_op jit(solution)/shard_map/ppermute | solution.py:146
  269.0 11.1 %shard_map.37 = f32[128,7168]{1,0:T(8,128)} custom-call(s32[5]{0:T(128)} %stack.89.where_ref, f32[128,7168]{1,0:T(8,128)} %reshape.19.rows_ref, bf16[256,512]{1,0:T(8,128)(2,1)} %pad_maximum_fusion.12.scaled_ref, f32[64,7168]{1,0:T(8,128)} %bitcast.125, f32[64,7168]{1,0:T(8,128)} %collective-permute-done.10.refs_1_, ...), custom_call_target="tpu_custom_call" | custom-call | flops 2818572288 | bytes 22020096 | tf_op jit(solution)/shard_map/pallas_call | solution.py:114
  (91 shorter events, 12.1 us)
Async XLA Ops:
  0.0 45.1 %collective-permute-start.3 = (f32[64,7168]{1,0:T(8,128)}, f32[64,7168]{1,0:T(8,128)}, u32[]{:S(2)}, u32[]{:S(2)}) collective-permute-start(f32[64,7168]{1,0:T(8,128)} %bitcast.122), channel_id=1, source_target_pairs={{2,0},{3,1},{4,2},{5,3},{6,4},{7,5},{10,8},{11,9},{12,10},{13,11},... | collective-permute-start | bytes 5505032 | tf_op jit(solution)/shard_map/ppermute | solution.py:146
  1.3 45.3 %collective-permute-start.1 = (f32[64,7168]{1,0:T(8,128)}, f32[64,7168]{1,0:T(8,128)}, u32[]{:S(2)}, u32[]{:S(2)}) collective-permute-start(f32[64,7168]{1,0:T(8,128)} %bitcast.123), channel_id=1, source_target_pairs={{0,2},{1,3},{2,4},{3,5},{4,6},{5,7},{8,10},{9,11},{10,12},{11,13},... | collective-permute-start | bytes 5505032 | tf_op jit(solution)/shard_map/ppermute | solution.py:146
  7.1 93.9 %collective-permute-start.10 = (f32[64,7168]{1,0:T(8,128)}, f32[64,7168]{1,0:T(8,128)}, u32[]{:S(2)}, u32[]{:S(2)}) collective-permute-start(f32[64,7168]{1,0:T(8,128)} %bitcast.124), channel_id=1, source_target_pairs={{0,1},{1,0},{2,3},{3,2},{4,5},{5,4},{6,7},{7,6},{8,9},{9,8},{10,11... | collective-permute-start | bytes 5505032 | tf_op jit(solution)/shard_map/ppermute | solution.py:146
  10.0 83.5 %collective-permute-start = (f32[16,4,7168]{2,1,0:T(4,128)}, f32[16,4,7168]{2,1,0:T(4,128)}, u32[]{:S(2)}, u32[]{:S(2)}) collective-permute-start(f32[16,4,7168]{2,1,0:T(4,128)} %dynamic-slice_bitcast_fusion.1), channel_id=1, source_target_pairs={{0,128},{8,136},{16,144},{24,152},{32,160},{40,168},{48,176},{56,1... | collective-permute-start | bytes 5505032 | tf_op jit(solution)/shard_map/ppermute | solution.py:167
  22.1 32.2 %all-to-all-start = ((f32[16,4,7168]{2,1,0:T(4,128)}), f32[16,4,7168]{2,1,0:T(4,128)S(1)}, u32[]{:S(2)}, u32[]{:S(2)}) async-start(f32[16,4,7168]{2,1,0:T(4,128)} %dynamic-slice_bitcast_fusion), calls=%async_computation | async-start | bytes 3670016 | tf_op jit(solution)/shard_map/all_to_all | solution.py:159
  45.1 117.0 %collective-permute-start.4 = (f32[64,7168]{1,0:T(8,128)}, f32[64,7168]{1,0:T(8,128)}, u32[]{:S(2)}, u32[]{:S(2)}) collective-permute-start(f32[64,7168]{1,0:T(8,128)} %collective-permute-done.3.refs_2_), channel_id=1, source_target_pairs={{2,0},{3,1},{4,2},{5,3},{10,8},{11,9},{12,10},{13,11},{18,16},{19,... | collective-permute-start | bytes 5505032 | tf_op jit(solution)/shard_map/ppermute | solution.py:146
  46.6 115.5 %collective-permute-start.2 = (f32[64,7168]{1,0:T(8,128)}, f32[64,7168]{1,0:T(8,128)}, u32[]{:S(2)}, u32[]{:S(2)}) collective-permute-start(f32[64,7168]{1,0:T(8,128)} %collective-permute-done.1.refs_6_), channel_id=1, source_target_pairs={{2,4},{3,5},{4,6},{5,7},{10,12},{11,13},{12,14},{13,15},{18,20},{1... | collective-permute-start | bytes 5505032 | tf_op jit(solution)/shard_map/ppermute | solution.py:146
  56.9 44.1 %copy-start.3 = (f32[7168,64]{0,1:T(8,128)S(1)}, f32[7168,64]{0,1:T(8,128)}, u32[]{:S(2)}) copy-start(f32[7168,64]{0,1:T(8,128)} %param.4) | copy-start | bytes 5505028
  56.9 122.6 %collective-permute-start.6 = (f32[64,7168]{1,0:T(8,128)}, f32[64,7168]{1,0:T(8,128)}, u32[]{:S(2)}, u32[]{:S(2)}) collective-permute-start(f32[64,7168]{1,0:T(8,128)} %collective-permute-done.3.refs_2_), channel_id=1, source_target_pairs={{0,1},{1,0},{2,3},{3,2},{4,5},{5,4},{6,7},{7,6},{8,9},{9,8},{10,11... | collective-permute-start | bytes 5505032 | tf_op jit(solution)/shard_map/ppermute | solution.py:146
  93.5 81.0 %collective-permute-start.7 = (f32[64,7168]{1,0:T(8,128)}, f32[64,7168]{1,0:T(8,128)}, u32[]{:S(2)}, u32[]{:S(2)}) collective-permute-start(f32[64,7168]{1,0:T(8,128)} %collective-permute-done.1.refs_6_), channel_id=1, source_target_pairs={{0,1},{1,0},{2,3},{3,2},{4,5},{5,4},{6,7},{7,6},{8,9},{9,8},{10,11... | collective-permute-start | bytes 5505032 | tf_op jit(solution)/shard_map/ppermute | solution.py:146
  93.5 72.9 %all-to-all-start.1 = ((f32[16,4,7168]{2,1,0:T(4,128)}), f32[16,4,7168]{2,1,0:T(4,128)}, u32[]{:S(2)}, u32[]{:S(2)}) async-start(f32[16,4,7168]{2,1,0:T(4,128)} %collective-permute-done), calls=%async_computation.1 | async-start | bytes 3670016 | tf_op jit(solution)/shard_map/all_to_all | solution.py:159
  163.8 23.9 %copy-start.2 = (f32[64,7168]{1,0:T(8,128)}, f32[64,7168]{1,0:T(8,128)S(1)}, u32[]{:S(2)}) copy-start(f32[64,7168]{1,0:T(8,128)S(1)} %broadcast_select_fusion.8.refs_4_) | copy-start | bytes 5505028
  164.3 21.4 %collective-permute-start.8 = (f32[64,7168]{1,0:T(8,128)S(1)}, f32[64,7168]{1,0:T(8,128)}, u32[]{:S(2)}, u32[]{:S(2)}) collective-permute-start(f32[64,7168]{1,0:T(8,128)S(1)} %broadcast_select_fusion.8.refs_4_), channel_id=1, source_target_pairs={{0,1},{1,0},{2,3},{3,2},{4,5},{5,4},{6,7},{7,6},{8,9},{9,8},{10,11... | collective-permute-start | bytes 5505032 | tf_op jit(solution)/shard_map/ppermute | solution.py:146
  164.3 45.2 %collective-permute-start.5 = (f32[64,7168]{1,0:T(8,128)S(1)}, f32[64,7168]{1,0:T(8,128)}, u32[]{:S(2)}, u32[]{:S(2)}) collective-permute-start(f32[64,7168]{1,0:T(8,128)S(1)} %broadcast_select_fusion.8.refs_4_), channel_id=1, source_target_pairs={{4,6},{5,7},{2,0},{3,1},{12,14},{13,15},{10,8},{11,9},{20,22},{21,... | collective-permute-start | bytes 5505032 | tf_op jit(solution)/shard_map/ppermute | solution.py:146
  174.5 3.1 %copy-start = (f32[128,7168]{1,0:T(8,128)S(1)}, f32[128,7168]{1,0:T(8,128)}, u32[]{:S(2)}) copy-start(f32[128,7168]{1,0:T(8,128)} %reshape.19.rows_ref) | copy-start | bytes 11010052
  181.9 1.9 copy-start.6
  181.9 2.0 copy-start.7
  185.7 2.1 copy-start.4
  191.8 2.4 collective-permute-start.9
  209.5 4.0 %collective-permute-start.11 = (f32[64,7168]{1,0:T(8,128)}, f32[64,7168]{1,0:T(8,128)S(1)}, u32[]{:S(2)}, u32[]{:S(2)}) collective-permute-start(f32[64,7168]{1,0:T(8,128)} %collective-permute-done.5.refs_8_), channel_id=1, source_target_pairs={{0,1},{1,0},{2,3},{3,2},{4,5},{5,4},{6,7},{7,6},{8,9},{9,8},{10,11... | collective-permute-start | bytes 5505032 | tf_op jit(solution)/shard_map/ppermute | solution.py:146
  213.5 2.5 copy-start.5
  213.5 3.3 %copy-start.1 = (f32[128,7168]{1,0:T(8,128)S(1)}, f32[128,7168]{1,0:T(8,128)}, u32[]{:S(2)}) copy-start(f32[128,7168]{1,0:T(8,128)} %reshape.19.rows_ref) | copy-start | bytes 11010052
  218.8 5.9 %collective-permute-start.12 = (f32[256,128]{1,0:T(8,128)S(1)}, f32[256,128]{1,0:T(8,128)S(1)}, u32[]{:S(2)}, u32[]{:S(2)}) collective-permute-start(f32[256,128]{1,0:T(8,128)S(1)} %get-tuple-element.55), channel_id=1, source_target_pairs={{0,8},{8,16},{16,24},{24,0},{32,40},{40,48},{48,56},{56,32},{64,72... | collective-permute-start | bytes 393224 | tf_op jit(solution)/shard_map/ppermute | solution.py:51
  220.3 7.9 %collective-permute-start.13 = (f32[256,128]{1,0:T(8,128)S(1)}, f32[256,128]{1,0:T(8,128)S(1)}, u32[]{:S(2)}, u32[]{:S(2)}) collective-permute-start(f32[256,128]{1,0:T(8,128)S(1)} %get-tuple-element.56), channel_id=1, source_target_pairs={{0,16},{8,24},{16,0},{24,8},{32,48},{40,56},{48,32},{56,40},{64,80... | collective-permute-start | bytes 393224 | tf_op jit(solution)/shard_map/ppermute | solution.py:51
  221.5 7.8 %collective-permute-start.14 = (f32[256,128]{1,0:T(8,128)S(1)}, f32[256,128]{1,0:T(8,128)S(1)}, u32[]{:S(2)}, u32[]{:S(2)}) collective-permute-start(f32[256,128]{1,0:T(8,128)S(1)} %get-tuple-element.57), channel_id=1, source_target_pairs={{0,24},{8,0},{16,8},{24,16},{32,56},{40,32},{48,40},{56,48},{64,88... | collective-permute-start | bytes 393224 | tf_op jit(solution)/shard_map/ppermute | solution.py:51
  229.3 7.0 %collective-permute-start.15 = (f32[256,128]{1,0:T(8,128)S(1)}, f32[256,128]{1,0:T(8,128)S(1)}, u32[]{:S(2)}, u32[]{:S(2)}) collective-permute-start(f32[256,128]{1,0:T(8,128)S(1)} %fusion.30), channel_id=1, source_target_pairs={{0,32},{8,40},{16,48},{24,56},{32,64},{40,72},{48,80},{56,88},{64,... | collective-permute-start | bytes 393224 | tf_op jit(solution)/shard_map/ppermute | solution.py:51
  230.9 8.4 %collective-permute-start.16 = (f32[256,128]{1,0:T(8,128)S(1)}, f32[256,128]{1,0:T(8,128)S(1)}, u32[]{:S(2)}, u32[]{:S(2)}) collective-permute-start(f32[256,128]{1,0:T(8,128)S(1)} %fusion.30), channel_id=1, source_target_pairs={{0,64},{8,72},{16,80},{24,88},{32,96},{40,104},{48,112},{56,120},{... | collective-permute-start | bytes 393224 | tf_op jit(solution)/shard_map/ppermute | solution.py:51
  233.8 5.5 %collective-permute-start.17 = (f32[256,128]{1,0:T(8,128)S(1)}, f32[256,128]{1,0:T(8,128)S(1)}, u32[]{:S(2)}, u32[]{:S(2)}) collective-permute-start(f32[256,128]{1,0:T(8,128)S(1)} %fusion.30), channel_id=1, source_target_pairs={{0,96},{8,104},{16,112},{24,120},{32,0},{40,8},{48,16},{56,24},{64... | collective-permute-start | bytes 393224 | tf_op jit(solution)/shard_map/ppermute | solution.py:51
  239.3 27.3 %copy-start.8 = (f32[2,256,256]{2,1,0:T(8,128)S(1)}, f32[2,256,256]{2,1,0:T(8,128)}, u32[]{:S(2)}) copy-start(f32[2,256,256]{2,1,0:T(8,128)} %param.5) | copy-start | bytes 1572868
  239.3 11.3 %collective-permute-start.18 = (f32[256,128]{1,0:T(8,128)S(1)}, f32[256,128]{1,0:T(8,128)S(1)}, u32[]{:S(2)}, u32[]{:S(2)}) collective-permute-start(f32[256,128]{1,0:T(8,128)S(1)} %add_add_fusion), channel_id=1, source_target_pairs={{0,128},{8,136},{16,144},{24,152},{32,160},{40,168},{48,176},{56,1... | collective-permute-start | bytes 393224 | tf_op jit(solution)/shard_map/ppermute | solution.py:51
  250.8 9.7 %collective-permute-start.19 = (f32[128,128]{1,0:T(8,128)S(1)}, f32[128,128]{1,0:T(8,128)S(1)}, u32[]{:S(2)}, u32[]{:S(2)}) collective-permute-start(f32[128,128]{1,0:T(8,128)S(1)} %get-tuple-element.50), channel_id=1, source_target_pairs={{0,24},{8,0},{16,8},{24,16},{32,56},{40,32},{48,40},{56,48},{64,88... | collective-permute-start | bytes 196616 | tf_op jit(solution)/shard_map/ppermute | solution.py:51
  251.6 9.5 %collective-permute-start.20 = (f32[128,128]{1,0:T(8,128)S(1)}, f32[128,128]{1,0:T(8,128)S(1)}, u32[]{:S(2)}, u32[]{:S(2)}) collective-permute-start(f32[128,128]{1,0:T(8,128)S(1)} %get-tuple-element.50), channel_id=1, source_target_pairs={{0,16},{8,24},{16,0},{24,8},{32,48},{40,56},{48,32},{56,40},{64,80... | collective-permute-start | bytes 196616 | tf_op jit(solution)/shard_map/ppermute | solution.py:51
  253.1 8.0 %collective-permute-start.21 = (f32[128,128]{1,0:T(8,128)S(1)}, f32[128,128]{1,0:T(8,128)S(1)}, u32[]{:S(2)}, u32[]{:S(2)}) collective-permute-start(f32[128,128]{1,0:T(8,128)S(1)} %get-tuple-element.50), channel_id=1, source_target_pairs={{0,8},{8,16},{16,24},{24,0},{32,40},{40,48},{48,56},{56,32},{64,72... | collective-permute-start | bytes 196616 | tf_op jit(solution)/shard_map/ppermute | solution.py:51
  255.4 7.0 %collective-permute-start.22 = (f32[128,128]{1,0:T(8,128)S(1)}, f32[128,128]{1,0:T(8,128)S(1)}, u32[]{:S(2)}, u32[]{:S(2)}) collective-permute-start(f32[128,128]{1,0:T(8,128)S(1)} %get-tuple-element.49), channel_id=1, source_target_pairs={{0,6},{1,7},{2,0},{3,1},{4,2},{5,3},{6,4},{7,5},{8,14},{9,15},{10,... | collective-permute-start | bytes 196616 | tf_op jit(solution)/shard_map/ppermute | solution.py:146
  260.5 5.2 %collective-permute-start.23 = (f32[128,128]{1,0:T(8,128)S(1)}, f32[128,128]{1,0:T(8,128)S(1)}, u32[]{:S(2)}, u32[]{:S(2)}) collective-permute-start(f32[128,128]{1,0:T(8,128)S(1)} %get-tuple-element.49), channel_id=1, source_target_pairs={{0,4},{1,5},{2,6},{3,7},{4,0},{5,1},{6,2},{7,3},{8,12},{9,13},{10,... | collective-permute-start | bytes 196616 | tf_op jit(solution)/shard_map/ppermute | solution.py:146
  260.5 6.1 %collective-permute-start.24 = (f32[128,128]{1,0:T(8,128)S(1)}, f32[128,128]{1,0:T(8,128)S(1)}, u32[]{:S(2)}, u32[]{:S(2)}) collective-permute-start(f32[128,128]{1,0:T(8,128)S(1)} %get-tuple-element.49), channel_id=1, source_target_pairs={{0,2},{1,3},{2,4},{3,5},{4,6},{5,7},{6,0},{7,1},{8,10},{9,11},{10,... | collective-permute-start | bytes 196616 | tf_op jit(solution)/shard_map/ppermute | solution.py:146

commit v10 on v7

--- a/solution.py
+++ b/solution.py
@@ -191,9 +191,8 @@
         (last, cross, on_mine, on_two, on_above, on_below)
     )
     last_other = send(last, SIBLING)
-    both = lax.optimization_barrier(jnp.concatenate([last, last_other], axis=0))
+    both = lax.optimization_barrier(ordered(last, last_other, 0))
     on_last = matmul_nt(rows, both)
-    on_last = jnp.where(core == 0, on_last, jnp.roll(on_last, 64, axis=1))
     zero = jnp.zeros_like(on_last)
     slots = jnp.stack(
         [

time: 277 us -> 279 us (level)
    select_n x5 -> x6, other arithmetic: 10.4 us -> 12.9 us  [ordered(): jnp.where(core == 0, piece, other)]
where the time goes in v10:
time: 279 us; the launch traced here: 278 us
  waiting for transfers between devices  150 us (54%)
  starting transfers between devices  63 us (23%)
  local copies, waits for them, and re-layouts  22.1 us (8%)
  other arithmetic  16 us (6%)
  matrix products  14.1 us (5%)
  Pallas kernels  11.1 us (4%)
    ppermute x14, waiting for transfers between devices, send(): return lax.ppermute(value, 'pcol', pairs)  97.8 us
    ppermute x1, waiting for transfers between devices, body(): arriving = over_plane(lax.ppermute(leaving, 'prow', FAR))  36.6 us
    ppermute x10, starting transfers between devices, send(): return lax.ppermute(value, 'prow', pairs)  21.9 us
    ppermute x14, starting transfers between devices, send(): return lax.ppermute(value, 'pcol', pairs)  18.9 us
    all_to_all x2, starting transfers between devices, over_plane(): lax.all_to_all(value, 'prow', split_axis=0, concat_axis=0, tiled=True, ax...  15 us
    dot_general x6, matrix products, matmul_nt(): lax.dot_general(left, right, (((1,), (1,)), ((), ())), precision=lax.Prec...  13.1 us
    select_n x6, other arithmetic, ordered(): jnp.where(core == 0, piece, other)  12.9 us
    pallas_call x1, Pallas kernels, update(): pl.pallas_call(update_kernel, out_shape=jax.ShapeDtypeStruct(rows.shape,...  11.1 us
  transfers between devices with their start and end apart: 27, of which 17 were waited for; matrix products, arithmetic and copies ran while one was open for 16% of the time, Pallas kernels for 0%

profile of v10, /device:TPU:2, one launch (start us, length us, event | category | flops | bytes accessed | tf_op | source)
XLA Modules:
  0.0 277.9 jit_solution(17390278966884571713)
XLA Ops:
  0.0 1.3 collective-permute-start.3
  1.3 5.8 %collective-permute-start.1 = (f32[64,7168]{1,0:T(8,128)}, f32[64,7168]{1,0:T(8,128)}, u32[]{:S(2)}, u32[]{:S(2)}) collective-permute-start(f32[64,7168]{1,0:T(8,128)} %bitcast.123), channel_id=1, source_target_pairs={{0,2},{1,3},{2,4},{3,5},{4,6},{5,7},{8,10},{9,11},{10,12},{11,13},... | collective-permute-start | bytes 5505032 | tf_op jit(solution)/shard_map/ppermute | solution.py:146
  7.1 2.9 %dynamic-slice_bitcast_fusion.1 = f32[16,4,7168]{2,1,0:T(4,128)} fusion(f32[4,32,7168]{2,0,1:T(4,128)} %bitcast.126, s32[]{:T(128)S(6)} %select_n.198), kind=kLoop, calls=%fused_computation.17 | loop fusion | bytes 3670020 | tf_op jit(solution)/shard_map/dynamic_slice | solution.py:166
  10.0 7.2 %collective-permute-start = (f32[16,4,7168]{2,1,0:T(4,128)}, f32[16,4,7168]{2,1,0:T(4,128)}, u32[]{:S(2)}, u32[]{:S(2)}) collective-permute-start(f32[16,4,7168]{2,1,0:T(4,128)} %dynamic-slice_bitcast_fusion.1), channel_id=1, source_target_pairs={{0,128},{8,136},{16,144},{24,152},{32,160},{40,168},{48,176},{56,1... | collective-permute-start | bytes 5505032 | tf_op jit(solution)/shard_map/ppermute | solution.py:167
  19.3 2.9 %dynamic-slice_bitcast_fusion = f32[16,4,7168]{2,1,0:T(4,128)} fusion(f32[4,32,7168]{2,0,1:T(4,128)} %bitcast.127, s32[]{:T(128)S(6)} %select_n.199), kind=kLoop, calls=%fused_computation.16 | loop fusion | bytes 3670020 | tf_op jit(solution)/shard_map/dynamic_slice | solution.py:169
  22.1 7.5 %all-to-all-start = ((f32[16,4,7168]{2,1,0:T(4,128)}), f32[16,4,7168]{2,1,0:T(4,128)S(1)}, u32[]{:S(2)}, u32[]{:S(2)}) async-start(f32[16,4,7168]{2,1,0:T(4,128)} %dynamic-slice_bitcast_fusion), calls=%async_computation | async-start | bytes 3670016 | tf_op jit(solution)/shard_map/all_to_all | solution.py:159
  29.6 15.5 %collective-permute-done.3.refs_2_ = f32[64,7168]{1,0:T(8,128)} collective-permute-done((f32[64,7168]{1,0:T(8,128)}, f32[64,7168]{1,0:T(8,128)}, u32[]{:S(2)}, u32[]{:S(2)}) %collective-permute-start.3) | collective-permute-done | bytes 1835040 | tf_op jit(solution)/shard_map/ppermute | solution.py:146
  45.1 1.3 collective-permute-start.4
  46.6 1.9 collective-permute-start.2
  48.5 5.9 %all-to-all-done = f32[16,4,7168]{2,1,0:T(4,128)S(1)} async-done(((f32[16,4,7168]{2,1,0:T(4,128)}), f32[16,4,7168]{2,1,0:T(4,128)S(1)}, u32[]{:S(2)}, u32[]{:S(2)}) %all-to-all-start) | async-done | bytes 1835040 | tf_op jit(solution)/shard_map/all_to_all | solution.py:159
  54.3 2.6 pad.4
  56.9 36.6 %collective-permute-done = f32[16,4,7168]{2,1,0:T(4,128)} collective-permute-done((f32[16,4,7168]{2,1,0:T(4,128)}, f32[16,4,7168]{2,1,0:T(4,128)}, u32[]{:S(2)}, u32[]{:S(2)}) %collective-permute-start) | collective-permute-done | bytes 1835040 | tf_op jit(solution)/shard_map/ppermute | solution.py:167
  93.5 7.5 %all-to-all-start.1 = ((f32[16,4,7168]{2,1,0:T(4,128)}), f32[16,4,7168]{2,1,0:T(4,128)}, u32[]{:S(2)}, u32[]{:S(2)}) async-start(f32[16,4,7168]{2,1,0:T(4,128)} %collective-permute-done), calls=%async_computation.1 | async-start | bytes 3670016 | tf_op jit(solution)/shard_map/all_to_all | solution.py:159
  101.0 3.7 %broadcast_select_fusion.3 = (f32[64,7168]{1,0:T(8,128)}, f32[64,7168]{1,0:T(8,128)}) fusion(f32[64,7168]{1,0:T(8,128)} %collective-permute-done.9.refs_1_, pred[]{:T(512)S(6)} %eq.21, f32[7168,64]{0,1:T(8,128)S(1)} %copy-done.3), kind=kLoop, calls=%fused_computation.24 | loop fusion | flops 917504 | bytes 7340033 | tf_op jit(solution)/shard_map/jit(_where)/select_n | solution.py:150
  104.7 57.4 %collective-permute-done.4 = f32[64,7168]{1,0:T(8,128)} collective-permute-done((f32[64,7168]{1,0:T(8,128)}, f32[64,7168]{1,0:T(8,128)}, u32[]{:S(2)}, u32[]{:S(2)}) %collective-permute-start.4) | collective-permute-done | bytes 1835040 | tf_op jit(solution)/shard_map/ppermute | solution.py:146
  162.1 1.7 broadcast_select_fusion.10.refs_4_
  164.5 1.5 collective-permute-start.5
  166.6 2.9 %constant_dynamic-update-slice_fusion = f32[32,4,7168]{2,1,0:T(4,128)} fusion(f32[32,4,7168]{2,1,0:T(4,128)} %pad.4, f32[16,4,7168]{2,1,0:T(4,128)} %all-to-all-done.1, s32[]{:T(128)S(6)} %select_n.202), kind=kLoop, calls=%fused_computation.121 | loop fusion | bytes 3670020 | tf_op jit(solution)/shard_map/dynamic_update_slice | solution.py:175
  169.5 5.3 %reshape.19.rows_ref = f32[128,7168]{1,0:T(8,128)} reshape(f32[32,4,7168]{2,1,0:T(4,128)} %constant_dynamic-update-slice_fusion) | data formatting | bytes 7340032 | tf_op jit(solution)/shard_map/reshape | solution.py:177
  174.8 2.5 broadcast_select_fusion.7
  177.9 1.9 fusion.8
  179.8 2.4 broadcast_select_fusion.9
  182.2 1.9 fusion.9
  184.2 1.7 fusion
  185.9 1.8 broadcast_select_fusion.5
  187.8 1.9 fusion.7
  189.7 4.1 %fusion.4 = f32[64,128]{1,0:T(8,128)S(1)} fusion(f32[64,7168]{1,0:T(8,128)S(1)} %get-tuple-element.26, f32[64,7168]{1,0:T(8,128)S(1)} %get-tuple-element.25, f32[64,7168]{1,0:T(8,128)S(1)} %get-tuple-element.24, f32[64,7168]{1,0:T(8,128)S(1)} %get-tuple-element.23, f32[64,7168]{1,0:T(8,128)S(1)} %get-tuple-element.22, f32[64,7168]{1,0:T(8,128)S(1)} %get-tuple-element.21, ...), kind=kOutput, calls=%fused_computation.8 | convolution fusion | flops 357826560 | bytes 16547843 | tf_op jit(solution)/shard_map/dot_general | solution.py:40
  193.7 15.9 %collective-permute-done.5.refs_8_ = f32[64,7168]{1,0:T(8,128)} collective-permute-done((f32[64,7168]{1,0:T(8,128)S(1)}, f32[64,7168]{1,0:T(8,128)}, u32[]{:S(2)}, u32[]{:S(2)}) %collective-permute-start.5) | collective-permute-done | bytes 1835040 | tf_op jit(solution)/shard_map/ppermute | solution.py:146
  209.6 4.0 %collective-permute-done.10.refs_9_ = f32[64,7168]{1,0:T(8,128)S(1)} collective-permute-done((f32[64,7168]{1,0:T(8,128)}, f32[64,7168]{1,0:T(8,128)S(1)}, u32[]{:S(2)}, u32[]{:S(2)}) %collective-permute-start.10) | collective-permute-done | bytes 1835040 | tf_op jit(solution)/shard_map/ppermute | solution.py:146
  213.6 2.5 broadcast_select_fusion.1
  216.5 1.7 copy-done.1
  218.2 1.7 fusion.55
  220.0 1.6 collective-permute-start.11
  221.6 1.1 collective-permute-start.12
  222.7 2.2 collective-permute-start.13
  224.9 3.8 %collective-permute-done.12 = f32[192,128]{1,0:T(8,128)S(1)} collective-permute-done((f32[192,128]{1,0:T(8,128)S(1)}, f32[192,128]{1,0:T(8,128)S(1)}, u32[]{:S(2)}, u32[]{:S(2)}) %collective-permute-start.12) | collective-permute-done | bytes 98336 | tf_op jit(solution)/shard_map/ppermute | solution.py:51
  229.1 1.7 collective-permute-start.14
  230.7 2.9 %collective-permute-start.15 = (f32[192,128]{1,0:T(8,128)S(1)}, f32[192,128]{1,0:T(8,128)S(1)}, u32[]{:S(2)}, u32[]{:S(2)}) collective-permute-start(f32[192,128]{1,0:T(8,128)S(1)} %fusion.35), channel_id=1, source_target_pairs={{0,64},{8,72},{16,80},{24,88},{32,96},{40,104},{48,112},{56,120},{... | collective-permute-start | bytes 294920 | tf_op jit(solution)/shard_map/ppermute | solution.py:51
  233.6 1.3 collective-permute-start.16
  236.0 1.2 collective-permute-done.15
  238.3 6.6 %collective-permute-start.17 = (f32[192,128]{1,0:T(8,128)S(1)}, f32[192,128]{1,0:T(8,128)S(1)}, u32[]{:S(2)}, u32[]{:S(2)}) collective-permute-start(f32[192,128]{1,0:T(8,128)S(1)} %add_add_fusion), channel_id=1, source_target_pairs={{0,128},{8,136},{16,144},{24,152},{32,160},{40,168},{48,176},{56,1... | collective-permute-start | bytes 294920 | tf_op jit(solution)/shard_map/ppermute | solution.py:51
  245.6 2.0 collective-permute-done.17
  247.7 1.7 collective-permute-start.18
  249.4 1.1 collective-permute-start.19
  250.5 1.7 collective-permute-start.20
  252.3 6.1 %collective-permute-start.22 = (f32[128,128]{1,0:T(8,128)S(1)}, f32[128,128]{1,0:T(8,128)S(1)}, u32[]{:S(2)}, u32[]{:S(2)}) collective-permute-start(f32[128,128]{1,0:T(8,128)S(1)} %pad_maximum_fusion.17), channel_id=1, source_target_pairs={{0,6},{1,7},{2,0},{3,1},{4,2},{5,3},{6,4},{7,5},{8,14},{9,15},{10,... | collective-permute-start | bytes 196616 | tf_op jit(solution)/shard_map/ppermute | solution.py:146
  260.9 3.0 %collective-permute-done.23 = f32[128,128]{1,0:T(8,128)S(1)} collective-permute-done((f32[128,128]{1,0:T(8,128)S(1)}, f32[128,128]{1,0:T(8,128)S(1)}, u32[]{:S(2)}, u32[]{:S(2)}) %collective-permute-start.23) | collective-permute-done | bytes 65568 | tf_op jit(solution)/shard_map/ppermute | solution.py:146
  266.8 11.1 %shard_map.37 = f32[128,7168]{1,0:T(8,128)} custom-call(s32[5]{0:T(128)} %stack.89.where_ref, f32[128,7168]{1,0:T(8,128)} %reshape.19.rows_ref, bf16[256,512]{1,0:T(8,128)(2,1)} %pad_maximum_fusion.12.scaled_ref, f32[64,7168]{1,0:T(8,128)} %bitcast.125, f32[64,7168]{1,0:T(8,128)} %collective-permute-done.9.refs_1_, ...), custom_call_target="tpu_custom_call" | custom-call | flops 2818572288 | bytes 22020096 | tf_op jit(solution)/shard_map/pallas_call | solution.py:114
  (93 shorter events, 12.0 us)
Async XLA Ops:
  0.0 45.1 %collective-permute-start.3 = (f32[64,7168]{1,0:T(8,128)}, f32[64,7168]{1,0:T(8,128)}, u32[]{:S(2)}, u32[]{:S(2)}) collective-permute-start(f32[64,7168]{1,0:T(8,128)} %bitcast.122), channel_id=1, source_target_pairs={{2,0},{3,1},{4,2},{5,3},{6,4},{7,5},{10,8},{11,9},{12,10},{13,11},... | collective-permute-start | bytes 5505032 | tf_op jit(solution)/shard_map/ppermute | solution.py:146
  1.3 45.3 %collective-permute-start.1 = (f32[64,7168]{1,0:T(8,128)}, f32[64,7168]{1,0:T(8,128)}, u32[]{:S(2)}, u32[]{:S(2)}) collective-permute-start(f32[64,7168]{1,0:T(8,128)} %bitcast.123), channel_id=1, source_target_pairs={{0,2},{1,3},{2,4},{3,5},{4,6},{5,7},{8,10},{9,11},{10,12},{11,13},... | collective-permute-start | bytes 5505032 | tf_op jit(solution)/shard_map/ppermute | solution.py:146
  7.1 93.9 %collective-permute-start.9 = (f32[64,7168]{1,0:T(8,128)}, f32[64,7168]{1,0:T(8,128)}, u32[]{:S(2)}, u32[]{:S(2)}) collective-permute-start(f32[64,7168]{1,0:T(8,128)} %bitcast.124), channel_id=1, source_target_pairs={{0,1},{1,0},{2,3},{3,2},{4,5},{5,4},{6,7},{7,6},{8,9},{9,8},{10,11... | collective-permute-start | bytes 5505032 | tf_op jit(solution)/shard_map/ppermute | solution.py:146
  10.0 83.5 %collective-permute-start = (f32[16,4,7168]{2,1,0:T(4,128)}, f32[16,4,7168]{2,1,0:T(4,128)}, u32[]{:S(2)}, u32[]{:S(2)}) collective-permute-start(f32[16,4,7168]{2,1,0:T(4,128)} %dynamic-slice_bitcast_fusion.1), channel_id=1, source_target_pairs={{0,128},{8,136},{16,144},{24,152},{32,160},{40,168},{48,176},{56,1... | collective-permute-start | bytes 5505032 | tf_op jit(solution)/shard_map/ppermute | solution.py:167
  22.1 32.2 %all-to-all-start = ((f32[16,4,7168]{2,1,0:T(4,128)}), f32[16,4,7168]{2,1,0:T(4,128)S(1)}, u32[]{:S(2)}, u32[]{:S(2)}) async-start(f32[16,4,7168]{2,1,0:T(4,128)} %dynamic-slice_bitcast_fusion), calls=%async_computation | async-start | bytes 3670016 | tf_op jit(solution)/shard_map/all_to_all | solution.py:159
  45.1 117.0 %collective-permute-start.4 = (f32[64,7168]{1,0:T(8,128)}, f32[64,7168]{1,0:T(8,128)}, u32[]{:S(2)}, u32[]{:S(2)}) collective-permute-start(f32[64,7168]{1,0:T(8,128)} %collective-permute-done.3.refs_2_), channel_id=1, source_target_pairs={{2,0},{3,1},{4,2},{5,3},{10,8},{11,9},{12,10},{13,11},{18,16},{19,... | collective-permute-start | bytes 5505032 | tf_op jit(solution)/shard_map/ppermute | solution.py:146
  46.6 115.5 %collective-permute-start.2 = (f32[64,7168]{1,0:T(8,128)}, f32[64,7168]{1,0:T(8,128)}, u32[]{:S(2)}, u32[]{:S(2)}) collective-permute-start(f32[64,7168]{1,0:T(8,128)} %collective-permute-done.1.refs_6_), channel_id=1, source_target_pairs={{2,4},{3,5},{4,6},{5,7},{10,12},{11,13},{12,14},{13,15},{18,20},{1... | collective-permute-start | bytes 5505032 | tf_op jit(solution)/shard_map/ppermute | solution.py:146
  56.9 44.1 %copy-start.3 = (f32[7168,64]{0,1:T(8,128)S(1)}, f32[7168,64]{0,1:T(8,128)}, u32[]{:S(2)}) copy-start(f32[7168,64]{0,1:T(8,128)} %param.4) | copy-start | bytes 5505028
  56.9 117.9 %collective-permute-start.7 = (f32[64,7168]{1,0:T(8,128)}, f32[64,7168]{1,0:T(8,128)}, u32[]{:S(2)}, u32[]{:S(2)}) collective-permute-start(f32[64,7168]{1,0:T(8,128)} %collective-permute-done.1.refs_6_), channel_id=1, source_target_pairs={{0,1},{1,0},{2,3},{3,2},{4,5},{5,4},{6,7},{7,6},{8,9},{9,8},{10,11... | collective-permute-start | bytes 5505032 | tf_op jit(solution)/shard_map/ppermute | solution.py:146
  93.5 86.3 %collective-permute-start.6 = (f32[64,7168]{1,0:T(8,128)}, f32[64,7168]{1,0:T(8,128)}, u32[]{:S(2)}, u32[]{:S(2)}) collective-permute-start(f32[64,7168]{1,0:T(8,128)} %collective-permute-done.3.refs_2_), channel_id=1, source_target_pairs={{0,1},{1,0},{2,3},{3,2},{4,5},{5,4},{6,7},{7,6},{8,9},{9,8},{10,11... | collective-permute-start | bytes 5505032 | tf_op jit(solution)/shard_map/ppermute | solution.py:146
  93.5 73.1 %all-to-all-start.1 = ((f32[16,4,7168]{2,1,0:T(4,128)}), f32[16,4,7168]{2,1,0:T(4,128)}, u32[]{:S(2)}, u32[]{:S(2)}) async-start(f32[16,4,7168]{2,1,0:T(4,128)} %collective-permute-done), calls=%async_computation.1 | async-start | bytes 3670016 | tf_op jit(solution)/shard_map/all_to_all | solution.py:159
  163.8 25.8 %copy-start.2 = (f32[64,7168]{1,0:T(8,128)}, f32[64,7168]{1,0:T(8,128)S(1)}, u32[]{:S(2)}) copy-start(f32[64,7168]{1,0:T(8,128)S(1)} %broadcast_select_fusion.10.refs_4_) | copy-start | bytes 5505028
  164.5 21.4 %collective-permute-start.8 = (f32[64,7168]{1,0:T(8,128)S(1)}, f32[64,7168]{1,0:T(8,128)}, u32[]{:S(2)}, u32[]{:S(2)}) collective-permute-start(f32[64,7168]{1,0:T(8,128)S(1)} %broadcast_select_fusion.10.refs_4_), channel_id=1, source_target_pairs={{0,1},{1,0},{2,3},{3,2},{4,5},{5,4},{6,7},{7,6},{8,9},{9,8},{10,11... | collective-permute-start | bytes 5505032 | tf_op jit(solution)/shard_map/ppermute | solution.py:146
  164.5 45.2 %collective-permute-start.5 = (f32[64,7168]{1,0:T(8,128)S(1)}, f32[64,7168]{1,0:T(8,128)}, u32[]{:S(2)}, u32[]{:S(2)}) collective-permute-start(f32[64,7168]{1,0:T(8,128)S(1)} %broadcast_select_fusion.10.refs_4_), channel_id=1, source_target_pairs={{4,6},{5,7},{2,0},{3,1},{12,14},{13,15},{10,8},{11,9},{20,22},{21,... | collective-permute-start | bytes 5505032 | tf_op jit(solution)/shard_map/ppermute | solution.py:146
  174.8 3.1 %copy-start = (f32[128,7168]{1,0:T(8,128)S(1)}, f32[128,7168]{1,0:T(8,128)}, u32[]{:S(2)}) copy-start(f32[128,7168]{1,0:T(8,128)} %reshape.19.rows_ref) | copy-start | bytes 11010052
  182.1 1.9 copy-start.6
  182.2 2.0 copy-start.7
  187.7 1.9 copy-start.4
  209.6 4.0 %collective-permute-start.10 = (f32[64,7168]{1,0:T(8,128)}, f32[64,7168]{1,0:T(8,128)S(1)}, u32[]{:S(2)}, u32[]{:S(2)}) collective-permute-start(f32[64,7168]{1,0:T(8,128)} %collective-permute-done.5.refs_8_), channel_id=1, source_target_pairs={{0,1},{1,0},{2,3},{3,2},{4,5},{5,4},{6,7},{7,6},{8,9},{9,8},{10,11... | collective-permute-start | bytes 5505032 | tf_op jit(solution)/shard_map/ppermute | solution.py:146
  213.6 2.5 copy-start.5
  216.1 2.0 copy-start.1
  220.0 4.9 %collective-permute-start.11 = (f32[192,128]{1,0:T(8,128)S(1)}, f32[192,128]{1,0:T(8,128)S(1)}, u32[]{:S(2)}, u32[]{:S(2)}) collective-permute-start(f32[192,128]{1,0:T(8,128)S(1)} %get-tuple-element.54), channel_id=1, source_target_pairs={{0,8},{8,16},{16,24},{24,0},{32,40},{40,48},{48,56},{56,32},{64,72... | collective-permute-start | bytes 294920 | tf_op jit(solution)/shard_map/ppermute | solution.py:51
  221.6 7.2 %collective-permute-start.12 = (f32[192,128]{1,0:T(8,128)S(1)}, f32[192,128]{1,0:T(8,128)S(1)}, u32[]{:S(2)}, u32[]{:S(2)}) collective-permute-start(f32[192,128]{1,0:T(8,128)S(1)} %get-tuple-element.55), channel_id=1, source_target_pairs={{0,16},{8,24},{16,0},{24,8},{32,48},{40,56},{48,32},{56,40},{64,80... | collective-permute-start | bytes 294920 | tf_op jit(solution)/shard_map/ppermute | solution.py:51
  222.7 6.4 %collective-permute-start.13 = (f32[192,128]{1,0:T(8,128)S(1)}, f32[192,128]{1,0:T(8,128)S(1)}, u32[]{:S(2)}, u32[]{:S(2)}) collective-permute-start(f32[192,128]{1,0:T(8,128)S(1)} %get-tuple-element.56), channel_id=1, source_target_pairs={{0,24},{8,0},{16,8},{24,16},{32,56},{40,32},{48,40},{56,48},{64,88... | collective-permute-start | bytes 294920 | tf_op jit(solution)/shard_map/ppermute | solution.py:51
  229.1 30.5 %copy-start.8 = (f32[2,256,256]{2,1,0:T(8,128)S(1)}, f32[2,256,256]{2,1,0:T(8,128)}, u32[]{:S(2)}) copy-start(f32[2,256,256]{2,1,0:T(8,128)} %param.5) | copy-start | bytes 1572868
  229.1 7.0 %collective-permute-start.14 = (f32[192,128]{1,0:T(8,128)S(1)}, f32[192,128]{1,0:T(8,128)S(1)}, u32[]{:S(2)}, u32[]{:S(2)}) collective-permute-start(f32[192,128]{1,0:T(8,128)S(1)} %fusion.35), channel_id=1, source_target_pairs={{0,32},{8,40},{16,48},{24,56},{32,64},{40,72},{48,80},{56,88},{64,... | collective-permute-start | bytes 294920 | tf_op jit(solution)/shard_map/ppermute | solution.py:51
  230.7 6.5 %collective-permute-start.15 = (f32[192,128]{1,0:T(8,128)S(1)}, f32[192,128]{1,0:T(8,128)S(1)}, u32[]{:S(2)}, u32[]{:S(2)}) collective-permute-start(f32[192,128]{1,0:T(8,128)S(1)} %fusion.35), channel_id=1, source_target_pairs={{0,64},{8,72},{16,80},{24,88},{32,96},{40,104},{48,112},{56,120},{... | collective-permute-start | bytes 294920 | tf_op jit(solution)/shard_map/ppermute | solution.py:51
  233.6 4.6 %collective-permute-start.16 = (f32[192,128]{1,0:T(8,128)S(1)}, f32[192,128]{1,0:T(8,128)S(1)}, u32[]{:S(2)}, u32[]{:S(2)}) collective-permute-start(f32[192,128]{1,0:T(8,128)S(1)} %fusion.35), channel_id=1, source_target_pairs={{0,96},{8,104},{16,112},{24,120},{32,0},{40,8},{48,16},{56,24},{64... | collective-permute-start | bytes 294920 | tf_op jit(solution)/shard_map/ppermute | solution.py:51
  238.3 9.2 %collective-permute-start.17 = (f32[192,128]{1,0:T(8,128)S(1)}, f32[192,128]{1,0:T(8,128)S(1)}, u32[]{:S(2)}, u32[]{:S(2)}) collective-permute-start(f32[192,128]{1,0:T(8,128)S(1)} %add_add_fusion), channel_id=1, source_target_pairs={{0,128},{8,136},{16,144},{24,152},{32,160},{40,168},{48,176},{56,1... | collective-permute-start | bytes 294920 | tf_op jit(solution)/shard_map/ppermute | solution.py:51
  247.6 4.7 %collective-permute-start.21 = (f32[64,128]{1,0:T(8,128)S(1)}, f32[64,128]{1,0:T(8,128)S(1)}, u32[]{:S(2)}, u32[]{:S(2)}) collective-permute-start(f32[64,128]{1,0:T(8,128)S(1)} %slice.121), channel_id=1, source_target_pairs={{0,1},{1,0},{2,3},{3,2},{4,5},{5,4},{6,7},{7,6},{8,9},{9,8},{10,11... | collective-permute-start | bytes 98312 | tf_op jit(solution)/shard_map/ppermute | solution.py:146
  247.7 10.7 %collective-permute-start.18 = (f32[128,128]{1,0:T(8,128)S(1)}, f32[128,128]{1,0:T(8,128)S(1)}, u32[]{:S(2)}, u32[]{:S(2)}) collective-permute-start(f32[128,128]{1,0:T(8,128)S(1)} %slice.120), channel_id=1, source_target_pairs={{0,24},{8,0},{16,8},{24,16},{32,56},{40,32},{48,40},{56,48},{64,88... | collective-permute-start | bytes 196616 | tf_op jit(solution)/shard_map/ppermute | solution.py:51
  249.4 10.0 %collective-permute-start.19 = (f32[128,128]{1,0:T(8,128)S(1)}, f32[128,128]{1,0:T(8,128)S(1)}, u32[]{:S(2)}, u32[]{:S(2)}) collective-permute-start(f32[128,128]{1,0:T(8,128)S(1)} %slice.120), channel_id=1, source_target_pairs={{0,16},{8,24},{16,0},{24,8},{32,48},{40,56},{48,32},{56,40},{64,80... | collective-permute-start | bytes 196616 | tf_op jit(solution)/shard_map/ppermute | solution.py:51
  250.5 8.9 %collective-permute-start.20 = (f32[128,128]{1,0:T(8,128)S(1)}, f32[128,128]{1,0:T(8,128)S(1)}, u32[]{:S(2)}, u32[]{:S(2)}) collective-permute-start(f32[128,128]{1,0:T(8,128)S(1)} %slice.120), channel_id=1, source_target_pairs={{0,8},{8,16},{16,24},{24,0},{32,40},{40,48},{48,56},{56,32},{64,72... | collective-permute-start | bytes 196616 | tf_op jit(solution)/shard_map/ppermute | solution.py:51
  252.3 8.6 %collective-permute-start.22 = (f32[128,128]{1,0:T(8,128)S(1)}, f32[128,128]{1,0:T(8,128)S(1)}, u32[]{:S(2)}, u32[]{:S(2)}) collective-permute-start(f32[128,128]{1,0:T(8,128)S(1)} %pad_maximum_fusion.17), channel_id=1, source_target_pairs={{0,6},{1,7},{2,0},{3,1},{4,2},{5,3},{6,4},{7,5},{8,14},{9,15},{10,... | collective-permute-start | bytes 196616 | tf_op jit(solution)/shard_map/ppermute | solution.py:146
  258.4 5.5 %collective-permute-start.23 = (f32[128,128]{1,0:T(8,128)S(1)}, f32[128,128]{1,0:T(8,128)S(1)}, u32[]{:S(2)}, u32[]{:S(2)}) collective-permute-start(f32[128,128]{1,0:T(8,128)S(1)} %pad_maximum_fusion.17), channel_id=1, source_target_pairs={{0,4},{1,5},{2,6},{3,7},{4,0},{5,1},{6,2},{7,3},{8,12},{9,13},{10,... | collective-permute-start | bytes 196616 | tf_op jit(solution)/shard_map/ppermute | solution.py:146
  258.4 6.4 %collective-permute-start.24 = (f32[128,128]{1,0:T(8,128)S(1)}, f32[128,128]{1,0:T(8,128)S(1)}, u32[]{:S(2)}, u32[]{:S(2)}) collective-permute-start(f32[128,128]{1,0:T(8,128)S(1)} %pad_maximum_fusion.17), channel_id=1, source_target_pairs={{0,2},{1,3},{2,4},{3,5},{4,6},{5,7},{6,0},{7,1},{8,10},{9,11},{10,... | collective-permute-start | bytes 196616 | tf_op jit(solution)/shard_map/ppermute | solution.py:146
